TPU v7x, 32 devices: a whole 2x2x4 slice. The times are simulated.
32 devices in a mesh: seq: 4 (over y, x), dp: 8 (over z, core).
Axes of the slice: x: 2, y: 2, z: 4, core: 2. Of those that a mesh axis runs over, the one named last changes fastest.
Arguments:
- hidden_in: bfloat16 [8, 1024, 1536], P('dp', 'seq'), may hold values from -6 to 6
- lengths: int32 [8], P('dp'), may hold values from 256 to 1024, as said below
- routes: int32 [8, 1024, 4], P('dp', 'seq'), may hold values from 0 to 31, all different within a row
- gates: float32 [8, 1024, 4], P('dp', 'seq'), may hold values from 0.1 to 0.4
- priority: int32 [8, 4, 1024], P('dp', 'seq'), may hold values from 0 to 1023, each once within a row
- attn_gain: bfloat16 [1536], P(('seq', 'dp')), may hold values from 0.5 to 1.5
- mlp_gain: bfloat16 [1536], P(('seq', 'dp')), may hold values from 0.5 to 1.5
- w_query: bfloat16 [1536, 1536], P(('seq', 'dp')), may hold values from -0.15625 to 0.15625
- key_projection: bfloat16 [1536, 256], P(('seq', 'dp')), may hold values from -0.15625 to 0.15625
- value_projection: bfloat16 [1536, 256], P(('seq', 'dp')), may hold values from -0.15625 to 0.15625
- w_out: bfloat16 [1536, 1536], P(('seq', 'dp')), may hold values from -2 to 2
- w_gate: bfloat16 [32, 1536, 768], P('dp', 'seq'), may hold values from -0.15625 to 0.15625
- w_up: bfloat16 [32, 1536, 768], P('dp', 'seq'), may hold values from -0.15625 to 0.15625
- w_down: bfloat16 [32, 768, 1536], P('dp', 'seq'), may hold values from -0.21875 to 0.21875
- cotangent: bfloat16 [8, 1024, 1536], P('dp', 'seq'), may hold values from -6 to 6
Outputs:
- layer_out: float32 [8, 1024, 1536], P('dp', 'seq')
- input_grad: float32 [8, 1024, 1536], P('dp', 'seq')
- attn_gain_grad: float32 [1536], P(('seq', 'dp'))
- mlp_gain_grad: float32 [1536], P(('seq', 'dp'))
- query_weight_grad: float32 [1536, 1536], P(('seq', 'dp'))
- key_weight_grad: float32 [1536, 256], P(('seq', 'dp'))
- value_weight_grad: float32 [1536, 256], P(('seq', 'dp'))
- out_weight_grad: float32 [1536, 1536], P(('seq', 'dp'))
- gate_weight_grad: float32 [32, 1536, 768], P('dp', 'seq')
- up_weight_grad: float32 [32, 1536, 768], P('dp', 'seq')
- down_weight_grad: float32 [32, 768, 1536], P('dp', 'seq')
Inputs may be any that keep to these rules, and one draw needn't show every extreme that they name: Positions below lengths[s] of slot s are valid, the rest padding; in every draw some slot is full. `routes`: each token names 4 different experts. `priority`: for each slot and block index, the 1024 entries are a permutation; entry t_local * 4 + k is the claiming rank of the pair of the block's token t_local and its k-th route.
All inputs are finite; a program needn't handle non-finite values.
Results may differ from a plain program's by a relative error of at most 0.015.
Values may be sent and summed in bfloat16 or wider, within the bound.
A program may use at most 256 MiB of HBM per device.

v0:
```python
import math

import jax
import jax.numpy as jnp
from jax import lax
from jax.sharding import PartitionSpec as P

HEAD_DIM = 128
EXPERTS = 32
TOP = 4
CAP = 40


EPSILON = 1e-06
ROPE_BASE = 10000.0
NEG_FILL = -1e30


def rope_angles(positions, head_size):
    half_dim = head_size // 2
    frequency = ROPE_BASE ** (-(2.0 * jnp.arange(half_dim, dtype=jnp.float32)) / head_size)
    angles = positions.astype(jnp.float32)[:, None] * frequency[None, :]
    return (jnp.cos(angles)[:, None, :], jnp.sin(angles)[:, None, :])


def apply_rotary(values, cosine_lookup, sine_lookup):
    half_dim = values.shape[-1] // 2
    lower_half = values[..., :half_dim]
    upper_half = values[..., half_dim:]
    return jnp.concatenate(
        [
            lower_half * cosine_lookup - upper_half * sine_lookup,
            upper_half * cosine_lookup + lower_half * sine_lookup,
        ],
        axis=-1,
    )


def unrotate(incoming, cosine_lookup, sine_lookup):
    half_dim = incoming.shape[-1] // 2
    lower_half = incoming[..., :half_dim]
    upper_half = incoming[..., half_dim:]
    return jnp.concatenate(
        [
            lower_half * cosine_lookup + upper_half * sine_lookup,
            upper_half * cosine_lookup - lower_half * sine_lookup,
        ],
        axis=-1,
    )


def route_slots(route_rows, order_rank, valid_rows, experts, capacity):
    pair_routes = route_rows.reshape(-1)
    pair_count = pair_routes.shape[0]
    is_live = jnp.repeat(valid_rows, route_rows.shape[1])
    onehot = (
        (pair_routes[:, None] == jnp.arange(experts, dtype=jnp.int32)[None, :]) & is_live[:, None]
    ).astype(jnp.int32)
    by_rank = jnp.argsort(order_rank)
    sorted_hot = onehot[by_rank]
    before = jnp.cumsum(sorted_hot, axis=0) - sorted_hot
    rank_sorted = jnp.sum(before * sorted_hot, axis=1)
    claim_rank = rank_sorted[order_rank]
    is_kept = is_live & (claim_rank < capacity)
    target = jnp.where(is_kept, pair_routes * capacity + claim_rank, experts * capacity)
    source_pair = jnp.full((experts * capacity + 1,), pair_count, jnp.int32)
    source_pair = source_pair.at[target].set(jnp.arange(pair_count, dtype=jnp.int32))
    return (source_pair[: experts * capacity], target)


def masked_scores(query_group, key_head, query_pos, key_pos, length, score_scale):
    scores = (
        jnp.einsum("qgd,kd->gqk", query_group, key_head, preferred_element_type=jnp.float32)
        * score_scale
    )
    key_mask = (key_pos[None, :] <= query_pos[:, None]) & (key_pos[None, :] < length)
    return jnp.where(key_mask[None], scores, NEG_FILL)


def head_forward(query_group, key_head, value_head, query_pos, key_pos, length, score_scale):
    scores = masked_scores(query_group, key_head, query_pos, key_pos, length, score_scale)
    row_max = jnp.max(scores, axis=-1, keepdims=True)
    exp_scores = jnp.exp(scores - row_max)
    exp_total = jnp.sum(exp_scores, axis=-1, keepdims=True)
    attn_probs = (exp_scores / exp_total).astype(jnp.bfloat16)
    head_out = jnp.einsum("gqk,kd->qgd", attn_probs, value_head, preferred_element_type=jnp.float32)
    return (head_out, (row_max + jnp.log(exp_total))[..., 0])


def head_backward(
    query_group, key_head, value_head, head_grad, log_total, query_pos, key_pos, length, score_scale
):
    scores = masked_scores(query_group, key_head, query_pos, key_pos, length, score_scale)
    attn_probs = jnp.exp(scores - log_total[..., None])
    prob_grad = jnp.einsum("qgd,kd->gqk", head_grad, value_head, preferred_element_type=jnp.float32)
    row_delta = jnp.sum(attn_probs * prob_grad, axis=-1, keepdims=True)
    score_grad = (attn_probs * (prob_grad - row_delta)).astype(jnp.bfloat16)
    query_part = (
        jnp.einsum("gqk,kd->qgd", score_grad, key_head, preferred_element_type=jnp.float32)
        * score_scale
    )
    key_part = (
        jnp.einsum("gqk,qgd->kd", score_grad, query_group, preferred_element_type=jnp.float32)
        * score_scale
    )
    value_part = jnp.einsum(
        "gqk,qgd->kd",
        attn_probs.astype(jnp.bfloat16),
        head_grad,
        preferred_element_type=jnp.float32,
    )
    return (query_part, key_part, value_part)


def norm_back(values, scale_rows, gain_vec, incoming):
    weighted = incoming * gain_vec
    inner_mean = jnp.mean(weighted * values, axis=-1, keepdims=True)
    values_grad = scale_rows * weighted - values * scale_rows * scale_rows * scale_rows * inner_mean
    return (values_grad, jnp.sum(incoming * values * scale_rows, axis=0))


def split_heads(gathered, kv_heads):
    return gathered.reshape(gathered.shape[0], kv_heads, HEAD_DIM).transpose(1, 0, 2)


def on_device(
    hidden_in,
    lengths,
    routes,
    gates,
    priority,
    attn_gain,
    mlp_gain,
    w_query,
    key_projection,
    value_projection,
    w_out,
    w_gate,
    w_up,
    w_down,
    cotangent,
):
    local_rows = hidden_in.shape[1]
    model_width = hidden_in.shape[2]
    dp_count = lax.axis_size("dp")
    sequence_extent = local_rows * lax.axis_size("seq")
    query_pos = lax.axis_index("seq") * local_rows + jnp.arange(local_rows, dtype=jnp.int32)
    key_pos = jnp.arange(sequence_extent, dtype=jnp.int32)
    length = lengths[0]
    is_valid = query_pos < length
    score_scale = 1.0 / math.sqrt(HEAD_DIM)
    q_heads = w_query.shape[1] // HEAD_DIM
    kv_heads = key_projection.shape[1] // HEAD_DIM
    group_size = q_heads // kv_heads
    pair_count = local_rows * TOP
    cosine_lookup, sine_lookup = rope_angles(query_pos, HEAD_DIM)
    attn_full = (
        lax.all_gather(attn_gain, ("seq", "dp"), axis=0, tiled=True),
        lax.all_gather(mlp_gain, ("seq", "dp"), axis=0, tiled=True),
        lax.all_gather(w_query, ("seq", "dp"), axis=0, tiled=True),
        lax.all_gather(key_projection, ("seq", "dp"), axis=0, tiled=True),
        lax.all_gather(value_projection, ("seq", "dp"), axis=0, tiled=True),
        lax.all_gather(w_out, ("seq", "dp"), axis=0, tiled=True),
    )
    gain_one, gain_two, query_full, key_full, value_full, out_full = attn_full
    expert_full = (
        lax.all_gather(w_gate, "seq", axis=1, tiled=True),
        lax.all_gather(w_up, "seq", axis=1, tiled=True),
        lax.all_gather(w_down, "seq", axis=1, tiled=True),
    )
    gate_full, up_full, down_full = expert_full
    inputs = hidden_in[0].astype(jnp.float32)
    scale_one = lax.rsqrt(jnp.mean(inputs * inputs, axis=-1, keepdims=True) + EPSILON)
    normed = (inputs * scale_one * gain_one.astype(jnp.float32)).astype(jnp.bfloat16)
    query_rows = jnp.dot(normed, query_full, preferred_element_type=jnp.float32)
    key_matrix_rows = jnp.dot(normed, key_full, preferred_element_type=jnp.float32)
    value_matrix_rows = jnp.dot(normed, value_full, preferred_element_type=jnp.float32).astype(
        jnp.bfloat16
    )
    query_rotated = apply_rotary(
        query_rows.reshape(local_rows, q_heads, HEAD_DIM), cosine_lookup, sine_lookup
    ).astype(jnp.bfloat16)
    key_rotated = apply_rotary(
        key_matrix_rows.reshape(local_rows, kv_heads, HEAD_DIM), cosine_lookup, sine_lookup
    ).astype(jnp.bfloat16)
    key_rotated = key_rotated.reshape(local_rows, kv_heads * HEAD_DIM)
    key_all, value_all = (
        lax.all_gather(key_rotated, "seq", axis=0, tiled=True),
        lax.all_gather(value_matrix_rows, "seq", axis=0, tiled=True),
    )
    query_head_groups = query_rotated.reshape(local_rows, kv_heads, group_size, HEAD_DIM).transpose(
        1, 0, 2, 3
    )
    attended, log_total = lax.map(
        lambda operands: head_forward(
            operands[0], operands[1], operands[2], query_pos, key_pos, length, score_scale
        ),
        (query_head_groups, split_heads(key_all, kv_heads), split_heads(value_all, kv_heads)),
    )
    attended = (
        attended.transpose(1, 0, 2, 3).reshape(local_rows, q_heads * HEAD_DIM).astype(jnp.bfloat16)
    )
    branch = jnp.dot(attended, out_full, preferred_element_type=jnp.float32)
    middle = inputs + branch
    scale_two = lax.rsqrt(jnp.mean(middle * middle, axis=-1, keepdims=True) + EPSILON)
    moe_input = (middle * scale_two * gain_two.astype(jnp.float32)).astype(jnp.bfloat16)
    source_pair, target = route_slots(routes[0], priority[0, 0], is_valid, EXPERTS, CAP)
    token_of = jnp.where(source_pair < pair_count, source_pair // TOP, local_rows)
    padded = jnp.concatenate([moe_input, jnp.zeros((1, model_width), jnp.bfloat16)], axis=0)
    send_rows = padded[token_of].reshape(dp_count, -1, CAP, model_width)
    slot_rows = lax.all_to_all(send_rows, "dp", split_axis=0, concat_axis=0, tiled=True)
    gate_pre = jnp.einsum(
        "secd,edf->secf", slot_rows, gate_full, preferred_element_type=jnp.float32
    )
    up_pre = jnp.einsum("secd,edf->secf", slot_rows, up_full, preferred_element_type=jnp.float32)
    expert_hidden = (jax.nn.silu(gate_pre) * up_pre).astype(jnp.bfloat16)
    expert_out = jnp.einsum(
        "secf,efd->secd", expert_hidden, down_full, preferred_element_type=jnp.float32
    )
    rows_in, rows_out, gate_pre, up_pre = (
        slot_rows,
        expert_out.astype(jnp.bfloat16),
        gate_pre,
        up_pre,
    )
    returned = lax.all_to_all(rows_out, "dp", split_axis=0, concat_axis=0, tiled=True)
    flat_back = jnp.concatenate(
        [returned.reshape(-1, model_width), jnp.zeros((1, model_width), jnp.bfloat16)], axis=0
    )
    pair_rows = flat_back[target].reshape(local_rows, TOP, model_width).astype(jnp.float32)
    gate_rows = gates[0]
    layer_out = middle + jnp.sum(gate_rows[:, :, None] * pair_rows, axis=1)
    refreshed = (
        lax.all_gather(attn_gain, ("seq", "dp"), axis=0, tiled=True),
        lax.all_gather(mlp_gain, ("seq", "dp"), axis=0, tiled=True),
        lax.all_gather(w_query, ("seq", "dp"), axis=0, tiled=True),
        lax.all_gather(key_projection, ("seq", "dp"), axis=0, tiled=True),
        lax.all_gather(value_projection, ("seq", "dp"), axis=0, tiled=True),
        lax.all_gather(w_out, ("seq", "dp"), axis=0, tiled=True),
    )
    gain_one, gain_two, query_full, key_full, value_full, out_full = refreshed
    gate_full, up_full, down_full = (
        lax.all_gather(w_gate, "seq", axis=1, tiled=True),
        lax.all_gather(w_up, "seq", axis=1, tiled=True),
        lax.all_gather(w_down, "seq", axis=1, tiled=True),
    )
    key_all, value_all = (
        lax.all_gather(key_rotated, "seq", axis=0, tiled=True),
        lax.all_gather(value_matrix_rows, "seq", axis=0, tiled=True),
    )
    out_grad = cotangent[0].astype(jnp.float32) * is_valid[:, None].astype(jnp.float32)
    pair_grad = (
        (gate_rows[:, :, None] * out_grad[:, None, :])
        .astype(jnp.bfloat16)
        .reshape(pair_count, model_width)
    )
    pair_pad = jnp.concatenate([pair_grad, jnp.zeros((1, model_width), jnp.bfloat16)], axis=0)
    grad_send = pair_pad[source_pair].reshape(dp_count, -1, CAP, model_width)
    grad_rows = lax.all_to_all(grad_send, "dp", split_axis=0, concat_axis=0, tiled=True)
    gate_sigmoid = jax.nn.sigmoid(gate_pre)
    gate_act = gate_pre * gate_sigmoid
    gate_slope = gate_sigmoid * (1.0 + gate_pre * (1.0 - gate_sigmoid))
    expert_hidden = (gate_act * up_pre).astype(jnp.bfloat16)
    hidden_grad = jnp.einsum(
        "secd,efd->secf", grad_rows, down_full, preferred_element_type=jnp.float32
    )
    down_grad = jnp.einsum(
        "secf,secd->efd", expert_hidden, grad_rows, preferred_element_type=jnp.float32
    )
    gate_pre_grad = (hidden_grad * up_pre * gate_slope).astype(jnp.bfloat16)
    up_pre_grad = (hidden_grad * gate_act).astype(jnp.bfloat16)
    gate_grad = jnp.einsum(
        "secd,secf->edf", rows_in, gate_pre_grad, preferred_element_type=jnp.float32
    )
    up_grad = jnp.einsum("secd,secf->edf", rows_in, up_pre_grad, preferred_element_type=jnp.float32)
    row_grad = jnp.einsum(
        "secf,edf->secd", gate_pre_grad, gate_full, preferred_element_type=jnp.float32
    )
    row_grad = (
        row_grad
        + jnp.einsum("secf,edf->secd", up_pre_grad, up_full, preferred_element_type=jnp.float32)
    ).astype(jnp.bfloat16)
    row_back = lax.all_to_all(row_grad, "dp", split_axis=0, concat_axis=0, tiled=True)
    flat_grad = jnp.concatenate(
        [row_back.reshape(-1, model_width), jnp.zeros((1, model_width), jnp.bfloat16)], axis=0
    )
    moe_input_grad = jnp.sum(
        flat_grad[target].reshape(local_rows, TOP, model_width).astype(jnp.float32), axis=1
    )
    middle_norm_grad, gain_two_grad = norm_back(
        middle, scale_two, gain_two.astype(jnp.float32), moe_input_grad
    )
    middle_grad = out_grad + middle_norm_grad
    branch_grad = middle_grad.astype(jnp.bfloat16)
    out_weight_grad = jnp.einsum(
        "tf,td->fd", attended, branch_grad, preferred_element_type=jnp.float32
    )
    attended_grad = jnp.einsum(
        "td,fd->tf", branch_grad, out_full, preferred_element_type=jnp.float32
    ).astype(jnp.bfloat16)
    attended_grad = attended_grad.reshape(local_rows, kv_heads, group_size, HEAD_DIM).transpose(
        1, 0, 2, 3
    )
    query_part, key_part, value_part = lax.map(
        lambda operands: head_backward(
            operands[0],
            operands[1],
            operands[2],
            operands[3],
            operands[4],
            query_pos,
            key_pos,
            length,
            score_scale,
        ),
        (
            query_head_groups,
            split_heads(key_all, kv_heads),
            split_heads(value_all, kv_heads),
            attended_grad,
            log_total,
        ),
    )
    kv_terms = jnp.concatenate(
        [
            key_part.transpose(1, 0, 2).reshape(sequence_extent, kv_heads * HEAD_DIM),
            value_part.transpose(1, 0, 2).reshape(sequence_extent, kv_heads * HEAD_DIM),
        ],
        axis=1,
    )
    kv_mine = lax.psum_scatter(
        kv_terms.astype(jnp.bfloat16), "seq", scatter_dimension=0, tiled=True
    ).astype(jnp.float32)
    kv_width = kv_heads * HEAD_DIM
    key_grad = unrotate(
        kv_mine[:, :kv_width].reshape(local_rows, kv_heads, HEAD_DIM), cosine_lookup, sine_lookup
    )
    key_grad = key_grad.reshape(local_rows, kv_width).astype(jnp.bfloat16)
    value_grad = kv_mine[:, kv_width:].astype(jnp.bfloat16)
    query_grad = unrotate(
        query_part.transpose(1, 0, 2, 3).reshape(local_rows, q_heads, HEAD_DIM),
        cosine_lookup,
        sine_lookup,
    )
    query_grad = query_grad.reshape(local_rows, q_heads * HEAD_DIM).astype(jnp.bfloat16)
    query_weight_grad = jnp.einsum(
        "td,tf->df", normed, query_grad, preferred_element_type=jnp.float32
    )
    key_weight_grad = jnp.einsum("td,tf->df", normed, key_grad, preferred_element_type=jnp.float32)
    value_weight_grad = jnp.einsum(
        "td,tf->df", normed, value_grad, preferred_element_type=jnp.float32
    )
    normed_grad = jnp.einsum(
        "tf,df->td", query_grad, query_full, preferred_element_type=jnp.float32
    )
    normed_grad = normed_grad + jnp.einsum(
        "tf,df->td", key_grad, key_full, preferred_element_type=jnp.float32
    )
    normed_grad = normed_grad + jnp.einsum(
        "tf,df->td", value_grad, value_full, preferred_element_type=jnp.float32
    )
    input_norm_grad, gain_one_grad = norm_back(
        inputs, scale_one, gain_one.astype(jnp.float32), normed_grad
    )
    input_grad = middle_grad + input_norm_grad
    expert_grads = (
        lax.psum_scatter(
            gate_grad.astype(jnp.bfloat16), "seq", scatter_dimension=1, tiled=True
        ).astype(jnp.float32),
        lax.psum_scatter(
            up_grad.astype(jnp.bfloat16), "seq", scatter_dimension=1, tiled=True
        ).astype(jnp.float32),
        lax.psum_scatter(
            down_grad.astype(jnp.bfloat16), "seq", scatter_dimension=1, tiled=True
        ).astype(jnp.float32),
    )
    attn_grads = (
        lax.psum_scatter(gain_one_grad, ("seq", "dp"), scatter_dimension=0, tiled=True),
        lax.psum_scatter(gain_two_grad, ("seq", "dp"), scatter_dimension=0, tiled=True),
        lax.psum_scatter(query_weight_grad, ("seq", "dp"), scatter_dimension=0, tiled=True),
        lax.psum_scatter(key_weight_grad, ("seq", "dp"), scatter_dimension=0, tiled=True),
        lax.psum_scatter(value_weight_grad, ("seq", "dp"), scatter_dimension=0, tiled=True),
        lax.psum_scatter(out_weight_grad, ("seq", "dp"), scatter_dimension=0, tiled=True),
    )
    return (
        layer_out[None],
        input_grad[None],
        attn_grads[0],
        attn_grads[1],
        attn_grads[2],
        attn_grads[3],
        attn_grads[4],
        attn_grads[5],
        expert_grads[0],
        expert_grads[1],
        expert_grads[2],
    )


def solution(mesh):
    return jax.shard_map(
        on_device,
        mesh=mesh,
        in_specs=(
            P("dp", "seq", None),
            P("dp"),
            P("dp", "seq", None),
            P("dp", "seq", None),
            P("dp", "seq", None),
            P(("seq", "dp")),
            P(("seq", "dp")),
            P(("seq", "dp"), None),
            P(("seq", "dp"), None),
            P(("seq", "dp"), None),
            P(("seq", "dp"), None),
            P("dp", "seq", None),
            P("dp", "seq", None),
            P("dp", "seq", None),
            P("dp", "seq", None),
        ),
        out_specs=(
            P("dp", "seq", None),
            P("dp", "seq", None),
            P(("seq", "dp")),
            P(("seq", "dp")),
            P(("seq", "dp"), None),
            P(("seq", "dp"), None),
            P(("seq", "dp"), None),
            P(("seq", "dp"), None),
            P("dp", "seq", None),
            P("dp", "seq", None),
            P("dp", "seq", None),
        ),
        check_vma=False,
    )
```

profile of v0, /device:TPU:0, one launch (start us, length us, event | category | flops | bytes accessed | tf_op | source)
XLA Modules:
  0.0 1561.6 jit_solution(10795423455773729336)
XLA Ops:
  15.3 42.4 %all-reduce.9 = (bf16[1536]{0:T(1024)(128)(2,1)S(1)}, bf16[1536]{0:T(1024)(128)(2,1)}) all-reduce(bf16[1536]{0:T(1024)(128)(2,1)S(1)} %dynamic-update-slice, bf16[1536]{0:T(1024)(128)(2,1)S(1)} %dynamic-update-slice.1), channel_id=1, replica_groups=mesh['seq'=4,'dp'=8] {'seq','dp'}, use_global_device_ids=true, to_apply=%add.4 | all-reduce | flops 3072 | bytes 12288
  58.0 45.2 %all_gather.47 = bf16[1536,256]{1,0:T(8,128)(2,1)S(1)} all-gather(bf16[48,256]{1,0:T(8,128)(2,1)S(1)} %copy-done.41), channel_id=1, replica_groups=mesh['seq'=4,'dp'=8] {'seq','dp'}, dimensions={0}, use_global_device_ids=true | all-gather | bytes 811008 | tf_op jit(solution)/shard_map/all_gather | solution.py:161
  106.4 15.2 all_gather.48
  121.9 43.1 %all_gather.45 = bf16[1536,256]{1,0:T(8,128)(2,1)S(1)} all-gather(bf16[48,256]{1,0:T(8,128)(2,1)} %param.28), channel_id=1, replica_groups=mesh['seq'=4,'dp'=8] {'seq','dp'}, dimensions={0}, use_global_device_ids=true | all-gather | bytes 811008 | tf_op jit(solution)/shard_map/all_gather | solution.py:162
  165.4 15.3 all_gather.46
  233.5 10.6 while.32
  282.1 66.6 %all-to-all-done = bf16[8,4,40,1536]{3,2,1,0:T(8,128)(2,1)} async-done(((bf16[8,4,40,1536]{3,2,1,0:T(8,128)(2,1)}), bf16[8,4,40,1536]{3,2,1,0:T(8,128)(2,1)}, u32[]{:S(2)}, u32[]{:S(2)}) %all-to-all-start) | async-done | bytes 3932192 | tf_op jit(solution)/shard_map/all_to_all | solution.py:211
  374.0 67.9 %all-to-all-done.2 = bf16[8,4,40,1536]{3,2,1,0:T(8,128)(2,1)} async-done(((bf16[8,4,40,1536]{3,2,1,0:T(8,128)(2,1)}), bf16[8,4,40,1536]{3,2,1,0:T(8,128)(2,1)}, u32[]{:S(2)}, u32[]{:S(2)}) %all-to-all-start.2) | async-done | bytes 3932192 | tf_op jit(solution)/shard_map/all_to_all | solution.py:259
  447.5 13.3 fusion.86
  460.8 13.1 fusion.68
  473.9 11.7 fusion.94
  504.3 79.0 %all-to-all-done.3 = bf16[8,4,40,1536]{3,2,1,0:T(8,128)(2,1)} async-done(((bf16[8,4,40,1536]{3,2,1,0:T(8,128)(2,1)}), bf16[8,4,40,1536]{3,2,1,0:T(8,128)(2,1)}, u32[]{:S(2)}, u32[]{:S(2)}) %all-to-all-start.3) | async-done | bytes 3932192 | tf_op jit(solution)/shard_map/all_to_all | solution.py:283
  614.3 61.9 %all-to-all-done.1 = bf16[8,4,40,1536]{3,2,1,0:T(8,128)(2,1)} async-done(((bf16[8,4,40,1536]{3,2,1,0:T(8,128)(2,1)}), bf16[8,4,40,1536]{3,2,1,0:T(8,128)(2,1)}, u32[]{:S(2)}, u32[]{:S(2)}) %all-to-all-start.1) | async-done | bytes 3932192 | tf_op jit(solution)/shard_map/all_to_all | solution.py:226
  709.6 31.6 %while.33 = (s32[]{:T(128)}, f32[2,256,6,128]{1,3,2,0:T(8,128)}, bf16[2,1024,128]{1,2,0:T(8,128)(2,1)}, bf16[2,1024,128]{1,2,0:T(8,128)(2,1)}, bf16[2,1024,128]{...) while((s32[]{:T(128)}, f32[2,256,6,128]{1,3,2,0:T(8,128)}, ...), condition=%wide.region_16.17_spmd.clone.clone.clone, body=%wide.region_14.16_spmd.clone.clone.sunk.clone | while | flops 2037841664 | bytes 84726488 | solution.py:304
  754.9 10.7 bitcast_convert_fusion.2
  767.1 10.5 bitcast_convert_fusion.1
  802.6 37.5 %all-reduce.8 = (f32[1536]{0:T(1024)S(1)}, f32[1536]{0:T(1024)S(1)}) all-reduce(f32[1536]{0:T(1024)S(1)} %get-tuple-element.280, f32[1536]{0:T(1024)S(1)} %copy-done.38), channel_id=3, replica_groups=mesh['seq'=4,'dp'=8] {'seq','dp'}, use_global_device_ids=true, to_apply=%region_20.21.clone | all-reduce | flops 3072 | bytes 24576
  844.3 24.3 %reduce-scatter.23.cloned.1.call-done = bf16[4,192,1536]{2,1,0:T(8,128)(2,1)} async-done(((bf16[4,768,1536]{2,1,0:T(8,128)(2,1)}), bf16[4,192,1536]{2,1,0:T(8,128)(2,1)}) %reduce-scatter.23.cloned.1.call-update) | async-done | bytes 2359312 | tf_op jit(solution)/shard_map/reduce_scatter | solution.py:373
  873.1 94.0 %reduce-scatter.19.cloned.1.call-done = bf16[4,384,768]{2,1,0:T(8,128)(2,1)} async-done(((bf16[4,1536,768]{2,1,0:T(8,128)(2,1)}), bf16[4,384,768]{2,1,0:T(8,128)(2,1)}) %reduce-scatter.19.cloned.1.call-update) | async-done | bytes 2359312 | tf_op jit(solution)/shard_map/reduce_scatter | solution.py:367
  971.3 94.2 %reduce-scatter.21.cloned.1.call-done = bf16[4,384,768]{2,1,0:T(8,128)(2,1)} async-done(((bf16[4,1536,768]{2,1,0:T(8,128)(2,1)}), bf16[4,384,768]{2,1,0:T(8,128)(2,1)}) %reduce-scatter.21.cloned.1.call-update) | async-done | bytes 2359312 | tf_op jit(solution)/shard_map/reduce_scatter | solution.py:370
  1069.8 99.3 %reduce-scatter.13.cloned.1.call-done = f32[48,256]{1,0:T(8,128)} async-done(((f32[1536,256]{1,0:T(8,128)}), f32[48,256]{1,0:T(8,128)}) %reduce-scatter.13.cloned.1.call-update) | async-done | bytes 49168 | tf_op jit(solution)/shard_map/reduce_scatter | solution.py:381
  1169.2 102.8 %reduce-scatter.15.cloned.1.call-done = f32[48,256]{1,0:T(8,128)} async-done(((f32[1536,256]{1,0:T(8,128)}), f32[48,256]{1,0:T(8,128)}) %reduce-scatter.15.cloned.1.call-update) | async-done | bytes 49168 | tf_op jit(solution)/shard_map/reduce_scatter | solution.py:382
  1271.9 141.9 %reduce-scatter.17.cloned.1.call-done = f32[48,1536]{1,0:T(8,128)} async-done(((f32[1536,1536]{1,0:T(8,128)}), f32[48,1536]{1,0:T(8,128)}) %reduce-scatter.17.cloned.1.call-update) | async-done | bytes 294928 | tf_op jit(solution)/shard_map/reduce_scatter | solution.py:383
  1413.8 141.0 %reduce-scatter.11.cloned.1.call-done = f32[48,1536]{1,0:T(8,128)} async-done(((f32[1536,1536]{1,0:T(8,128)}), f32[48,1536]{1,0:T(8,128)}) %reduce-scatter.11.cloned.1.call-update) | async-done | bytes 294928 | tf_op jit(solution)/shard_map/reduce_scatter | solution.py:380
  (312 shorter events, 314.3 us)
Async XLA Ops:
  7.2 211.4 %all-gather.6.cloned.1.call-start = ((), (), s32[]{:S(2)}) async-start(), calls=%async_computation.12 | async-start | bytes 4866048 | tf_op jit(solution)/shard_map/all_gather | solution.py:160
  7.9 236.3 %all-gather.8.cloned.1.call-start = ((), (), s32[]{:S(2)}) async-start(), calls=%async_computation.13 | async-start | bytes 4866048 | tf_op jit(solution)/shard_map/all_gather | solution.py:163
  8.7 344.8 %all-gather.10.cloned.1.call-start = ((), (), s32[]{:S(2)}) async-start(), calls=%async_computation.14 | async-start | bytes 11796480 | tf_op jit(solution)/shard_map/all_gather | solution.py:167
  9.4 48.5 %copy-start.41 = (bf16[48,256]{1,0:T(8,128)(2,1)S(1)}, bf16[48,256]{1,0:T(8,128)(2,1)}, u32[]{:S(2)}) copy-start(bf16[48,256]{1,0:T(8,128)(2,1)} %param.27) | copy-start | bytes 73732
  9.4 354.5 %all-gather.12.cloned.1.call-start = ((), (), s32[]{:S(2)}) async-start(), calls=%async_computation.15 | async-start | bytes 11796480 | tf_op jit(solution)/shard_map/all_gather | solution.py:168
  10.0 437.5 %all-gather.14.cloned.1.call-start = ((), (), s32[]{:S(2)}) async-start(), calls=%async_computation.16 | async-start | bytes 11796480 | tf_op jit(solution)/shard_map/all_gather | solution.py:169
  57.7 167.5 %copy-start.32 = (f32[1536]{0:T(1024)}, f32[1536]{0:T(1024)S(1)}, u32[]{:S(2)}) copy-start(f32[1536]{0:T(1024)S(1)} %convert_element_type.183) | copy-start | bytes 18436
  58.0 107.0 %copy-start.35 = (f32[256]{0:T(256)}, f32[256]{0:T(256)S(1)}, u32[]{:S(2)}) copy-start(f32[256]{0:T(256)S(1)} %add_rsqrt_fusion.1) | copy-start | bytes 3076
  104.7 124.4 %copy-start.26 = (f32[256,64]{0,1:T(8,128)}, f32[256,64]{0,1:T(8,128)S(1)}, u32[]{:S(2)}) copy-start(f32[256,64]{0,1:T(8,128)S(1)} %get-tuple-element.345) | copy-start | bytes 196612
  104.7 124.4 %copy-start.28 = (f32[256,64]{0,1:T(8,128)}, f32[256,64]{0,1:T(8,128)S(1)}, u32[]{:S(2)}) copy-start(f32[256,64]{0,1:T(8,128)S(1)} %get-tuple-element.346) | copy-start | bytes 196612
  255.6 93.1 %all-to-all-start = ((bf16[8,4,40,1536]{3,2,1,0:T(8,128)(2,1)}), bf16[8,4,40,1536]{3,2,1,0:T(8,128)(2,1)}, u32[]{:S(2)}, u32[]{:S(2)}) async-start(bf16[8,4,40,1536]{3,2,1,0:T(8,128)(2,1)} %bitcast.416), calls=%async_computation | async-start | bytes 7864320 | tf_op jit(solution)/shard_map/all_to_all | solution.py:211
  348.7 93.1 %all-to-all-start.2 = ((bf16[8,4,40,1536]{3,2,1,0:T(8,128)(2,1)}), bf16[8,4,40,1536]{3,2,1,0:T(8,128)(2,1)}, u32[]{:S(2)}, u32[]{:S(2)}) async-start(bf16[8,4,40,1536]{3,2,1,0:T(8,128)(2,1)} %bitcast.417), calls=%async_computation.2 | async-start | bytes 7864320 | tf_op jit(solution)/shard_map/all_to_all | solution.py:259
  490.1 93.2 %all-to-all-start.3 = ((bf16[8,4,40,1536]{3,2,1,0:T(8,128)(2,1)}), bf16[8,4,40,1536]{3,2,1,0:T(8,128)(2,1)}, u32[]{:S(2)}, u32[]{:S(2)}) async-start(bf16[8,4,40,1536]{3,2,1,0:T(8,128)(2,1)} %copy.88), calls=%async_computation.3 | async-start | bytes 7864320 | tf_op jit(solution)/shard_map/all_to_all | solution.py:283
  504.3 83.8 %copy-start.48 = (s32[1024,1]{0,1:T(1,128)S(1)}, s32[1024,1]{0,1:T(1,128)}, u32[]{:S(2)}) copy-start(s32[1024,1]{0,1:T(1,128)} %copy-done.47) | copy-start | bytes 12292
  504.3 83.8 %copy-start.18 = (bf16[1024,256]{1,0:T(8,128)(2,1)S(1)}, bf16[1024,256]{1,0:T(8,128)(2,1)}, u32[]{:S(2)}) copy-start(bf16[1024,256]{1,0:T(8,128)(2,1)} %copy-done.17) | copy-start | bytes 1572868
  583.3 92.9 %all-to-all-start.1 = ((bf16[8,4,40,1536]{3,2,1,0:T(8,128)(2,1)}), bf16[8,4,40,1536]{3,2,1,0:T(8,128)(2,1)}, u32[]{:S(2)}, u32[]{:S(2)}) async-start(bf16[8,4,40,1536]{3,2,1,0:T(8,128)(2,1)} %copy.85), calls=%async_computation.1 | async-start | bytes 7864320 | tf_op jit(solution)/shard_map/all_to_all | solution.py:226
  587.9 189.9 %reduce-scatter.9.cloned.1.call-start = ((), (), s32[]{:S(2)}) async-start(), calls=%async_computation.17 | async-start | bytes 1310720 | tf_op jit(solution)/shard_map/reduce_scatter | solution.py:331
  743.6 125.0 %reduce-scatter.23.cloned.1.call-start = ((), (), s32[]{:S(2)}) async-start(), calls=%async_computation.24 | async-start | bytes 11796480 | tf_op jit(solution)/shard_map/reduce_scatter | solution.py:373
  753.3 213.8 %reduce-scatter.19.cloned.1.call-start = ((), (), s32[]{:S(2)}) async-start(), calls=%async_computation.22 | async-start | bytes 11796480 | tf_op jit(solution)/shard_map/reduce_scatter | solution.py:367
  765.6 300.0 %reduce-scatter.21.cloned.1.call-start = ((), (), s32[]{:S(2)}) async-start(), calls=%async_computation.23 | async-start | bytes 11796480 | tf_op jit(solution)/shard_map/reduce_scatter | solution.py:370
  777.7 391.5 %reduce-scatter.13.cloned.1.call-start = ((), (), s32[]{:S(2)}) async-start(), calls=%async_computation.19 | async-start | bytes 1622016 | tf_op jit(solution)/shard_map/reduce_scatter | solution.py:381
  780.6 491.3 %reduce-scatter.15.cloned.1.call-start = ((), (), s32[]{:S(2)}) async-start(), calls=%async_computation.20 | async-start | bytes 1622016 | tf_op jit(solution)/shard_map/reduce_scatter | solution.py:382
  783.4 630.5 %reduce-scatter.17.cloned.1.call-start = ((), (), s32[]{:S(2)}) async-start(), calls=%async_computation.21 | async-start | bytes 9732096 | tf_op jit(solution)/shard_map/reduce_scatter | solution.py:383
  788.5 766.3 %reduce-scatter.11.cloned.1.call-start = ((), (), s32[]{:S(2)}) async-start(), calls=%async_computation.18 | async-start | bytes 9732096 | tf_op jit(solution)/shard_map/reduce_scatter | solution.py:380
  (53 other events, 308.6 us)
Sparse Core Ops, SparseCore 0:
  11.0 67.7 all-gather.5
  81.8 68.0 all-gather.7
  151.8 99.5 all-gather.9
  253.1 96.3 all-gather.11
  351.1 96.3 all-gather.13
  743.7 25.6 reduce-scatter.8
  772.8 95.7 reduce-scatter.22
  872.0 95.0 reduce-scatter.18
  970.5 95.0 reduce-scatter.20
  1072.1 97.0 reduce-scatter.12
  1175.8 96.0 reduce-scatter.14
  1279.2 134.5 reduce-scatter.16
  1420.3 134.4 reduce-scatter.10
where the time goes:
time: 1570 us; the launch traced here: 1560 us
  waiting for transfers between devices  982 us (63%)
  blocking collectives  199 us (13%)
  matrix products  159 us (10%)
  local copies, waits for them, and re-layouts  111 us (7%)
  other arithmetic  75.1 us (5%)
  starting transfers between devices  19.2 us (1%)
  between operations  15.8 us (1%)
    reduce_scatter x1, waiting for transfers between devices, on_device(): lax.psum_scatter(out_weight_grad, ('seq', 'dp'), scatter_dimension=0, til...  142 us
    reduce_scatter x1, waiting for transfers between devices, on_device(): lax.psum_scatter(query_weight_grad, ('seq', 'dp'), scatter_dimension=0, t...  141 us
    reduce_scatter x1, waiting for transfers between devices, on_device(): lax.psum_scatter(value_weight_grad, ('seq', 'dp'), scatter_dimension=0, t...  103 us
    reduce_scatter x1, waiting for transfers between devices, on_device(): lax.psum_scatter(key_weight_grad, ('seq', 'dp'), scatter_dimension=0, til...  99.3 us
    reduce_scatter x1, waiting for transfers between devices, on_device(): lax.psum_scatter(up_grad.astype(jnp.bfloat16), 'seq', scatter_dimension=1...  94.2 us
    reduce_scatter x1, waiting for transfers between devices, on_device(): lax.psum_scatter(gate_grad.astype(jnp.bfloat16), 'seq', scatter_dimension...  94 us
    unnamed x2, blocking collectives  79.8 us
    all_to_all x1, waiting for transfers between devices, on_device(): lax.all_to_all(row_grad, 'dp', split_axis=0, concat_axis=0, tiled=True)  79 us
  transfers between devices with their start and end apart: 17, of which 12 were waited for; matrix products, arithmetic and copies ran while one was open for 15% of the time, Pallas kernels for 0%

commit v1 on v0

v1 whole, which is shorter than its diff:
```python
import math

import jax
import jax.numpy as jnp
from jax import lax
from jax.sharding import PartitionSpec as P

HEAD_DIM = 128
EXPERTS = 32
TOP = 4
CAP = 40

EPSILON = 1e-06
ROPE_BASE = 10000.0
NEG_FILL = -1e30
LANES = 128
BOTH = ("seq", "dp")
BF16 = jnp.bfloat16
F32 = jnp.float32


def rope_angles(positions, head_size):
    half_dim = head_size // 2
    frequency = ROPE_BASE ** (-(2.0 * jnp.arange(half_dim, dtype=F32)) / head_size)
    angles = positions.astype(F32)[:, None] * frequency[None, :]
    return (jnp.cos(angles)[:, None, :], jnp.sin(angles)[:, None, :])


def apply_rotary(values, cosine_lookup, sine_lookup):
    half_dim = values.shape[-1] // 2
    lower_half = values[..., :half_dim]
    upper_half = values[..., half_dim:]
    return jnp.concatenate(
        [
            lower_half * cosine_lookup - upper_half * sine_lookup,
            upper_half * cosine_lookup + lower_half * sine_lookup,
        ],
        axis=-1,
    )


def dot(left, right, contract):
    return lax.dot_general(left, right, (contract, ((), ())), preferred_element_type=F32)


def nn(left, right):
    return dot(left, right, ((1,), (0,)))


def nt(left, right):
    return dot(left, right, ((1,), (1,)))


def tn(left, right):
    return dot(left, right, ((0,), (0,)))


def claim_places(routes, priority, is_valid):
    pair_routes = routes.reshape(-1)
    live = jnp.repeat(is_valid, TOP)
    key = jnp.where(live, pair_routes, -1)
    earlier = (key[None, :] == pair_routes[:, None]) & (priority[None, :] < priority[:, None])
    place = jnp.sum(earlier.astype(F32), axis=1).astype(jnp.int32)
    return pair_routes, place, live & (place < CAP)


def masked_scores(query_group, key_head, query_pos, key_pos, length, score_scale):
    scores = (
        jnp.einsum("qgd,kd->gqk", query_group, key_head, preferred_element_type=F32) * score_scale
    )
    key_mask = (key_pos[None, :] <= query_pos[:, None]) & (key_pos[None, :] < length)
    return jnp.where(key_mask[None], scores, NEG_FILL)


def head_forward(query_group, key_head, value_head, query_pos, key_pos, length, score_scale):
    scores = masked_scores(query_group, key_head, query_pos, key_pos, length, score_scale)
    row_max = jnp.max(scores, axis=-1, keepdims=True)
    exp_scores = jnp.exp(scores - row_max)
    exp_total = jnp.sum(exp_scores, axis=-1, keepdims=True)
    attn_probs = (exp_scores / exp_total).astype(BF16)
    head_out = jnp.einsum("gqk,kd->qgd", attn_probs, value_head, preferred_element_type=F32)
    return (head_out, (row_max + jnp.log(exp_total))[..., 0])


def head_backward(
    query_group, key_head, value_head, head_grad, log_total, query_pos, key_pos, length, score_scale
):
    scores = masked_scores(query_group, key_head, query_pos, key_pos, length, score_scale)
    attn_probs = jnp.exp(scores - log_total[..., None])
    prob_grad = jnp.einsum("qgd,kd->gqk", head_grad, value_head, preferred_element_type=F32)
    row_delta = jnp.sum(attn_probs * prob_grad, axis=-1, keepdims=True)
    score_grad = (attn_probs * (prob_grad - row_delta)).astype(BF16)
    query_part = (
        jnp.einsum("gqk,kd->qgd", score_grad, key_head, preferred_element_type=F32) * score_scale
    )
    key_part = (
        jnp.einsum("gqk,qgd->kd", score_grad, query_group, preferred_element_type=F32) * score_scale
    )
    value_part = jnp.einsum(
        "gqk,qgd->kd", attn_probs.astype(BF16), head_grad, preferred_element_type=F32
    )
    return (query_part, key_part, value_part)


def norm_back(values, scale_rows, gain_vec, incoming):
    weighted = incoming * gain_vec
    inner_mean = jnp.mean(weighted * values, axis=-1, keepdims=True)
    values_grad = scale_rows * weighted - values * scale_rows * scale_rows * scale_rows * inner_mean
    return (values_grad, jnp.sum(incoming * values * scale_rows, axis=0))


def split_heads(gathered, kv_heads):
    return gathered.reshape(gathered.shape[0], kv_heads, HEAD_DIM).transpose(1, 0, 2)


def swap(blocks, axes):
    return lax.all_to_all(blocks, axes, split_axis=0, concat_axis=0, tiled=True)


def on_device(
    hidden_in,
    lengths,
    routes,
    gates,
    priority,
    attn_gain,
    mlp_gain,
    w_query,
    key_projection,
    value_projection,
    w_out,
    w_gate,
    w_up,
    w_down,
    cotangent,
):
    rows = hidden_in.shape[1]
    width = hidden_in.shape[2]
    dp_count = lax.axis_size("dp")
    seq_count = lax.axis_size("seq")
    devices = dp_count * seq_count
    own_experts = w_gate.shape[0]
    sharers = seq_count // own_experts
    hidden_units = w_gate.shape[2]
    my_seq = lax.axis_index("seq")
    extent = rows * seq_count
    query_pos = my_seq * rows + jnp.arange(rows, dtype=jnp.int32)
    key_pos = jnp.arange(extent, dtype=jnp.int32)
    length = lengths[0]
    is_valid = query_pos < length
    score_scale = 1.0 / math.sqrt(HEAD_DIM)
    q_width = w_query.shape[1]
    kv_width = key_projection.shape[1]
    q_heads = q_width // HEAD_DIM
    kv_heads = kv_width // HEAD_DIM
    group_size = q_heads // kv_heads
    cosine_lookup, sine_lookup = rope_angles(query_pos, HEAD_DIM)

    gain_block = jnp.concatenate(
        [attn_gain[:, None], mlp_gain[:, None], jnp.zeros((attn_gain.shape[0], LANES - 2), BF16)],
        axis=1,
    )
    packed = jnp.concatenate([w_query, key_projection, value_projection, gain_block], axis=1)
    packed_full = lax.all_gather(packed, BOTH, axis=0, tiled=True)
    out_full = lax.all_gather(w_out, BOTH, axis=0, tiled=True)
    query_full = packed_full[:, :q_width]
    key_full = packed_full[:, q_width : q_width + kv_width]
    value_full = packed_full[:, q_width + kv_width : q_width + 2 * kv_width]
    gain_one = packed_full[:, q_width + 2 * kv_width].astype(F32)
    gain_two = packed_full[:, q_width + 2 * kv_width + 1].astype(F32)

    gate_full = swap(jnp.repeat(w_gate, sharers, axis=0), "seq").reshape(width, hidden_units)
    up_full = swap(jnp.repeat(w_up, sharers, axis=0), "seq").reshape(width, hidden_units)
    down_full = swap(jnp.repeat(w_down, sharers, axis=0), "seq").reshape(hidden_units, width)

    pair_routes, place, kept = claim_places(routes[0], priority[0, 0], is_valid)
    holder = (pair_routes // own_experts) * seq_count + (pair_routes % own_experts) * sharers
    holder = holder + my_seq * sharers // seq_count
    slots = devices * CAP
    target = jnp.where(kept, holder * CAP + place, slots).reshape(rows, TOP)
    slot_ids = jnp.arange(slots, dtype=jnp.int32)
    hits = target[:, :, None] == slot_ids[None, None, :]
    gate_rows = gates[0]
    token_hot = jnp.any(hits, axis=1).astype(BF16)
    slot_gate = jnp.sum(jnp.where(hits, gate_rows[:, :, None], 0.0), axis=(0, 1))

    live_cotangent = jnp.where(is_valid[:, None], cotangent[0], jnp.zeros((), BF16))
    out_grad = live_cotangent.astype(F32)
    grad_send = (tn(token_hot, live_cotangent) * slot_gate[:, None]).astype(BF16)
    grad_rows = swap(grad_send.reshape(devices, CAP, width), ("dp", "seq")).reshape(slots, width)

    inputs = hidden_in[0].astype(F32)
    scale_one = lax.rsqrt(jnp.mean(inputs * inputs, axis=-1, keepdims=True) + EPSILON)
    normed = (inputs * scale_one * gain_one).astype(BF16)
    query_rows = nn(normed, query_full)
    key_matrix_rows = nn(normed, key_full)
    value_matrix_rows = nn(normed, value_full).astype(BF16)
    query_rotated = apply_rotary(
        query_rows.reshape(rows, q_heads, HEAD_DIM), cosine_lookup, sine_lookup
    ).astype(BF16)
    key_rotated = apply_rotary(
        key_matrix_rows.reshape(rows, kv_heads, HEAD_DIM), cosine_lookup, sine_lookup
    ).astype(BF16)
    key_rotated = key_rotated.reshape(rows, kv_width)
    kv_mine = jnp.concatenate([key_rotated, value_matrix_rows], axis=1)
    kv_all = swap(jnp.broadcast_to(kv_mine[None], (seq_count, rows, 2 * kv_width)), "seq")
    kv_all = kv_all.reshape(extent, 2 * kv_width)
    key_all, value_all = kv_all[:, :kv_width], kv_all[:, kv_width:]
    query_head_groups = query_rotated.reshape(rows, kv_heads, group_size, HEAD_DIM).transpose(
        1, 0, 2, 3
    )
    key_heads, value_heads = split_heads(key_all, kv_heads), split_heads(value_all, kv_heads)
    attended, log_total = lax.map(
        lambda operands: head_forward(
            operands[0], operands[1], operands[2], query_pos, key_pos, length, score_scale
        ),
        (query_head_groups, key_heads, value_heads),
    )
    attended = attended.transpose(1, 0, 2, 3).reshape(rows, q_width).astype(BF16)
    middle = inputs + nn(attended, out_full)
    scale_two = lax.rsqrt(jnp.mean(middle * middle, axis=-1, keepdims=True) + EPSILON)
    moe_input = (middle * scale_two * gain_two).astype(BF16)

    send_rows = tn(token_hot, moe_input).astype(BF16).reshape(devices, CAP, width)
    slot_rows = swap(send_rows, ("dp", "seq")).reshape(slots, width)
    gate_pre = nn(slot_rows, gate_full)
    up_pre = nn(slot_rows, up_full)
    gate_sigmoid = jax.nn.sigmoid(gate_pre)
    gate_act = gate_pre * gate_sigmoid
    gate_slope = gate_sigmoid * (1.0 + gate_pre * (1.0 - gate_sigmoid))
    expert_hidden = (gate_act * up_pre).astype(BF16)
    hidden_grad = nt(grad_rows, down_full)
    gate_pre_grad = (hidden_grad * up_pre * gate_slope).astype(BF16)
    up_pre_grad = (hidden_grad * gate_act).astype(BF16)
    row_grad = (nt(gate_pre_grad, gate_full) + nt(up_pre_grad, up_full)).astype(BF16)
    row_back = swap(row_grad.reshape(devices, CAP, width), ("dp", "seq")).reshape(slots, width)

    gate_grad = tn(slot_rows, gate_pre_grad).astype(BF16)
    up_grad = tn(slot_rows, up_pre_grad).astype(BF16)
    down_grad = tn(expert_hidden, grad_rows).astype(BF16)

    def to_owners(grad):
        pieces = swap(grad.reshape(seq_count, -1, grad.shape[1]), "seq")
        pieces = pieces.reshape((own_experts, sharers) + pieces.shape[1:])
        return jnp.sum(pieces.astype(F32), axis=1)

    expert_grads = (to_owners(gate_grad), to_owners(up_grad), to_owners(down_grad))

    expert_out = nn(expert_hidden, down_full).astype(BF16)
    returned = swap(expert_out.reshape(devices, CAP, width), ("dp", "seq")).reshape(slots, width)
    gate_high = gate_rows.astype(BF16)
    gate_low = (gate_rows - gate_high.astype(F32)).astype(BF16)

    def gate_hot(weights):
        return jnp.sum(
            jnp.where(hits, weights.astype(F32)[:, :, None], 0.0), axis=1
        ).astype(BF16)

    layer_out = middle + nn(gate_hot(gate_high), returned) + nn(gate_hot(gate_low), returned)

    moe_input_grad = nn(token_hot, row_back)
    middle_norm_grad, gain_two_grad = norm_back(middle, scale_two, gain_two, moe_input_grad)
    middle_grad = out_grad + middle_norm_grad
    branch_grad = middle_grad.astype(BF16)
    out_weight_grad = tn(attended, branch_grad)
    attended_grad = nt(branch_grad, out_full).astype(BF16)
    attended_grad = attended_grad.reshape(rows, kv_heads, group_size, HEAD_DIM).transpose(
        1, 0, 2, 3
    )
    query_part, key_part, value_part = lax.map(
        lambda operands: head_backward(
            operands[0],
            operands[1],
            operands[2],
            operands[3],
            operands[4],
            query_pos,
            key_pos,
            length,
            score_scale,
        ),
        (query_head_groups, key_heads, value_heads, attended_grad, log_total),
    )
    kv_terms = jnp.concatenate(
        [
            key_part.transpose(1, 0, 2).reshape(extent, kv_width),
            value_part.transpose(1, 0, 2).reshape(extent, kv_width),
        ],
        axis=1,
    ).astype(BF16)
    kv_back = swap(kv_terms.reshape(seq_count, rows, 2 * kv_width), "seq")
    kv_sum = jnp.sum(kv_back.astype(F32), axis=0)
    key_grad = apply_rotary(
        kv_sum[:, :kv_width].reshape(rows, kv_heads, HEAD_DIM), cosine_lookup, -sine_lookup
    )
    key_grad = key_grad.reshape(rows, kv_width).astype(BF16)
    value_grad = kv_sum[:, kv_width:].astype(BF16)
    query_grad = apply_rotary(
        query_part.transpose(1, 0, 2, 3).reshape(rows, q_heads, HEAD_DIM),
        cosine_lookup,
        -sine_lookup,
    )
    query_grad = query_grad.reshape(rows, q_width).astype(BF16)
    normed_grad = nt(query_grad, query_full) + nt(key_grad, key_full) + nt(value_grad, value_full)
    input_norm_grad, gain_one_grad = norm_back(inputs, scale_one, gain_one, normed_grad)
    input_grad = middle_grad + input_norm_grad

    def with_gain(parts, gain_grad):
        column = jnp.pad(gain_grad[:, None].astype(BF16), ((0, 0), (0, LANES - 1)))
        return jnp.concatenate([p.astype(BF16) for p in parts] + [column], axis=1)

    out_terms = with_gain([out_weight_grad], gain_two_grad)
    out_owned = lax.psum_scatter(out_terms, BOTH, scatter_dimension=0, tiled=True).astype(F32)
    query_terms = with_gain(
        [tn(normed, query_grad), tn(normed, key_grad), tn(normed, value_grad)], gain_one_grad
    )
    owned = lax.psum_scatter(query_terms, BOTH, scatter_dimension=0, tiled=True).astype(F32)
    return (
        layer_out[None],
        input_grad[None],
        owned[:, q_width + 2 * kv_width],
        out_owned[:, width],
        owned[:, :q_width],
        owned[:, q_width : q_width + kv_width],
        owned[:, q_width + kv_width : q_width + 2 * kv_width],
        out_owned[:, :width],
        *expert_grads,
    )


def solution(mesh):
    part = P("dp", "seq", None)
    both = P(BOTH)
    both_rows = P(BOTH, None)
    return jax.shard_map(
        on_device,
        mesh=mesh,
        in_specs=(part, P("dp"), part, part, part, both, both)
        + (both_rows,) * 4
        + (part,) * 4,
        out_specs=(part, part, both, both) + (both_rows,) * 4 + (part,) * 3,
        check_vma=False,
    )
```

time: 1570 us -> 818 us (0.52)
  waiting for transfers between devices: 982 us -> 488 us
  blocking collectives: 199 us -> 0 us
  local copies, waits for them, and re-layouts: 111 us -> 55.3 us
  starting transfers between devices: 19.2 us -> 59.6 us
  other arithmetic: 75.1 us -> 49.7 us
  matrix products: 159 us -> 141 us
    reduce_scatter x8 -> x0, waiting for transfers between devices: 698 us -> none  [the longest x1 142 us: on_device(): lax.psum_scatter(out_weight_grad, ('seq', 'dp'), scatter_dimension=0, til...]
    all_gather x4 -> x0, blocking collectives: 119 us -> none  [the longest x1 45.2 us: on_device(): lax.all_gather(key_projection, ('seq', 'dp'), axis=0, tiled=True)]
    all_gather x5 -> x2, waiting for transfers between devices: 5.74 us -> 86.2 us  [the longest x1 74.3 us: on_device(): packed_full = lax.all_gather(packed, BOTH, axis=0, tiled=True)]
    unnamed x2 -> x0, blocking collectives: 79.8 us -> none
    all_to_all x4 -> x12, waiting for transfers between devices: 275 us -> 339 us  [swap(): return lax.all_to_all(blocks, axes, split_axis=0, concat_axis=0, tiled=True)]
    unnamed x13 -> x6, waiting for transfers between devices: 3.24 us -> 63 us
    all_to_all x4 -> x12, starting transfers between devices: 18.7 us -> 59.3 us  [swap(): return lax.all_to_all(blocks, axes, split_axis=0, concat_axis=0, tiled=True)]
    gather x6 -> x0, local copies, waits for them, and re-layouts: 38 us -> none  [the longest x1 9.89 us: on_device(): flat_back[target].reshape(local_rows, TOP, model_width).astype(jnp.float32)]
  transfers between devices with their start and end apart: 17 -> 16, of which waited for: 12 -> 12; matrix products, arithmetic and copies ran while one was open for 15% -> 26% of each run, Pallas kernels for 0% -> 0%
where the time goes in v1:
time: 818 us; the launch traced here: 809 us
  waiting for transfers between devices  488 us (60%)
  matrix products  141 us (17%)
  starting transfers between devices  59.6 us (7%)
  local copies, waits for them, and re-layouts  55.3 us (7%)
  other arithmetic  49.7 us (6%)
  between operations  15.4 us (2%)
    all_to_all x12, waiting for transfers between devices, swap(): return lax.all_to_all(blocks, axes, split_axis=0, concat_axis=0, tiled=True)  339 us
    dot_general x26, matrix products, dot(): lax.dot_general(left, right, (contract, ((), ())), preferred_element_type...  117 us
    all_gather x1, waiting for transfers between devices, on_device(): packed_full = lax.all_gather(packed, BOTH, axis=0, tiled=True)  74.3 us
    unnamed x6, waiting for transfers between devices  63 us
    all_to_all x12, starting transfers between devices, swap(): return lax.all_to_all(blocks, axes, split_axis=0, concat_axis=0, tiled=True)  59.3 us
    unnamed x76, local copies, waits for them, and re-layouts  24.8 us
  transfers between devices with their start and end apart: 16, of which 12 were waited for; matrix products, arithmetic and copies ran while one was open for 26% of the time, Pallas kernels for 0%

profile of v1, /device:TPU:0, one launch (start us, length us, event | category | flops | bytes accessed | tf_op | source)
XLA Modules:
  0.0 809.5 jit_solution(17693209590262347487)
XLA Ops:
  18.9 74.3 %all-gather.3.cloned.1.call-done = bf16[1536,2176]{1,0:T(8,128)(2,1)} async-done(((bf16[48,2176]{1,0:T(8,128)(2,1)}), bf16[1536,2176]{1,0:T(8,128)(2,1)}) %all-gather.3.cloned.1.call-update) | async-done | bytes 6684688 | tf_op jit(solution)/shard_map/all_gather | solution.py:164
  106.2 12.1 %all-to-all-done = bf16[4,256,512]{1,2,0:T(8,128)(2,1)S(1)} async-done(((bf16[4,256,512]{1,2,0:T(8,128)(2,1)}), bf16[4,256,512]{1,2,0:T(8,128)(2,1)S(1)}, u32[]{:S(2)}, u32[]{:S(2)}) %all-to-all-start) | async-done | bytes 1048608 | tf_op jit(solution)/shard_map/all_to_all | solution.py:117
  143.2 13.5 %all-to-all-done.3 = bf16[4,384,768]{2,1,0:T(8,128)(2,1)} async-done(((bf16[4,384,768]{2,1,0:T(8,128)(2,1)}), bf16[4,384,768]{2,1,0:T(8,128)(2,1)}, u32[]{:S(2)}, u32[]{:S(2)}) %all-to-all-start.3) | async-done | bytes 2359328 | tf_op jit(solution)/shard_map/all_to_all | solution.py:117
  161.4 11.8 %while.32 = (s32[]{:T(128)}, bf16[2,256,6,128]{1,3,2,0:T(8,128)(2,1)S(1)}, f32[2,6,256]{2,1,0:T(8,128)}, bf16[2,1024,128]{1,2,0:T(8,128)(2,1)S(1)}, s32[]{:T(128...) while((s32[]{:T(128)}, ...), condition=%wide.region_4.5_spmd.clone.clone.clone, body=%wide.region_1.4_spmd.clone.clone.sunk.clone | while | flops 824704768 | bytes 21688424 | solution.py:213
  173.2 12.0 %all-gather.5.cloned.1.call-done = bf16[1536,1536]{1,0:T(8,128)(2,1)} async-done(((bf16[48,1536]{1,0:T(8,128)(2,1)}), bf16[1536,1536]{1,0:T(8,128)(2,1)}) %all-gather.5.cloned.1.call-update) | async-done | bytes 4718608 | tf_op jit(solution)/shard_map/all_gather | solution.py:165
  204.9 80.9 %all-to-all-done.1 = bf16[32,40,1536]{2,1,0:T(8,128)(2,1)} async-done(((bf16[32,40,1536]{2,1,0:T(8,128)(2,1)}), bf16[32,40,1536]{2,1,0:T(8,128)(2,1)}, u32[]{:S(2)}, u32[]{:S(2)}) %all-to-all-start.1) | async-done | bytes 3932192 | tf_op jit(solution)/shard_map/all_to_all | solution.py:117
  291.8 8.0 fusion.137
  299.9 8.0 fusion.138
  307.9 72.5 %all-to-all-done.6 = bf16[32,40,1536]{2,1,0:T(8,128)(2,1)} async-done(((bf16[32,40,1536]{2,1,0:T(8,128)(2,1)}), bf16[32,40,1536]{2,1,0:T(8,128)(2,1)}, u32[]{:S(2)}, u32[]{:S(2)}) %all-to-all-start.6) | async-done | bytes 3932192 | tf_op jit(solution)/shard_map/all_to_all | solution.py:117
  380.3 10.8 %multiply_convert_fusion = (bf16[1280,768]{1,0:T(8,128)(2,1)S(1)}, bf16[1280,768]{1,0:T(8,128)(2,1)S(1)}, bf16[1280,768]{1,0:T(8,128)(2,1)}) fusion(f32[1280,768]{1,0:T(8,128)} %fusion.137, f32[1280,768]{1,0:T(8,128)} %fusion.138, bf16[1280,1536]{1,0:T(8,128)(2,1)} %bitcast.33, bf16[768,1536]{1,0:T(8,128)(2,1)} %bitcast.27), kind=kOutput, calls=%fused_computation.99 | convolution fusion | flops 3034644480 | bytes 20054016 | tf_op jit(solution)/shard_map/dot_general | solution.py:43
  397.5 6.9 fusion.71
  410.2 7.6 convolution_convert_fusion.2
  417.8 6.9 convolution_convert_fusion.6
  424.7 6.9 convolution_convert_fusion.5
  431.7 6.6 convolution_convert_fusion.4
  438.3 60.3 %all-to-all-done.7 = bf16[32,40,1536]{2,1,0:T(8,128)(2,1)} async-done(((bf16[32,40,1536]{2,1,0:T(8,128)(2,1)}), bf16[32,40,1536]{2,1,0:T(8,128)(2,1)}, u32[]{:S(2)}, u32[]{:S(2)}) %all-to-all-start.7) | async-done | bytes 3932192 | tf_op jit(solution)/shard_map/all_to_all | solution.py:117
  517.0 7.8 copy.129
  535.5 27.6 %while.33 = (s32[]{:T(128)}, f32[2,256,6,128]{1,3,2,0:T(8,128)}, bf16[2,1024,128]{2,1,0:T(8,128)(2,1)}, bf16[2,1024,128]{2,1,0:T(8,128)(2,1)}, bf16[2,1024,128]{...) while((s32[]{:T(128)}, f32[2,256,6,128]{1,3,2,0:T(8,128)}, ...), condition=%wide.region_14.15_spmd.clone.clone.clone, body=%wide.region_12.14_spmd.clone.clone.sunk.clone | while | flops 2037710592 | bytes 64019724 | solution.py:270
  579.3 14.5 %all-to-all-done.8 = bf16[4,256,512]{2,1,0:T(8,128)(2,1)S(1)} async-done(((bf16[4,256,512]{2,1,0:T(8,128)(2,1)}), bf16[4,256,512]{2,1,0:T(8,128)(2,1)S(1)}, u32[]{:S(2)}, u32[]{:S(2)}) %all-to-all-start.8) | async-done | bytes 1048608 | tf_op jit(solution)/shard_map/all_to_all | solution.py:117
  608.7 16.0 %all-to-all-done.11 = bf16[4,192,1536]{2,1,0:T(8,128)(2,1)} async-done(((bf16[4,192,1536]{2,1,0:T(8,128)(2,1)}), bf16[4,192,1536]{2,1,0:T(8,128)(2,1)}, u32[]{:S(2)}, u32[]{:S(2)}) %all-to-all-start.11) | async-done | bytes 2359328 | tf_op jit(solution)/shard_map/all_to_all | solution.py:117
  624.7 7.1 all-to-all-start.5
  637.7 9.4 %copy.127 = bf16[1536,2176]{1,0:T(8,128)(2,1)} copy(bf16[1536,2176]{0,1:T(8,128)(2,1)} %fusion.73) | data formatting | bytes 13369344
  660.3 63.3 %all-to-all-done.5 = bf16[32,40,1536]{2,1,0:T(8,128)(2,1)} async-done(((bf16[32,40,1536]{2,1,0:T(8,128)(2,1)}), bf16[32,40,1536]{2,1,0:T(8,128)(2,1)}, u32[]{:S(2)}, u32[]{:S(2)}) %all-to-all-start.5) | async-done | bytes 3932192 | tf_op jit(solution)/shard_map/all_to_all | solution.py:117
  736.1 62.2 %reduce-scatter.7.cloned.1.call-done = bf16[48,2176]{1,0:T(8,128)(2,1)} async-done(((bf16[1536,2176]{1,0:T(8,128)(2,1)}), bf16[48,2176]{1,0:T(8,128)(2,1)}) %reduce-scatter.7.cloned.1.call-update) | async-done | bytes 208912
  (246 shorter events, 226.3 us)
Async XLA Ops:
  7.2 85.9 %all-gather.3.cloned.1.call-start = ((), (), s32[]{:S(2)}) async-start(), calls=%async_computation.14 | async-start | bytes 6893568 | tf_op jit(solution)/shard_map/all_gather | solution.py:164
  10.5 87.9 %all-to-all-start.2 = ((bf16[4,384,768]{2,1,0:T(8,128)(2,1)}), bf16[4,384,768]{2,1,0:T(8,128)(2,1)}, u32[]{:S(2)}, u32[]{:S(2)}) async-start(bf16[4,384,768]{2,1,0:T(8,128)(2,1)} %param.30), calls=%async_computation.2 | async-start | bytes 4718592 | tf_op jit(solution)/shard_map/all_to_all | solution.py:117
  15.7 169.4 %all-gather.5.cloned.1.call-start = ((), (), s32[]{:S(2)}) async-start(), calls=%async_computation.15 | async-start | bytes 4866048 | tf_op jit(solution)/shard_map/all_gather | solution.py:165
  17.4 86.9 %copy-start.28 = (pred[256]{0:T(512)(128)(4,1)}, pred[256]{0:T(512)(128)(4,1)S(1)}, u32[]{:S(2)}) copy-start(pred[256]{0:T(512)(128)(4,1)S(1)} %fusion.128) | copy-start | bytes 772
  18.9 119.2 %copy-start.14 = (f32[256,64]{0,1:T(8,128)}, f32[256,64]{0,1:T(8,128)S(1)}, u32[]{:S(2)}) copy-start(f32[256,64]{0,1:T(8,128)S(1)} %get-tuple-element.407) | copy-start | bytes 196612
  18.9 115.4 %copy-start.26 = (f32[256]{0:T(256)}, f32[256]{0:T(256)S(1)}, u32[]{:S(2)}) copy-start(f32[256]{0:T(256)S(1)} %add_rsqrt_fusion.1) | copy-start | bytes 3076
  96.2 38.0 %copy-start.22 = (f32[1536]{0:T(1024)}, f32[1536]{0:T(1024)S(1)}, u32[]{:S(2)}) copy-start(f32[1536]{0:T(1024)S(1)} %get-tuple-element.340) | copy-start | bytes 18436
  99.5 18.7 %all-to-all-start = ((bf16[4,256,512]{1,2,0:T(8,128)(2,1)}), bf16[4,256,512]{1,2,0:T(8,128)(2,1)S(1)}, u32[]{:S(2)}, u32[]{:S(2)}) async-start(bf16[4,256,512]{1,2,0:T(8,128)(2,1)} %broadcast_in_dim.142), calls=%async_computation | async-start | bytes 2097152 | tf_op jit(solution)/shard_map/all_to_all | solution.py:117
  118.3 38.4 %all-to-all-start.3 = ((bf16[4,384,768]{2,1,0:T(8,128)(2,1)}), bf16[4,384,768]{2,1,0:T(8,128)(2,1)}, u32[]{:S(2)}, u32[]{:S(2)}) async-start(bf16[4,384,768]{2,1,0:T(8,128)(2,1)} %param.31), calls=%async_computation.3 | async-start | bytes 4718592 | tf_op jit(solution)/shard_map/all_to_all | solution.py:117
  156.7 36.0 %all-to-all-start.4 = ((bf16[4,192,1536]{2,1,0:T(8,128)(2,1)}), bf16[4,192,1536]{2,1,0:T(8,128)(2,1)}, u32[]{:S(2)}, u32[]{:S(2)}) async-start(bf16[4,192,1536]{2,1,0:T(8,128)(2,1)} %param.32), calls=%async_computation.4 | async-start | bytes 4718592 | tf_op jit(solution)/shard_map/all_to_all | solution.py:117
  189.4 317.7 %copy-start = (f32[256,1536]{1,0:T(8,128)}, f32[256,1536]{1,0:T(8,128)S(1)}, u32[]{:S(2)}) copy-start(f32[256,1536]{1,0:T(8,128)S(1)} %get-tuple-element.409) | copy-start | bytes 4718596
  192.7 93.1 %all-to-all-start.1 = ((bf16[32,40,1536]{2,1,0:T(8,128)(2,1)}), bf16[32,40,1536]{2,1,0:T(8,128)(2,1)}, u32[]{:S(2)}, u32[]{:S(2)}) async-start(bf16[32,40,1536]{2,1,0:T(8,128)(2,1)} %bitcast.377), calls=%async_computation.1 | async-start | bytes 7864320 | tf_op jit(solution)/shard_map/all_to_all | solution.py:117
  285.8 94.5 %all-to-all-start.6 = ((bf16[32,40,1536]{2,1,0:T(8,128)(2,1)}), bf16[32,40,1536]{2,1,0:T(8,128)(2,1)}, u32[]{:S(2)}, u32[]{:S(2)}) async-start(bf16[32,40,1536]{2,1,0:T(8,128)(2,1)} %bitcast.391), calls=%async_computation.6 | async-start | bytes 7864320 | tf_op jit(solution)/shard_map/all_to_all | solution.py:117
  404.4 94.2 %all-to-all-start.7 = ((bf16[32,40,1536]{2,1,0:T(8,128)(2,1)}), bf16[32,40,1536]{2,1,0:T(8,128)(2,1)}, u32[]{:S(2)}, u32[]{:S(2)}) async-start(bf16[32,40,1536]{2,1,0:T(8,128)(2,1)} %bitcast.390), calls=%async_computation.7 | async-start | bytes 7864320 | tf_op jit(solution)/shard_map/all_to_all | solution.py:117
  498.6 32.3 %all-to-all-start.9 = ((bf16[4,384,768]{2,1,0:T(8,128)(2,1)}), bf16[4,384,768]{2,1,0:T(8,128)(2,1)}, u32[]{:S(2)}, u32[]{:S(2)}) async-start(bf16[4,384,768]{2,1,0:T(8,128)(2,1)} %bitcast.394), calls=%async_computation.9 | async-start | bytes 4718592 | tf_op jit(solution)/shard_map/all_to_all | solution.py:117
  503.1 230.3 %reduce-scatter.9.cloned.1.call-start = ((), (), s32[]{:S(2)}) async-start(), calls=%async_computation.17 | async-start | bytes 5271552
  530.9 37.1 %all-to-all-start.10 = ((bf16[4,384,768]{2,1,0:T(8,128)(2,1)}), bf16[4,384,768]{2,1,0:T(8,128)(2,1)}, u32[]{:S(2)}, u32[]{:S(2)}) async-start(bf16[4,384,768]{2,1,0:T(8,128)(2,1)} %bitcast.393), calls=%async_computation.10 | async-start | bytes 4718592 | tf_op jit(solution)/shard_map/all_to_all | solution.py:117
  568.0 25.8 %all-to-all-start.8 = ((bf16[4,256,512]{2,1,0:T(8,128)(2,1)}), bf16[4,256,512]{2,1,0:T(8,128)(2,1)S(1)}, u32[]{:S(2)}, u32[]{:S(2)}) async-start(bf16[4,256,512]{2,1,0:T(8,128)(2,1)} %pad_maximum_fusion), calls=%async_computation.8 | async-start | bytes 2097152 | tf_op jit(solution)/shard_map/all_to_all | solution.py:117
  579.3 19.3 %copy-start.27 = (f32[256]{0:T(256)S(1)}, f32[256]{0:T(256)}, u32[]{:S(2)}) copy-start(f32[256]{0:T(256)} %copy-done.26) | copy-start | bytes 3076
  593.8 30.9 %all-to-all-start.11 = ((bf16[4,192,1536]{2,1,0:T(8,128)(2,1)}), bf16[4,192,1536]{2,1,0:T(8,128)(2,1)}, u32[]{:S(2)}, u32[]{:S(2)}) async-start(bf16[4,192,1536]{2,1,0:T(8,128)(2,1)} %bitcast.392), calls=%async_computation.11 | async-start | bytes 4718592 | tf_op jit(solution)/shard_map/all_to_all | solution.py:117
  624.7 98.9 %all-to-all-start.5 = ((bf16[32,40,1536]{2,1,0:T(8,128)(2,1)}), bf16[32,40,1536]{2,1,0:T(8,128)(2,1)}, u32[]{:S(2)}, u32[]{:S(2)}) async-start(bf16[32,40,1536]{2,1,0:T(8,128)(2,1)} %bitcast.389), calls=%async_computation.5 | async-start | bytes 7864320 | tf_op jit(solution)/shard_map/all_to_all | solution.py:117
  631.8 166.6 %reduce-scatter.7.cloned.1.call-start = ((), (), s32[]{:S(2)}) async-start(), calls=%async_computation.16 | async-start | bytes 6893568
  655.6 68.0 %copy-start.1 = (f32[256,1536]{1,0:T(8,128)S(1)}, f32[256,1536]{1,0:T(8,128)}, u32[]{:S(2)}) copy-start(f32[256,1536]{1,0:T(8,128)} %copy-done) | copy-start | bytes 4718596
  655.6 68.0 %copy-start.12 = (bf16[256,1280]{1,0:T(8,128)(2,1)S(1)}, bf16[256,1280]{1,0:T(8,128)(2,1)}, u32[]{:S(2)}) copy-start(bf16[256,1280]{1,0:T(8,128)(2,1)} %get-tuple-element.347) | copy-start | bytes 1966084
  (35 other events, 196.1 us)
Sparse Core Ops, SparseCore 0:
  11.6 81.4 all-gather.2
  96.2 88.8 all-gather.4
  525.0 136.9 reduce-scatter.8
  668.4 129.9 reduce-scatter.6

commit v2 on v1

--- a/solution.py
+++ b/solution.py
@@ -1,8 +1,11 @@
+import functools
 import math
 
 import jax
 import jax.numpy as jnp
 from jax import lax
+from jax.experimental import pallas as pl
+from jax.experimental.pallas import tpu as pltpu
 from jax.sharding import PartitionSpec as P
 
 HEAD_DIM = 128
@@ -115,6 +118,62 @@
 
 def swap(blocks, axes):
     return lax.all_to_all(blocks, axes, split_axis=0, concat_axis=0, tiled=True)
+
+
+MESH_IDS = pl.DeviceIdType.MESH
+
+
+def exchange_kernel(count, n, block_of, *refs):
+    sources, targets = refs[:n], refs[n : 2 * n]
+    send_sems, recv_sems, local_sems = refs[2 * n :]
+    me = lax.axis_index("seq")
+    barrier = pltpu.get_barrier_semaphore()
+    for step in range(1, count):
+        peer = lax.rem(me + step, count)
+        pl.semaphore_signal(barrier, inc=1, device_id={"seq": peer}, device_id_type=MESH_IDS)
+    pl.semaphore_wait(barrier, count - 1)
+    copies = []
+    for i in range(n):
+        for step in range(1, count):
+            peer = lax.rem(me + step, count)
+            copy = pltpu.make_async_remote_copy(
+                src_ref=block_of(sources[i], peer),
+                dst_ref=targets[i].at[me],
+                send_sem=send_sems.at[i, step - 1],
+                recv_sem=recv_sems.at[i, step - 1],
+                device_id={"seq": peer},
+                device_id_type=MESH_IDS,
+            )
+            copy.start()
+            copies.append(copy)
+        copy = pltpu.make_async_copy(
+            block_of(sources[i], me), targets[i].at[me], local_sems.at[i]
+        )
+        copy.start()
+        copies.append(copy)
+    for copy in copies:
+        copy.wait()
+
+
+def seq_exchange(arrays, collective_id, block_of, block_shapes, name):
+    count, n = lax.axis_size("seq"), len(arrays)
+    sent = sum(math.prod(shape) for shape in block_shapes) * (count - 1) * 2
+    return pl.pallas_call(
+        functools.partial(exchange_kernel, count, n, block_of),
+        out_shape=[jax.ShapeDtypeStruct((count,) + shape, BF16) for shape in block_shapes],
+        in_specs=[pl.BlockSpec(memory_space=pl.ANY)] * n,
+        out_specs=[pl.BlockSpec(memory_space=pl.ANY)] * n,
+        scratch_shapes=[
+            pltpu.SemaphoreType.DMA((n, count - 1)),
+            pltpu.SemaphoreType.DMA((n, count - 1)),
+            pltpu.SemaphoreType.DMA((n,)),
+        ],
+        compiler_params=pltpu.CompilerParams(
+            collective_id=collective_id, vmem_limit_bytes=4 << 20
+        ),
+        cost_estimate=pl.CostEstimate(flops=0, bytes_accessed=20 * sent, transcendentals=0),
+        name=name,
+    )(*arrays)
 
 
 def on_device(
@@ -161,18 +220,6 @@
         axis=1,
     )
     packed = jnp.concatenate([w_query, key_projection, value_projection, gain_block], axis=1)
-    packed_full = lax.all_gather(packed, BOTH, axis=0, tiled=True)
-    out_full = lax.all_gather(w_out, BOTH, axis=0, tiled=True)
-    query_full = packed_full[:, :q_width]
-    key_full = packed_full[:, q_width : q_width + kv_width]
-    value_full = packed_full[:, q_width + kv_width : q_width + 2 * kv_width]
-    gain_one = packed_full[:, q_width + 2 * kv_width].astype(F32)
-    gain_two = packed_full[:, q_width + 2 * kv_width + 1].astype(F32)
-
-    gate_full = swap(jnp.repeat(w_gate, sharers, axis=0), "seq").reshape(width, hidden_units)
-    up_full = swap(jnp.repeat(w_up, sharers, axis=0), "seq").reshape(width, hidden_units)
-    down_full = swap(jnp.repeat(w_down, sharers, axis=0), "seq").reshape(hidden_units, width)
-
     pair_routes, place, kept = claim_places(routes[0], priority[0, 0], is_valid)
     holder = (pair_routes // own_experts) * seq_count + (pair_routes % own_experts) * sharers
     holder = holder + my_seq * sharers // seq_count
@@ -187,7 +234,18 @@
     live_cotangent = jnp.where(is_valid[:, None], cotangent[0], jnp.zeros((), BF16))
     out_grad = live_cotangent.astype(F32)
     grad_send = (tn(token_hot, live_cotangent) * slot_gate[:, None]).astype(BF16)
+    grad_send, hidden_in, packed, w_out = lax.optimization_barrier(
+        (grad_send, hidden_in, packed, w_out)
+    )
     grad_rows = swap(grad_send.reshape(devices, CAP, width), ("dp", "seq")).reshape(slots, width)
+
+    packed_full = lax.all_gather(packed, BOTH, axis=0, tiled=True)
+    out_full = lax.all_gather(w_out, BOTH, axis=0, tiled=True)
+    query_full = packed_full[:, :q_width]
+    key_full = packed_full[:, q_width : q_width + kv_width]
+    value_full = packed_full[:, q_width + kv_width : q_width + 2 * kv_width]
+    gain_one = packed_full[:, q_width + 2 * kv_width].astype(F32)
+    gain_two = packed_full[:, q_width + 2 * kv_width + 1].astype(F32)
 
     inputs = hidden_in[0].astype(F32)
     scale_one = lax.rsqrt(jnp.mean(inputs * inputs, axis=-1, keepdims=True) + EPSILON)
@@ -203,7 +261,9 @@
     ).astype(BF16)
     key_rotated = key_rotated.reshape(rows, kv_width)
     kv_mine = jnp.concatenate([key_rotated, value_matrix_rows], axis=1)
-    kv_all = swap(jnp.broadcast_to(kv_mine[None], (seq_count, rows, 2 * kv_width)), "seq")
+    (kv_all,) = seq_exchange(
+        [kv_mine], 1, lambda ref, peer: ref, [(rows, 2 * kv_width)], "gather_keys"
+    )
     kv_all = kv_all.reshape(extent, 2 * kv_width)
     key_all, value_all = kv_all[:, :kv_width], kv_all[:, kv_width:]
     query_head_groups = query_rotated.reshape(rows, kv_heads, group_size, HEAD_DIM).transpose(
@@ -222,7 +282,20 @@
     moe_input = (middle * scale_two * gain_two).astype(BF16)
 
     send_rows = tn(token_hot, moe_input).astype(BF16).reshape(devices, CAP, width)
+    send_rows, grad_rows, w_gate, w_up, w_down = lax.optimization_barrier(
+        (send_rows, grad_rows, w_gate, w_up, w_down)
+    )
     slot_rows = swap(send_rows, ("dp", "seq")).reshape(slots, width)
+    gate_full, up_full, down_full = seq_exchange(
+        [w_gate, w_up, w_down],
+        2,
+        lambda ref, peer: ref.at[peer // sharers],
+        [w_gate.shape[1:], w_up.shape[1:], w_down.shape[1:]],
+        "gather_expert",
+    )
+    gate_full = gate_full.reshape(width, hidden_units)
+    up_full = up_full.reshape(width, hidden_units)
+    down_full = down_full.reshape(hidden_units, width)
     gate_pre = nn(slot_rows, gate_full)
     up_pre = nn(slot_rows, up_full)
     gate_sigmoid = jax.nn.sigmoid(gate_pre)
@@ -239,25 +312,25 @@
     up_grad = tn(slot_rows, up_pre_grad).astype(BF16)
     down_grad = tn(expert_hidden, grad_rows).astype(BF16)
 
-    def to_owners(grad):
-        pieces = swap(grad.reshape(seq_count, -1, grad.shape[1]), "seq")
-        pieces = pieces.reshape((own_experts, sharers) + pieces.shape[1:])
-        return jnp.sum(pieces.astype(F32), axis=1)
-
-    expert_grads = (to_owners(gate_grad), to_owners(up_grad), to_owners(down_grad))
+    pieces = seq_exchange(
+        [g.reshape(seq_count, -1, g.shape[1]) for g in (gate_grad, up_grad, down_grad)],
+        3,
+        lambda ref, peer: ref.at[peer],
+        [w_gate.shape[1:], w_up.shape[1:], w_down.shape[1:]],
+        "return_expert_grads",
+    )
+
+    row_back, *pieces = lax.optimization_barrier((row_back, *pieces))
+
+    def owned_sum(piece):
+        piece = piece.reshape((own_experts, sharers) + piece.shape[1:])
+        return jnp.sum(piece.astype(F32), axis=1)
+
+    expert_grads = [owned_sum(piece) for piece in pieces]
 
     expert_out = nn(expert_hidden, down_full).astype(BF16)
+    expert_out, row_back = lax.optimization_barrier((expert_out, row_back))
     returned = swap(expert_out.reshape(devices, CAP, width), ("dp", "seq")).reshape(slots, width)
-    gate_high = gate_rows.astype(BF16)
-    gate_low = (gate_rows - gate_high.astype(F32)).astype(BF16)
-
-    def gate_hot(weights):
-        return jnp.sum(
-            jnp.where(hits, weights.astype(F32)[:, :, None], 0.0), axis=1
-        ).astype(BF16)
-
-    layer_out = middle + nn(gate_hot(gate_high), returned) + nn(gate_hot(gate_low), returned)
-
     moe_input_grad = nn(token_hot, row_back)
     middle_norm_grad, gain_two_grad = norm_back(middle, scale_two, gain_two, moe_input_grad)
     middle_grad = out_grad + middle_norm_grad
@@ -288,7 +361,13 @@
         ],
         axis=1,
     ).astype(BF16)
-    kv_back = swap(kv_terms.reshape(seq_count, rows, 2 * kv_width), "seq")
+    (kv_back,) = seq_exchange(
+        [kv_terms.reshape(seq_count, rows, 2 * kv_width)],
+        4,
+        lambda ref, peer: ref.at[peer],
+        [(rows, 2 * kv_width)],
+        "return_key_grads",
+    )
     kv_sum = jnp.sum(kv_back.astype(F32), axis=0)
     key_grad = apply_rotary(
         kv_sum[:, :kv_width].reshape(rows, kv_heads, HEAD_DIM), cosine_lookup, -sine_lookup
@@ -314,7 +393,18 @@
     query_terms = with_gain(
         [tn(normed, query_grad), tn(normed, key_grad), tn(normed, value_grad)], gain_one_grad
     )
+    returned, query_terms = lax.optimization_barrier((returned, query_terms))
     owned = lax.psum_scatter(query_terms, BOTH, scatter_dimension=0, tiled=True).astype(F32)
+    gate_high = gate_rows.astype(BF16)
+    gate_low = (gate_rows - gate_high.astype(F32)).astype(BF16)
+
+    def gate_hot(weights):
+        return jnp.sum(
+            jnp.where(hits, weights.astype(F32)[:, :, None], 0.0), axis=1
+        ).astype(BF16)
+
+    layer_out = middle + nn(gate_hot(gate_high), returned) + nn(gate_hot(gate_low), returned)
+
     return (
         layer_out[None],
         input_grad[None],

time: 818 us -> 818 us (level)
  Pallas kernels: 0 us -> 284 us
  waiting for transfers between devices: 488 us -> 238 us
  starting transfers between devices: 59.6 us -> 19.8 us
  matrix products: 141 us -> 125 us
  local copies, waits for them, and re-layouts: 55.3 us -> 69.4 us
  other arithmetic: 49.7 us -> 59.6 us
    all_to_all x12 -> x4, waiting for transfers between devices: 339 us -> 12.8 us  [swap(): return lax.all_to_all(blocks, axes, split_axis=0, concat_axis=0, tiled=True)]
    pallas_call x0 -> x4, Pallas kernels: none -> 284 us  [seq_exchange(): pl.pallas_call(functools.partial(exchange_kernel, count, n, block_of), ou...]
    unnamed x6, waiting for transfers between devices: 63 us -> 108 us
    all_to_all x12 -> x4, starting transfers between devices: 59.3 us -> 19.6 us  [swap(): return lax.all_to_all(blocks, axes, split_axis=0, concat_axis=0, tiled=True)]
    all_gather x1, waiting for transfers between devices: 74.3 us -> 108 us  [on_device(): packed_full = lax.all_gather(packed, BOTH, axis=0, tiled=True)]
    dot_general x26, matrix products: 117 us -> 97.1 us  [dot(): lax.dot_general(left, right, (contract, ((), ())), preferred_element_type...]
    unnamed x76 -> x106, local copies, waits for them, and re-layouts: 24.8 us -> 38.7 us
    concatenate x2, other arithmetic: 8.44 us -> 16.8 us  [with_gain(): return jnp.concatenate([p.astype(BF16) for p in parts] + [column], axis=1)]
  transfers between devices with their start and end apart: 16 -> 8, of which waited for: 12 -> 4; matrix products, arithmetic and copies ran while one was open for 26% -> 22% of each run, Pallas kernels for 0% -> 35%
where the time goes in v2:
time: 818 us; the launch traced here: 812 us
  Pallas kernels  284 us (35%)
  waiting for transfers between devices  238 us (29%)
  matrix products  125 us (15%)
  local copies, waits for them, and re-layouts  69.4 us (8%)
  other arithmetic  59.6 us (7%)
  starting transfers between devices  19.8 us (2%)
  between operations  15.9 us (2%)
    pallas_call x4, Pallas kernels, seq_exchange(): pl.pallas_call(functools.partial(exchange_kernel, count, n, block_of), ou...  284 us
    unnamed x6, waiting for transfers between devices  108 us
    all_gather x1, waiting for transfers between devices, on_device(): packed_full = lax.all_gather(packed, BOTH, axis=0, tiled=True)  108 us
    dot_general x26, matrix products, dot(): lax.dot_general(left, right, (contract, ((), ())), preferred_element_type...  97.1 us
    unnamed x106, local copies, waits for them, and re-layouts  38.7 us
    all_to_all x4, starting transfers between devices, swap(): return lax.all_to_all(blocks, axes, split_axis=0, concat_axis=0, tiled=True)  19.6 us
    concatenate x2, other arithmetic, with_gain(): return jnp.concatenate([p.astype(BF16) for p in parts] + [column], axis=1)  16.8 us
  transfers between devices with their start and end apart: 8, of which 4 were waited for; matrix products, arithmetic and copies ran while one was open for 22% of the time, Pallas kernels for 35%

profile of v2, /device:TPU:0, one launch (start us, length us, event | category | flops | bytes accessed | tf_op | source)
XLA Modules:
  0.0 811.5 jit_solution(12744787586953750952)
XLA Ops:
  24.6 7.4 all-to-all-start
  34.1 107.5 %all-gather.3.cloned.1.call-done = bf16[1536,2176]{1,0:T(8,128)(2,1)} async-done(((bf16[48,2176]{1,0:T(8,128)(2,1)}), bf16[1536,2176]{1,0:T(8,128)(2,1)}) %all-gather.3.cloned.1.call-update) | async-done | bytes 6684688 | tf_op jit(solution)/shard_map/all_gather | solution.py:242
  141.6 4.8 slice_bitcast_fusion
  146.4 6.8 copy.121
  167.0 19.6 %gather_keys.1 = bf16[4,256,512]{2,1,0:T(8,128)(2,1)S(1)} custom-call(bf16[256,512]{1,0:T(8,128)(2,1)S(1)} %pad_maximum_fusion.1.refs_0_), custom_call_target="tpu_custom_call" | custom-call | bytes 15728640 | tf_op jit(solution)/shard_map/gather_keys/pallas_call | solution.py:161
  191.1 10.6 %while.32 = (s32[]{:T(128)}, bf16[2,256,6,128]{1,3,2,0:T(8,128)(2,1)S(1)}, f32[2,6,256]{2,1,0:T(8,128)S(1)}, bf16[2,1024,128]{1,2,0:T(8,128)(2,1)S(1)}, s32[]{:T...) while((s32[]{:T(128)}, ...), condition=%wide.region_7.8_spmd.clone.clone.clone, body=%wide.region_4.7_spmd.clone.clone.sunk.clone | while | flops 824704768 | bytes 21692512 | solution.py:273
  201.7 9.5 %all-gather.5.cloned.1.call-done = bf16[1536,1536]{1,0:T(8,128)(2,1)} async-done(((bf16[48,1536]{1,0:T(8,128)(2,1)}), bf16[1536,1536]{1,0:T(8,128)(2,1)}) %all-gather.5.cloned.1.call-update) | async-done | bytes 4718608 | tf_op jit(solution)/shard_map/all_gather | solution.py:243
  226.7 124.1 %gather_expert.1 = (bf16[4,384,768]{2,1,0:T(8,128)(2,1)S(1)}, bf16[4,384,768]{2,1,0:T(8,128)(2,1)S(1)}, bf16[4,192,1536]{2,1,0:T(8,128)(2,1)S(1)}) custom-call(bf16[4,384,768]{2,1,0:T(8,128)(2,1)S(1)} %copy-done, bf16[4,384,768]{2,1,0:T(8,128)(2,1)S(1)} %copy-done.1, bf16[4,192,1536]{2,1,0:T(8,128)(2,1)S(1)} %copy-done.2), custom_call_target="tpu_custom_call" | custom-call | bytes 106168320 | tf_op jit(solution)/shard_map/gather_expert/pallas_call | solution.py:161
  355.1 6.2 fusion.138
  361.4 5.5 fusion.137
  366.9 6.6 multiply_convert_fusion
  376.9 5.3 fusion.71
  386.5 6.2 convolution_convert_fusion.5
  392.7 5.4 convolution_convert_fusion.6
  398.1 5.8 convolution_convert_fusion.4
  403.9 110.2 %return_expert_grads.1 = (bf16[4,384,768]{2,1,0:T(8,128)(2,1)S(1)}, bf16[4,384,768]{2,1,0:T(8,128)(2,1)S(1)}, bf16[4,192,1536]{2,1,0:T(8,128)(2,1)S(1)}) custom-call(bf16[4,384,768]{2,1,0:T(8,128)(2,1)S(1)} %bitcast.378, bf16[4,384,768]{2,1,0:T(8,128)(2,1)S(1)} %bitcast.377, bf16[4,192,1536]{2,1,0:T(8,128)(2,1)S(1)} %bitcast.379), custom_call_target="tpu_custom_call" | custom-call | bytes 106168320 | tf_op jit(solution)/shard_map/return_expert_grads/pallas_call | solution.py:161
  531.1 7.7 copy.144
  538.8 5.1 convolution_convert_fusion.9
  550.4 32.6 %while.33 = (s32[]{:T(128)}, f32[2,256,6,128]{1,3,2,0:T(8,128)}, bf16[2,1024,128]{2,1,0:T(8,128)(2,1)}, bf16[2,1024,128]{2,1,0:T(8,128)(2,1)}, bf16[2,1024,128]{...) while((s32[]{:T(128)}, f32[2,256,6,128]{1,3,2,0:T(8,128)}, ...), condition=%wide.region_13.14_spmd.clone.clone.clone, body=%wide.region_11.13_spmd.clone.clone.sunk.clone | while | flops 2037710592 | bytes 75554056 | solution.py:343
  588.8 29.9 %return_key_grads.1 = bf16[4,256,512]{2,1,0:T(8,128)(2,1)S(1)} custom-call(bf16[4,256,512]{2,1,0:T(8,128)(2,1)S(1)} %pad_maximum_fusion.refs_0_), custom_call_target="tpu_custom_call" | custom-call | bytes 15728640 | tf_op jit(solution)/shard_map/return_key_grads/pallas_call | solution.py:161
  631.8 14.2 %fusion.73 = bf16[1536,2176]{0,1:T(8,128)(2,1)} fusion(bf16[1536,1]{0,1:T(2,128)(2,1)S(1)} %convert_element_type.313, bf16[1536,256]{0,1:T(8,128)(2,1)S(1)} %convolution_convert_fusion.8, bf16[1536,256]{0,1:T(8,128)(2,1)S(1)} %convolution_convert_fusion.7, bf16[1536,1536]{0,1:T(8,128)(2,1)S(1)} %convolution_convert_fusion), kind=kLoop, calls=%fused_computation.88 | loop fusion | flops 33423360 | bytes 12979200 | tf_op jit(solution)/shard_map/concatenate | solution.py:389
  646.0 12.8 %all-to-all-done.3 = bf16[32,40,1536]{2,1,0:T(8,128)(2,1)} async-done(((bf16[32,40,1536]{2,1,0:T(8,128)(2,1)}), bf16[32,40,1536]{2,1,0:T(8,128)(2,1)}, u32[]{:S(2)}, u32[]{:S(2)}) %all-to-all-start.3) | async-done | bytes 3932192 | tf_op jit(solution)/shard_map/all_to_all | solution.py:120
  658.8 9.6 %copy.142 = bf16[1536,2176]{1,0:T(8,128)(2,1)} copy(bf16[1536,2176]{0,1:T(8,128)(2,1)} %fusion.73) | data formatting | bytes 13369344
  693.1 107.0 %reduce-scatter.7.cloned.1.call-done = bf16[48,2176]{1,0:T(8,128)(2,1)} async-done(((bf16[1536,2176]{1,0:T(8,128)(2,1)}), bf16[48,2176]{1,0:T(8,128)(2,1)}) %reduce-scatter.7.cloned.1.call-update) | async-done | bytes 208912
  (262 shorter events, 178.0 us)
Async XLA Ops:
  7.2 134.4 %all-gather.3.cloned.1.call-start = ((), (), s32[]{:S(2)}) async-start(), calls=%async_computation.6 | async-start | bytes 6893568 | tf_op jit(solution)/shard_map/all_gather | solution.py:242
  9.3 10.0 %copy-start.45 = (pred[256]{0:T(512)(128)(4,1)}, pred[256]{0:T(512)(128)(4,1)S(1)}, u32[]{:S(2)}) copy-start(pred[256]{0:T(512)(128)(4,1)S(1)} %fusion.129) | copy-start | bytes 772
  14.0 9.7 %copy-start.30 = (pred[256,1280]{1,0:T(8,128)(4,1)}, pred[256,1280]{1,0:T(8,128)(4,1)S(1)}, u32[]{:S(2)}) copy-start(pred[256,1280]{1,0:T(8,128)(4,1)S(1)} %fusion.74) | copy-start | bytes 983044
  24.6 8.3 %copy-start.19 = (bf16[1,256,1536]{2,1,0:T(8,128)(2,1)S(1)}, bf16[1,256,1536]{2,1,0:T(8,128)(2,1)}, u32[]{:S(2)}) copy-start(bf16[1,256,1536]{2,1,0:T(8,128)(2,1)} %param.19) | copy-start | bytes 2359300
  24.6 194.9 %all-to-all-start = ((bf16[32,40,1536]{2,1,0:T(8,128)(2,1)}), bf16[32,40,1536]{2,1,0:T(8,128)(2,1)}, u32[]{:S(2)}, u32[]{:S(2)}) async-start(bf16[32,40,1536]{2,1,0:T(8,128)(2,1)} %bitcast.395), calls=%async_computation | async-start | bytes 7864320 | tf_op jit(solution)/shard_map/all_to_all | solution.py:120
  32.0 179.2 %all-gather.5.cloned.1.call-start = ((), (), s32[]{:S(2)}) async-start(), calls=%async_computation.7 | async-start | bytes 4866048 | tf_op jit(solution)/shard_map/all_gather | solution.py:243
  33.1 132.3 %copy-start.43 = (f32[256]{0:T(256)}, f32[256]{0:T(256)S(1)}, u32[]{:S(2)}) copy-start(f32[256]{0:T(256)S(1)} %add_rsqrt_fusion.1) | copy-start | bytes 3076
  34.1 131.2 %copy-start.32 = (f32[256,64]{0,1:T(8,128)}, f32[256,64]{0,1:T(8,128)S(1)}, u32[]{:S(2)}) copy-start(f32[256,64]{0,1:T(8,128)S(1)} %get-tuple-element.453) | copy-start | bytes 196612
  157.2 8.3 %copy-start.39 = (f32[1536]{0:T(1024)}, f32[1536]{0:T(1024)S(1)}, u32[]{:S(2)}) copy-start(f32[1536]{0:T(1024)S(1)} %get-tuple-element.386) | copy-start | bytes 18436
  201.7 13.4 %copy-start.14 = (bf16[2,256,6,128]{3,1,2,0:T(8,128)(2,1)}, bf16[2,256,6,128]{3,1,2,0:T(8,128)(2,1)S(1)}, u32[]{:S(2)}) copy-start(bf16[2,256,6,128]{3,1,2,0:T(8,128)(2,1)S(1)} %get-tuple-element.692) | copy-start | bytes 2359300
  201.7 13.4 %copy-start.22 = (bf16[2,256,6,128]{1,3,2,0:T(8,128)(2,1)}, bf16[2,256,6,128]{1,3,2,0:T(8,128)(2,1)S(1)}, u32[]{:S(2)}) copy-start(bf16[2,256,6,128]{1,3,2,0:T(8,128)(2,1)S(1)} %get-tuple-element.154) | copy-start | bytes 2359300
  219.4 135.7 %all-to-all-start.1 = ((bf16[32,40,1536]{2,1,0:T(8,128)(2,1)}), bf16[32,40,1536]{2,1,0:T(8,128)(2,1)}, u32[]{:S(2)}, u32[]{:S(2)}) async-start(bf16[32,40,1536]{2,1,0:T(8,128)(2,1)} %bitcast.386), calls=%async_computation.1 | async-start | bytes 7864320 | tf_op jit(solution)/shard_map/all_to_all | solution.py:120
  355.1 6.2 copy-start.12
  373.5 24.6 %copy-start.47 = (bf16[1280,768]{1,0:T(8,128)(2,1)}, bf16[1280,768]{1,0:T(8,128)(2,1)S(1)}, u32[]{:S(2)}) copy-start(bf16[1280,768]{1,0:T(8,128)(2,1)S(1)} %get-tuple-element.438) | copy-start | bytes 5898244
  382.2 139.5 %all-to-all-start.2 = ((bf16[32,40,1536]{2,1,0:T(8,128)(2,1)}), bf16[32,40,1536]{2,1,0:T(8,128)(2,1)}, u32[]{:S(2)}, u32[]{:S(2)}) async-start(bf16[32,40,1536]{2,1,0:T(8,128)(2,1)} %bitcast.396), calls=%async_computation.2 | async-start | bytes 7864320 | tf_op jit(solution)/shard_map/all_to_all | solution.py:120
  386.4 294.2 %reduce-scatter.9.cloned.1.call-start = ((), (), s32[]{:S(2)}) async-start(), calls=%async_computation.9 | async-start | bytes 5271552
  403.9 113.1 %copy-start.8 = (bf16[4,192,1536]{2,1,0:T(8,128)(2,1)S(1)}, bf16[4,192,1536]{2,1,0:T(8,128)(2,1)}, u32[]{:S(2)}) copy-start(bf16[4,192,1536]{2,1,0:T(8,128)(2,1)} %copy-done.6) | copy-start | bytes 7077892
  403.9 113.1 %copy-start.48 = (bf16[1280,768]{1,0:T(8,128)(2,1)S(1)}, bf16[1280,768]{1,0:T(8,128)(2,1)}, u32[]{:S(2)}) copy-start(bf16[1280,768]{1,0:T(8,128)(2,1)} %copy-done.47) | copy-start | bytes 5898244
  546.2 112.6 %all-to-all-start.3 = ((bf16[32,40,1536]{2,1,0:T(8,128)(2,1)}), bf16[32,40,1536]{2,1,0:T(8,128)(2,1)}, u32[]{:S(2)}, u32[]{:S(2)}) async-start(bf16[32,40,1536]{2,1,0:T(8,128)(2,1)} %bitcast.394), calls=%async_computation.3 | async-start | bytes 7864320 | tf_op jit(solution)/shard_map/all_to_all | solution.py:120
  550.3 249.8 %reduce-scatter.7.cloned.1.call-start = ((), (), s32[]{:S(2)}) async-start(), calls=%async_computation.8 | async-start | bytes 6893568
  555.5 7.0 copy-start.36
  571.7 7.1 copy-start.36
  587.6 31.4 %copy-start.33 = (f32[256,64]{0,1:T(8,128)S(1)}, f32[256,64]{0,1:T(8,128)}, u32[]{:S(2)}) copy-start(f32[256,64]{0,1:T(8,128)} %copy-done.32) | copy-start | bytes 196612
  587.6 31.4 %copy-start.35 = (f32[256,64]{0,1:T(8,128)S(1)}, f32[256,64]{0,1:T(8,128)}, u32[]{:S(2)}) copy-start(f32[256,64]{0,1:T(8,128)} %get-tuple-element.451) | copy-start | bytes 196612
  (41 other events, 124.2 us)
Sparse Core Ops, SparseCore 0:
  24.7 116.8 all-gather.2
  144.6 66.5 all-gather.4
  538.9 137.9 reduce-scatter.8
  683.5 116.6 reduce-scatter.6

commit v3 on v2

--- a/solution.py
+++ b/solution.py
@@ -220,6 +220,16 @@
         axis=1,
     )
     packed = jnp.concatenate([w_query, key_projection, value_projection, gain_block], axis=1)
+    packed_full = lax.all_gather(packed, BOTH, axis=0, tiled=True)
+    out_full = lax.all_gather(w_out, BOTH, axis=0, tiled=True)
+    gate_full, up_full = seq_exchange(
+        [w_gate, w_up],
+        2,
+        lambda ref, peer: ref.at[peer // sharers],
+        [w_gate.shape[1:], w_up.shape[1:]],
+        "gather_gate_up",
+    )
+
     pair_routes, place, kept = claim_places(routes[0], priority[0, 0], is_valid)
     holder = (pair_routes // own_experts) * seq_count + (pair_routes % own_experts) * sharers
     holder = holder + my_seq * sharers // seq_count
@@ -234,25 +244,20 @@
     live_cotangent = jnp.where(is_valid[:, None], cotangent[0], jnp.zeros((), BF16))
     out_grad = live_cotangent.astype(F32)
     grad_send = (tn(token_hot, live_cotangent) * slot_gate[:, None]).astype(BF16)
-    grad_send, hidden_in, packed, w_out = lax.optimization_barrier(
-        (grad_send, hidden_in, packed, w_out)
-    )
-    grad_rows = swap(grad_send.reshape(devices, CAP, width), ("dp", "seq")).reshape(slots, width)
-
-    packed_full = lax.all_gather(packed, BOTH, axis=0, tiled=True)
-    out_full = lax.all_gather(w_out, BOTH, axis=0, tiled=True)
-    query_full = packed_full[:, :q_width]
-    key_full = packed_full[:, q_width : q_width + kv_width]
-    value_full = packed_full[:, q_width + kv_width : q_width + 2 * kv_width]
+    packed_full, gate_full, up_full, grad_send = lax.optimization_barrier(
+        (packed_full, gate_full, up_full, grad_send)
+    )
     gain_one = packed_full[:, q_width + 2 * kv_width].astype(F32)
     gain_two = packed_full[:, q_width + 2 * kv_width + 1].astype(F32)
+    grad_rows = swap(grad_send.reshape(devices, CAP, width), ("dp", "seq")).reshape(slots, width)
 
     inputs = hidden_in[0].astype(F32)
     scale_one = lax.rsqrt(jnp.mean(inputs * inputs, axis=-1, keepdims=True) + EPSILON)
     normed = (inputs * scale_one * gain_one).astype(BF16)
-    query_rows = nn(normed, query_full)
-    key_matrix_rows = nn(normed, key_full)
-    value_matrix_rows = nn(normed, value_full).astype(BF16)
+    projected = nn(normed, packed_full)
+    query_rows = projected[:, :q_width]
+    key_matrix_rows = projected[:, q_width : q_width + kv_width]
+    value_matrix_rows = projected[:, q_width + kv_width : q_width + 2 * kv_width].astype(BF16)
     query_rotated = apply_rotary(
         query_rows.reshape(rows, q_heads, HEAD_DIM), cosine_lookup, sine_lookup
     ).astype(BF16)
@@ -282,17 +287,12 @@
     moe_input = (middle * scale_two * gain_two).astype(BF16)
 
     send_rows = tn(token_hot, moe_input).astype(BF16).reshape(devices, CAP, width)
-    send_rows, grad_rows, w_gate, w_up, w_down = lax.optimization_barrier(
-        (send_rows, grad_rows, w_gate, w_up, w_down)
-    )
+    send_rows, grad_rows, w_down = lax.optimization_barrier((send_rows, grad_rows, w_down))
     slot_rows = swap(send_rows, ("dp", "seq")).reshape(slots, width)
-    gate_full, up_full, down_full = seq_exchange(
-        [w_gate, w_up, w_down],
-        2,
-        lambda ref, peer: ref.at[peer // sharers],
-        [w_gate.shape[1:], w_up.shape[1:], w_down.shape[1:]],
-        "gather_expert",
-    )
+    (down_full,) = seq_exchange(
+        [w_down], 5, lambda ref, peer: ref.at[peer // sharers], [w_down.shape[1:]], "gather_down"
+    )
+    slot_rows, down_full = lax.optimization_barrier((slot_rows, down_full))
     gate_full = gate_full.reshape(width, hidden_units)
     up_full = up_full.reshape(width, hidden_units)
     down_full = down_full.reshape(hidden_units, width)
@@ -312,21 +312,23 @@
     up_grad = tn(slot_rows, up_pre_grad).astype(BF16)
     down_grad = tn(expert_hidden, grad_rows).astype(BF16)
 
-    pieces = seq_exchange(
-        [g.reshape(seq_count, -1, g.shape[1]) for g in (gate_grad, up_grad, down_grad)],
-        3,
-        lambda ref, peer: ref.at[peer],
-        [w_gate.shape[1:], w_up.shape[1:], w_down.shape[1:]],
-        "return_expert_grads",
-    )
-
-    row_back, *pieces = lax.optimization_barrier((row_back, *pieces))
+    def to_owners(grads, collective_id, name):
+        return seq_exchange(
+            [g.reshape(seq_count, -1, g.shape[1]) for g in grads],
+            collective_id,
+            lambda ref, peer: ref.at[peer],
+            [(g.shape[0] // seq_count, g.shape[1]) for g in grads],
+            name,
+        )
+
+    (gate_pieces,) = to_owners([gate_grad], 3, "return_gate_grad")
+    row_back, gate_pieces, up_grad, down_grad = lax.optimization_barrier(
+        (row_back, gate_pieces, up_grad, down_grad)
+    )
 
     def owned_sum(piece):
         piece = piece.reshape((own_experts, sharers) + piece.shape[1:])
         return jnp.sum(piece.astype(F32), axis=1)
-
-    expert_grads = [owned_sum(piece) for piece in pieces]
 
     expert_out = nn(expert_hidden, down_full).astype(BF16)
     expert_out, row_back = lax.optimization_barrier((expert_out, row_back))
@@ -335,8 +337,17 @@
     middle_norm_grad, gain_two_grad = norm_back(middle, scale_two, gain_two, moe_input_grad)
     middle_grad = out_grad + middle_norm_grad
     branch_grad = middle_grad.astype(BF16)
-    out_weight_grad = tn(attended, branch_grad)
+    no_grad = jnp.zeros((rows, LANES), BF16)
+
+    def with_gain(terms, gain_grad):
+        column = jnp.zeros((width, LANES), BF16).at[:, 0].set(gain_grad.astype(BF16))
+        return lax.dynamic_update_slice(terms, column, (0, terms.shape[1] - LANES))
+
+    out_terms = with_gain(
+        tn(attended, jnp.concatenate([branch_grad, no_grad], axis=1)).astype(BF16), gain_two_grad
+    )
     attended_grad = nt(branch_grad, out_full).astype(BF16)
+    attended_grad, out_terms = lax.optimization_barrier((attended_grad, out_terms))
     attended_grad = attended_grad.reshape(rows, kv_heads, group_size, HEAD_DIM).transpose(
         1, 0, 2, 3
     )
@@ -380,21 +391,20 @@
         -sine_lookup,
     )
     query_grad = query_grad.reshape(rows, q_width).astype(BF16)
-    normed_grad = nt(query_grad, query_full) + nt(key_grad, key_full) + nt(value_grad, value_full)
+    projected_grad = jnp.concatenate([query_grad, key_grad, value_grad, no_grad], axis=1)
+    returned, projected_grad = lax.optimization_barrier((returned, projected_grad))
+    normed_grad = nt(projected_grad, packed_full)
     input_norm_grad, gain_one_grad = norm_back(inputs, scale_one, gain_one, normed_grad)
     input_grad = middle_grad + input_norm_grad
 
-    def with_gain(parts, gain_grad):
-        column = jnp.pad(gain_grad[:, None].astype(BF16), ((0, 0), (0, LANES - 1)))
-        return jnp.concatenate([p.astype(BF16) for p in parts] + [column], axis=1)
-
-    out_terms = with_gain([out_weight_grad], gain_two_grad)
-    out_owned = lax.psum_scatter(out_terms, BOTH, scatter_dimension=0, tiled=True).astype(F32)
-    query_terms = with_gain(
-        [tn(normed, query_grad), tn(normed, key_grad), tn(normed, value_grad)], gain_one_grad
-    )
-    returned, query_terms = lax.optimization_barrier((returned, query_terms))
+    out_owned = lax.psum_scatter(out_terms, BOTH, scatter_dimension=0, tiled=True)
+    query_terms = with_gain(tn(normed, projected_grad).astype(BF16), gain_one_grad)
+    query_terms, up_grad, down_grad = lax.optimization_barrier((query_terms, up_grad, down_grad))
     owned = lax.psum_scatter(query_terms, BOTH, scatter_dimension=0, tiled=True).astype(F32)
+    pieces = to_owners([up_grad, down_grad], 6, "return_up_down_grads")
+    out_owned, *pieces = lax.optimization_barrier((out_owned, *pieces))
+    out_owned = out_owned.astype(F32)
+    expert_grads = [owned_sum(piece) for piece in (gate_pieces, *pieces)]
     gate_high = gate_rows.astype(BF16)
     gate_low = (gate_rows - gate_high.astype(F32)).astype(BF16)
 

time: 818 us -> 739 us (0.903)
  waiting for transfers between devices: 238 us -> 159 us
  local copies, waits for them, and re-layouts: 69.4 us -> 47 us
  Pallas kernels: 284 us -> 306 us
    unnamed x6 -> x4, waiting for transfers between devices: 108 us -> 1.41 us
    all_gather x1, waiting for transfers between devices: 108 us -> 15 us  [on_device(): packed_full = lax.all_gather(packed, BOTH, axis=0, tiled=True)]
    reduce_scatter x0 -> x2, waiting for transfers between devices: none -> 49.7 us  [the longest x1 49.7 us: on_device(): lax.psum_scatter(query_terms, BOTH, scatter_dimension=0, tiled=True)]
    all_to_all x4, waiting for transfers between devices: 12.8 us -> 61.6 us  [swap(): return lax.all_to_all(blocks, axes, split_axis=0, concat_axis=0, tiled=True)]
    unnamed x106 -> x115, local copies, waits for them, and re-layouts: 38.7 us -> 14 us
    pallas_call x4 -> x6, Pallas kernels: 284 us -> 306 us  [seq_exchange(): pl.pallas_call(functools.partial(exchange_kernel, count, n, block_of), ou...]
    all_gather x1, waiting for transfers between devices: 9.51 us -> 31.5 us  [on_device(): out_full = lax.all_gather(w_out, BOTH, axis=0, tiled=True)]
    concatenate x2 -> x1, other arithmetic: 16.8 us -> 1.35 us  [on_device(): jnp.concatenate([query_grad, key_grad, value_grad, no_grad], axis=1)]
  transfers between devices with their start and end apart: 8 -> 8, of which waited for: 4 -> 7; matrix products, arithmetic and copies ran while one was open for 22% -> 22% of each run, Pallas kernels for 35% -> 42%
where the time goes in v3:
time: 739 us; the launch traced here: 732 us
  Pallas kernels  306 us (41%)
  waiting for transfers between devices  159 us (22%)
  matrix products  128 us (17%)
  other arithmetic  51.6 us (7%)
  local copies, waits for them, and re-layouts  47 us (6%)
  starting transfers between devices  24.6 us (3%)
  between operations  15.7 us (2%)
    pallas_call x6, Pallas kernels, seq_exchange(): pl.pallas_call(functools.partial(exchange_kernel, count, n, block_of), ou...  306 us
    dot_general x20, matrix products, dot(): lax.dot_general(left, right, (contract, ((), ())), preferred_element_type...  100 us
    all_to_all x4, waiting for transfers between devices, swap(): return lax.all_to_all(blocks, axes, split_axis=0, concat_axis=0, tiled=True)  61.6 us
    reduce_scatter x1, waiting for transfers between devices, on_device(): lax.psum_scatter(query_terms, BOTH, scatter_dimension=0, tiled=True)  49.7 us
    all_gather x1, waiting for transfers between devices, on_device(): out_full = lax.all_gather(w_out, BOTH, axis=0, tiled=True)  31.5 us
    all_to_all x4, starting transfers between devices, swap(): return lax.all_to_all(blocks, axes, split_axis=0, concat_axis=0, tiled=True)  24.5 us
    all_gather x1, waiting for transfers between devices, on_device(): packed_full = lax.all_gather(packed, BOTH, axis=0, tiled=True)  15 us
  transfers between devices with their start and end apart: 8, of which 7 were waited for; matrix products, arithmetic and copies ran while one was open for 22% of the time, Pallas kernels for 42%

profile of v3, /device:TPU:0, one launch (start us, length us, event | category | flops | bytes accessed | tf_op | source)
XLA Modules:
  0.0 732.5 jit_solution(5840456044441569524)
XLA Ops:
  20.5 63.1 %gather_gate_up.1 = (bf16[4,384,768]{2,1,0:T(8,128)(2,1)S(1)}, bf16[4,384,768]{2,1,0:T(8,128)(2,1)S(1)}) custom-call(bf16[4,384,768]{2,1,0:T(8,128)(2,1)S(1)} %copy-done.1, bf16[4,384,768]{2,1,0:T(8,128)(2,1)S(1)} %copy-done.2), custom_call_target="tpu_custom_call" | custom-call | bytes 70778880 | tf_op jit(solution)/shard_map/gather_gate_up/pallas_call | solution.py:161
  94.1 15.0 %all-gather.3.cloned.1.call-done = bf16[1536,2176]{1,0:T(8,128)(2,1)} async-done(((bf16[48,2176]{1,0:T(8,128)(2,1)}), bf16[1536,2176]{1,0:T(8,128)(2,1)}) %all-gather.3.cloned.1.call-update) | async-done | bytes 6684688 | tf_op jit(solution)/shard_map/all_gather | solution.py:223
  131.7 32.6 %gather_keys.1 = bf16[4,256,512]{2,1,0:T(8,128)(2,1)S(1)} custom-call(bf16[256,512]{1,0:T(8,128)(2,1)S(1)} %pad_maximum_fusion.2.refs_0_), custom_call_target="tpu_custom_call" | custom-call | bytes 15728640 | tf_op jit(solution)/shard_map/gather_keys/pallas_call | solution.py:161
  169.5 10.6 %while.34 = (s32[]{:T(128)}, bf16[2,256,6,128]{1,3,2,0:T(8,128)(2,1)S(1)}, f32[2,6,256]{2,1,0:T(8,128)S(1)}, bf16[2,1024,128]{1,2,0:T(8,128)(2,1)}, s32[]{:T(128...) while((s32[]{:T(128)}, ...), condition=%wide.region_7.8_spmd.clone.clone.clone, body=%wide.region_4.7_spmd.clone.clone.sunk.clone | while | flops 824704768 | bytes 23789692 | solution.py:278
  180.1 31.5 %all-gather.5.cloned.1.call-done = bf16[1536,1536]{1,0:T(8,128)(2,1)} async-done(((bf16[48,1536]{1,0:T(8,128)(2,1)}), bf16[1536,1536]{1,0:T(8,128)(2,1)}) %all-gather.5.cloned.1.call-update) | async-done | bytes 4718608 | tf_op jit(solution)/shard_map/all_gather | solution.py:224
  223.1 5.9 all-to-all-start.1
  229.0 68.9 %gather_down.1 = bf16[4,192,1536]{2,1,0:T(8,128)(2,1)S(1)} custom-call(bf16[4,192,1536]{2,1,0:T(8,128)(2,1)S(1)} %copy-done.3), custom_call_target="tpu_custom_call" | custom-call | bytes 35389440 | tf_op jit(solution)/shard_map/gather_down/pallas_call | solution.py:161
  299.4 18.5 %all-to-all-done.1 = bf16[32,40,1536]{2,1,0:T(8,128)(2,1)} async-done(((bf16[32,40,1536]{2,1,0:T(8,128)(2,1)}), bf16[32,40,1536]{2,1,0:T(8,128)(2,1)}, u32[]{:S(2)}, u32[]{:S(2)}) %all-to-all-start.1) | async-done | bytes 3932192 | tf_op jit(solution)/shard_map/all_to_all | solution.py:120
  317.9 6.2 fusion.115
  324.1 5.5 fusion.114
  329.6 7.9 %multiply_convert_fusion = (bf16[1280,768]{1,0:T(8,128)(2,1)S(1)}, bf16[1280,768]{1,0:T(8,128)(2,1)S(1)}, bf16[1280,768]{1,0:T(8,128)(2,1)}) fusion(f32[1280,768]{1,0:T(8,128)S(1)} %fusion.114, f32[1280,768]{1,0:T(8,128)S(1)} %fusion.115, bf16[1280,1536]{1,0:T(8,128)(2,1)} %bitcast.22, bf16[768,1536]{1,0:T(8,128)(2,1)S(1)} %bitcast.332), kind=kOutput, calls=%fused_computation.90 | convolution fusion | flops 3034644480 | bytes 20054016 | tf_op jit(solution)/shard_map/dot_general | solution.py:46
  340.8 5.3 fusion.69
  346.1 5.3 all-to-all-start.2
  353.5 5.4 convolution_convert_fusion.6
  358.9 61.5 %return_gate_grad.1 = bf16[4,384,768]{2,1,0:T(8,128)(2,1)S(1)} custom-call(bf16[4,384,768]{2,1,0:T(8,128)(2,1)S(1)} %bitcast.334), custom_call_target="tpu_custom_call" | custom-call | bytes 35389440 | tf_op jit(solution)/shard_map/return_gate_grad/pallas_call | solution.py:161
  425.1 6.9 convolution_convert_fusion.4
  432.0 6.8 convolution_convert_fusion.5
  459.2 9.5 %all-to-all-start.3 = ((bf16[32,40,1536]{2,1,0:T(8,128)(2,1)}), bf16[32,40,1536]{2,1,0:T(8,128)(2,1)}, u32[]{:S(2)}, u32[]{:S(2)}) async-start(bf16[32,40,1536]{2,1,0:T(8,128)(2,1)} %bitcast.345), calls=%async_computation.3 | async-start | bytes 7864320 | tf_op jit(solution)/shard_map/all_to_all | solution.py:120
  469.8 32.4 %while.35 = (s32[]{:T(128)}, f32[2,256,6,128]{1,3,2,0:T(8,128)}, bf16[2,1024,128]{2,1,0:T(8,128)(2,1)}, bf16[2,1024,128]{2,1,0:T(8,128)(2,1)}, bf16[2,1024,128]{...) while((s32[]{:T(128)}, f32[2,256,6,128]{1,3,2,0:T(8,128)}, ...), condition=%wide.region_15.16_spmd.clone.clone.clone, body=%wide.region_13.15_spmd.clone.clone.sunk.clone | while | flops 2037710592 | bytes 75554056 | solution.py:354
  508.0 26.8 %return_key_grads.1 = bf16[4,256,512]{2,1,0:T(8,128)(2,1)S(1)} custom-call(bf16[4,256,512]{2,1,0:T(8,128)(2,1)S(1)} %pad_maximum_fusion.refs_0_), custom_call_target="tpu_custom_call" | custom-call | bytes 15728640 | tf_op jit(solution)/shard_map/return_key_grads/pallas_call | solution.py:161
  540.2 38.5 %all-to-all-done.3 = bf16[32,40,1536]{2,1,0:T(8,128)(2,1)} async-done(((bf16[32,40,1536]{2,1,0:T(8,128)(2,1)}), bf16[32,40,1536]{2,1,0:T(8,128)(2,1)}, u32[]{:S(2)}, u32[]{:S(2)}) %all-to-all-start.3) | async-done | bytes 3932192 | tf_op jit(solution)/shard_map/all_to_all | solution.py:120
  578.7 6.9 fusion.85
  596.5 52.9 %return_up_down_grads.1 = (bf16[4,384,768]{2,1,0:T(8,128)(2,1)S(1)}, bf16[4,192,1536]{2,1,0:T(8,128)(2,1)S(1)}) custom-call(bf16[4,384,768]{2,1,0:T(8,128)(2,1)S(1)} %bitcast.331, bf16[4,192,1536]{2,1,0:T(8,128)(2,1)S(1)} %bitcast.330), custom_call_target="tpu_custom_call" | custom-call | bytes 70778880 | tf_op jit(solution)/shard_map/return_up_down_grads/pallas_call | solution.py:161
  671.3 49.7 %reduce-scatter.3.cloned.1.call-done = bf16[48,2176]{1,0:T(8,128)(2,1)} async-done(((bf16[1536,2176]{1,0:T(8,128)(2,1)}), bf16[48,2176]{1,0:T(8,128)(2,1)}) %reduce-scatter.3.cloned.1.call-update) | async-done | bytes 208912 | tf_op jit(solution)/shard_map/reduce_scatter | solution.py:403
  (284 shorter events, 185.6 us)
Async XLA Ops:
  7.2 11.7 %copy-start.1 = (bf16[4,384,768]{2,1,0:T(8,128)(2,1)S(1)}, bf16[4,384,768]{2,1,0:T(8,128)(2,1)}, u32[]{:S(2)}) copy-start(bf16[4,384,768]{2,1,0:T(8,128)(2,1)} %refs_0_.1) | copy-start | bytes 7077892
  7.2 102.0 %all-gather.3.cloned.1.call-start = ((), (), s32[]{:S(2)}) async-start(), calls=%async_computation.6 | async-start | bytes 6893568 | tf_op jit(solution)/shard_map/all_gather | solution.py:223
  10.6 201.1 %all-gather.5.cloned.1.call-start = ((), (), s32[]{:S(2)}) async-start(), calls=%async_computation.7 | async-start | bytes 4866048 | tf_op jit(solution)/shard_map/all_gather | solution.py:224
  16.6 109.1 %copy-start.36 = (f32[256,64]{0,1:T(8,128)}, f32[256,64]{0,1:T(8,128)S(1)}, u32[]{:S(2)}) copy-start(f32[256,64]{0,1:T(8,128)S(1)} %get-tuple-element.447) | copy-start | bytes 196612
  20.5 66.0 %copy-start.19 = (bf16[1,256,1536]{2,1,0:T(8,128)(2,1)S(1)}, bf16[1,256,1536]{2,1,0:T(8,128)(2,1)}, u32[]{:S(2)}) copy-start(bf16[1,256,1536]{2,1,0:T(8,128)(2,1)} %param.23) | copy-start | bytes 2359300
  20.5 66.3 %copy-start.51 = (s32[256,4]{0,1:T(4,128)S(1)}, s32[256,4]{0,1:T(4,128)}, u32[]{:S(2)}) copy-start(s32[256,4]{0,1:T(4,128)} %copy.109) | copy-start | bytes 12292
  20.5 67.3 %copy-start.50 = (f32[1,256,4]{1,2,0:T(4,128)S(1)}, f32[1,256,4]{1,2,0:T(4,128)}, u32[]{:S(2)}) copy-start(f32[1,256,4]{1,2,0:T(4,128)} %param.26) | copy-start | bytes 12292
  20.5 70.4 %copy-start.38 = (bf16[1,256,1536]{2,1,0:T(8,128)(2,1)S(1)}, bf16[1,256,1536]{2,1,0:T(8,128)(2,1)}, u32[]{:S(2)}) copy-start(bf16[1,256,1536]{2,1,0:T(8,128)(2,1)} %param.37) | copy-start | bytes 2359300
  20.5 70.4 %copy-start.56 = (pred[256]{0:T(512)(128)(4,1)S(1)}, pred[256]{0:T(512)(128)(4,1)}, u32[]{:S(2)}) copy-start(pred[256]{0:T(512)(128)(4,1)} %copy-done.55) | copy-start | bytes 772
  87.8 27.3 %copy-start.53 = (f32[256]{0:T(256)}, f32[256]{0:T(256)S(1)}, u32[]{:S(2)}) copy-start(f32[256]{0:T(256)S(1)} %add_rsqrt_fusion.1) | copy-start | bytes 3076
  109.2 114.0 %all-to-all-start = ((bf16[32,40,1536]{2,1,0:T(8,128)(2,1)}), bf16[32,40,1536]{2,1,0:T(8,128)(2,1)}, u32[]{:S(2)}, u32[]{:S(2)}) async-start(bf16[32,40,1536]{2,1,0:T(8,128)(2,1)} %bitcast.346), calls=%async_computation | async-start | bytes 7864320 | tf_op jit(solution)/shard_map/all_to_all | solution.py:120
  180.1 35.4 %copy-start.14 = (bf16[2,256,6,128]{3,1,2,0:T(8,128)(2,1)}, bf16[2,256,6,128]{3,1,2,0:T(8,128)(2,1)S(1)}, u32[]{:S(2)}) copy-start(bf16[2,256,6,128]{3,1,2,0:T(8,128)(2,1)S(1)} %get-tuple-element.686) | copy-start | bytes 2359300
  180.1 35.4 %copy-start.22 = (bf16[2,256,6,128]{1,3,2,0:T(8,128)(2,1)}, bf16[2,256,6,128]{1,3,2,0:T(8,128)(2,1)S(1)}, u32[]{:S(2)}) copy-start(bf16[2,256,6,128]{1,3,2,0:T(8,128)(2,1)S(1)} %get-tuple-element.185) | copy-start | bytes 2359300
  223.1 94.8 %all-to-all-start.1 = ((bf16[32,40,1536]{2,1,0:T(8,128)(2,1)}), bf16[32,40,1536]{2,1,0:T(8,128)(2,1)}, u32[]{:S(2)}, u32[]{:S(2)}) async-start(bf16[32,40,1536]{2,1,0:T(8,128)(2,1)} %bitcast.339), calls=%async_computation.1 | async-start | bytes 7864320 | tf_op jit(solution)/shard_map/all_to_all | solution.py:120
  346.1 94.2 %all-to-all-start.2 = ((bf16[32,40,1536]{2,1,0:T(8,128)(2,1)}), bf16[32,40,1536]{2,1,0:T(8,128)(2,1)}, u32[]{:S(2)}, u32[]{:S(2)}) async-start(bf16[32,40,1536]{2,1,0:T(8,128)(2,1)} %bitcast.347), calls=%async_computation.2 | async-start | bytes 7864320 | tf_op jit(solution)/shard_map/all_to_all | solution.py:120
  358.9 61.6 %copy-start.8 = (bf16[4,192,1536]{2,1,0:T(8,128)(2,1)S(1)}, bf16[4,192,1536]{2,1,0:T(8,128)(2,1)}, u32[]{:S(2)}) copy-start(bf16[4,192,1536]{2,1,0:T(8,128)(2,1)} %copy-done.6) | copy-start | bytes 7077892
  358.9 61.6 %copy-start.58 = (bf16[1280,768]{1,0:T(8,128)(2,1)S(1)}, bf16[1280,768]{1,0:T(8,128)(2,1)}, u32[]{:S(2)}) copy-start(bf16[1280,768]{1,0:T(8,128)(2,1)} %get-tuple-element.432) | copy-start | bytes 5898244
  459.2 119.5 %all-to-all-start.3 = ((bf16[32,40,1536]{2,1,0:T(8,128)(2,1)}), bf16[32,40,1536]{2,1,0:T(8,128)(2,1)}, u32[]{:S(2)}, u32[]{:S(2)}) async-start(bf16[32,40,1536]{2,1,0:T(8,128)(2,1)} %bitcast.345), calls=%async_computation.3 | async-start | bytes 7864320 | tf_op jit(solution)/shard_map/all_to_all | solution.py:120
  468.7 182.2 %reduce-scatter.5.cloned.1.call-start = ((), (), s32[]{:S(2)}) async-start(), calls=%async_computation.9 | async-start | bytes 5271552 | tf_op jit(solution)/shard_map/reduce_scatter | solution.py:400
  469.5 251.6 %reduce-scatter.3.cloned.1.call-start = ((), (), s32[]{:S(2)}) async-start(), calls=%async_computation.8 | async-start | bytes 6893568 | tf_op jit(solution)/shard_map/reduce_scatter | solution.py:403
  506.8 28.3 %copy-start.35 = (f32[256,64]{1,0:T(8,128)S(1)}, f32[256,64]{1,0:T(8,128)}, u32[]{:S(2)}) copy-start(f32[256,64]{1,0:T(8,128)} %copy.110) | copy-start | bytes 196612
  508.0 29.2 %copy-start.37 = (f32[256,64]{0,1:T(8,128)S(1)}, f32[256,64]{0,1:T(8,128)}, u32[]{:S(2)}) copy-start(f32[256,64]{0,1:T(8,128)} %copy-done.36) | copy-start | bytes 196612
  537.1 41.5 %copy-start.47 = (f32[1536]{0:T(1024)S(1)}, f32[1536]{0:T(1024)}, u32[]{:S(2)}) copy-start(f32[1536]{0:T(1024)} %copy-done.46) | copy-start | bytes 18436
  537.1 41.5 %copy-start.54 = (f32[256]{0:T(256)S(1)}, f32[256]{0:T(256)}, u32[]{:S(2)}) copy-start(f32[256]{0:T(256)} %copy-done.53) | copy-start | bytes 3076
  (52 other events, 198.9 us)
Sparse Core Ops, SparseCore 0:
  11.6 97.4 all-gather.2
  112.2 99.4 all-gather.4
  475.1 122.5 reduce-scatter.4
  604.3 116.7 reduce-scatter.2

commit v4 on v3

--- a/solution.py
+++ b/solution.py
@@ -123,35 +123,293 @@
 MESH_IDS = pl.DeviceIdType.MESH
 
 
-def exchange_kernel(count, n, block_of, *refs):
-    sources, targets = refs[:n], refs[n : 2 * n]
-    send_sems, recv_sems, local_sems = refs[2 * n :]
+def torus_place():
+    seq, dp = lax.axis_index("seq"), lax.axis_index("dp")
+    return seq // 2, seq % 2, dp // 2, dp % 2
+
+
+def torus_id(a, b, z, c):
+    return {"seq": 2 * a + b, "dp": 2 * z + c}
+
+
+def torus_peers(line):
+    a, b, z, c = torus_place()
+    peers = [torus_id(a, b, z, 1 - c), torus_id(a, 1 - b, z, c), torus_id(1 - a, b, z, c)]
+    peers.append(torus_id(1 - a, 1 - b, z, c))
+    return peers + [torus_id(a, b, lax.rem(z + k, line), c) for k in range(1, line)]
+
+
+def greet(peers):
+    barrier = pltpu.get_barrier_semaphore()
+    for peer in peers:
+        pl.semaphore_signal(barrier, inc=1, device_id=peer, device_id_type=MESH_IDS)
+    pl.semaphore_wait(barrier, len(peers))
+
+
+def column_chunks(widths, limit):
+    chunks = []
+    for k, whole in enumerate(widths):
+        start = 0
+        while start < whole:
+            size = limit if whole - start >= 2 * limit else whole - start
+            chunks.append((k, start, size))
+            start += size
+    return chunks
+
+
+def remote(src, dst, sems, i, j, device_id):
+    send, recv = sems
+    return pltpu.make_async_remote_copy(
+        src_ref=src,
+        dst_ref=dst,
+        send_sem=send.at[i, j],
+        recv_sem=recv.at[i, j],
+        device_id=device_id,
+        device_id_type=MESH_IDS,
+    )
+
+
+def start_exchange(count, sources, targets, block_of, sems):
+    send_sems, recv_sems, local_sems = sems
     me = lax.axis_index("seq")
-    barrier = pltpu.get_barrier_semaphore()
-    for step in range(1, count):
-        peer = lax.rem(me + step, count)
-        pl.semaphore_signal(barrier, inc=1, device_id={"seq": peer}, device_id_type=MESH_IDS)
-    pl.semaphore_wait(barrier, count - 1)
     copies = []
-    for i in range(n):
+    for i, source in enumerate(sources):
         for step in range(1, count):
             peer = lax.rem(me + step, count)
-            copy = pltpu.make_async_remote_copy(
-                src_ref=block_of(sources[i], peer),
-                dst_ref=targets[i].at[me],
-                send_sem=send_sems.at[i, step - 1],
-                recv_sem=recv_sems.at[i, step - 1],
-                device_id={"seq": peer},
-                device_id_type=MESH_IDS,
+            copies.append(
+                pltpu.make_async_remote_copy(
+                    src_ref=block_of(source, peer),
+                    dst_ref=targets[i].at[me],
+                    send_sem=send_sems.at[i, step - 1],
+                    recv_sem=recv_sems.at[i, step - 1],
+                    device_id={"seq": peer},
+                    device_id_type=MESH_IDS,
+                )
             )
-            copy.start()
-            copies.append(copy)
-        copy = pltpu.make_async_copy(
-            block_of(sources[i], me), targets[i].at[me], local_sems.at[i]
+        copies.append(
+            pltpu.make_async_copy(block_of(source, me), targets[i].at[me], local_sems.at[i])
         )
+    for copy in copies:
         copy.start()
-        copies.append(copy)
-    for copy in copies:
+    return copies
+
+
+def exchange_sems(n, count):
+    return [
+        pltpu.SemaphoreType.DMA((n, count - 1)),
+        pltpu.SemaphoreType.DMA((n, count - 1)),
+        pltpu.SemaphoreType.DMA((n,)),
+    ]
+
+
+def gather_kernel(line, chunks, n, extras, block_of, *refs):
+    sources, more_sources = refs[:n], refs[n : n + extras]
+    refs = refs[n + extras :]
+    targets, more_targets = refs[:n], refs[n : n + extras]
+    send, recv, local, *more_sems = refs[n + extras :]
+    sems = (send, recv)
+    a, b, z, c = torus_place()
+    greet(torus_peers(line))
+    more = start_exchange(4, more_sources, more_targets, block_of, more_sems) if extras else []
+    sent = []
+
+    def start(copy):
+        copy.start()
+        sent.append(copy)
+        return copy
+
+    arriving = []
+    for i, (k, first, size) in enumerate(chunks):
+        cols = pl.ds(first, size)
+        own = targets[k].at[a, b, z, c, :, cols]
+        keep = pltpu.make_async_copy(sources[k].at[:, cols], own, local.at[i])
+        keep.start()
+        waits = []
+        for step in range(1, line):
+            peer = torus_id(a, b, lax.rem(z + step, line), c)
+            waits.append(start(remote(sources[k].at[:, cols], own, sems, i, 2 + step, peer)))
+        arriving.append((keep, waits))
+    pending = []
+    for i, (k, first, size) in enumerate(chunks):
+        keep, waits = arriving[i]
+        keep.wait()
+        for copy in waits:
+            copy.wait_recv()
+        block = targets[k].at[a, b, :, c, :, pl.ds(first, size)]
+        peer = torus_id(a, 1 - b, z, c) if i % 2 == 0 else torus_id(1 - a, b, z, c)
+        pending.append(start(remote(block, block, sems, i, 1, peer)))
+    second = []
+    for i, (k, first, size) in enumerate(chunks):
+        pending[i].wait_recv()
+        cols = pl.ds(first, size)
+        if i % 2 == 0:
+            block, peer = targets[k].at[a, :, :, c, :, cols], torus_id(1 - a, b, z, c)
+        else:
+            block, peer = targets[k].at[:, b, :, c, :, cols], torus_id(a, 1 - b, z, c)
+        second.append(start(remote(block, block, sems, i, 2, peer)))
+    third = []
+    for i, (k, first, size) in enumerate(chunks):
+        second[i].wait_recv()
+        block = targets[k].at[:, :, :, c, :, pl.ds(first, size)]
+        third.append(start(remote(block, block, sems, i, 0, torus_id(a, b, z, 1 - c))))
+    for copy in third:
+        copy.wait_recv()
+    for copy in sent:
+        copy.wait_send()
+    for copy in more:
+        copy.wait()
+
+
+def staged_gather(arrays, extras, block_of, collective_id, name):
+    seq_count, line = lax.axis_size("seq"), lax.axis_size("dp") // 2
+    rows, n = arrays[0].shape[0], len(arrays)
+    chunks = column_chunks([x.shape[1] for x in arrays], 512)
+    m = len(chunks)
+    shape = (seq_count // 2, 2, line, 2, rows)
+    size = sum(x.shape[1] for x in arrays) * rows * 64
+    count = n + len(extras)
+    outs = pl.pallas_call(
+        functools.partial(gather_kernel, line, chunks, n, len(extras), block_of),
+        out_shape=[jax.ShapeDtypeStruct(shape + (x.shape[1],), BF16) for x in arrays]
+        + [jax.ShapeDtypeStruct((seq_count,) + x.shape[1:], BF16) for x in extras],
+        in_specs=[pl.BlockSpec(memory_space=pl.ANY)] * count,
+        out_specs=[pl.BlockSpec(memory_space=pl.ANY)] * count,
+        scratch_shapes=[
+            pltpu.SemaphoreType.DMA((m, 2 + line)),
+            pltpu.SemaphoreType.DMA((m, 2 + line)),
+            pltpu.SemaphoreType.DMA((m,)),
+        ]
+        + (exchange_sems(len(extras), seq_count) if extras else []),
+        compiler_params=pltpu.CompilerParams(
+            collective_id=collective_id, vmem_limit_bytes=4 << 20
+        ),
+        cost_estimate=pl.CostEstimate(flops=0, bytes_accessed=10 * size, transcendentals=0),
+        name=name,
+    )(*arrays, *extras)
+    return [o.reshape(-1, o.shape[-1]) for o in outs]
+
+
+def scatter_kernel(line, chunks, n, extras, block_of, *refs):
+    m = len(chunks)
+    sources, more_sources = refs[:n], refs[n : n + extras]
+    refs = refs[n + extras :]
+    targets, more_targets = refs[:n], refs[n : n + extras]
+    scratch = refs[n + extras :]
+    owns, ins1, accs2, ins2, accs3, ins3, ins4 = (scratch[m * s : m * (s + 1)] for s in range(7))
+    send, recv, local, *more_sems = scratch[7 * m :]
+    sems = (send, recv)
+    a, b, z, c = torus_place()
+    greet(torus_peers(line))
+    sent = []
+
+    def start(copy):
+        copy.start()
+        sent.append(copy)
+        return copy
+
+    def add_lines(target, left, right):
+        def one(j, carry):
+            target[j] = (left[j].astype(F32) + right[j].astype(F32)).astype(BF16)
+            return carry
+
+        lax.fori_loop(0, line, one, 0)
+
+    first_stage = []
+    for i, (k, first, size) in enumerate(chunks):
+        cols = pl.ds(first, size)
+        keep = pltpu.make_async_copy(sources[k].at[:, :, :, c, :, cols], owns[i], local.at[i])
+        keep.start()
+        swap_core = remote(
+            sources[k].at[:, :, :, 1 - c, :, cols], ins1[i], sems, i, 0, torus_id(a, b, z, 1 - c)
+        )
+        first_stage.append((keep, start(swap_core)))
+    more = start_exchange(4, more_sources, more_targets, block_of, more_sems) if extras else []
+    second_stage = []
+    for i in range(m):
+        keep, copy = first_stage[i]
+        keep.wait()
+        copy.wait_recv()
+        for p in range(2):
+            for q in range(2):
+                add_lines(owns[i].at[p, q], owns[i].at[p, q], ins1[i].at[p, q])
+        if i % 2 == 0:
+            block, peer = owns[i].at[:, 1 - b], torus_id(a, 1 - b, z, c)
+        else:
+            block, peer = owns[i].at[1 - a], torus_id(1 - a, b, z, c)
+        second_stage.append(start(remote(block, ins2[i], sems, i, 1, peer)))
+    third_stage = []
+    for i in range(m):
+        second_stage[i].wait_recv()
+        for p in range(2):
+            mine = owns[i].at[p, b] if i % 2 == 0 else owns[i].at[a, p]
+            add_lines(accs2[i].at[p], mine, ins2[i].at[p])
+        if i % 2 == 0:
+            block, peer = accs2[i].at[1 - a], torus_id(1 - a, b, z, c)
+        else:
+            block, peer = accs2[i].at[1 - b], torus_id(a, 1 - b, z, c)
+        third_stage.append(start(remote(block, ins3[i], sems, i, 2, peer)))
+    last_stage = []
+    for i in range(m):
+        third_stage[i].wait_recv()
+        add_lines(accs3[i], accs2[i].at[a if i % 2 == 0 else b], ins3[i])
+        copies = []
+        for step in range(1, line):
+            to = lax.rem(z + step, line)
+            copies.append(
+                start(
+                    remote(
+                        accs3[i].at[to], ins4[i].at[z], sems, i, 2 + step, torus_id(a, b, to, c)
+                    )
+                )
+            )
+        last_stage.append(copies)
+    for i, (k, first, size) in enumerate(chunks):
+        total = accs3[i][z].astype(F32)
+        for step in range(1, line):
+            last_stage[i][step - 1].wait_recv()
+            total = total + ins4[i][lax.rem(z + line - step, line)].astype(F32)
+        targets[k][:, first : first + size] = total
+    for copy in sent:
+        copy.wait_send()
+    for copy in more:
+        copy.wait()
+
+
+def staged_scatter(arrays, extras, block_of, collective_id, name):
+    seq_count, line = lax.axis_size("seq"), lax.axis_size("dp") // 2
+    rows, n = arrays[0].shape[0] // (2 * line * seq_count), len(arrays)
+    chunks = column_chunks([x.shape[1] for x in arrays], 512)
+    m = len(chunks)
+    leads = [(2, 2, line), (2, 2, line), (2, line), (2, line), (line,), (line,), (line,)]
+    size = sum(x.shape[1] for x in arrays) * rows * 64
+    anywhere = pl.BlockSpec(memory_space=pl.ANY)
+    return pl.pallas_call(
+        functools.partial(scatter_kernel, line, chunks, n, len(extras), block_of),
+        out_shape=[jax.ShapeDtypeStruct((rows, x.shape[1]), F32) for x in arrays]
+        + [jax.ShapeDtypeStruct((seq_count,) + x.shape[1:], BF16) for x in extras],
+        in_specs=[anywhere] * (n + len(extras)),
+        out_specs=[pl.BlockSpec(memory_space=pltpu.VMEM)] * n + [anywhere] * len(extras),
+        scratch_shapes=[
+            pltpu.VMEM(lead + (rows, width), BF16) for lead in leads for _, _, width in chunks
+        ]
+        + [
+            pltpu.SemaphoreType.DMA((m, 2 + line)),
+            pltpu.SemaphoreType.DMA((m, 2 + line)),
+            pltpu.SemaphoreType.DMA((m,)),
+        ]
+        + (exchange_sems(len(extras), seq_count) if extras else []),
+        compiler_params=pltpu.CompilerParams(
+            collective_id=collective_id, vmem_limit_bytes=36 << 20
+        ),
+        cost_estimate=pl.CostEstimate(flops=0, bytes_accessed=size, transcendentals=0),
+        name=name,
+    )(*[x.reshape(2, 2, line, 2, rows, x.shape[1]) for x in arrays], *extras)
+
+
+def exchange_kernel(count, n, block_of, *refs):
+    me = lax.axis_index("seq")
+    greet([{"seq": lax.rem(me + step, count)} for step in range(1, count)])
+    for copy in start_exchange(count, refs[:n], refs[n : 2 * n], block_of, refs[2 * n :]):
         copy.wait()
 
 
@@ -163,11 +421,7 @@
         out_shape=[jax.ShapeDtypeStruct((count,) + shape, BF16) for shape in block_shapes],
         in_specs=[pl.BlockSpec(memory_space=pl.ANY)] * n,
         out_specs=[pl.BlockSpec(memory_space=pl.ANY)] * n,
-        scratch_shapes=[
-            pltpu.SemaphoreType.DMA((n, count - 1)),
-            pltpu.SemaphoreType.DMA((n, count - 1)),
-            pltpu.SemaphoreType.DMA((n,)),
-        ],
+        scratch_shapes=exchange_sems(n, count),
         compiler_params=pltpu.CompilerParams(
             collective_id=collective_id, vmem_limit_bytes=4 << 20
         ),
@@ -220,15 +474,18 @@
         axis=1,
     )
     packed = jnp.concatenate([w_query, key_projection, value_projection, gain_block], axis=1)
-    packed_full = lax.all_gather(packed, BOTH, axis=0, tiled=True)
-    out_full = lax.all_gather(w_out, BOTH, axis=0, tiled=True)
-    gate_full, up_full = seq_exchange(
-        [w_gate, w_up],
-        2,
-        lambda ref, peer: ref.at[peer // sharers],
-        [w_gate.shape[1:], w_up.shape[1:]],
-        "gather_gate_up",
-    )
+    staged = seq_count == 4 and w_query.shape[0] % 16 == 0
+    owner_block = lambda ref, peer: ref.at[peer // sharers]
+    piece_block = lambda ref, peer: ref.at[peer]
+
+    if staged:
+        packed_full, out_full, gate_full = staged_gather(
+            [packed, w_out], [w_gate], owner_block, 2, "gather_attention_weights"
+        )
+    else:
+        packed_full = lax.all_gather(packed, BOTH, axis=0, tiled=True)
+        out_full = lax.all_gather(w_out, BOTH, axis=0, tiled=True)
+        (gate_full,) = seq_exchange([w_gate], 2, owner_block, [w_gate.shape[1:]], "gather_gate")
 
     pair_routes, place, kept = claim_places(routes[0], priority[0, 0], is_valid)
     holder = (pair_routes // own_experts) * seq_count + (pair_routes % own_experts) * sharers
@@ -244,8 +501,8 @@
     live_cotangent = jnp.where(is_valid[:, None], cotangent[0], jnp.zeros((), BF16))
     out_grad = live_cotangent.astype(F32)
     grad_send = (tn(token_hot, live_cotangent) * slot_gate[:, None]).astype(BF16)
-    packed_full, gate_full, up_full, grad_send = lax.optimization_barrier(
-        (packed_full, gate_full, up_full, grad_send)
+    packed_full, out_full, gate_full, grad_send = lax.optimization_barrier(
+        (packed_full, out_full, gate_full, grad_send)
     )
     gain_one = packed_full[:, q_width + 2 * kv_width].astype(F32)
     gain_two = packed_full[:, q_width + 2 * kv_width + 1].astype(F32)
@@ -287,12 +544,14 @@
     moe_input = (middle * scale_two * gain_two).astype(BF16)
 
     send_rows = tn(token_hot, moe_input).astype(BF16).reshape(devices, CAP, width)
-    send_rows, grad_rows, w_down = lax.optimization_barrier((send_rows, grad_rows, w_down))
+    send_rows, grad_rows, w_up, w_down = lax.optimization_barrier(
+        (send_rows, grad_rows, w_up, w_down)
+    )
     slot_rows = swap(send_rows, ("dp", "seq")).reshape(slots, width)
-    (down_full,) = seq_exchange(
-        [w_down], 5, lambda ref, peer: ref.at[peer // sharers], [w_down.shape[1:]], "gather_down"
-    )
-    slot_rows, down_full = lax.optimization_barrier((slot_rows, down_full))
+    up_full, down_full = seq_exchange(
+        [w_up, w_down], 5, owner_block, [w_up.shape[1:], w_down.shape[1:]], "gather_up_down"
+    )
+    slot_rows, up_full, down_full = lax.optimization_barrier((slot_rows, up_full, down_full))
     gate_full = gate_full.reshape(width, hidden_units)
     up_full = up_full.reshape(width, hidden_units)
     down_full = down_full.reshape(hidden_units, width)
@@ -312,18 +571,18 @@
     up_grad = tn(slot_rows, up_pre_grad).astype(BF16)
     down_grad = tn(expert_hidden, grad_rows).astype(BF16)
 
-    def to_owners(grads, collective_id, name):
-        return seq_exchange(
-            [g.reshape(seq_count, -1, g.shape[1]) for g in grads],
-            collective_id,
-            lambda ref, peer: ref.at[peer],
-            [(g.shape[0] // seq_count, g.shape[1]) for g in grads],
-            name,
-        )
-
-    (gate_pieces,) = to_owners([gate_grad], 3, "return_gate_grad")
-    row_back, gate_pieces, up_grad, down_grad = lax.optimization_barrier(
-        (row_back, gate_pieces, up_grad, down_grad)
+    def pieces_of(grad):
+        return grad.reshape(seq_count, -1, grad.shape[1])
+
+    gate_pieces, up_pieces = seq_exchange(
+        [pieces_of(gate_grad), pieces_of(up_grad)],
+        3,
+        piece_block,
+        [w_gate.shape[1:], w_up.shape[1:]],
+        "return_gate_up_grads",
+    )
+    row_back, gate_pieces, up_pieces, down_grad = lax.optimization_barrier(
+        (row_back, gate_pieces, up_pieces, down_grad)
     )
 
     def owned_sum(piece):
@@ -339,13 +598,7 @@
     branch_grad = middle_grad.astype(BF16)
     no_grad = jnp.zeros((rows, LANES), BF16)
 
-    def with_gain(terms, gain_grad):
-        column = jnp.zeros((width, LANES), BF16).at[:, 0].set(gain_grad.astype(BF16))
-        return lax.dynamic_update_slice(terms, column, (0, terms.shape[1] - LANES))
-
-    out_terms = with_gain(
-        tn(attended, jnp.concatenate([branch_grad, no_grad], axis=1)).astype(BF16), gain_two_grad
-    )
+    out_terms = tn(attended, branch_grad).astype(BF16)
     attended_grad = nt(branch_grad, out_full).astype(BF16)
     attended_grad, out_terms = lax.optimization_barrier((attended_grad, out_terms))
     attended_grad = attended_grad.reshape(rows, kv_heads, group_size, HEAD_DIM).transpose(
@@ -392,19 +645,31 @@
     )
     query_grad = query_grad.reshape(rows, q_width).astype(BF16)
     projected_grad = jnp.concatenate([query_grad, key_grad, value_grad, no_grad], axis=1)
-    returned, projected_grad = lax.optimization_barrier((returned, projected_grad))
     normed_grad = nt(projected_grad, packed_full)
     input_norm_grad, gain_one_grad = norm_back(inputs, scale_one, gain_one, normed_grad)
     input_grad = middle_grad + input_norm_grad
 
-    out_owned = lax.psum_scatter(out_terms, BOTH, scatter_dimension=0, tiled=True)
-    query_terms = with_gain(tn(normed, projected_grad).astype(BF16), gain_one_grad)
-    query_terms, up_grad, down_grad = lax.optimization_barrier((query_terms, up_grad, down_grad))
-    owned = lax.psum_scatter(query_terms, BOTH, scatter_dimension=0, tiled=True).astype(F32)
-    pieces = to_owners([up_grad, down_grad], 6, "return_up_down_grads")
-    out_owned, *pieces = lax.optimization_barrier((out_owned, *pieces))
-    out_owned = out_owned.astype(F32)
-    expert_grads = [owned_sum(piece) for piece in (gate_pieces, *pieces)]
+    gain_columns = jnp.zeros((width, LANES), BF16)
+    gain_columns = gain_columns.at[:, 0].set(gain_one_grad.astype(BF16))
+    gain_columns = gain_columns.at[:, 1].set(gain_two_grad.astype(BF16))
+    query_terms = lax.dynamic_update_slice(
+        tn(normed, projected_grad).astype(BF16), gain_columns, (0, projected_grad.shape[1] - LANES)
+    )
+    down_pieces = pieces_of(down_grad)
+    if staged:
+        out_owned, owned, down_pieces = staged_scatter(
+            [out_terms, query_terms], [down_pieces], piece_block, 6, "scatter_attention_grads"
+        )
+    else:
+        terms = jnp.concatenate([out_terms, query_terms], axis=1)
+        terms = lax.psum_scatter(terms, BOTH, scatter_dimension=0, tiled=True).astype(F32)
+        out_owned, owned = terms[:, :width], terms[:, width:]
+        (down_pieces,) = seq_exchange(
+            [down_pieces], 6, piece_block, [w_down.shape[1:]], "return_down_grads"
+        )
+    returned, owned = lax.optimization_barrier((returned, owned))
+    expert_grads = [owned_sum(piece) for piece in (gate_pieces, up_pieces, down_pieces)]
+
     gate_high = gate_rows.astype(BF16)
     gate_low = (gate_rows - gate_high.astype(F32)).astype(BF16)
 
@@ -419,11 +684,11 @@
         layer_out[None],
         input_grad[None],
         owned[:, q_width + 2 * kv_width],
-        out_owned[:, width],
+        owned[:, q_width + 2 * kv_width + 1],
         owned[:, :q_width],
         owned[:, q_width : q_width + kv_width],
         owned[:, q_width + kv_width : q_width + 2 * kv_width],
-        out_owned[:, :width],
+        out_owned,
         *expert_grads,
     )
 

time: 739 us -> 689 us (0.932)
  waiting for transfers between devices: 159 us -> 15.7 us
  Pallas kernels: 306 us -> 424 us
  between operations: 15.7 us -> 2.62 us
  other arithmetic: 51.6 us -> 44.1 us
    pallas_call x0 -> x2, Pallas kernels: none -> 183 us  [the longest x1 101 us: staged_scatter(): pl.pallas_call(functools.partial(scatter_kernel, line, chunks, n, len(ext...]
    pallas_call x6 -> x4, Pallas kernels: 306 us -> 241 us  [seq_exchange(): pl.pallas_call(functools.partial(exchange_kernel, count, n, block_of), ou...]
    reduce_scatter x2 -> x0, waiting for transfers between devices: 49.7 us -> none  [the longest x1 49.7 us: on_device(): lax.psum_scatter(query_terms, BOTH, scatter_dimension=0, tiled=True)]
    all_gather x2 -> x0, waiting for transfers between devices: 46.5 us -> none  [the longest x1 31.5 us: on_device(): out_full = lax.all_gather(w_out, BOTH, axis=0, tiled=True)]
    all_to_all x4, waiting for transfers between devices: 61.6 us -> 15.7 us  [swap(): return lax.all_to_all(blocks, axes, split_axis=0, concat_axis=0, tiled=True)]
    optimization_barrier x0 -> x1, local copies, waits for them, and re-layouts: none -> 9.83 us  [on_device(): lax.optimization_barrier((packed_full, out_full, gate_full, grad_send))]
    unnamed x115 -> x136, local copies, waits for them, and re-layouts: 14 us -> 18.5 us
  transfers between devices with their start and end apart: 8 -> 4, of which waited for: 7 -> 1; matrix products, arithmetic and copies ran while one was open for 22% -> 20% of each run, Pallas kernels for 42% -> 50%
where the time goes in v4:
time: 689 us; the launch traced here: 682 us
  Pallas kernels  424 us (62%)
  matrix products  127 us (18%)
  local copies, waits for them, and re-layouts  50.4 us (7%)
  other arithmetic  44.1 us (6%)
  starting transfers between devices  18 us (3%)
  waiting for transfers between devices  15.7 us (2%)
    pallas_call x4, Pallas kernels, seq_exchange(): pl.pallas_call(functools.partial(exchange_kernel, count, n, block_of), ou...  241 us
    pallas_call x1, Pallas kernels, staged_scatter(): pl.pallas_call(functools.partial(scatter_kernel, line, chunks, n, len(ext...  101 us
    dot_general x20, matrix products, dot(): lax.dot_general(left, right, (contract, ((), ())), preferred_element_type...  98.2 us
    pallas_call x1, Pallas kernels, staged_gather(): pl.pallas_call(functools.partial(gather_kernel, line, chunks, n, len(extr...  82.5 us
    unnamed x136, local copies, waits for them, and re-layouts  18.5 us
    all_to_all x4, starting transfers between devices, swap(): return lax.all_to_all(blocks, axes, split_axis=0, concat_axis=0, tiled=True)  18 us
    all_to_all x4, waiting for transfers between devices, swap(): return lax.all_to_all(blocks, axes, split_axis=0, concat_axis=0, tiled=True)  15.7 us
  transfers between devices with their start and end apart: 4, of which 1 were waited for; matrix products, arithmetic and copies ran while one was open for 20% of the time, Pallas kernels for 50%

profile of v4, /device:TPU:0, one launch (start us, length us, event | category | flops | bytes accessed | tf_op | source)
XLA Modules:
  0.0 682.1 jit_solution(7359406672785478653)
XLA Ops:
  12.8 4.5 fusion.70
  17.5 82.5 %gather_attention_weights.1 = (bf16[2,2,4,2,48,2176]{5,4,3,2,1,0:T(8,128)(2,1)S(1)}, bf16[2,2,4,2,48,1536]{5,4,3,2,1,0:T(8,128)(2,1)S(1)}, bf16[4,384,768]{2,1,0:T(8,128)(2,1)S(1)}) custom-call(bf16[48,2176]{1,0:T(8,128)(2,1)S(1)} %concatenate.43.refs_0_, bf16[48,1536]{1,0:T(8,128)(2,1)S(1)} %copy-done.10, bf16[4,384,768]{2,1,0:T(8,128)(2,1)S(1)} %copy-done.4), custom_call_target="tpu_custom_call" | custom-call | bytes 114032640 | tf_op jit(solution)/shard_map/gather_attention_weights/pallas_call | solution.py:271
  110.2 9.8 %copy.114 = bf16[1536,2176]{0,1:T(8,128)(2,1)} copy(bf16[1536,2176]{1,0:T(8,128)(2,1)} %bitcast.336) | data formatting | bytes 13369344 | tf_op jit(solution)/shard_map/optimization_barrier | solution.py:504
  121.2 5.0 fusion.93
  134.5 26.8 %gather_keys.1 = bf16[4,256,512]{2,1,0:T(8,128)(2,1)S(1)} custom-call(bf16[256,512]{1,0:T(8,128)(2,1)S(1)} %pad_maximum_fusion.2.refs_0_), custom_call_target="tpu_custom_call" | custom-call | bytes 15728640 | tf_op jit(solution)/shard_map/gather_keys/pallas_call | solution.py:419
  163.8 10.6 %while.34 = (s32[]{:T(128)}, bf16[2,256,6,128]{1,3,2,0:T(8,128)(2,1)S(1)}, f32[2,6,256]{2,1,0:T(8,128)S(1)}, bf16[2,1024,128]{1,2,0:T(8,128)(2,1)S(1)}, s32[]{:T...) while((s32[]{:T(128)}, ...), condition=%wide.region_7.8_spmd.clone.clone.clone, body=%wide.region_4.7_spmd.clone.clone.sunk.clone | while | flops 824704768 | bytes 21692512 | solution.py:535
  183.1 15.7 %all-to-all-done = bf16[32,40,1536]{2,1,0:T(8,128)(2,1)} async-done(((bf16[32,40,1536]{2,1,0:T(8,128)(2,1)}), bf16[32,40,1536]{2,1,0:T(8,128)(2,1)}, u32[]{:S(2)}, u32[]{:S(2)}) %all-to-all-start) | async-done | bytes 3932192 | tf_op jit(solution)/shard_map/all_to_all | solution.py:120
  198.7 6.1 all-to-all-start.1
  206.5 100.6 %gather_up_down.1 = (bf16[4,384,768]{2,1,0:T(8,128)(2,1)S(1)}, bf16[4,192,1536]{2,1,0:T(8,128)(2,1)S(1)}) custom-call(bf16[4,384,768]{2,1,0:T(8,128)(2,1)S(1)} %copy-done.5, bf16[4,192,1536]{2,1,0:T(8,128)(2,1)S(1)} %copy-done.6), custom_call_target="tpu_custom_call" | custom-call | bytes 70778880 | tf_op jit(solution)/shard_map/gather_up_down/pallas_call | solution.py:419
  310.0 6.2 fusion.117
  316.3 5.5 fusion.116
  321.8 7.9 %multiply_convert_fusion = (bf16[1280,768]{1,0:T(8,128)(2,1)S(1)}, bf16[1280,768]{1,0:T(8,128)(2,1)S(1)}, bf16[1280,768]{1,0:T(8,128)(2,1)}) fusion(f32[1280,768]{1,0:T(8,128)S(1)} %fusion.116, f32[1280,768]{1,0:T(8,128)S(1)} %fusion.117, bf16[1280,1536]{1,0:T(8,128)(2,1)} %bitcast.25, bf16[768,1536]{1,0:T(8,128)(2,1)S(1)} %bitcast.346), kind=kOutput, calls=%fused_computation.90 | convolution fusion | flops 3034644480 | bytes 20054016 | tf_op jit(solution)/shard_map/dot_general | solution.py:46
  333.0 5.1 fusion.69
  344.3 6.0 convolution_convert_fusion.5
  350.3 5.4 convolution_convert_fusion.6
  355.7 88.7 %return_gate_up_grads.1 = (bf16[4,384,768]{2,1,0:T(8,128)(2,1)S(1)}, bf16[4,384,768]{2,1,0:T(8,128)(2,1)S(1)}) custom-call(bf16[4,384,768]{2,1,0:T(8,128)(2,1)S(1)} %bitcast.342, bf16[4,384,768]{2,1,0:T(8,128)(2,1)S(1)} %bitcast.341), custom_call_target="tpu_custom_call" | custom-call | bytes 70778880 | tf_op jit(solution)/shard_map/return_gate_up_grads/pallas_call | solution.py:419
  445.9 4.7 convolution_convert_fusion.2
  450.6 6.8 %convolution_convert_fusion.4 = bf16[768,1536]{1,0:T(8,128)(2,1)} fusion(bf16[1280,768]{1,0:T(8,128)(2,1)S(1)} %copy-done.63, bf16[1280,1536]{1,0:T(8,128)(2,1)} %bitcast.25), kind=kOutput, calls=%fused_computation.95 | convolution fusion | flops 3021078528 | bytes 8257536 | tf_op jit(solution)/shard_map/dot_general | solution.py:46
  457.5 4.7 multiply_reduce_fusion
  475.6 31.6 %while.35 = (s32[]{:T(128)}, f32[2,256,6,128]{1,3,2,0:T(8,128)}, bf16[2,1024,128]{2,1,0:T(8,128)(2,1)}, bf16[2,1024,128]{2,1,0:T(8,128)(2,1)}, bf16[2,1024,128]{...) while((s32[]{:T(128)}, f32[2,256,6,128]{1,3,2,0:T(8,128)}, ...), condition=%wide.region_13.14_spmd.clone.clone.clone, body=%wide.region_11.13_spmd.clone.clone.sunk.clone | while | flops 2037710592 | bytes 73456872 | solution.py:607
  513.0 24.6 %return_key_grads.1 = bf16[4,256,512]{2,1,0:T(8,128)(2,1)S(1)} custom-call(bf16[4,256,512]{2,1,0:T(8,128)(2,1)S(1)} %pad_maximum_fusion.refs_0_), custom_call_target="tpu_custom_call" | custom-call | bytes 15728640 | tf_op jit(solution)/shard_map/return_key_grads/pallas_call | solution.py:419
  541.8 7.7 %fusion.85 = (f32[256]{0:T(256)}, bf16[1536]{0:T(1024)(128)(2,1)S(1)}, f32[256,1536]{1,0:T(8,128)}) fusion(bf16[1,256,1536]{2,1,0:T(8,128)(2,1)} %param.23, f32[1536]{0:T(1024)S(1)} %copy-done.53, f32[256]{0:T(256)S(1)} %copy-done.59, bf16[1536,2176]{1,0:T(8,128)(2,1)} %bitcast.338, bf16[256,256]{0,1:T(8,128)(2,1)S(1)} %copy.132, ...), kind=kOutput, calls=%fused_computation.119 | convolution fusion | flops 1718483200 | bytes 10108160 | tf_op jit(solution)/shard_map/dot_general | solution.py:46
  559.7 100.5 %scatter_attention_grads.1 = (f32[48,1536]{1,0:T(8,128)S(1)}, f32[48,2176]{1,0:T(8,128)S(1)}, bf16[4,192,1536]{2,1,0:T(8,128)(2,1)S(1)}) custom-call(bf16[2,2,4,2,48,1536]{5,4,3,2,1,0:T(8,128)(2,1)S(1)} %bitcast.331, bf16[2,2,4,2,48,2176]{5,4,3,2,1,0:T(8,128)(2,1)S(1)} %bitcast.339, bf16[4,192,1536]{2,1,0:T(8,128)(2,1)S(1)} %bitcast.343), custom_call_target="tpu_custom_call" | custom-call | bytes 11403264 | tf_op jit(solution)/shard_map/scatter_attention_grads/pallas_call | solution.py:386
  676.7 4.5 fusion.73
  (285 shorter events, 149.7 us)
Async XLA Ops:
  2.7 10.0 %copy-start.56 = (pred[256]{0:T(512)(128)(4,1)}, pred[256]{0:T(512)(128)(4,1)S(1)}, u32[]{:S(2)}) copy-start(pred[256]{0:T(512)(128)(4,1)S(1)} %fusion.111) | copy-start | bytes 772
  7.5 9.8 %copy-start.35 = (pred[256,1280]{1,0:T(8,128)(4,1)}, pred[256,1280]{1,0:T(8,128)(4,1)S(1)}, u32[]{:S(2)}) copy-start(pred[256,1280]{1,0:T(8,128)(4,1)S(1)} %fusion.71) | copy-start | bytes 983044
  106.3 92.4 %all-to-all-start = ((bf16[32,40,1536]{2,1,0:T(8,128)(2,1)}), bf16[32,40,1536]{2,1,0:T(8,128)(2,1)}, u32[]{:S(2)}, u32[]{:S(2)}) async-start(bf16[32,40,1536]{2,1,0:T(8,128)(2,1)} %bitcast.357), calls=%async_computation | async-start | bytes 7864320 | tf_op jit(solution)/shard_map/all_to_all | solution.py:120
  110.2 10.7 %copy-start.29 = (bf16[1,256,1536]{2,1,0:T(8,128)(2,1)S(1)}, bf16[1,256,1536]{2,1,0:T(8,128)(2,1)}, u32[]{:S(2)}) copy-start(bf16[1,256,1536]{2,1,0:T(8,128)(2,1)} %param.23) | copy-start | bytes 2359300
  120.9 5.3 copy-start.52
  121.2 5.0 copy-start.58
  174.4 5.4 copy-start.19
  198.7 6.1 copy-start.5
  198.7 111.3 %all-to-all-start.1 = ((bf16[32,40,1536]{2,1,0:T(8,128)(2,1)}), bf16[32,40,1536]{2,1,0:T(8,128)(2,1)}, u32[]{:S(2)}, u32[]{:S(2)}) async-start(bf16[32,40,1536]{2,1,0:T(8,128)(2,1)} %bitcast.350), calls=%async_computation.1 | async-start | bytes 7864320 | tf_op jit(solution)/shard_map/all_to_all | solution.py:120
  310.0 6.2 copy-start.12
  316.3 5.5 copy-start.14
  338.0 119.4 %all-to-all-start.2 = ((bf16[32,40,1536]{2,1,0:T(8,128)(2,1)}), bf16[32,40,1536]{2,1,0:T(8,128)(2,1)}, u32[]{:S(2)}, u32[]{:S(2)}) async-start(bf16[32,40,1536]{2,1,0:T(8,128)(2,1)} %bitcast.358), calls=%async_computation.2 | async-start | bytes 7864320 | tf_op jit(solution)/shard_map/all_to_all | solution.py:120
  355.7 90.2 %copy-start.15 = (bf16[4,192,1536]{2,1,0:T(8,128)(2,1)S(1)}, bf16[4,192,1536]{2,1,0:T(8,128)(2,1)}, u32[]{:S(2)}) copy-start(bf16[4,192,1536]{2,1,0:T(8,128)(2,1)} %copy-done.13) | copy-start | bytes 7077892
  355.7 90.2 %copy-start.63 = (bf16[1280,768]{1,0:T(8,128)(2,1)S(1)}, bf16[1280,768]{1,0:T(8,128)(2,1)}, u32[]{:S(2)}) copy-start(bf16[1280,768]{1,0:T(8,128)(2,1)} %get-tuple-element.436) | copy-start | bytes 5898244
  450.6 6.8 %copy-start.37 = (pred[256,1280]{1,0:T(8,128)(4,1)S(1)}, pred[256,1280]{1,0:T(8,128)(4,1)}, u32[]{:S(2)}) copy-start(pred[256,1280]{1,0:T(8,128)(4,1)} %copy-done.35) | copy-start | bytes 983044
  457.5 4.8 copy-start.22
  457.5 4.8 copy-start.46
  471.6 199.7 %all-to-all-start.3 = ((bf16[32,40,1536]{2,1,0:T(8,128)(2,1)}), bf16[32,40,1536]{2,1,0:T(8,128)(2,1)}, u32[]{:S(2)}, u32[]{:S(2)}) async-start(bf16[32,40,1536]{2,1,0:T(8,128)(2,1)} %bitcast.356), calls=%async_computation.3 | async-start | bytes 7864320 | tf_op jit(solution)/shard_map/all_to_all | solution.py:120
  513.0 25.0 %copy-start.42 = (f32[256,64]{1,0:T(8,128)S(1)}, f32[256,64]{1,0:T(8,128)}, u32[]{:S(2)}) copy-start(f32[256,64]{1,0:T(8,128)} %copy-done.41) | copy-start | bytes 196612
  540.0 9.5 %copy-start.50 = (bf16[256,256]{0,1:T(8,128)(2,1)}, bf16[256,256]{0,1:T(8,128)(2,1)S(1)}, u32[]{:S(2)}) copy-start(bf16[256,256]{0,1:T(8,128)(2,1)S(1)} %copy.132) | copy-start | bytes 393220
  541.8 7.7 %copy-start.45 = (bf16[256,12,128]{0,2,1:T(8,128)(2,1)}, bf16[256,12,128]{0,2,1:T(8,128)(2,1)S(1)}, u32[]{:S(2)}) copy-start(bf16[256,12,128]{0,2,1:T(8,128)(2,1)S(1)} %pad_maximum_fusion.1) | copy-start | bytes 2359300
  541.8 9.5 %copy-start.61 = (bf16[1536]{0:T(1024)(128)(2,1)S(1)}, bf16[1536]{0:T(1024)(128)(2,1)}, u32[]{:S(2)}) copy-start(bf16[1536]{0:T(1024)(128)(2,1)} %get-tuple-element.383) | copy-start | bytes 9220
  549.5 6.0 copy-start.51
  552.2 7.5 %slice-start = ((s8[4718592]{0:T(1024)(128)(4,1)}), s8[524288]{0:T(1024)(128)(4,1)S(1)}, s32[]{:S(2)}) async-start(s8[4718592]{0:T(1024)(128)(4,1)} %bitcast.329), calls=%async_computation.4 | async-start | bytes 1048576
  (54 other events, 171.9 us)

commit v5 on v4

--- a/solution.py
+++ b/solution.py
@@ -146,14 +146,13 @@
     pl.semaphore_wait(barrier, len(peers))
 
 
-def column_chunks(widths, limit):
+def column_chunks(widths, parts):
     chunks = []
-    for k, whole in enumerate(widths):
-        start = 0
-        while start < whole:
-            size = limit if whole - start >= 2 * limit else whole - start
-            chunks.append((k, start, size))
-            start += size
+    for part in range(parts):
+        for k, whole in enumerate(widths):
+            tiles = whole // LANES
+            first, end = tiles * part // parts, tiles * (part + 1) // parts
+            chunks.append((k, first * LANES, (end - first) * LANES))
     return chunks
 
 
@@ -202,6 +201,14 @@
     ]
 
 
+def in_steps(count, stages):
+    for step in range((count + 1) // 2 + len(stages) - 1):
+        for behind, stage in enumerate(stages):
+            for i in (2 * (step - behind), 2 * (step - behind) + 1):
+                if 0 <= i < count:
+                    stage(i)
+
+
 def gather_kernel(line, chunks, n, extras, block_of, *refs):
     sources, more_sources = refs[:n], refs[n : n + extras]
     refs = refs[n + extras :]
@@ -218,41 +225,57 @@
         sent.append(copy)
         return copy
 
-    arriving = []
-    for i, (k, first, size) in enumerate(chunks):
+    along_line, first_hop, second_hop, third_hop = {}, {}, {}, {}
+
+    def send_line(i):
+        k, first, size = chunks[i]
         cols = pl.ds(first, size)
         own = targets[k].at[a, b, z, c, :, cols]
         keep = pltpu.make_async_copy(sources[k].at[:, cols], own, local.at[i])
         keep.start()
-        waits = []
-        for step in range(1, line):
-            peer = torus_id(a, b, lax.rem(z + step, line), c)
-            waits.append(start(remote(sources[k].at[:, cols], own, sems, i, 2 + step, peer)))
-        arriving.append((keep, waits))
-    pending = []
-    for i, (k, first, size) in enumerate(chunks):
-        keep, waits = arriving[i]
+        along_line[i] = [
+            start(
+                remote(
+                    sources[k].at[:, cols],
+                    own,
+                    sems,
+                    i,
+                    2 + step,
+                    torus_id(a, b, lax.rem(z + step, line), c),
+                )
+            )
+            for step in range(1, line)
+        ]
+        along_line[i].append(keep)
+
+    def send_first(i):
+        k, first, size = chunks[i]
+        *copies, keep = along_line[i]
         keep.wait()
-        for copy in waits:
+        for copy in copies:
             copy.wait_recv()
         block = targets[k].at[a, b, :, c, :, pl.ds(first, size)]
         peer = torus_id(a, 1 - b, z, c) if i % 2 == 0 else torus_id(1 - a, b, z, c)
-        pending.append(start(remote(block, block, sems, i, 1, peer)))
-    second = []
-    for i, (k, first, size) in enumerate(chunks):
-        pending[i].wait_recv()
+        first_hop[i] = start(remote(block, block, sems, i, 1, peer))
+
+    def send_second(i):
+        k, first, size = chunks[i]
+        first_hop[i].wait_recv()
         cols = pl.ds(first, size)
         if i % 2 == 0:
             block, peer = targets[k].at[a, :, :, c, :, cols], torus_id(1 - a, b, z, c)
         else:
             block, peer = targets[k].at[:, b, :, c, :, cols], torus_id(a, 1 - b, z, c)
-        second.append(start(remote(block, block, sems, i, 2, peer)))
-    third = []
-    for i, (k, first, size) in enumerate(chunks):
-        second[i].wait_recv()
+        second_hop[i] = start(remote(block, block, sems, i, 2, peer))
+
+    def send_third(i):
+        k, first, size = chunks[i]
+        second_hop[i].wait_recv()
         block = targets[k].at[:, :, :, c, :, pl.ds(first, size)]
-        third.append(start(remote(block, block, sems, i, 0, torus_id(a, b, z, 1 - c))))
-    for copy in third:
+        third_hop[i] = start(remote(block, block, sems, i, 0, torus_id(a, b, z, 1 - c)))
+
+    in_steps(len(chunks), [send_line, send_first, send_second, send_third])
+    for copy in third_hop.values():
         copy.wait_recv()
     for copy in sent:
         copy.wait_send()
@@ -260,10 +283,10 @@
         copy.wait()
 
 
-def staged_gather(arrays, extras, block_of, collective_id, name):
+def staged_gather(arrays, extras, block_of, collective_id, name, parts=6):
     seq_count, line = lax.axis_size("seq"), lax.axis_size("dp") // 2
     rows, n = arrays[0].shape[0], len(arrays)
-    chunks = column_chunks([x.shape[1] for x in arrays], 512)
+    chunks = column_chunks([x.shape[1] for x in arrays], parts)
     m = len(chunks)
     shape = (seq_count // 2, 2, line, 2, rows)
     size = sum(x.shape[1] for x in arrays) * rows * 64
@@ -314,19 +337,20 @@
 
         lax.fori_loop(0, line, one, 0)
 
-    first_stage = []
-    for i, (k, first, size) in enumerate(chunks):
+    between_cores, first_hop, second_hop, along_line = {}, {}, {}, {}
+
+    def send_core(i):
+        k, first, size = chunks[i]
         cols = pl.ds(first, size)
         keep = pltpu.make_async_copy(sources[k].at[:, :, :, c, :, cols], owns[i], local.at[i])
         keep.start()
         swap_core = remote(
             sources[k].at[:, :, :, 1 - c, :, cols], ins1[i], sems, i, 0, torus_id(a, b, z, 1 - c)
         )
-        first_stage.append((keep, start(swap_core)))
-    more = start_exchange(4, more_sources, more_targets, block_of, more_sems) if extras else []
-    second_stage = []
-    for i in range(m):
-        keep, copy = first_stage[i]
+        between_cores[i] = (keep, start(swap_core))
+
+    def send_first(i):
+        keep, copy = between_cores[i]
         keep.wait()
         copy.wait_recv()
         for p in range(2):
@@ -336,10 +360,10 @@
             block, peer = owns[i].at[:, 1 - b], torus_id(a, 1 - b, z, c)
         else:
             block, peer = owns[i].at[1 - a], torus_id(1 - a, b, z, c)
-        second_stage.append(start(remote(block, ins2[i], sems, i, 1, peer)))
-    third_stage = []
-    for i in range(m):
-        second_stage[i].wait_recv()
+        first_hop[i] = start(remote(block, ins2[i], sems, i, 1, peer))
+
+    def send_second(i):
+        first_hop[i].wait_recv()
         for p in range(2):
             mine = owns[i].at[p, b] if i % 2 == 0 else owns[i].at[a, p]
             add_lines(accs2[i].at[p], mine, ins2[i].at[p])
@@ -347,38 +371,38 @@
             block, peer = accs2[i].at[1 - a], torus_id(1 - a, b, z, c)
         else:
             block, peer = accs2[i].at[1 - b], torus_id(a, 1 - b, z, c)
-        third_stage.append(start(remote(block, ins3[i], sems, i, 2, peer)))
-    last_stage = []
-    for i in range(m):
-        third_stage[i].wait_recv()
+        second_hop[i] = start(remote(block, ins3[i], sems, i, 2, peer))
+
+    def send_line(i):
+        second_hop[i].wait_recv()
         add_lines(accs3[i], accs2[i].at[a if i % 2 == 0 else b], ins3[i])
         copies = []
         for step in range(1, line):
             to = lax.rem(z + step, line)
-            copies.append(
-                start(
-                    remote(
-                        accs3[i].at[to], ins4[i].at[z], sems, i, 2 + step, torus_id(a, b, to, c)
-                    )
-                )
-            )
-        last_stage.append(copies)
-    for i, (k, first, size) in enumerate(chunks):
+            peer = torus_id(a, b, to, c)
+            copies.append(start(remote(accs3[i].at[to], ins4[i].at[z], sems, i, 2 + step, peer)))
+        along_line[i] = copies
+
+    def finish(i):
+        k, first, size = chunks[i]
         total = accs3[i][z].astype(F32)
         for step in range(1, line):
-            last_stage[i][step - 1].wait_recv()
+            along_line[i][step - 1].wait_recv()
             total = total + ins4[i][lax.rem(z + line - step, line)].astype(F32)
         targets[k][:, first : first + size] = total
+
+    more = start_exchange(4, more_sources, more_targets, block_of, more_sems) if extras else []
+    in_steps(m, [send_core, send_first, send_second, send_line, finish])
     for copy in sent:
         copy.wait_send()
     for copy in more:
         copy.wait()
 
 
-def staged_scatter(arrays, extras, block_of, collective_id, name):
+def staged_scatter(arrays, extras, block_of, collective_id, name, parts=6):
     seq_count, line = lax.axis_size("seq"), lax.axis_size("dp") // 2
     rows, n = arrays[0].shape[0] // (2 * line * seq_count), len(arrays)
-    chunks = column_chunks([x.shape[1] for x in arrays], 512)
+    chunks = column_chunks([x.shape[1] for x in arrays], parts)
     m = len(chunks)
     leads = [(2, 2, line), (2, 2, line), (2, line), (2, line), (line,), (line,), (line,)]
     size = sum(x.shape[1] for x in arrays) * rows * 64
@@ -401,7 +425,7 @@
         compiler_params=pltpu.CompilerParams(
             collective_id=collective_id, vmem_limit_bytes=36 << 20
         ),
-        cost_estimate=pl.CostEstimate(flops=0, bytes_accessed=size, transcendentals=0),
+        cost_estimate=pl.CostEstimate(flops=0, bytes_accessed=10 * size, transcendentals=0),
         name=name,
     )(*[x.reshape(2, 2, line, 2, rows, x.shape[1]) for x in arrays], *extras)
 
@@ -428,6 +452,24 @@
         cost_estimate=pl.CostEstimate(flops=0, bytes_accessed=20 * sent, transcendentals=0),
         name=name,
     )(*arrays)
+
+
+def seq_permutes(block_for):
+    count, me = lax.axis_size("seq"), lax.axis_index("seq")
+    pieces = [block_for(me)]
+    for step in range(1, count):
+        ring = [(i, (i + step) % count) for i in range(count)]
+        pieces.append(lax.ppermute(block_for(lax.rem(me + step, count)), "seq", ring))
+    return pieces
+
+
+def in_seq_order(pieces, dtype):
+    count, me = len(pieces), lax.axis_index("seq")
+    whole = jnp.zeros((count,) + pieces[0].shape, dtype)
+    for step, piece in enumerate(pieces):
+        place = lax.rem(me + count - step, count)
+        whole = lax.dynamic_update_index_in_dim(whole, piece.astype(dtype), place, 0)
+    return whole
 
 
 def on_device(
@@ -475,17 +517,21 @@
     )
     packed = jnp.concatenate([w_query, key_projection, value_projection, gain_block], axis=1)
     staged = seq_count == 4 and w_query.shape[0] % 16 == 0
-    owner_block = lambda ref, peer: ref.at[peer // sharers]
-    piece_block = lambda ref, peer: ref.at[peer]
-
+
+    def expert_pieces(weights):
+        def block_for(peer):
+            return lax.dynamic_index_in_dim(weights, peer // sharers, 0, keepdims=False)
+
+        return seq_permutes(block_for)
+
+    gate_parts = expert_pieces(w_gate)
     if staged:
-        packed_full, out_full, gate_full = staged_gather(
-            [packed, w_out], [w_gate], owner_block, 2, "gather_attention_weights"
+        packed_full, out_full = staged_gather(
+            [packed, w_out], [], None, 2, "gather_attention_weights"
         )
     else:
         packed_full = lax.all_gather(packed, BOTH, axis=0, tiled=True)
         out_full = lax.all_gather(w_out, BOTH, axis=0, tiled=True)
-        (gate_full,) = seq_exchange([w_gate], 2, owner_block, [w_gate.shape[1:]], "gather_gate")
 
     pair_routes, place, kept = claim_places(routes[0], priority[0, 0], is_valid)
     holder = (pair_routes // own_experts) * seq_count + (pair_routes % own_experts) * sharers
@@ -501,9 +547,10 @@
     live_cotangent = jnp.where(is_valid[:, None], cotangent[0], jnp.zeros((), BF16))
     out_grad = live_cotangent.astype(F32)
     grad_send = (tn(token_hot, live_cotangent) * slot_gate[:, None]).astype(BF16)
-    packed_full, out_full, gate_full, grad_send = lax.optimization_barrier(
-        (packed_full, out_full, gate_full, grad_send)
-    )
+    packed_full, out_full, gate_parts, grad_send, w_up, w_down = lax.optimization_barrier(
+        (packed_full, out_full, gate_parts, grad_send, w_up, w_down)
+    )
+    up_parts, down_parts = expert_pieces(w_up), expert_pieces(w_down)
     gain_one = packed_full[:, q_width + 2 * kv_width].astype(F32)
     gain_two = packed_full[:, q_width + 2 * kv_width + 1].astype(F32)
     grad_rows = swap(grad_send.reshape(devices, CAP, width), ("dp", "seq")).reshape(slots, width)
@@ -544,17 +591,14 @@
     moe_input = (middle * scale_two * gain_two).astype(BF16)
 
     send_rows = tn(token_hot, moe_input).astype(BF16).reshape(devices, CAP, width)
-    send_rows, grad_rows, w_up, w_down = lax.optimization_barrier(
-        (send_rows, grad_rows, w_up, w_down)
-    )
+    send_rows, grad_rows, up_parts = lax.optimization_barrier((send_rows, grad_rows, up_parts))
     slot_rows = swap(send_rows, ("dp", "seq")).reshape(slots, width)
-    up_full, down_full = seq_exchange(
-        [w_up, w_down], 5, owner_block, [w_up.shape[1:], w_down.shape[1:]], "gather_up_down"
-    )
-    slot_rows, up_full, down_full = lax.optimization_barrier((slot_rows, up_full, down_full))
-    gate_full = gate_full.reshape(width, hidden_units)
-    up_full = up_full.reshape(width, hidden_units)
-    down_full = down_full.reshape(hidden_units, width)
+    gate_full = in_seq_order(gate_parts, BF16).reshape(width, hidden_units)
+    up_full = in_seq_order(up_parts, BF16).reshape(width, hidden_units)
+    down_full = in_seq_order(down_parts, BF16).reshape(hidden_units, width)
+    slot_rows, gate_full, up_full, down_full = lax.optimization_barrier(
+        (slot_rows, gate_full, up_full, down_full)
+    )
     gate_pre = nn(slot_rows, gate_full)
     up_pre = nn(slot_rows, up_full)
     gate_sigmoid = jax.nn.sigmoid(gate_pre)
@@ -571,24 +615,21 @@
     up_grad = tn(slot_rows, up_pre_grad).astype(BF16)
     down_grad = tn(expert_hidden, grad_rows).astype(BF16)
 
-    def pieces_of(grad):
-        return grad.reshape(seq_count, -1, grad.shape[1])
-
-    gate_pieces, up_pieces = seq_exchange(
-        [pieces_of(gate_grad), pieces_of(up_grad)],
-        3,
-        piece_block,
-        [w_gate.shape[1:], w_up.shape[1:]],
-        "return_gate_up_grads",
-    )
-    row_back, gate_pieces, up_pieces, down_grad = lax.optimization_barrier(
-        (row_back, gate_pieces, up_pieces, down_grad)
-    )
-
-    def owned_sum(piece):
-        piece = piece.reshape((own_experts, sharers) + piece.shape[1:])
-        return jnp.sum(piece.astype(F32), axis=1)
-
+    def to_owners(grad):
+        grad = grad.reshape(seq_count, -1, grad.shape[1])
+
+        def block_for(peer):
+            return lax.dynamic_index_in_dim(grad, peer, 0, keepdims=False)
+
+        return seq_permutes(block_for)
+
+    def owned_sum(pieces):
+        whole = in_seq_order(pieces, F32)
+        return jnp.sum(whole.reshape((own_experts, sharers) + whole.shape[1:]), axis=1)
+
+    gate_grad_parts, up_grad_parts = to_owners(gate_grad), to_owners(up_grad)
+    row_back, down_grad = lax.optimization_barrier((row_back, down_grad))
+    down_grad_parts = to_owners(down_grad)
     expert_out = nn(expert_hidden, down_full).astype(BF16)
     expert_out, row_back = lax.optimization_barrier((expert_out, row_back))
     returned = swap(expert_out.reshape(devices, CAP, width), ("dp", "seq")).reshape(slots, width)
@@ -655,20 +696,18 @@
     query_terms = lax.dynamic_update_slice(
         tn(normed, projected_grad).astype(BF16), gain_columns, (0, projected_grad.shape[1] - LANES)
     )
-    down_pieces = pieces_of(down_grad)
+    query_terms, down_grad_parts = lax.optimization_barrier((query_terms, down_grad_parts))
+    grad_parts = [gate_grad_parts, up_grad_parts, down_grad_parts]
     if staged:
-        out_owned, owned, down_pieces = staged_scatter(
-            [out_terms, query_terms], [down_pieces], piece_block, 6, "scatter_attention_grads"
+        out_owned, owned = staged_scatter(
+            [out_terms, query_terms], [], None, 6, "scatter_attention_grads"
         )
     else:
         terms = jnp.concatenate([out_terms, query_terms], axis=1)
         terms = lax.psum_scatter(terms, BOTH, scatter_dimension=0, tiled=True).astype(F32)
         out_owned, owned = terms[:, :width], terms[:, width:]
-        (down_pieces,) = seq_exchange(
-            [down_pieces], 6, piece_block, [w_down.shape[1:]], "return_down_grads"
-        )
     returned, owned = lax.optimization_barrier((returned, owned))
-    expert_grads = [owned_sum(piece) for piece in (gate_pieces, up_pieces, down_pieces)]
+    expert_grads = [owned_sum(parts) for parts in grad_parts]
 
     gate_high = gate_rows.astype(BF16)
     gate_low = (gate_rows - gate_high.astype(F32)).astype(BF16)

time: 689 us -> 663 us (0.962)
  Pallas kernels: 424 us -> 207 us
  waiting for transfers between devices: 15.7 us -> 157 us
  starting transfers between devices: 18 us -> 51.1 us
  local copies, waits for them, and re-layouts: 50.4 us -> 65.4 us
    pallas_call x4 -> x2, Pallas kernels: 241 us -> 73.8 us  [seq_exchange(): pl.pallas_call(functools.partial(exchange_kernel, count, n, block_of), ou...]
    ppermute x0 -> x18, waiting for transfers between devices: none -> 146 us  [seq_permutes(): lax.ppermute(block_for(lax.rem(me + step, count)), 'seq', ring)]
    pallas_call x1, Pallas kernels: 101 us -> 67.3 us  [staged_scatter(): pl.pallas_call(functools.partial(scatter_kernel, line, chunks, n, len(ext...]
    ppermute x0 -> x18, starting transfers between devices: none -> 25.2 us  [seq_permutes(): lax.ppermute(block_for(lax.rem(me + step, count)), 'seq', ring)]
    pallas_call x1, Pallas kernels: 82.5 us -> 66 us  [staged_gather(): pl.pallas_call(functools.partial(gather_kernel, line, chunks, n, len(extr...]
    dynamic_update_slice x0 -> x12, other arithmetic: none -> 15.4 us  [in_seq_order(): lax.dynamic_update_index_in_dim(whole, piece.astype(dtype), place, 0)]
    dynamic_update_slice x0 -> x11, local copies, waits for them, and re-layouts: none -> 9.16 us  [in_seq_order(): lax.dynamic_update_index_in_dim(whole, piece.astype(dtype), place, 0)]
    convert_element_type x3 -> x0, other arithmetic: 8.23 us -> none  [owned_sum(): return jnp.sum(piece.astype(F32), axis=1)]
  transfers between devices with their start and end apart: 4 -> 22, of which waited for: 1 -> 13; matrix products, arithmetic and copies ran while one was open for 20% -> 23% of each run, Pallas kernels for 50% -> 32%
where the time goes in v5:
time: 663 us; the launch traced here: 654 us
  Pallas kernels  207 us (31%)
  waiting for transfers between devices  157 us (24%)
  matrix products  125 us (19%)
  local copies, waits for them, and re-layouts  65.4 us (10%)
  starting transfers between devices  51.1 us (8%)
  other arithmetic  44.7 us (7%)
    ppermute x18, waiting for transfers between devices, seq_permutes(): lax.ppermute(block_for(lax.rem(me + step, count)), 'seq', ring)  146 us
    dot_general x20, matrix products, dot(): lax.dot_general(left, right, (contract, ((), ())), preferred_element_type...  98.7 us
    pallas_call x2, Pallas kernels, seq_exchange(): pl.pallas_call(functools.partial(exchange_kernel, count, n, block_of), ou...  73.8 us
    pallas_call x1, Pallas kernels, staged_scatter(): pl.pallas_call(functools.partial(scatter_kernel, line, chunks, n, len(ext...  67.3 us
    pallas_call x1, Pallas kernels, staged_gather(): pl.pallas_call(functools.partial(gather_kernel, line, chunks, n, len(extr...  66 us
    all_to_all x4, starting transfers between devices, swap(): return lax.all_to_all(blocks, axes, split_axis=0, concat_axis=0, tiled=True)  25.9 us
    ppermute x18, starting transfers between devices, seq_permutes(): lax.ppermute(block_for(lax.rem(me + step, count)), 'seq', ring)  25.2 us
    dynamic_update_slice x12, other arithmetic, in_seq_order(): lax.dynamic_update_index_in_dim(whole, piece.astype(dtype), place, 0)  15.4 us
  transfers between devices with their start and end apart: 22, of which 13 were waited for; matrix products, arithmetic and copies ran while one was open for 23% of the time, Pallas kernels for 32%

profile of v5, /device:TPU:0, one launch (start us, length us, event | category | flops | bytes accessed | tf_op | source)
XLA Modules:
  0.0 654.0 jit_solution(14417197163295712292)
XLA Ops:
  19.9 66.0 %gather_attention_weights.1 = (bf16[2,2,4,2,48,2176]{5,4,3,2,1,0:T(8,128)(2,1)S(1)}, bf16[2,2,4,2,48,1536]{5,4,3,2,1,0:T(8,128)(2,1)S(1)}) custom-call(bf16[48,2176]{1,0:T(8,128)(2,1)S(1)} %concatenate.43.refs_0_, bf16[48,1536]{1,0:T(8,128)(2,1)S(1)} %copy-done.2), custom_call_target="tpu_custom_call" | custom-call | bytes 114032640 | tf_op jit(solution)/shard_map/gather_attention_weights/pallas_call | solution.py:294
  94.2 10.0 %copy.114 = bf16[1536,2176]{0,1:T(8,128)(2,1)} copy(bf16[1536,2176]{1,0:T(8,128)(2,1)} %bitcast.430) | data formatting | bytes 13369344 | tf_op jit(solution)/shard_map/optimization_barrier | solution.py:550
  111.9 5.8 all-to-all-start
  119.9 46.2 %gather_keys.1 = bf16[4,256,512]{2,1,0:T(8,128)(2,1)S(1)} custom-call(bf16[256,512]{1,0:T(8,128)(2,1)S(1)} %pad_maximum_fusion.2.refs_0_), custom_call_target="tpu_custom_call" | custom-call | bytes 15728640 | tf_op jit(solution)/shard_map/gather_keys/pallas_call | solution.py:443
  176.8 13.3 %while.34 = (s32[]{:T(128)}, bf16[2,256,6,128]{1,3,2,0:T(8,128)(2,1)}, f32[2,6,256]{2,1,0:T(8,128)}, bf16[2,1024,128]{1,2,0:T(8,128)(2,1)S(1)}, s32[]{:T(128)}, ...) while((s32[]{:T(128)}, ...), condition=%wide.region_7.8_spmd.clone.clone.clone, body=%wide.region_4.7_spmd.clone.clone.sunk.clone | while | flops 824704768 | bytes 21688924 | solution.py:582
  197.6 9.2 %collective-permute-done.4 = bf16[384,768]{1,0:T(8,128)(2,1)} collective-permute-done((bf16[384,768]{1,0:T(8,128)(2,1)}, bf16[384,768]{1,0:T(8,128)(2,1)}, u32[]{:S(2)}, u32[]{:S(2)}) %collective-permute-start.4) | collective-permute-done | bytes 589856 | tf_op jit(solution)/shard_map/ppermute | solution.py:462
  207.1 10.7 %all-to-all-start.1 = ((bf16[32,40,1536]{2,1,0:T(8,128)(2,1)}), bf16[32,40,1536]{2,1,0:T(8,128)(2,1)}, u32[]{:S(2)}, u32[]{:S(2)}) async-start(bf16[32,40,1536]{2,1,0:T(8,128)(2,1)} %bitcast.435), calls=%async_computation.1 | async-start | bytes 7864320 | tf_op jit(solution)/shard_map/all_to_all | solution.py:120
  227.3 47.5 %collective-permute-done.6 = bf16[192,1536]{1,0:T(8,128)(2,1)S(1)} collective-permute-done((bf16[192,1536]{1,0:T(8,128)(2,1)S(1)}, bf16[192,1536]{1,0:T(8,128)(2,1)S(1)}, u32[]{:S(2)}, u32[]{:S(2)}) %collective-permute-start.6) | collective-permute-done | bytes 589856 | tf_op jit(solution)/shard_map/ppermute | solution.py:462
  274.8 7.8 %collective-permute-done.7 = bf16[192,1536]{1,0:T(8,128)(2,1)S(1)} collective-permute-done((bf16[192,1536]{1,0:T(8,128)(2,1)S(1)}, bf16[192,1536]{1,0:T(8,128)(2,1)S(1)}, u32[]{:S(2)}, u32[]{:S(2)}) %collective-permute-start.7) | collective-permute-done | bytes 589856 | tf_op jit(solution)/shard_map/ppermute | solution.py:462
  295.2 11.4 %all-to-all-done.1 = bf16[32,40,1536]{2,1,0:T(8,128)(2,1)} async-done(((bf16[32,40,1536]{2,1,0:T(8,128)(2,1)}), bf16[32,40,1536]{2,1,0:T(8,128)(2,1)}, u32[]{:S(2)}, u32[]{:S(2)}) %all-to-all-start.1) | async-done | bytes 3932192 | tf_op jit(solution)/shard_map/all_to_all | solution.py:120
  306.7 6.2 fusion.117
  318.4 7.9 %multiply_convert_fusion = (bf16[1280,768]{1,0:T(8,128)(2,1)S(1)}, bf16[1280,768]{1,0:T(8,128)(2,1)S(1)}, bf16[1280,768]{1,0:T(8,128)(2,1)}) fusion(f32[1280,768]{1,0:T(8,128)S(1)} %fusion.116, f32[1280,768]{1,0:T(8,128)S(1)} %fusion.117, bf16[1280,1536]{1,0:T(8,128)(2,1)} %bitcast.28, bf16[768,1536]{1,0:T(8,128)(2,1)S(1)} %bitcast.442), kind=kOutput, calls=%fused_computation.90 | convolution fusion | flops 3034644480 | bytes 20054016 | tf_op jit(solution)/shard_map/dot_general | solution.py:46
  329.7 6.5 fusion.69
  344.4 6.1 convolution_convert_fusion.4
  357.8 6.8 %convolution_convert_fusion.6 = bf16[768,1536]{1,0:T(8,128)(2,1)} fusion(bf16[1280,768]{1,0:T(8,128)(2,1)S(1)} %copy-done.60, bf16[1280,1536]{1,0:T(8,128)(2,1)} %bitcast.28), kind=kOutput, calls=%fused_computation.97 | convolution fusion | flops 3021078528 | bytes 8257536 | tf_op jit(solution)/shard_map/dot_general | solution.py:46
  381.5 17.0 %collective-permute-done.15 = bf16[384,768]{1,0:T(8,128)(2,1)S(1)} collective-permute-done((bf16[384,768]{1,0:T(8,128)(2,1)S(1)}, bf16[384,768]{1,0:T(8,128)(2,1)S(1)}, u32[]{:S(2)}, u32[]{:S(2)}) %collective-permute-start.15) | collective-permute-done | bytes 589856 | tf_op jit(solution)/shard_map/ppermute | solution.py:462
  399.6 8.0 %collective-permute-done.16 = bf16[384,768]{1,0:T(8,128)(2,1)S(1)} collective-permute-done((bf16[384,768]{1,0:T(8,128)(2,1)S(1)}, bf16[384,768]{1,0:T(8,128)(2,1)S(1)}, u32[]{:S(2)}, u32[]{:S(2)}) %collective-permute-start.16) | collective-permute-done | bytes 589856 | tf_op jit(solution)/shard_map/ppermute | solution.py:462
  412.0 20.4 %collective-permute-done.12 = bf16[384,768]{1,0:T(8,128)(2,1)S(1)} collective-permute-done((bf16[384,768]{1,0:T(8,128)(2,1)S(1)}, bf16[384,768]{1,0:T(8,128)(2,1)S(1)}, u32[]{:S(2)}, u32[]{:S(2)}) %collective-permute-start.12) | collective-permute-done | bytes 589856 | tf_op jit(solution)/shard_map/ppermute | solution.py:462
  449.8 5.6 convolution_convert_fusion.1
  461.1 28.6 %while.35 = (s32[]{:T(128)}, f32[2,256,6,128]{1,3,2,0:T(8,128)}, bf16[2,1024,128]{2,1,0:T(8,128)(2,1)}, bf16[2,1024,128]{2,1,0:T(8,128)(2,1)}, bf16[2,1024,128]{...) while((s32[]{:T(128)}, f32[2,256,6,128]{1,3,2,0:T(8,128)}, ...), condition=%wide.region_13.14_spmd.clone.clone.clone, body=%wide.region_11.13_spmd.clone.clone.sunk.clone | while | flops 2037710592 | bytes 62969064 | solution.py:648
  493.6 27.6 %return_key_grads.1 = bf16[4,256,512]{2,1,0:T(8,128)(2,1)S(1)} custom-call(bf16[4,256,512]{2,1,0:T(8,128)(2,1)S(1)} %pad_maximum_fusion.refs_0_), custom_call_target="tpu_custom_call" | custom-call | bytes 15728640 | tf_op jit(solution)/shard_map/return_key_grads/pallas_call | solution.py:443
  523.8 7.4 %fusion.85 = (f32[256]{0:T(256)}, bf16[1536]{0:T(1024)(128)(2,1)S(1)}, f32[256,1536]{1,0:T(8,128)}) fusion(bf16[1,256,1536]{2,1,0:T(8,128)(2,1)S(1)} %copy-done.10, f32[1536]{0:T(1024)S(1)} %copy-done.46, f32[256]{0:T(256)S(1)} %copy-done.54, bf16[1536,2176]{1,0:T(8,128)(2,1)} %bitcast.432, bf16[256,256]{0,1:T(8,128)(2,1)S(1)} %copy.132, ...), kind=kOutput, calls=%fused_computation.119 | convolution fusion | flops 1718483200 | bytes 10108160 | tf_op jit(solution)/shard_map/dot_general | solution.py:46
  545.9 20.4 %collective-permute-done.10 = bf16[192,1536]{1,0:T(8,128)(2,1)S(1)} collective-permute-done((bf16[192,1536]{1,0:T(8,128)(2,1)}, bf16[192,1536]{1,0:T(8,128)(2,1)S(1)}, u32[]{:S(2)}, u32[]{:S(2)}) %collective-permute-start.10) | collective-permute-done | bytes 589856 | tf_op jit(solution)/shard_map/ppermute | solution.py:462
  566.4 67.3 %scatter_attention_grads.1 = (f32[48,1536]{1,0:T(8,128)S(1)}, f32[48,2176]{1,0:T(8,128)S(1)}) custom-call(bf16[2,2,4,2,48,1536]{5,4,3,2,1,0:T(8,128)(2,1)S(1)} %bitcast.425, bf16[2,2,4,2,48,2176]{5,4,3,2,1,0:T(8,128)(2,1)S(1)} %bitcast.433), custom_call_target="tpu_custom_call" | custom-call | bytes 114032640 | tf_op jit(solution)/shard_map/scatter_attention_grads/pallas_call | solution.py:410
  (349 shorter events, 229.0 us)
Async XLA Ops:
  3.8 90.3 %collective-permute-start = (bf16[384,768]{1,0:T(8,128)(2,1)}, bf16[384,768]{1,0:T(8,128)(2,1)S(1)}, u32[]{:S(2)}, u32[]{:S(2)}) collective-permute-start(bf16[384,768]{1,0:T(8,128)(2,1)} %get-tuple-element.466), channel_id=1, source_target_pairs={{0,8},{8,16},{16,24},{24,0},{1,9},{9,17},{17,25},{25,1},{2,10},{10... | collective-permute-start | bytes 1769480 | tf_op jit(solution)/shard_map/ppermute | solution.py:462
  6.8 87.4 %collective-permute-start.1 = (bf16[384,768]{1,0:T(8,128)(2,1)}, bf16[384,768]{1,0:T(8,128)(2,1)}, u32[]{:S(2)}, u32[]{:S(2)}) collective-permute-start(bf16[384,768]{1,0:T(8,128)(2,1)} %get-tuple-element.468), channel_id=1, source_target_pairs={{0,16},{8,24},{16,0},{24,8},{1,17},{9,25},{17,1},{25,9},{2,18},{10... | collective-permute-start | bytes 1769480 | tf_op jit(solution)/shard_map/ppermute | solution.py:462
  8.3 85.9 %collective-permute-start.2 = (bf16[384,768]{1,0:T(8,128)(2,1)}, bf16[384,768]{1,0:T(8,128)(2,1)}, u32[]{:S(2)}, u32[]{:S(2)}) collective-permute-start(bf16[384,768]{1,0:T(8,128)(2,1)} %get-tuple-element.465), channel_id=1, source_target_pairs={{0,24},{8,0},{16,8},{24,16},{1,25},{9,1},{17,9},{25,17},{2,26},{10... | collective-permute-start | bytes 1769480 | tf_op jit(solution)/shard_map/ppermute | solution.py:462
  14.7 103.1 %copy-start.29 = (f32[256,64]{0,1:T(8,128)}, f32[256,64]{0,1:T(8,128)S(1)}, u32[]{:S(2)}) copy-start(f32[256,64]{0,1:T(8,128)S(1)} %get-tuple-element.483) | copy-start | bytes 196612
  111.9 95.1 %all-to-all-start = ((bf16[32,40,1536]{2,1,0:T(8,128)(2,1)}), bf16[32,40,1536]{2,1,0:T(8,128)(2,1)}, u32[]{:S(2)}, u32[]{:S(2)}) async-start(bf16[32,40,1536]{2,1,0:T(8,128)(2,1)} %bitcast.440), calls=%async_computation | async-start | bytes 7864320 | tf_op jit(solution)/shard_map/all_to_all | solution.py:120
  171.8 25.8 %collective-permute-start.3 = (bf16[384,768]{1,0:T(8,128)(2,1)}, bf16[384,768]{1,0:T(8,128)(2,1)}, u32[]{:S(2)}, u32[]{:S(2)}) collective-permute-start(bf16[384,768]{1,0:T(8,128)(2,1)} %get-tuple-element.463), channel_id=1, source_target_pairs={{0,8},{8,16},{16,24},{24,0},{1,9},{9,17},{17,25},{25,1},{2,10},{10... | collective-permute-start | bytes 1769480 | tf_op jit(solution)/shard_map/ppermute | solution.py:462
  174.6 32.2 %collective-permute-start.4 = (bf16[384,768]{1,0:T(8,128)(2,1)}, bf16[384,768]{1,0:T(8,128)(2,1)}, u32[]{:S(2)}, u32[]{:S(2)}) collective-permute-start(bf16[384,768]{1,0:T(8,128)(2,1)} %get-tuple-element.462), channel_id=1, source_target_pairs={{0,16},{8,24},{16,0},{24,8},{1,17},{9,25},{17,1},{25,9},{2,18},{10... | collective-permute-start | bytes 1769480 | tf_op jit(solution)/shard_map/ppermute | solution.py:462
  176.3 30.7 %collective-permute-start.5 = (bf16[384,768]{1,0:T(8,128)(2,1)}, bf16[384,768]{1,0:T(8,128)(2,1)}, u32[]{:S(2)}, u32[]{:S(2)}) collective-permute-start(bf16[384,768]{1,0:T(8,128)(2,1)} %get-tuple-element.461), channel_id=1, source_target_pairs={{0,24},{8,0},{16,8},{24,16},{1,25},{9,1},{17,9},{25,17},{2,26},{10... | collective-permute-start | bytes 1769480 | tf_op jit(solution)/shard_map/ppermute | solution.py:462
  194.4 254.7 %copy-start.3 = (f32[256,1536]{1,0:T(8,128)}, f32[256,1536]{1,0:T(8,128)S(1)}, u32[]{:S(2)}) copy-start(f32[256,1536]{1,0:T(8,128)S(1)} %get-tuple-element.485) | copy-start | bytes 4718596
  207.1 99.6 %all-to-all-start.1 = ((bf16[32,40,1536]{2,1,0:T(8,128)(2,1)}), bf16[32,40,1536]{2,1,0:T(8,128)(2,1)}, u32[]{:S(2)}, u32[]{:S(2)}) async-start(bf16[32,40,1536]{2,1,0:T(8,128)(2,1)} %bitcast.435), calls=%async_computation.1 | async-start | bytes 7864320 | tf_op jit(solution)/shard_map/all_to_all | solution.py:120
  219.7 55.1 %collective-permute-start.6 = (bf16[192,1536]{1,0:T(8,128)(2,1)S(1)}, bf16[192,1536]{1,0:T(8,128)(2,1)S(1)}, u32[]{:S(2)}, u32[]{:S(2)}) collective-permute-start(bf16[192,1536]{1,0:T(8,128)(2,1)S(1)} %get-tuple-element.459), channel_id=1, source_target_pairs={{0,8},{8,16},{16,24},{24,0},{1,9},{9,17},{17,25},{25,1},{2,10},{10... | collective-permute-start | bytes 1769480 | tf_op jit(solution)/shard_map/ppermute | solution.py:462
  221.4 61.3 %collective-permute-start.7 = (bf16[192,1536]{1,0:T(8,128)(2,1)S(1)}, bf16[192,1536]{1,0:T(8,128)(2,1)S(1)}, u32[]{:S(2)}, u32[]{:S(2)}) collective-permute-start(bf16[192,1536]{1,0:T(8,128)(2,1)S(1)} %get-tuple-element.458), channel_id=1, source_target_pairs={{0,16},{8,24},{16,0},{24,8},{1,17},{9,25},{17,1},{25,9},{2,18},{10... | collective-permute-start | bytes 1769480 | tf_op jit(solution)/shard_map/ppermute | solution.py:462
  222.9 63.8 %collective-permute-start.8 = (bf16[192,1536]{1,0:T(8,128)(2,1)S(1)}, bf16[192,1536]{1,0:T(8,128)(2,1)S(1)}, u32[]{:S(2)}, u32[]{:S(2)}) collective-permute-start(bf16[192,1536]{1,0:T(8,128)(2,1)S(1)} %get-tuple-element.457), channel_id=1, source_target_pairs={{0,24},{8,0},{16,8},{24,16},{1,25},{9,1},{17,9},{25,17},{2,26},{10... | collective-permute-start | bytes 1769480 | tf_op jit(solution)/shard_map/ppermute | solution.py:462
  336.2 108.6 %all-to-all-start.2 = ((bf16[32,40,1536]{2,1,0:T(8,128)(2,1)}), bf16[32,40,1536]{2,1,0:T(8,128)(2,1)}, u32[]{:S(2)}, u32[]{:S(2)}) async-start(bf16[32,40,1536]{2,1,0:T(8,128)(2,1)} %bitcast.441), calls=%async_computation.2 | async-start | bytes 7864320 | tf_op jit(solution)/shard_map/all_to_all | solution.py:120
  350.6 47.9 %collective-permute-start.15 = (bf16[384,768]{1,0:T(8,128)(2,1)S(1)}, bf16[384,768]{1,0:T(8,128)(2,1)S(1)}, u32[]{:S(2)}, u32[]{:S(2)}) collective-permute-start(bf16[384,768]{1,0:T(8,128)(2,1)S(1)} %get-tuple-element.449), channel_id=1, source_target_pairs={{0,8},{8,16},{16,24},{24,0},{1,9},{9,17},{17,25},{25,1},{2,10},{10... | collective-permute-start | bytes 1769480 | tf_op jit(solution)/shard_map/ppermute | solution.py:462
  369.4 38.3 %collective-permute-start.16 = (bf16[384,768]{1,0:T(8,128)(2,1)S(1)}, bf16[384,768]{1,0:T(8,128)(2,1)S(1)}, u32[]{:S(2)}, u32[]{:S(2)}) collective-permute-start(bf16[384,768]{1,0:T(8,128)(2,1)S(1)} %get-tuple-element.448), channel_id=1, source_target_pairs={{0,16},{8,24},{16,0},{24,8},{1,17},{9,25},{17,1},{25,9},{2,18},{10... | collective-permute-start | bytes 1769480 | tf_op jit(solution)/shard_map/ppermute | solution.py:462
  374.5 36.4 %collective-permute-start.17 = (bf16[384,768]{1,0:T(8,128)(2,1)S(1)}, bf16[384,768]{1,0:T(8,128)(2,1)S(1)}, u32[]{:S(2)}, u32[]{:S(2)}) collective-permute-start(bf16[384,768]{1,0:T(8,128)(2,1)S(1)} %get-tuple-element.447), channel_id=1, source_target_pairs={{0,24},{8,0},{16,8},{24,16},{1,25},{9,1},{17,9},{25,17},{2,26},{10... | collective-permute-start | bytes 1769480 | tf_op jit(solution)/shard_map/ppermute | solution.py:462
  380.2 52.3 %collective-permute-start.12 = (bf16[384,768]{1,0:T(8,128)(2,1)S(1)}, bf16[384,768]{1,0:T(8,128)(2,1)S(1)}, u32[]{:S(2)}, u32[]{:S(2)}) collective-permute-start(bf16[384,768]{1,0:T(8,128)(2,1)S(1)} %get-tuple-element.452), channel_id=1, source_target_pairs={{0,8},{8,16},{16,24},{24,0},{1,9},{9,17},{17,25},{25,1},{2,10},{10... | collective-permute-start | bytes 1769480 | tf_op jit(solution)/shard_map/ppermute | solution.py:462
  380.7 57.4 %collective-permute-start.13 = (bf16[384,768]{1,0:T(8,128)(2,1)S(1)}, bf16[384,768]{1,0:T(8,128)(2,1)S(1)}, u32[]{:S(2)}, u32[]{:S(2)}) collective-permute-start(bf16[384,768]{1,0:T(8,128)(2,1)S(1)} %get-tuple-element.451), channel_id=1, source_target_pairs={{0,16},{8,24},{16,0},{24,8},{1,17},{9,25},{17,1},{25,9},{2,18},{10... | collective-permute-start | bytes 1769480 | tf_op jit(solution)/shard_map/ppermute | solution.py:462
  398.5 45.2 %collective-permute-start.14 = (bf16[384,768]{1,0:T(8,128)(2,1)S(1)}, bf16[384,768]{1,0:T(8,128)(2,1)S(1)}, u32[]{:S(2)}, u32[]{:S(2)}) collective-permute-start(bf16[384,768]{1,0:T(8,128)(2,1)S(1)} %get-tuple-element.450), channel_id=1, source_target_pairs={{0,24},{8,0},{16,8},{24,16},{1,25},{9,1},{17,9},{25,17},{2,26},{10... | collective-permute-start | bytes 1769480 | tf_op jit(solution)/shard_map/ppermute | solution.py:462
  457.1 186.2 %all-to-all-start.3 = ((bf16[32,40,1536]{2,1,0:T(8,128)(2,1)}), bf16[32,40,1536]{2,1,0:T(8,128)(2,1)}, u32[]{:S(2)}, u32[]{:S(2)}) async-start(bf16[32,40,1536]{2,1,0:T(8,128)(2,1)} %bitcast.439), calls=%async_computation.3 | async-start | bytes 7864320 | tf_op jit(solution)/shard_map/all_to_all | solution.py:120
  534.4 31.9 %collective-permute-start.10 = (bf16[192,1536]{1,0:T(8,128)(2,1)}, bf16[192,1536]{1,0:T(8,128)(2,1)S(1)}, u32[]{:S(2)}, u32[]{:S(2)}) collective-permute-start(bf16[192,1536]{1,0:T(8,128)(2,1)} %get-tuple-element.454), channel_id=1, source_target_pairs={{0,16},{8,24},{16,0},{24,8},{1,17},{9,25},{17,1},{25,9},{2,18},{10... | collective-permute-start | bytes 1769480 | tf_op jit(solution)/shard_map/ppermute | solution.py:462
  535.7 30.7 %collective-permute-start.11 = (bf16[192,1536]{1,0:T(8,128)(2,1)}, bf16[192,1536]{1,0:T(8,128)(2,1)}, u32[]{:S(2)}, u32[]{:S(2)}) collective-permute-start(bf16[192,1536]{1,0:T(8,128)(2,1)} %get-tuple-element.453), channel_id=1, source_target_pairs={{0,24},{8,0},{16,8},{24,16},{1,25},{9,1},{17,9},{25,17},{2,26},{10... | collective-permute-start | bytes 1769480 | tf_op jit(solution)/shard_map/ppermute | solution.py:462
  535.7 30.7 %collective-permute-start.9 = (bf16[192,1536]{1,0:T(8,128)(2,1)}, bf16[192,1536]{1,0:T(8,128)(2,1)}, u32[]{:S(2)}, u32[]{:S(2)}) collective-permute-start(bf16[192,1536]{1,0:T(8,128)(2,1)} %get-tuple-element.455), channel_id=1, source_target_pairs={{0,8},{8,16},{16,24},{24,0},{1,9},{9,17},{17,25},{25,1},{2,10},{10... | collective-permute-start | bytes 1769480 | tf_op jit(solution)/shard_map/ppermute | solution.py:462
  (71 other events, 842.2 us)

commit v6 on v5

--- a/solution.py
+++ b/solution.py
@@ -152,7 +152,8 @@
         for k, whole in enumerate(widths):
             tiles = whole // LANES
             first, end = tiles * part // parts, tiles * (part + 1) // parts
-            chunks.append((k, first * LANES, (end - first) * LANES))
+            if end > first:
+                chunks.append((k, first * LANES, (end - first) * LANES))
     return chunks
 
 
@@ -306,7 +307,7 @@
         compiler_params=pltpu.CompilerParams(
             collective_id=collective_id, vmem_limit_bytes=4 << 20
         ),
-        cost_estimate=pl.CostEstimate(flops=0, bytes_accessed=10 * size, transcendentals=0),
+        cost_estimate=pl.CostEstimate(flops=0, bytes_accessed=size, transcendentals=0),
         name=name,
     )(*arrays, *extras)
     return [o.reshape(-1, o.shape[-1]) for o in outs]
@@ -425,7 +426,7 @@
         compiler_params=pltpu.CompilerParams(
             collective_id=collective_id, vmem_limit_bytes=36 << 20
         ),
-        cost_estimate=pl.CostEstimate(flops=0, bytes_accessed=10 * size, transcendentals=0),
+        cost_estimate=pl.CostEstimate(flops=0, bytes_accessed=size, transcendentals=0),
         name=name,
     )(*[x.reshape(2, 2, line, 2, rows, x.shape[1]) for x in arrays], *extras)
 
@@ -449,7 +450,7 @@
         compiler_params=pltpu.CompilerParams(
             collective_id=collective_id, vmem_limit_bytes=4 << 20
         ),
-        cost_estimate=pl.CostEstimate(flops=0, bytes_accessed=20 * sent, transcendentals=0),
+        cost_estimate=pl.CostEstimate(flops=0, bytes_accessed=sent, transcendentals=0),
         name=name,
     )(*arrays)
 
@@ -515,7 +516,7 @@
         [attn_gain[:, None], mlp_gain[:, None], jnp.zeros((attn_gain.shape[0], LANES - 2), BF16)],
         axis=1,
     )
-    packed = jnp.concatenate([w_query, key_projection, value_projection, gain_block], axis=1)
+    packed = jnp.concatenate([w_query, key_projection, value_projection], axis=1)
     staged = seq_count == 4 and w_query.shape[0] % 16 == 0
 
     def expert_pieces(weights):
@@ -524,14 +525,20 @@
 
         return seq_permutes(block_for)
 
-    gate_parts = expert_pieces(w_gate)
     if staged:
-        packed_full, out_full = staged_gather(
-            [packed, w_out], [], None, 2, "gather_attention_weights"
+        packed_full, gains_full, out_full, gate_full = staged_gather(
+            [packed, gain_block, w_out],
+            [w_gate],
+            lambda ref, peer: ref.at[peer // sharers],
+            2,
+            "gather_attention_weights",
         )
+        gate_full = gate_full.reshape(width, hidden_units)
     else:
         packed_full = lax.all_gather(packed, BOTH, axis=0, tiled=True)
+        gains_full = lax.all_gather(gain_block, BOTH, axis=0, tiled=True)
         out_full = lax.all_gather(w_out, BOTH, axis=0, tiled=True)
+        gate_full = in_seq_order(expert_pieces(w_gate), BF16).reshape(width, hidden_units)
 
     pair_routes, place, kept = claim_places(routes[0], priority[0, 0], is_valid)
     holder = (pair_routes // own_experts) * seq_count + (pair_routes % own_experts) * sharers
@@ -547,12 +554,13 @@
     live_cotangent = jnp.where(is_valid[:, None], cotangent[0], jnp.zeros((), BF16))
     out_grad = live_cotangent.astype(F32)
     grad_send = (tn(token_hot, live_cotangent) * slot_gate[:, None]).astype(BF16)
-    packed_full, out_full, gate_parts, grad_send, w_up, w_down = lax.optimization_barrier(
-        (packed_full, out_full, gate_parts, grad_send, w_up, w_down)
+    packed_full, gains_full, out_full, gate_full, grad_send, w_up, w_down = (
+        lax.optimization_barrier(
+            (packed_full, gains_full, out_full, gate_full, grad_send, w_up, w_down)
+        )
     )
     up_parts, down_parts = expert_pieces(w_up), expert_pieces(w_down)
-    gain_one = packed_full[:, q_width + 2 * kv_width].astype(F32)
-    gain_two = packed_full[:, q_width + 2 * kv_width + 1].astype(F32)
+    gain_one, gain_two = gains_full[:, 0].astype(F32), gains_full[:, 1].astype(F32)
     grad_rows = swap(grad_send.reshape(devices, CAP, width), ("dp", "seq")).reshape(slots, width)
 
     inputs = hidden_in[0].astype(F32)
@@ -593,7 +601,6 @@
     send_rows = tn(token_hot, moe_input).astype(BF16).reshape(devices, CAP, width)
     send_rows, grad_rows, up_parts = lax.optimization_barrier((send_rows, grad_rows, up_parts))
     slot_rows = swap(send_rows, ("dp", "seq")).reshape(slots, width)
-    gate_full = in_seq_order(gate_parts, BF16).reshape(width, hidden_units)
     up_full = in_seq_order(up_parts, BF16).reshape(width, hidden_units)
     down_full = in_seq_order(down_parts, BF16).reshape(hidden_units, width)
     slot_rows, gate_full, up_full, down_full = lax.optimization_barrier(
@@ -637,8 +644,6 @@
     middle_norm_grad, gain_two_grad = norm_back(middle, scale_two, gain_two, moe_input_grad)
     middle_grad = out_grad + middle_norm_grad
     branch_grad = middle_grad.astype(BF16)
-    no_grad = jnp.zeros((rows, LANES), BF16)
-
     out_terms = tn(attended, branch_grad).astype(BF16)
     attended_grad = nt(branch_grad, out_full).astype(BF16)
     attended_grad, out_terms = lax.optimization_barrier((attended_grad, out_terms))
@@ -666,6 +671,7 @@
         ],
         axis=1,
     ).astype(BF16)
+    kv_terms, down_grad_parts = lax.optimization_barrier((kv_terms, down_grad_parts))
     (kv_back,) = seq_exchange(
         [kv_terms.reshape(seq_count, rows, 2 * kv_width)],
         4,
@@ -685,45 +691,35 @@
         -sine_lookup,
     )
     query_grad = query_grad.reshape(rows, q_width).astype(BF16)
-    projected_grad = jnp.concatenate([query_grad, key_grad, value_grad, no_grad], axis=1)
+    projected_grad = jnp.concatenate([query_grad, key_grad, value_grad], axis=1)
     normed_grad = nt(projected_grad, packed_full)
     input_norm_grad, gain_one_grad = norm_back(inputs, scale_one, gain_one, normed_grad)
     input_grad = middle_grad + input_norm_grad
 
-    gain_columns = jnp.zeros((width, LANES), BF16)
-    gain_columns = gain_columns.at[:, 0].set(gain_one_grad.astype(BF16))
-    gain_columns = gain_columns.at[:, 1].set(gain_two_grad.astype(BF16))
-    query_terms = lax.dynamic_update_slice(
-        tn(normed, projected_grad).astype(BF16), gain_columns, (0, projected_grad.shape[1] - LANES)
-    )
-    query_terms, down_grad_parts = lax.optimization_barrier((query_terms, down_grad_parts))
+    lane = lax.broadcasted_iota(jnp.int32, (width, LANES), 1)
+    gain_terms = jnp.where(lane == 0, gain_one_grad[:, None], gain_two_grad[:, None])
+    gain_terms = jnp.where(lane < 2, gain_terms, 0.0).astype(BF16)
+    query_terms = tn(normed, projected_grad).astype(BF16)
     grad_parts = [gate_grad_parts, up_grad_parts, down_grad_parts]
     if staged:
-        out_owned, owned = staged_scatter(
-            [out_terms, query_terms], [], None, 6, "scatter_attention_grads"
+        out_owned, gains_owned, owned = staged_scatter(
+            [out_terms, gain_terms, query_terms], [], None, 6, "scatter_attention_grads"
         )
     else:
-        terms = jnp.concatenate([out_terms, query_terms], axis=1)
+        terms = jnp.concatenate([out_terms, gain_terms, query_terms], axis=1)
         terms = lax.psum_scatter(terms, BOTH, scatter_dimension=0, tiled=True).astype(F32)
-        out_owned, owned = terms[:, :width], terms[:, width:]
+        out_owned, gains_owned = terms[:, :width], terms[:, width : width + LANES]
+        owned = terms[:, width + LANES :]
     returned, owned = lax.optimization_barrier((returned, owned))
     expert_grads = [owned_sum(parts) for parts in grad_parts]
 
-    gate_high = gate_rows.astype(BF16)
-    gate_low = (gate_rows - gate_high.astype(F32)).astype(BF16)
-
-    def gate_hot(weights):
-        return jnp.sum(
-            jnp.where(hits, weights.astype(F32)[:, :, None], 0.0), axis=1
-        ).astype(BF16)
-
-    layer_out = middle + nn(gate_hot(gate_high), returned) + nn(gate_hot(gate_low), returned)
-
+    gate_hot = jnp.sum(jnp.where(hits, gate_rows[:, :, None], 0.0), axis=1).astype(BF16)
+    layer_out = middle + nn(gate_hot, returned)
     return (
         layer_out[None],
         input_grad[None],
-        owned[:, q_width + 2 * kv_width],
-        owned[:, q_width + 2 * kv_width + 1],
+        gains_owned[:, 0],
+        gains_owned[:, 1],
         owned[:, :q_width],
         owned[:, q_width : q_width + kv_width],
         owned[:, q_width + kv_width : q_width + 2 * kv_width],

time: 663 us -> 649 us (0.979)
  Pallas kernels: 207 us -> 231 us
  local copies, waits for them, and re-layouts: 65.4 us -> 53.1 us
  starting transfers between devices: 51.1 us -> 39.8 us
  waiting for transfers between devices: 157 us -> 146 us
    pallas_call x1, Pallas kernels: 66 us -> 84.8 us  [staged_gather(): pl.pallas_call(functools.partial(gather_kernel, line, chunks, n, len(extr...]
    ppermute x18 -> x15, waiting for transfers between devices: 146 us -> 134 us  [seq_permutes(): lax.ppermute(block_for(lax.rem(me + step, count)), 'seq', ring)]
    optimization_barrier x1 -> x2, local copies, waits for them, and re-layouts: 9.98 us -> 1.46 us  [the longest x1 0.93 us: on_device(): lax.optimization_barrier((packed_full, gains_full, out_full, gate_full, g...]
    dot_general x20 -> x19, matrix products: 98.7 us -> 91.3 us  [dot(): lax.dot_general(left, right, (contract, ((), ())), preferred_element_type...]
    pallas_call x2, Pallas kernels: 73.8 us -> 80.5 us  [seq_exchange(): pl.pallas_call(functools.partial(exchange_kernel, count, n, block_of), ou...]
    ppermute x18 -> x15, starting transfers between devices: 25.2 us -> 19.1 us  [seq_permutes(): lax.ppermute(block_for(lax.rem(me + step, count)), 'seq', ring)]
  transfers between devices with their start and end apart: 22 -> 19, of which waited for: 13 -> 12; matrix products, arithmetic and copies ran while one was open for 23% -> 23% of each run, Pallas kernels for 32% -> 23%
where the time goes in v6:
time: 649 us; the launch traced here: 642 us
  Pallas kernels  231 us (36%)
  waiting for transfers between devices  146 us (22%)
  matrix products  125 us (19%)
  local copies, waits for them, and re-layouts  53.1 us (8%)
  other arithmetic  45.1 us (7%)
  starting transfers between devices  39.8 us (6%)
    ppermute x15, waiting for transfers between devices, seq_permutes(): lax.ppermute(block_for(lax.rem(me + step, count)), 'seq', ring)  134 us
    dot_general x19, matrix products, dot(): lax.dot_general(left, right, (contract, ((), ())), preferred_element_type...  91.3 us
    pallas_call x1, Pallas kernels, staged_gather(): pl.pallas_call(functools.partial(gather_kernel, line, chunks, n, len(extr...  84.8 us
    pallas_call x2, Pallas kernels, seq_exchange(): pl.pallas_call(functools.partial(exchange_kernel, count, n, block_of), ou...  80.5 us
    pallas_call x1, Pallas kernels, staged_scatter(): pl.pallas_call(functools.partial(scatter_kernel, line, chunks, n, len(ext...  65.5 us
    all_to_all x4, starting transfers between devices, swap(): return lax.all_to_all(blocks, axes, split_axis=0, concat_axis=0, tiled=True)  20.7 us
    ppermute x15, starting transfers between devices, seq_permutes(): lax.ppermute(block_for(lax.rem(me + step, count)), 'seq', ring)  19.1 us
  transfers between devices with their start and end apart: 19, of which 12 were waited for; matrix products, arithmetic and copies ran while one was open for 23% of the time, Pallas kernels for 23%

profile of v6, /device:TPU:0, one launch (start us, length us, event | category | flops | bytes accessed | tf_op | source)
XLA Modules:
  0.0 642.4 jit_solution(278392175738402429)
XLA Ops:
  15.1 84.8 %gather_attention_weights.1 = (bf16[2,2,4,2,48,2048]{5,4,3,2,1,0:T(8,128)(2,1)S(1)}, bf16[2,2,4,2,48,128]{5,4,3,2,1,0:T(8,128)(2,1)S(1)}, bf16[2,2,4,2,48,1536]{...) custom-call(bf16[48,2048]{1,0:T(8,128)(2,1)S(1)} %pad_maximum_fusion.6.refs_0_, ...), custom_call_target="tpu_custom_call" | custom-call | bytes 11403264 | tf_op jit(solution)/shard_map/gather_attention_weights/pallas_call | solution.py:295
  137.1 53.8 %gather_keys.1 = bf16[4,256,512]{2,1,0:T(8,128)(2,1)S(1)} custom-call(bf16[256,512]{1,0:T(8,128)(2,1)S(1)} %pad_maximum_fusion.5.refs_0_), custom_call_target="tpu_custom_call" | custom-call | bytes 786432 | tf_op jit(solution)/shard_map/gather_keys/pallas_call | solution.py:444
  197.2 14.0 %while.32 = (s32[]{:T(128)}, bf16[2,256,6,128]{1,3,2,0:T(8,128)(2,1)}, f32[2,6,256]{2,1,0:T(8,128)S(1)}, bf16[2,1024,128]{1,2,0:T(8,128)(2,1)S(1)}, s32[]{:T(128...) while((s32[]{:T(128)}, ...), condition=%wide.region_7.8_spmd.clone.clone.clone, body=%wide.region_4.7_spmd.clone.clone.sunk.clone | while | flops 824704768 | bytes 21692512 | solution.py:590
  218.8 7.3 %all-to-all-start.1 = ((bf16[32,40,1536]{2,1,0:T(8,128)(2,1)}), bf16[32,40,1536]{2,1,0:T(8,128)(2,1)}, u32[]{:S(2)}, u32[]{:S(2)}) async-start(bf16[32,40,1536]{2,1,0:T(8,128)(2,1)} %bitcast.417), calls=%async_computation.1 | async-start | bytes 7864320 | tf_op jit(solution)/shard_map/all_to_all | solution.py:120
  233.1 50.1 %collective-permute-done.3 = bf16[192,1536]{1,0:T(8,128)(2,1)S(1)} collective-permute-done((bf16[192,1536]{1,0:T(8,128)(2,1)S(1)}, bf16[192,1536]{1,0:T(8,128)(2,1)S(1)}, u32[]{:S(2)}, u32[]{:S(2)}) %collective-permute-start.3) | collective-permute-done | bytes 589856 | tf_op jit(solution)/shard_map/ppermute | solution.py:463
  283.2 7.8 %collective-permute-done.4 = bf16[192,1536]{1,0:T(8,128)(2,1)S(1)} collective-permute-done((bf16[192,1536]{1,0:T(8,128)(2,1)S(1)}, bf16[192,1536]{1,0:T(8,128)(2,1)S(1)}, u32[]{:S(2)}, u32[]{:S(2)}) %collective-permute-start.4) | collective-permute-done | bytes 589856 | tf_op jit(solution)/shard_map/ppermute | solution.py:463
  303.4 11.6 %all-to-all-done.1 = bf16[32,40,1536]{2,1,0:T(8,128)(2,1)} async-done(((bf16[32,40,1536]{2,1,0:T(8,128)(2,1)}), bf16[32,40,1536]{2,1,0:T(8,128)(2,1)}, u32[]{:S(2)}, u32[]{:S(2)}) %all-to-all-start.1) | async-done | bytes 3932192 | tf_op jit(solution)/shard_map/all_to_all | solution.py:120
  315.1 6.1 fusion.116
  321.2 5.5 fusion.115
  326.7 7.9 %multiply_convert_fusion = (bf16[1280,768]{1,0:T(8,128)(2,1)S(1)}, bf16[1280,768]{1,0:T(8,128)(2,1)S(1)}, bf16[1280,768]{1,0:T(8,128)(2,1)}) fusion(f32[1280,768]{1,0:T(8,128)S(1)} %fusion.115, f32[1280,768]{1,0:T(8,128)S(1)} %fusion.116, bf16[1280,1536]{1,0:T(8,128)(2,1)} %bitcast.26, bf16[768,1536]{1,0:T(8,128)(2,1)S(1)} %bitcast.426), kind=kOutput, calls=%fused_computation.89 | convolution fusion | flops 3034644480 | bytes 20054016 | tf_op jit(solution)/shard_map/dot_general | solution.py:46
  337.8 6.6 %fusion.68 = bf16[1280,1536]{1,0:T(8,128)(2,1)} fusion(f32[1280,1536]{1,0:T(8,128)S(1)} %fusion.117, bf16[1280,768]{1,0:T(8,128)(2,1)S(1)} %get-tuple-element.421, bf16[1536,768]{1,0:T(8,128)(2,1)} %bitcast.36), kind=kOutput, calls=%fused_computation.79 | convolution fusion | flops 3023831040 | bytes 16121856 | tf_op jit(solution)/shard_map/dot_general | solution.py:46
  350.5 5.4 convolution_convert_fusion.4
  357.8 5.4 convolution_convert_fusion.5
  363.3 6.8 %convolution_convert_fusion.6 = bf16[768,1536]{1,0:T(8,128)(2,1)} fusion(bf16[1280,768]{1,0:T(8,128)(2,1)S(1)} %copy-done.45, bf16[1280,1536]{1,0:T(8,128)(2,1)} %bitcast.26), kind=kOutput, calls=%fused_computation.96 | convolution fusion | flops 3021078528 | bytes 8257536 | tf_op jit(solution)/shard_map/dot_general | solution.py:46
  386.7 19.9 %collective-permute-done.12 = bf16[384,768]{1,0:T(8,128)(2,1)S(1)} collective-permute-done((bf16[384,768]{1,0:T(8,128)(2,1)S(1)}, bf16[384,768]{1,0:T(8,128)(2,1)S(1)}, u32[]{:S(2)}, u32[]{:S(2)}) %collective-permute-start.12) | collective-permute-done | bytes 589856 | tf_op jit(solution)/shard_map/ppermute | solution.py:463
  407.8 8.0 %collective-permute-done.13 = bf16[384,768]{1,0:T(8,128)(2,1)S(1)} collective-permute-done((bf16[384,768]{1,0:T(8,128)(2,1)S(1)}, bf16[384,768]{1,0:T(8,128)(2,1)S(1)}, u32[]{:S(2)}, u32[]{:S(2)}) %collective-permute-start.13) | collective-permute-done | bytes 589856 | tf_op jit(solution)/shard_map/ppermute | solution.py:463
  420.2 20.4 %collective-permute-done.9 = bf16[384,768]{1,0:T(8,128)(2,1)S(1)} collective-permute-done((bf16[384,768]{1,0:T(8,128)(2,1)S(1)}, bf16[384,768]{1,0:T(8,128)(2,1)S(1)}, u32[]{:S(2)}, u32[]{:S(2)}) %collective-permute-start.9) | collective-permute-done | bytes 589856 | tf_op jit(solution)/shard_map/ppermute | solution.py:463
  457.3 5.5 convolution_convert_fusion.1
  476.2 31.6 %while.33 = (s32[]{:T(128)}, f32[2,256,6,128]{1,3,2,0:T(8,128)}, bf16[2,1024,128]{1,2,0:T(8,128)(2,1)}, bf16[2,1024,128]{1,2,0:T(8,128)(2,1)}, bf16[2,1024,128]{...) while((s32[]{:T(128)}, f32[2,256,6,128]{1,3,2,0:T(8,128)}, ...), condition=%wide.region_13.14_spmd.clone.clone.clone, body=%wide.region_11.13_spmd.clone.clone.sunk.clone | while | flops 2037841664 | bytes 87872248 | solution.py:653
  486.6 5.4 fusion.209
  512.9 10.1 %collective-permute-done.8 = bf16[192,1536]{1,0:T(8,128)(2,1)} collective-permute-done((bf16[192,1536]{1,0:T(8,128)(2,1)}, bf16[192,1536]{1,0:T(8,128)(2,1)}, u32[]{:S(2)}, u32[]{:S(2)}) %collective-permute-start.8) | collective-permute-done | bytes 589856 | tf_op jit(solution)/shard_map/ppermute | solution.py:463
  523.6 26.8 %return_key_grads.1 = bf16[4,256,512]{2,1,0:T(8,128)(2,1)S(1)} custom-call(bf16[4,256,512]{2,1,0:T(8,128)(2,1)S(1)} %bitcast.411), custom_call_target="tpu_custom_call" | custom-call | bytes 786432 | tf_op jit(solution)/shard_map/return_key_grads/pallas_call | solution.py:444
  551.9 6.0 fusion.84
  560.4 65.5 %scatter_attention_grads.1 = (f32[48,1536]{1,0:T(8,128)S(1)}, f32[48,128]{1,0:T(8,128)S(1)}, f32[48,2048]{1,0:T(8,128)S(1)}) custom-call(bf16[2,2,4,2,48,1536]{5,4,3,2,1,0:T(8,128)(2,1)S(1)} %bitcast.405, bf16[2,2,4,2,48,128]{5,4,3,2,1,0:T(8,128)(2,1)S(1)} %select_convert_fusion.refs_1_, bf16[2,2,4,2,48,2048]{5,4,3,2,1,0:T(8,128)(2,1)S(1)} %bitcast.402), custom_call_target="tpu_custom_call" | custom-call | bytes 11403264 | tf_op jit(solution)/shard_map/scatter_attention_grads/pallas_call | solution.py:411
  (302 shorter events, 212.9 us)
Async XLA Ops:
  107.8 111.0 %collective-permute-start = (bf16[384,768]{1,0:T(8,128)(2,1)}, bf16[384,768]{1,0:T(8,128)(2,1)}, u32[]{:S(2)}, u32[]{:S(2)}) collective-permute-start(bf16[384,768]{1,0:T(8,128)(2,1)} %get-tuple-element.440), channel_id=1, source_target_pairs={{0,8},{8,16},{16,24},{24,0},{1,9},{9,17},{17,25},{25,1},{2,10},{10... | collective-permute-start | bytes 1769480 | tf_op jit(solution)/shard_map/ppermute | solution.py:463
  109.2 109.5 %collective-permute-start.1 = (bf16[384,768]{1,0:T(8,128)(2,1)}, bf16[384,768]{1,0:T(8,128)(2,1)}, u32[]{:S(2)}, u32[]{:S(2)}) collective-permute-start(bf16[384,768]{1,0:T(8,128)(2,1)} %get-tuple-element.439), channel_id=1, source_target_pairs={{0,16},{8,24},{16,0},{24,8},{1,17},{9,25},{17,1},{25,9},{2,18},{10... | collective-permute-start | bytes 1769480 | tf_op jit(solution)/shard_map/ppermute | solution.py:463
  109.8 109.0 %collective-permute-start.2 = (bf16[384,768]{1,0:T(8,128)(2,1)}, bf16[384,768]{1,0:T(8,128)(2,1)}, u32[]{:S(2)}, u32[]{:S(2)}) collective-permute-start(bf16[384,768]{1,0:T(8,128)(2,1)} %get-tuple-element.438), channel_id=1, source_target_pairs={{0,24},{8,0},{16,8},{24,16},{1,25},{9,1},{17,9},{25,17},{2,26},{10... | collective-permute-start | bytes 1769480 | tf_op jit(solution)/shard_map/ppermute | solution.py:463
  111.2 107.6 %all-to-all-start = ((bf16[32,40,1536]{2,1,0:T(8,128)(2,1)}), bf16[32,40,1536]{2,1,0:T(8,128)(2,1)}, u32[]{:S(2)}, u32[]{:S(2)}) async-start(bf16[32,40,1536]{2,1,0:T(8,128)(2,1)} %bitcast.422), calls=%async_computation | async-start | bytes 7864320 | tf_op jit(solution)/shard_map/all_to_all | solution.py:120
  218.8 96.2 %all-to-all-start.1 = ((bf16[32,40,1536]{2,1,0:T(8,128)(2,1)}), bf16[32,40,1536]{2,1,0:T(8,128)(2,1)}, u32[]{:S(2)}, u32[]{:S(2)}) async-start(bf16[32,40,1536]{2,1,0:T(8,128)(2,1)} %bitcast.417), calls=%async_computation.1 | async-start | bytes 7864320 | tf_op jit(solution)/shard_map/all_to_all | solution.py:120
  228.0 55.1 %collective-permute-start.3 = (bf16[192,1536]{1,0:T(8,128)(2,1)S(1)}, bf16[192,1536]{1,0:T(8,128)(2,1)S(1)}, u32[]{:S(2)}, u32[]{:S(2)}) collective-permute-start(bf16[192,1536]{1,0:T(8,128)(2,1)S(1)} %get-tuple-element.436), channel_id=1, source_target_pairs={{0,8},{8,16},{16,24},{24,0},{1,9},{9,17},{17,25},{25,1},{2,10},{10... | collective-permute-start | bytes 1769480 | tf_op jit(solution)/shard_map/ppermute | solution.py:463
  229.8 61.3 %collective-permute-start.4 = (bf16[192,1536]{1,0:T(8,128)(2,1)S(1)}, bf16[192,1536]{1,0:T(8,128)(2,1)S(1)}, u32[]{:S(2)}, u32[]{:S(2)}) collective-permute-start(bf16[192,1536]{1,0:T(8,128)(2,1)S(1)} %get-tuple-element.435), channel_id=1, source_target_pairs={{0,16},{8,24},{16,0},{24,8},{1,17},{9,25},{17,1},{25,9},{2,18},{10... | collective-permute-start | bytes 1769480 | tf_op jit(solution)/shard_map/ppermute | solution.py:463
  231.2 63.8 %collective-permute-start.5 = (bf16[192,1536]{1,0:T(8,128)(2,1)S(1)}, bf16[192,1536]{1,0:T(8,128)(2,1)S(1)}, u32[]{:S(2)}, u32[]{:S(2)}) collective-permute-start(bf16[192,1536]{1,0:T(8,128)(2,1)S(1)} %get-tuple-element.434), channel_id=1, source_target_pairs={{0,24},{8,0},{16,8},{24,16},{1,25},{9,1},{17,9},{25,17},{2,26},{10... | collective-permute-start | bytes 1769480 | tf_op jit(solution)/shard_map/ppermute | solution.py:463
  344.4 108.6 %all-to-all-start.2 = ((bf16[32,40,1536]{2,1,0:T(8,128)(2,1)}), bf16[32,40,1536]{2,1,0:T(8,128)(2,1)}, u32[]{:S(2)}, u32[]{:S(2)}) async-start(bf16[32,40,1536]{2,1,0:T(8,128)(2,1)} %bitcast.423), calls=%async_computation.2 | async-start | bytes 7864320 | tf_op jit(solution)/shard_map/all_to_all | solution.py:120
  356.1 50.6 %collective-permute-start.12 = (bf16[384,768]{1,0:T(8,128)(2,1)S(1)}, bf16[384,768]{1,0:T(8,128)(2,1)S(1)}, u32[]{:S(2)}, u32[]{:S(2)}) collective-permute-start(bf16[384,768]{1,0:T(8,128)(2,1)S(1)} %get-tuple-element.426), channel_id=1, source_target_pairs={{0,8},{8,16},{16,24},{24,0},{1,9},{9,17},{17,25},{25,1},{2,10},{10... | collective-permute-start | bytes 1769480 | tf_op jit(solution)/shard_map/ppermute | solution.py:463
  374.8 41.0 %collective-permute-start.13 = (bf16[384,768]{1,0:T(8,128)(2,1)S(1)}, bf16[384,768]{1,0:T(8,128)(2,1)S(1)}, u32[]{:S(2)}, u32[]{:S(2)}) collective-permute-start(bf16[384,768]{1,0:T(8,128)(2,1)S(1)} %get-tuple-element.425), channel_id=1, source_target_pairs={{0,16},{8,24},{16,0},{24,8},{1,17},{9,25},{17,1},{25,9},{2,18},{10... | collective-permute-start | bytes 1769480 | tf_op jit(solution)/shard_map/ppermute | solution.py:463
  379.9 39.2 %collective-permute-start.14 = (bf16[384,768]{1,0:T(8,128)(2,1)S(1)}, bf16[384,768]{1,0:T(8,128)(2,1)S(1)}, u32[]{:S(2)}, u32[]{:S(2)}) collective-permute-start(bf16[384,768]{1,0:T(8,128)(2,1)S(1)} %get-tuple-element.424), channel_id=1, source_target_pairs={{0,24},{8,0},{16,8},{24,16},{1,25},{9,1},{17,9},{25,17},{2,26},{10... | collective-permute-start | bytes 1769480 | tf_op jit(solution)/shard_map/ppermute | solution.py:463
  385.4 55.3 %collective-permute-start.9 = (bf16[384,768]{1,0:T(8,128)(2,1)S(1)}, bf16[384,768]{1,0:T(8,128)(2,1)S(1)}, u32[]{:S(2)}, u32[]{:S(2)}) collective-permute-start(bf16[384,768]{1,0:T(8,128)(2,1)S(1)} %get-tuple-element.429), channel_id=1, source_target_pairs={{0,8},{8,16},{16,24},{24,0},{1,9},{9,17},{17,25},{25,1},{2,10},{10... | collective-permute-start | bytes 1769480 | tf_op jit(solution)/shard_map/ppermute | solution.py:463
  385.9 60.4 %collective-permute-start.10 = (bf16[384,768]{1,0:T(8,128)(2,1)S(1)}, bf16[384,768]{1,0:T(8,128)(2,1)S(1)}, u32[]{:S(2)}, u32[]{:S(2)}) collective-permute-start(bf16[384,768]{1,0:T(8,128)(2,1)S(1)} %get-tuple-element.428), channel_id=1, source_target_pairs={{0,16},{8,24},{16,0},{24,8},{1,17},{9,25},{17,1},{25,9},{2,18},{10... | collective-permute-start | bytes 1769480 | tf_op jit(solution)/shard_map/ppermute | solution.py:463
  406.7 45.3 %collective-permute-start.11 = (bf16[384,768]{1,0:T(8,128)(2,1)S(1)}, bf16[384,768]{1,0:T(8,128)(2,1)S(1)}, u32[]{:S(2)}, u32[]{:S(2)}) collective-permute-start(bf16[384,768]{1,0:T(8,128)(2,1)S(1)} %get-tuple-element.427), channel_id=1, source_target_pairs={{0,24},{8,0},{16,8},{24,16},{1,25},{9,1},{17,9},{25,17},{2,26},{10... | collective-permute-start | bytes 1769480 | tf_op jit(solution)/shard_map/ppermute | solution.py:463
  420.2 32.8 %copy-start.7 = (f32[256,1536]{1,0:T(8,128)S(1)}, f32[256,1536]{1,0:T(8,128)}, u32[]{:S(2)}) copy-start(f32[256,1536]{1,0:T(8,128)} %copy-done.6) | copy-start | bytes 4718596
  420.2 32.8 %copy-start.19 = (pred[256,1280]{1,0:T(8,128)(4,1)S(1)}, pred[256,1280]{1,0:T(8,128)(4,1)}, u32[]{:S(2)}) copy-start(pred[256,1280]{1,0:T(8,128)(4,1)} %copy-done.17) | copy-start | bytes 983044
  467.6 42.9 %collective-permute-start.6 = (bf16[192,1536]{1,0:T(8,128)(2,1)}, bf16[192,1536]{1,0:T(8,128)(2,1)}, u32[]{:S(2)}, u32[]{:S(2)}) collective-permute-start(bf16[192,1536]{1,0:T(8,128)(2,1)} %get-tuple-element.432), channel_id=1, source_target_pairs={{0,8},{8,16},{16,24},{24,0},{1,9},{9,17},{17,25},{25,1},{2,10},{10... | collective-permute-start | bytes 1769480 | tf_op jit(solution)/shard_map/ppermute | solution.py:463
  467.6 45.3 %collective-permute-start.7 = (bf16[192,1536]{1,0:T(8,128)(2,1)}, bf16[192,1536]{1,0:T(8,128)(2,1)}, u32[]{:S(2)}, u32[]{:S(2)}) collective-permute-start(bf16[192,1536]{1,0:T(8,128)(2,1)} %get-tuple-element.431), channel_id=1, source_target_pairs={{0,16},{8,24},{16,0},{24,8},{1,17},{9,25},{17,1},{25,9},{2,18},{10... | collective-permute-start | bytes 1769480 | tf_op jit(solution)/shard_map/ppermute | solution.py:463
  469.1 53.9 %collective-permute-start.8 = (bf16[192,1536]{1,0:T(8,128)(2,1)}, bf16[192,1536]{1,0:T(8,128)(2,1)}, u32[]{:S(2)}, u32[]{:S(2)}) collective-permute-start(bf16[192,1536]{1,0:T(8,128)(2,1)} %get-tuple-element.430), channel_id=1, source_target_pairs={{0,24},{8,0},{16,8},{24,16},{1,25},{9,1},{17,9},{25,17},{2,26},{10... | collective-permute-start | bytes 1769480 | tf_op jit(solution)/shard_map/ppermute | solution.py:463
  472.0 163.5 %all-to-all-start.3 = ((bf16[32,40,1536]{2,1,0:T(8,128)(2,1)}), bf16[32,40,1536]{2,1,0:T(8,128)(2,1)}, u32[]{:S(2)}, u32[]{:S(2)}) async-start(bf16[32,40,1536]{2,1,0:T(8,128)(2,1)} %bitcast.421), calls=%async_computation.3 | async-start | bytes 7864320 | tf_op jit(solution)/shard_map/all_to_all | solution.py:120
  476.2 31.7 %copy-start.31 = (f32[256,64]{0,1:T(8,128)S(1)}, f32[256,64]{0,1:T(8,128)}, u32[]{:S(2)}) copy-start(f32[256,64]{0,1:T(8,128)} %copy-done.30) | copy-start | bytes 196612
  523.5 27.2 %copy-start.29 = (f32[256,64]{1,0:T(8,128)S(1)}, f32[256,64]{1,0:T(8,128)}, u32[]{:S(2)}) copy-start(f32[256,64]{1,0:T(8,128)} %copy-done.28) | copy-start | bytes 196612
  523.5 27.2 %copy-start.35 = (f32[256,64]{1,0:T(8,128)S(1)}, f32[256,64]{1,0:T(8,128)}, u32[]{:S(2)}) copy-start(f32[256,64]{1,0:T(8,128)} %copy.121) | copy-start | bytes 196612
  (54 other events, 231.2 us)

commit v7 on v6

--- a/solution.py
+++ b/solution.py
@@ -83,26 +83,6 @@
     attn_probs = (exp_scores / exp_total).astype(BF16)
     head_out = jnp.einsum("gqk,kd->qgd", attn_probs, value_head, preferred_element_type=F32)
     return (head_out, (row_max + jnp.log(exp_total))[..., 0])
-
-
-def head_backward(
-    query_group, key_head, value_head, head_grad, log_total, query_pos, key_pos, length, score_scale
-):
-    scores = masked_scores(query_group, key_head, query_pos, key_pos, length, score_scale)
-    attn_probs = jnp.exp(scores - log_total[..., None])
-    prob_grad = jnp.einsum("qgd,kd->gqk", head_grad, value_head, preferred_element_type=F32)
-    row_delta = jnp.sum(attn_probs * prob_grad, axis=-1, keepdims=True)
-    score_grad = (attn_probs * (prob_grad - row_delta)).astype(BF16)
-    query_part = (
-        jnp.einsum("gqk,kd->qgd", score_grad, key_head, preferred_element_type=F32) * score_scale
-    )
-    key_part = (
-        jnp.einsum("gqk,qgd->kd", score_grad, query_group, preferred_element_type=F32) * score_scale
-    )
-    value_part = jnp.einsum(
-        "gqk,qgd->kd", attn_probs.astype(BF16), head_grad, preferred_element_type=F32
-    )
-    return (query_part, key_part, value_part)
 
 
 def norm_back(values, scale_rows, gain_vec, incoming):
@@ -431,28 +411,160 @@
     )(*[x.reshape(2, 2, line, 2, rows, x.shape[1]) for x in arrays], *extras)
 
 
-def exchange_kernel(count, n, block_of, *refs):
+def spread_kernel(count, parts, source, target, *sems):
     me = lax.axis_index("seq")
     greet([{"seq": lax.rem(me + step, count)} for step in range(1, count)])
-    for copy in start_exchange(count, refs[:n], refs[n : 2 * n], block_of, refs[2 * n :]):
+    size = source.shape[0] // parts
+    pieces = [pl.ds(part * size, size) for part in range(parts)]
+    sources = [source.at[piece] for piece in pieces]
+    targets = [target.at[:, piece] for piece in pieces]
+    for copy in start_exchange(count, sources, targets, lambda ref, peer: ref, sems):
         copy.wait()
 
 
-def seq_exchange(arrays, collective_id, block_of, block_shapes, name):
-    count, n = lax.axis_size("seq"), len(arrays)
-    sent = sum(math.prod(shape) for shape in block_shapes) * (count - 1) * 2
+def seq_spread(array, parts, collective_id, name):
+    count = lax.axis_size("seq")
     return pl.pallas_call(
-        functools.partial(exchange_kernel, count, n, block_of),
-        out_shape=[jax.ShapeDtypeStruct((count,) + shape, BF16) for shape in block_shapes],
-        in_specs=[pl.BlockSpec(memory_space=pl.ANY)] * n,
-        out_specs=[pl.BlockSpec(memory_space=pl.ANY)] * n,
-        scratch_shapes=exchange_sems(n, count),
+        functools.partial(spread_kernel, count, parts),
+        out_shape=jax.ShapeDtypeStruct((count,) + array.shape, BF16),
+        in_specs=[pl.BlockSpec(memory_space=pl.ANY)],
+        out_specs=pl.BlockSpec(memory_space=pl.ANY),
+        scratch_shapes=exchange_sems(parts, count),
         compiler_params=pltpu.CompilerParams(
             collective_id=collective_id, vmem_limit_bytes=4 << 20
         ),
-        cost_estimate=pl.CostEstimate(flops=0, bytes_accessed=sent, transcendentals=0),
+        cost_estimate=pl.CostEstimate(
+            flops=0, bytes_accessed=2 * count * array.size, transcendentals=0
+        ),
         name=name,
-    )(*arrays)
+    )(array)
+
+
+def rotate(values, cosines, sines):
+    return values * cosines + pltpu.roll(values, HEAD_DIM // 2, 1) * sines
+
+
+def attention_back_kernel(count, heads, kv_heads, *refs):
+    length_ref, q_ref, kv_ref, grad_ref, lse_ref, delta_ref, cos_ref, sin_ref, out_ref = refs[:9]
+    dq_ref, part_ref, leaving, arriving, send, recv = refs[9:]
+    me = lax.axis_index("seq")
+    rows, kv_width = q_ref.shape[0], kv_heads * HEAD_DIM
+    group, scale = heads // kv_heads, 1.0 / math.sqrt(HEAD_DIM)
+    greet([{"seq": lax.rem(me + step, count)} for step in range(1, count)])
+    length = length_ref[0]
+    query_pos = me * rows + lax.broadcasted_iota(jnp.int32, (rows, rows), 1)
+    key_local = lax.broadcasted_iota(jnp.int32, (rows, rows), 0)
+    dq_ref[...] = jnp.zeros_like(dq_ref)
+
+    def key_block(j):
+        key_pos = j * rows + key_local
+        mask = (key_pos <= query_pos) & (key_pos < length)
+        part_ref[...] = jnp.zeros_like(part_ref)
+        key_rows = pl.ds(pl.multiple_of(j * rows, rows), rows)
+        for g in range(kv_heads):
+            key_cols = slice(g * HEAD_DIM, (g + 1) * HEAD_DIM)
+            value_cols = slice(kv_width + g * HEAD_DIM, kv_width + (g + 1) * HEAD_DIM)
+
+            def one_head(i, carry):
+                h = g * group + i
+                cols = pl.ds(pl.multiple_of(h * HEAD_DIM, HEAD_DIM), HEAD_DIM)
+                keys, values = kv_ref[key_rows, key_cols], kv_ref[key_rows, value_cols]
+                queries, grads = q_ref[:, cols], grad_ref[:, cols]
+                scores = nt(keys, queries) * scale
+                probs = jnp.where(mask, jnp.exp(scores - lse_ref[pl.ds(h, 1), :]), 0.0)
+                prob_grad = nt(values, grads)
+                score_grad = (probs * (prob_grad - delta_ref[pl.ds(h, 1), :])).astype(BF16)
+                part_ref[:, key_cols] += nn(score_grad, queries)
+                part_ref[:, value_cols] += nn(probs.astype(BF16), grads)
+                dq_ref[:, cols] += tn(score_grad, keys)
+                return carry
+
+            lax.fori_loop(0, group, one_head, 0)
+        part_ref[:, :kv_width] = part_ref[:, :kv_width] * scale
+
+    def to_owner(j):
+        return pltpu.make_async_remote_copy(
+            src_ref=leaving.at[j],
+            dst_ref=arriving.at[me],
+            send_sem=send.at[j],
+            recv_sem=recv.at[me],
+            device_id={"seq": j},
+            device_id_type=MESH_IDS,
+        )
+
+    def other_block(j, carry):
+        key_block(j)
+        leaving[j] = part_ref[...].astype(BF16)
+        to_owner(j).start()
+        return carry
+
+    lax.fori_loop(0, me, other_block, 0)
+    key_block(me)
+    part_ref[...] = part_ref[...].astype(BF16).astype(F32)
+    cosines, sines = cos_ref[...], -sin_ref[...]
+
+    def one_query(h, carry):
+        cols = pl.ds(pl.multiple_of(h * HEAD_DIM, HEAD_DIM), HEAD_DIM)
+        out_ref[:, cols] = rotate(dq_ref[:, cols] * scale, cosines, sines).astype(BF16)
+        return carry
+
+    lax.fori_loop(0, heads, one_query, 0)
+
+    def add_arrived(m, carry):
+        pltpu.make_async_remote_copy(
+            src_ref=leaving.at[m],
+            dst_ref=arriving.at[m],
+            send_sem=send.at[m],
+            recv_sem=recv.at[m],
+            device_id={"seq": m},
+            device_id_type=MESH_IDS,
+        ).wait_recv()
+        part_ref[...] += arriving[m].astype(F32)
+        return carry
+
+    lax.fori_loop(me + 1, count, add_arrived, 0)
+    first = heads * HEAD_DIM
+    for g in range(kv_heads):
+        cols = slice(g * HEAD_DIM, (g + 1) * HEAD_DIM)
+        out_ref[:, first + g * HEAD_DIM : first + (g + 1) * HEAD_DIM] = rotate(
+            part_ref[:, cols], cosines, sines
+        ).astype(BF16)
+    out_ref[:, first + kv_width :] = part_ref[:, kv_width:].astype(BF16)
+
+    def sent(j, carry):
+        to_owner(j).wait_send()
+        return carry
+
+    lax.fori_loop(0, me, sent, 0)
+
+
+def attention_back(length, queries, kv_all, grads, lse, delta, cosines, sines, collective_id):
+    count = lax.axis_size("seq")
+    rows, q_width = queries.shape
+    kv_width = kv_all.shape[1] // 2
+    heads, kv_heads = q_width // HEAD_DIM, kv_width // HEAD_DIM
+    vmem = pl.BlockSpec(memory_space=pltpu.VMEM)
+    return pl.pallas_call(
+        functools.partial(attention_back_kernel, count, heads, kv_heads),
+        out_shape=jax.ShapeDtypeStruct((rows, q_width + 2 * kv_width), BF16),
+        in_specs=[pl.BlockSpec(memory_space=pltpu.SMEM)] + [vmem] * 7,
+        out_specs=vmem,
+        scratch_shapes=[
+            pltpu.VMEM((rows, q_width), F32),
+            pltpu.VMEM((rows, 2 * kv_width), F32),
+            pltpu.VMEM((count, rows, 2 * kv_width), BF16),
+            pltpu.VMEM((count, rows, 2 * kv_width), BF16),
+            pltpu.SemaphoreType.DMA((count,)),
+            pltpu.SemaphoreType.DMA((count,)),
+        ],
+        compiler_params=pltpu.CompilerParams(
+            collective_id=collective_id, vmem_limit_bytes=30 << 20
+        ),
+        cost_estimate=pl.CostEstimate(
+            flops=10 * count * rows * rows * q_width, bytes_accessed=1 << 20, transcendentals=0
+        ),
+        name="attention_backward",
+    )(length, queries, kv_all, grads, lse, delta, cosines, sines)
 
 
 def seq_permutes(block_for):
@@ -525,20 +637,15 @@
 
         return seq_permutes(block_for)
 
+    gate_parts = expert_pieces(w_gate)
     if staged:
-        packed_full, gains_full, out_full, gate_full = staged_gather(
-            [packed, gain_block, w_out],
-            [w_gate],
-            lambda ref, peer: ref.at[peer // sharers],
-            2,
-            "gather_attention_weights",
+        packed_full, gains_full, out_full = staged_gather(
+            [packed, gain_block, w_out], [], None, 2, "gather_attention_weights"
         )
-        gate_full = gate_full.reshape(width, hidden_units)
     else:
         packed_full = lax.all_gather(packed, BOTH, axis=0, tiled=True)
         gains_full = lax.all_gather(gain_block, BOTH, axis=0, tiled=True)
         out_full = lax.all_gather(w_out, BOTH, axis=0, tiled=True)
-        gate_full = in_seq_order(expert_pieces(w_gate), BF16).reshape(width, hidden_units)
 
     pair_routes, place, kept = claim_places(routes[0], priority[0, 0], is_valid)
     holder = (pair_routes // own_experts) * seq_count + (pair_routes % own_experts) * sharers
@@ -554,12 +661,9 @@
     live_cotangent = jnp.where(is_valid[:, None], cotangent[0], jnp.zeros((), BF16))
     out_grad = live_cotangent.astype(F32)
     grad_send = (tn(token_hot, live_cotangent) * slot_gate[:, None]).astype(BF16)
-    packed_full, gains_full, out_full, gate_full, grad_send, w_up, w_down = (
-        lax.optimization_barrier(
-            (packed_full, gains_full, out_full, gate_full, grad_send, w_up, w_down)
-        )
-    )
-    up_parts, down_parts = expert_pieces(w_up), expert_pieces(w_down)
+    packed_full, gains_full, out_full, gate_parts, grad_send = lax.optimization_barrier(
+        (packed_full, gains_full, out_full, gate_parts, grad_send)
+    )
     gain_one, gain_two = gains_full[:, 0].astype(F32), gains_full[:, 1].astype(F32)
     grad_rows = swap(grad_send.reshape(devices, CAP, width), ("dp", "seq")).reshape(slots, width)
 
@@ -578,10 +682,9 @@
     ).astype(BF16)
     key_rotated = key_rotated.reshape(rows, kv_width)
     kv_mine = jnp.concatenate([key_rotated, value_matrix_rows], axis=1)
-    (kv_all,) = seq_exchange(
-        [kv_mine], 1, lambda ref, peer: ref, [(rows, 2 * kv_width)], "gather_keys"
-    )
-    kv_all = kv_all.reshape(extent, 2 * kv_width)
+    kv_all = seq_spread(kv_mine, 8, 1, "gather_keys").reshape(extent, 2 * kv_width)
+    kv_all, w_up, w_down = lax.optimization_barrier((kv_all, w_up, w_down))
+    up_parts, down_parts = expert_pieces(w_up), expert_pieces(w_down)
     key_all, value_all = kv_all[:, :kv_width], kv_all[:, kv_width:]
     query_head_groups = query_rotated.reshape(rows, kv_heads, group_size, HEAD_DIM).transpose(
         1, 0, 2, 3
@@ -601,6 +704,7 @@
     send_rows = tn(token_hot, moe_input).astype(BF16).reshape(devices, CAP, width)
     send_rows, grad_rows, up_parts = lax.optimization_barrier((send_rows, grad_rows, up_parts))
     slot_rows = swap(send_rows, ("dp", "seq")).reshape(slots, width)
+    gate_full = in_seq_order(gate_parts, BF16).reshape(width, hidden_units)
     up_full = in_seq_order(up_parts, BF16).reshape(width, hidden_units)
     down_full = in_seq_order(down_parts, BF16).reshape(hidden_units, width)
     slot_rows, gate_full, up_full, down_full = lax.optimization_barrier(
@@ -647,51 +751,20 @@
     out_terms = tn(attended, branch_grad).astype(BF16)
     attended_grad = nt(branch_grad, out_full).astype(BF16)
     attended_grad, out_terms = lax.optimization_barrier((attended_grad, out_terms))
-    attended_grad = attended_grad.reshape(rows, kv_heads, group_size, HEAD_DIM).transpose(
-        1, 0, 2, 3
-    )
-    query_part, key_part, value_part = lax.map(
-        lambda operands: head_backward(
-            operands[0],
-            operands[1],
-            operands[2],
-            operands[3],
-            operands[4],
-            query_pos,
-            key_pos,
-            length,
-            score_scale,
-        ),
-        (query_head_groups, key_heads, value_heads, attended_grad, log_total),
-    )
-    kv_terms = jnp.concatenate(
-        [
-            key_part.transpose(1, 0, 2).reshape(extent, kv_width),
-            value_part.transpose(1, 0, 2).reshape(extent, kv_width),
-        ],
-        axis=1,
-    ).astype(BF16)
-    kv_terms, down_grad_parts = lax.optimization_barrier((kv_terms, down_grad_parts))
-    (kv_back,) = seq_exchange(
-        [kv_terms.reshape(seq_count, rows, 2 * kv_width)],
+    delta = attended_grad.astype(F32) * attended.astype(F32)
+    delta = jnp.sum(delta.reshape(rows, q_heads, HEAD_DIM), axis=-1).T
+    cosines, sines = cosine_lookup[:, 0], sine_lookup[:, 0]
+    projected_grad = attention_back(
+        lengths,
+        query_rotated.reshape(rows, q_width),
+        kv_all,
+        attended_grad,
+        log_total.reshape(q_heads, rows),
+        delta,
+        jnp.concatenate([cosines, cosines], axis=1),
+        jnp.concatenate([-sines, sines], axis=1),
         4,
-        lambda ref, peer: ref.at[peer],
-        [(rows, 2 * kv_width)],
-        "return_key_grads",
-    )
-    kv_sum = jnp.sum(kv_back.astype(F32), axis=0)
-    key_grad = apply_rotary(
-        kv_sum[:, :kv_width].reshape(rows, kv_heads, HEAD_DIM), cosine_lookup, -sine_lookup
-    )
-    key_grad = key_grad.reshape(rows, kv_width).astype(BF16)
-    value_grad = kv_sum[:, kv_width:].astype(BF16)
-    query_grad = apply_rotary(
-        query_part.transpose(1, 0, 2, 3).reshape(rows, q_heads, HEAD_DIM),
-        cosine_lookup,
-        -sine_lookup,
-    )
-    query_grad = query_grad.reshape(rows, q_width).astype(BF16)
-    projected_grad = jnp.concatenate([query_grad, key_grad, value_grad], axis=1)
+    )
     normed_grad = nt(projected_grad, packed_full)
     input_norm_grad, gain_one_grad = norm_back(inputs, scale_one, gain_one, normed_grad)
     input_grad = middle_grad + input_norm_grad
@@ -699,6 +772,7 @@
     lane = lax.broadcasted_iota(jnp.int32, (width, LANES), 1)
     gain_terms = jnp.where(lane == 0, gain_one_grad[:, None], gain_two_grad[:, None])
     gain_terms = jnp.where(lane < 2, gain_terms, 0.0).astype(BF16)
+    projected_grad, down_grad_parts = lax.optimization_barrier((projected_grad, down_grad_parts))
     query_terms = tn(normed, projected_grad).astype(BF16)
     grad_parts = [gate_grad_parts, up_grad_parts, down_grad_parts]
     if staged:

time: 649 us -> 638 us (0.983)
  matrix products: 125 us -> 98.1 us
  Pallas kernels: 231 us -> 243 us
  waiting for transfers between devices: 146 us -> 135 us
  starting transfers between devices: 39.8 us -> 48.6 us
  local copies, waits for them, and re-layouts: 53.1 us -> 60.4 us
    pallas_call x2, Pallas kernels: 80.5 us -> 102 us  [the longest x1 54.7 us: attention_back(): pl.pallas_call(functools.partial(attention_back_kernel, count, heads, kv_...]
    dot_general x8 -> x0, matrix products: 19.7 us -> none  [the longest x2 10.8 us: head_backward(): jnp.einsum('gqk,qgd->kd', attn_probs.astype(BF16), head_grad, preferred_e...]
    pallas_call x1, Pallas kernels: 84.8 us -> 68.1 us  [staged_gather(): pl.pallas_call(functools.partial(gather_kernel, line, chunks, n, len(extr...]
    ppermute x15 -> x18, waiting for transfers between devices: 134 us -> 123 us  [seq_permutes(): lax.ppermute(block_for(lax.rem(me + step, count)), 'seq', ring)]
    ppermute x15 -> x18, starting transfers between devices: 19.1 us -> 25.9 us  [seq_permutes(): lax.ppermute(block_for(lax.rem(me + step, count)), 'seq', ring)]
    pallas_call x1, Pallas kernels: 65.5 us -> 72.4 us  [staged_scatter(): pl.pallas_call(functools.partial(scatter_kernel, line, chunks, n, len(ext...]
  transfers between devices with their start and end apart: 19 -> 22, of which waited for: 12 -> 12; matrix products, arithmetic and copies ran while one was open for 23% -> 23% of each run, Pallas kernels for 23% -> 39%
where the time goes in v7:
time: 638 us; the launch traced here: 630 us
  Pallas kernels  243 us (38%)
  waiting for transfers between devices  135 us (21%)
  matrix products  98.1 us (15%)
  local copies, waits for them, and re-layouts  60.4 us (9%)
  starting transfers between devices  48.6 us (8%)
  other arithmetic  42.2 us (7%)
    ppermute x18, waiting for transfers between devices, seq_permutes(): lax.ppermute(block_for(lax.rem(me + step, count)), 'seq', ring)  123 us
    dot_general x19, matrix products, dot(): lax.dot_general(left, right, (contract, ((), ())), preferred_element_type...  90.1 us
    pallas_call x1, Pallas kernels, staged_scatter(): pl.pallas_call(functools.partial(scatter_kernel, line, chunks, n, len(ext...  72.4 us
    pallas_call x1, Pallas kernels, staged_gather(): pl.pallas_call(functools.partial(gather_kernel, line, chunks, n, len(extr...  68.1 us
    pallas_call x1, Pallas kernels, attention_back(): pl.pallas_call(functools.partial(attention_back_kernel, count, heads, kv_...  54.7 us
    pallas_call x1, Pallas kernels, seq_spread(): pl.pallas_call(functools.partial(spread_kernel, count, parts), out_shape=...  47.4 us
    ppermute x18, starting transfers between devices, seq_permutes(): lax.ppermute(block_for(lax.rem(me + step, count)), 'seq', ring)  25.9 us
    all_to_all x4, starting transfers between devices, swap(): return lax.all_to_all(blocks, axes, split_axis=0, concat_axis=0, tiled=True)  22.6 us
  transfers between devices with their start and end apart: 22, of which 12 were waited for; matrix products, arithmetic and copies ran while one was open for 23% of the time, Pallas kernels for 39%

profile of v7, /device:TPU:0, one launch (start us, length us, event | category | flops | bytes accessed | tf_op | source)
XLA Modules:
  0.0 629.8 jit_solution(14397119654674303295)
XLA Ops:
  18.2 68.1 %gather_attention_weights.1 = (bf16[2,2,4,2,48,2048]{5,4,3,2,1,0:T(8,128)(2,1)S(1)}, bf16[2,2,4,2,48,128]{5,4,3,2,1,0:T(8,128)(2,1)S(1)}, bf16[2,2,4,2,48,1536]{5,4,3,2,1,0:T(8,128)(2,1)S(1)}) custom-call(bf16[48,2048]{1,0:T(8,128)(2,1)S(1)} %pad_maximum_fusion.2.refs_0_, bf16[48,128]{1,0:T(8,128)(2,1)S(1)} %maximum_maximum_fusion.refs_1_, ...), custom_call_target="tpu_custom_call" | custom-call | bytes 11403264 | tf_op jit(solution)/shard_map/gather_attention_weights/pallas_call | solution.py:275
  101.9 5.8 all-to-all-start
  108.6 47.4 %gather_keys.1 = bf16[4,256,512]{2,1,0:T(8,128)(2,1)S(1)} custom-call(bf16[256,512]{1,0:T(8,128)(2,1)S(1)} %pad_maximum_fusion.1.source), custom_call_target="tpu_custom_call" | custom-call | bytes 1048576 | tf_op jit(solution)/shard_map/gather_keys/pallas_call | solution.py:427
  178.5 13.7 %while.14 = (s32[]{:T(128)}, bf16[2,256,6,128]{1,3,2,0:T(8,128)(2,1)S(1)}, f32[2,6,256]{2,1,0:T(8,128)}, bf16[2,1024,128]{1,2,0:T(8,128)(2,1)}, s32[]{:T(128)}, ...) while((s32[]{:T(128)}, ...), condition=%wide.region_7.8_spmd.clone.clone, body=%wide.region_4.7_spmd.clone.clone.sunk | while | flops 824704768 | bytes 23786112 | solution.py:693
  199.3 7.9 %collective-permute-done.4 = bf16[384,768]{1,0:T(8,128)(2,1)} collective-permute-done((bf16[384,768]{1,0:T(8,128)(2,1)}, bf16[384,768]{1,0:T(8,128)(2,1)}, u32[]{:S(2)}, u32[]{:S(2)}) %collective-permute-start.4) | collective-permute-done | bytes 589856 | tf_op jit(solution)/shard_map/ppermute | solution.py:575
  209.2 6.3 all-to-all-start.1
  226.1 46.4 %collective-permute-done.6 = bf16[192,1536]{1,0:T(8,128)(2,1)S(1)} collective-permute-done((bf16[192,1536]{1,0:T(8,128)(2,1)S(1)}, bf16[192,1536]{1,0:T(8,128)(2,1)S(1)}, u32[]{:S(2)}, u32[]{:S(2)}) %collective-permute-start.6) | collective-permute-done | bytes 589856 | tf_op jit(solution)/shard_map/ppermute | solution.py:575
  272.6 7.8 %collective-permute-done.7 = bf16[192,1536]{1,0:T(8,128)(2,1)S(1)} collective-permute-done((bf16[192,1536]{1,0:T(8,128)(2,1)S(1)}, bf16[192,1536]{1,0:T(8,128)(2,1)S(1)}, u32[]{:S(2)}, u32[]{:S(2)}) %collective-permute-start.7) | collective-permute-done | bytes 589856 | tf_op jit(solution)/shard_map/ppermute | solution.py:575
  292.9 11.5 %all-to-all-done.1 = bf16[32,40,1536]{2,1,0:T(8,128)(2,1)} async-done(((bf16[32,40,1536]{2,1,0:T(8,128)(2,1)}), bf16[32,40,1536]{2,1,0:T(8,128)(2,1)}, u32[]{:S(2)}, u32[]{:S(2)}) %all-to-all-start.1) | async-done | bytes 3932192 | tf_op jit(solution)/shard_map/all_to_all | solution.py:100
  304.4 6.2 fusion.65
  310.7 5.5 fusion.64
  316.2 7.9 %multiply_convert_fusion = (bf16[1280,768]{1,0:T(8,128)(2,1)S(1)}, bf16[1280,768]{1,0:T(8,128)(2,1)S(1)}, bf16[1280,768]{1,0:T(8,128)(2,1)}) fusion(f32[1280,768]{1,0:T(8,128)S(1)} %fusion.64, f32[1280,768]{1,0:T(8,128)S(1)} %fusion.65, bf16[1280,1536]{1,0:T(8,128)(2,1)} %bitcast.28, bf16[768,1536]{1,0:T(8,128)(2,1)S(1)} %bitcast.296), kind=kOutput, calls=%fused_computation.39 | convolution fusion | flops 3034644480 | bytes 20054016 | tf_op jit(solution)/shard_map/dot_general | solution.py:46
  327.5 6.4 %fusion.21 = bf16[1280,1536]{1,0:T(8,128)(2,1)} fusion(f32[1280,1536]{1,0:T(8,128)S(1)} %fusion.66, bf16[1280,768]{1,0:T(8,128)(2,1)S(1)} %get-tuple-element.214, bf16[1536,768]{1,0:T(8,128)(2,1)} %bitcast.43), kind=kOutput, calls=%fused_computation.29 | convolution fusion | flops 3023831040 | bytes 16121856 | tf_op jit(solution)/shard_map/dot_general | solution.py:46
  333.9 5.3 all-to-all-start.2
  343.9 6.0 convolution_convert_fusion.4
  351.9 5.4 convolution_convert_fusion.5
  357.3 6.8 %convolution_convert_fusion.6 = bf16[768,1536]{1,0:T(8,128)(2,1)} fusion(bf16[1280,768]{1,0:T(8,128)(2,1)S(1)} %copy-done.52, bf16[1280,1536]{1,0:T(8,128)(2,1)} %bitcast.28), kind=kOutput, calls=%fused_computation.46 | convolution fusion | flops 3021078528 | bytes 8257536 | tf_op jit(solution)/shard_map/dot_general | solution.py:46
  380.7 15.5 %collective-permute-done.15 = bf16[384,768]{1,0:T(8,128)(2,1)S(1)} collective-permute-done((bf16[384,768]{1,0:T(8,128)(2,1)S(1)}, bf16[384,768]{1,0:T(8,128)(2,1)S(1)}, u32[]{:S(2)}, u32[]{:S(2)}) %collective-permute-start.15) | collective-permute-done | bytes 589856 | tf_op jit(solution)/shard_map/ppermute | solution.py:575
  397.3 8.2 %collective-permute-done.16 = bf16[384,768]{1,0:T(8,128)(2,1)S(1)} collective-permute-done((bf16[384,768]{1,0:T(8,128)(2,1)S(1)}, bf16[384,768]{1,0:T(8,128)(2,1)S(1)}, u32[]{:S(2)}, u32[]{:S(2)}) %collective-permute-start.16) | collective-permute-done | bytes 589856 | tf_op jit(solution)/shard_map/ppermute | solution.py:575
  409.7 20.5 %collective-permute-done.12 = bf16[384,768]{1,0:T(8,128)(2,1)S(1)} collective-permute-done((bf16[384,768]{1,0:T(8,128)(2,1)S(1)}, bf16[384,768]{1,0:T(8,128)(2,1)S(1)}, u32[]{:S(2)}, u32[]{:S(2)}) %collective-permute-start.12) | collective-permute-done | bytes 589856 | tf_op jit(solution)/shard_map/ppermute | solution.py:575
  442.5 5.2 all-to-all-start.3
  471.6 54.7 %attention_backward.1 = bf16[256,2048]{1,0:T(8,128)(2,1)S(1)} custom-call(s32[1]{0:T(128)} %copy.117.refs_0_, bf16[256,1536]{1,0:T(8,128)(2,1)S(1)} %copy.71.refs_1_, bf16[1024,512]{1,0:T(8,128)(2,1)S(1)} %bitcast.278, bf16[256,1536]{1,0:T(8,128)(2,1)S(1)} %copy-done.2, f32[12,256]{1,0:T(8,128)S(1)} %reshape.503.refs_4_, f32[12,256]{1,0:T(8,128)S(1)} %bitcast.280, ...), custom_call_target="tpu_custom_call" | custom-call | flops 4026531840 | bytes 1048576 | tf_op jit(solution)/shard_map/attention_backward/pallas_call | solution.py:547
  526.4 6.1 fusion.37
  539.1 72.4 %scatter_attention_grads.1 = (f32[48,1536]{1,0:T(8,128)S(1)}, f32[48,128]{1,0:T(8,128)S(1)}, f32[48,2048]{1,0:T(8,128)S(1)}) custom-call(bf16[2,2,4,2,48,1536]{5,4,3,2,1,0:T(8,128)(2,1)S(1)} %bitcast.272, bf16[2,2,4,2,48,128]{5,4,3,2,1,0:T(8,128)(2,1)S(1)} %select_convert_fusion.refs_1_, bf16[2,2,4,2,48,2048]{5,4,3,2,1,0:T(8,128)(2,1)S(1)} %bitcast.269), custom_call_target="tpu_custom_call" | custom-call | bytes 11403264 | tf_op jit(solution)/shard_map/scatter_attention_grads/pallas_call | solution.py:391
  (284 shorter events, 193.3 us)
Async XLA Ops:
  3.8 91.7 %collective-permute-start = (bf16[384,768]{1,0:T(8,128)(2,1)}, bf16[384,768]{1,0:T(8,128)(2,1)}, u32[]{:S(2)}, u32[]{:S(2)}) collective-permute-start(bf16[384,768]{1,0:T(8,128)(2,1)} %get-tuple-element.236), channel_id=1, source_target_pairs={{0,8},{8,16},{16,24},{24,0},{1,9},{9,17},{17,25},{25,1},{2,10},{10... | collective-permute-start | bytes 1769480 | tf_op jit(solution)/shard_map/ppermute | solution.py:575
  6.8 88.7 %collective-permute-start.1 = (bf16[384,768]{1,0:T(8,128)(2,1)}, bf16[384,768]{1,0:T(8,128)(2,1)}, u32[]{:S(2)}, u32[]{:S(2)}) collective-permute-start(bf16[384,768]{1,0:T(8,128)(2,1)} %get-tuple-element.238), channel_id=1, source_target_pairs={{0,16},{8,24},{16,0},{24,8},{1,17},{9,25},{17,1},{25,9},{2,18},{10... | collective-permute-start | bytes 1769480 | tf_op jit(solution)/shard_map/ppermute | solution.py:575
  8.3 87.2 %collective-permute-start.2 = (bf16[384,768]{1,0:T(8,128)(2,1)}, bf16[384,768]{1,0:T(8,128)(2,1)}, u32[]{:S(2)}, u32[]{:S(2)}) collective-permute-start(bf16[384,768]{1,0:T(8,128)(2,1)} %get-tuple-element.235), channel_id=1, source_target_pairs={{0,24},{8,0},{16,8},{24,16},{1,25},{9,1},{17,9},{25,17},{2,26},{10... | collective-permute-start | bytes 1769480 | tf_op jit(solution)/shard_map/ppermute | solution.py:575
  17.0 90.7 %copy-start.30 = (f32[256,64]{1,0:T(8,128)}, f32[256,64]{1,0:T(8,128)S(1)}, u32[]{:S(2)}) copy-start(f32[256,64]{1,0:T(8,128)S(1)} %get-tuple-element.249) | copy-start | bytes 196612
  95.8 100.3 %copy-start.38 = (f32[1536]{0:T(1024)}, f32[1536]{0:T(1024)S(1)}, u32[]{:S(2)}) copy-start(f32[1536]{0:T(1024)S(1)} %get-tuple-element.190) | copy-start | bytes 18436
  101.9 107.4 %all-to-all-start = ((bf16[32,40,1536]{2,1,0:T(8,128)(2,1)}), bf16[32,40,1536]{2,1,0:T(8,128)(2,1)}, u32[]{:S(2)}, u32[]{:S(2)}) async-start(bf16[32,40,1536]{2,1,0:T(8,128)(2,1)} %bitcast.291), calls=%async_computation | async-start | bytes 7864320 | tf_op jit(solution)/shard_map/all_to_all | solution.py:100
  172.2 27.1 %collective-permute-start.3 = (bf16[384,768]{1,0:T(8,128)(2,1)}, bf16[384,768]{1,0:T(8,128)(2,1)}, u32[]{:S(2)}, u32[]{:S(2)}) collective-permute-start(bf16[384,768]{1,0:T(8,128)(2,1)} %get-tuple-element.233), channel_id=1, source_target_pairs={{0,8},{8,16},{16,24},{24,0},{1,9},{9,17},{17,25},{25,1},{2,10},{10... | collective-permute-start | bytes 1769480 | tf_op jit(solution)/shard_map/ppermute | solution.py:575
  175.5 31.8 %collective-permute-start.4 = (bf16[384,768]{1,0:T(8,128)(2,1)}, bf16[384,768]{1,0:T(8,128)(2,1)}, u32[]{:S(2)}, u32[]{:S(2)}) collective-permute-start(bf16[384,768]{1,0:T(8,128)(2,1)} %get-tuple-element.232), channel_id=1, source_target_pairs={{0,16},{8,24},{16,0},{24,8},{1,17},{9,25},{17,1},{25,9},{2,18},{10... | collective-permute-start | bytes 1769480 | tf_op jit(solution)/shard_map/ppermute | solution.py:575
  177.1 32.1 %collective-permute-start.5 = (bf16[384,768]{1,0:T(8,128)(2,1)}, bf16[384,768]{1,0:T(8,128)(2,1)}, u32[]{:S(2)}, u32[]{:S(2)}) collective-permute-start(bf16[384,768]{1,0:T(8,128)(2,1)} %get-tuple-element.231), channel_id=1, source_target_pairs={{0,24},{8,0},{16,8},{24,16},{1,25},{9,1},{17,9},{25,17},{2,26},{10... | collective-permute-start | bytes 1769480 | tf_op jit(solution)/shard_map/ppermute | solution.py:575
  209.2 95.2 %all-to-all-start.1 = ((bf16[32,40,1536]{2,1,0:T(8,128)(2,1)}), bf16[32,40,1536]{2,1,0:T(8,128)(2,1)}, u32[]{:S(2)}, u32[]{:S(2)}) async-start(bf16[32,40,1536]{2,1,0:T(8,128)(2,1)} %bitcast.283), calls=%async_computation.1 | async-start | bytes 7864320 | tf_op jit(solution)/shard_map/all_to_all | solution.py:100
  217.4 55.1 %collective-permute-start.6 = (bf16[192,1536]{1,0:T(8,128)(2,1)S(1)}, bf16[192,1536]{1,0:T(8,128)(2,1)S(1)}, u32[]{:S(2)}, u32[]{:S(2)}) collective-permute-start(bf16[192,1536]{1,0:T(8,128)(2,1)S(1)} %get-tuple-element.229), channel_id=1, source_target_pairs={{0,8},{8,16},{16,24},{24,0},{1,9},{9,17},{17,25},{25,1},{2,10},{10... | collective-permute-start | bytes 1769480 | tf_op jit(solution)/shard_map/ppermute | solution.py:575
  219.1 61.3 %collective-permute-start.7 = (bf16[192,1536]{1,0:T(8,128)(2,1)S(1)}, bf16[192,1536]{1,0:T(8,128)(2,1)S(1)}, u32[]{:S(2)}, u32[]{:S(2)}) collective-permute-start(bf16[192,1536]{1,0:T(8,128)(2,1)S(1)} %get-tuple-element.228), channel_id=1, source_target_pairs={{0,16},{8,24},{16,0},{24,8},{1,17},{9,25},{17,1},{25,9},{2,18},{10... | collective-permute-start | bytes 1769480 | tf_op jit(solution)/shard_map/ppermute | solution.py:575
  220.6 63.8 %collective-permute-start.8 = (bf16[192,1536]{1,0:T(8,128)(2,1)S(1)}, bf16[192,1536]{1,0:T(8,128)(2,1)S(1)}, u32[]{:S(2)}, u32[]{:S(2)}) collective-permute-start(bf16[192,1536]{1,0:T(8,128)(2,1)S(1)} %get-tuple-element.227), channel_id=1, source_target_pairs={{0,24},{8,0},{16,8},{24,16},{1,25},{9,1},{17,9},{25,17},{2,26},{10... | collective-permute-start | bytes 1769480 | tf_op jit(solution)/shard_map/ppermute | solution.py:575
  333.9 108.6 %all-to-all-start.2 = ((bf16[32,40,1536]{2,1,0:T(8,128)(2,1)}), bf16[32,40,1536]{2,1,0:T(8,128)(2,1)}, u32[]{:S(2)}, u32[]{:S(2)}) async-start(bf16[32,40,1536]{2,1,0:T(8,128)(2,1)} %bitcast.292), calls=%async_computation.2 | async-start | bytes 7864320 | tf_op jit(solution)/shard_map/all_to_all | solution.py:100
  350.1 46.1 %collective-permute-start.15 = (bf16[384,768]{1,0:T(8,128)(2,1)S(1)}, bf16[384,768]{1,0:T(8,128)(2,1)S(1)}, u32[]{:S(2)}, u32[]{:S(2)}) collective-permute-start(bf16[384,768]{1,0:T(8,128)(2,1)S(1)} %get-tuple-element.219), channel_id=1, source_target_pairs={{0,8},{8,16},{16,24},{24,0},{1,9},{9,17},{17,25},{25,1},{2,10},{10... | collective-permute-start | bytes 1769480 | tf_op jit(solution)/shard_map/ppermute | solution.py:575
  369.0 36.6 %collective-permute-start.16 = (bf16[384,768]{1,0:T(8,128)(2,1)S(1)}, bf16[384,768]{1,0:T(8,128)(2,1)S(1)}, u32[]{:S(2)}, u32[]{:S(2)}) collective-permute-start(bf16[384,768]{1,0:T(8,128)(2,1)S(1)} %get-tuple-element.218), channel_id=1, source_target_pairs={{0,16},{8,24},{16,0},{24,8},{1,17},{9,25},{17,1},{25,9},{2,18},{10... | collective-permute-start | bytes 1769480 | tf_op jit(solution)/shard_map/ppermute | solution.py:575
  374.1 34.5 %collective-permute-start.17 = (bf16[384,768]{1,0:T(8,128)(2,1)S(1)}, bf16[384,768]{1,0:T(8,128)(2,1)S(1)}, u32[]{:S(2)}, u32[]{:S(2)}) collective-permute-start(bf16[384,768]{1,0:T(8,128)(2,1)S(1)} %get-tuple-element.217), channel_id=1, source_target_pairs={{0,24},{8,0},{16,8},{24,16},{1,25},{9,1},{17,9},{25,17},{2,26},{10... | collective-permute-start | bytes 1769480 | tf_op jit(solution)/shard_map/ppermute | solution.py:575
  379.4 50.8 %collective-permute-start.12 = (bf16[384,768]{1,0:T(8,128)(2,1)S(1)}, bf16[384,768]{1,0:T(8,128)(2,1)S(1)}, u32[]{:S(2)}, u32[]{:S(2)}) collective-permute-start(bf16[384,768]{1,0:T(8,128)(2,1)S(1)} %get-tuple-element.222), channel_id=1, source_target_pairs={{0,8},{8,16},{16,24},{24,0},{1,9},{9,17},{17,25},{25,1},{2,10},{10... | collective-permute-start | bytes 1769480 | tf_op jit(solution)/shard_map/ppermute | solution.py:575
  379.9 56.1 %collective-permute-start.13 = (bf16[384,768]{1,0:T(8,128)(2,1)S(1)}, bf16[384,768]{1,0:T(8,128)(2,1)S(1)}, u32[]{:S(2)}, u32[]{:S(2)}) collective-permute-start(bf16[384,768]{1,0:T(8,128)(2,1)S(1)} %get-tuple-element.221), channel_id=1, source_target_pairs={{0,16},{8,24},{16,0},{24,8},{1,17},{9,25},{17,1},{25,9},{2,18},{10... | collective-permute-start | bytes 1769480 | tf_op jit(solution)/shard_map/ppermute | solution.py:575
  396.2 45.2 %collective-permute-start.14 = (bf16[384,768]{1,0:T(8,128)(2,1)S(1)}, bf16[384,768]{1,0:T(8,128)(2,1)S(1)}, u32[]{:S(2)}, u32[]{:S(2)}) collective-permute-start(bf16[384,768]{1,0:T(8,128)(2,1)S(1)} %get-tuple-element.220), channel_id=1, source_target_pairs={{0,24},{8,0},{16,8},{24,16},{1,25},{9,1},{17,9},{25,17},{2,26},{10... | collective-permute-start | bytes 1769480 | tf_op jit(solution)/shard_map/ppermute | solution.py:575
  442.5 180.3 %all-to-all-start.3 = ((bf16[32,40,1536]{2,1,0:T(8,128)(2,1)}), bf16[32,40,1536]{2,1,0:T(8,128)(2,1)}, u32[]{:S(2)}, u32[]{:S(2)}) async-start(bf16[32,40,1536]{2,1,0:T(8,128)(2,1)} %bitcast.290), calls=%async_computation.3 | async-start | bytes 7864320 | tf_op jit(solution)/shard_map/all_to_all | solution.py:100
  465.0 71.7 %collective-permute-start.10 = (bf16[192,1536]{1,0:T(8,128)(2,1)}, bf16[192,1536]{1,0:T(8,128)(2,1)}, u32[]{:S(2)}, u32[]{:S(2)}) collective-permute-start(bf16[192,1536]{1,0:T(8,128)(2,1)} %get-tuple-element.224), channel_id=1, source_target_pairs={{0,16},{8,24},{16,0},{24,8},{1,17},{9,25},{17,1},{25,9},{2,18},{10... | collective-permute-start | bytes 1769480 | tf_op jit(solution)/shard_map/ppermute | solution.py:575
  466.9 69.8 %collective-permute-start.11 = (bf16[192,1536]{1,0:T(8,128)(2,1)}, bf16[192,1536]{1,0:T(8,128)(2,1)}, u32[]{:S(2)}, u32[]{:S(2)}) collective-permute-start(bf16[192,1536]{1,0:T(8,128)(2,1)} %get-tuple-element.223), channel_id=1, source_target_pairs={{0,24},{8,0},{16,8},{24,16},{1,25},{9,1},{17,9},{25,17},{2,26},{10... | collective-permute-start | bytes 1769480 | tf_op jit(solution)/shard_map/ppermute | solution.py:575
  468.4 68.4 %collective-permute-start.9 = (bf16[192,1536]{1,0:T(8,128)(2,1)}, bf16[192,1536]{1,0:T(8,128)(2,1)}, u32[]{:S(2)}, u32[]{:S(2)}) collective-permute-start(bf16[192,1536]{1,0:T(8,128)(2,1)} %get-tuple-element.225), channel_id=1, source_target_pairs={{0,8},{8,16},{16,24},{24,0},{1,9},{9,17},{17,25},{25,1},{2,10},{10... | collective-permute-start | bytes 1769480 | tf_op jit(solution)/shard_map/ppermute | solution.py:575
  (59 other events, 755.3 us)

commit v8 on v7

--- a/solution.py
+++ b/solution.py
@@ -12,6 +12,7 @@
 EXPERTS = 32
 TOP = 4
 CAP = 40
+EARLY = 16
 
 EPSILON = 1e-06
 ROPE_BASE = 10000.0
@@ -182,8 +183,10 @@
     ]
 
 
-def in_steps(count, stages):
+def in_steps(count, stages, after=None):
     for step in range((count + 1) // 2 + len(stages) - 1):
+        if after is not None and step == (count + 1) // 2 + 1:
+            after()
         for behind, stage in enumerate(stages):
             for i in (2 * (step - behind), 2 * (step - behind) + 1):
                 if 0 <= i < count:
@@ -372,8 +375,13 @@
             total = total + ins4[i][lax.rem(z + line - step, line)].astype(F32)
         targets[k][:, first : first + size] = total
 
-    more = start_exchange(4, more_sources, more_targets, block_of, more_sems) if extras else []
-    in_steps(m, [send_core, send_first, send_second, send_line, finish])
+    more = []
+
+    def send_more():
+        if extras:
+            more.extend(start_exchange(4, more_sources, more_targets, block_of, more_sems))
+
+    in_steps(m, [send_core, send_first, send_second, send_line, finish], send_more)
     for copy in sent:
         copy.wait_send()
     for copy in more:
@@ -479,7 +487,7 @@
                 dq_ref[:, cols] += tn(score_grad, keys)
                 return carry
 
-            lax.fori_loop(0, group, one_head, 0)
+            lax.fori_loop(0, group, one_head, 0, unroll=3)
         part_ref[:, :kv_width] = part_ref[:, :kv_width] * scale
 
     def to_owner(j):
@@ -656,6 +664,14 @@
     hits = target[:, :, None] == slot_ids[None, None, :]
     gate_rows = gates[0]
     token_hot = jnp.any(hits, axis=1).astype(BF16)
+
+    def hot_of(first, size):
+        mine = kept & (place >= first) & (place < first + size)
+        spot = jnp.where(mine, holder * size + place - first, slots).reshape(rows, TOP)
+        ids = jnp.arange(devices * size, dtype=jnp.int32)
+        return jnp.any(spot[:, :, None] == ids[None, None, :], axis=1).astype(BF16)
+
+    early_hot, late_hot = hot_of(0, EARLY), hot_of(EARLY, CAP - EARLY)
     slot_gate = jnp.sum(jnp.where(hits, gate_rows[:, :, None], 0.0), axis=(0, 1))
 
     live_cotangent = jnp.where(is_valid[:, None], cotangent[0], jnp.zeros((), BF16))
@@ -665,7 +681,7 @@
         (packed_full, gains_full, out_full, gate_parts, grad_send)
     )
     gain_one, gain_two = gains_full[:, 0].astype(F32), gains_full[:, 1].astype(F32)
-    grad_rows = swap(grad_send.reshape(devices, CAP, width), ("dp", "seq")).reshape(slots, width)
+    grad_rows = swap(grad_send.reshape(devices, CAP, width), ("dp", "seq"))
 
     inputs = hidden_in[0].astype(F32)
     scale_one = lax.rsqrt(jnp.mean(inputs * inputs, axis=-1, keepdims=True) + EPSILON)
@@ -701,30 +717,57 @@
     scale_two = lax.rsqrt(jnp.mean(middle * middle, axis=-1, keepdims=True) + EPSILON)
     moe_input = (middle * scale_two * gain_two).astype(BF16)
 
-    send_rows = tn(token_hot, moe_input).astype(BF16).reshape(devices, CAP, width)
-    send_rows, grad_rows, up_parts = lax.optimization_barrier((send_rows, grad_rows, up_parts))
-    slot_rows = swap(send_rows, ("dp", "seq")).reshape(slots, width)
+    def to_experts(hot):
+        return tn(hot, moe_input).astype(BF16).reshape(devices, -1, width)
+
+    early_send, late_send = to_experts(early_hot), to_experts(late_hot)
+    query_flat = query_rotated.reshape(rows, q_width)
+    early_send, late_send, grad_rows, up_parts, query_flat, attended = lax.optimization_barrier(
+        (early_send, late_send, grad_rows, up_parts, query_flat, attended)
+    )
+    early_rows = swap(early_send, ("dp", "seq"))
+    early_rows, late_send = lax.optimization_barrier((early_rows, late_send))
+    late_rows = swap(late_send, ("dp", "seq"))
     gate_full = in_seq_order(gate_parts, BF16).reshape(width, hidden_units)
     up_full = in_seq_order(up_parts, BF16).reshape(width, hidden_units)
     down_full = in_seq_order(down_parts, BF16).reshape(hidden_units, width)
-    slot_rows, gate_full, up_full, down_full = lax.optimization_barrier(
-        (slot_rows, gate_full, up_full, down_full)
-    )
-    gate_pre = nn(slot_rows, gate_full)
-    up_pre = nn(slot_rows, up_full)
-    gate_sigmoid = jax.nn.sigmoid(gate_pre)
-    gate_act = gate_pre * gate_sigmoid
-    gate_slope = gate_sigmoid * (1.0 + gate_pre * (1.0 - gate_sigmoid))
-    expert_hidden = (gate_act * up_pre).astype(BF16)
-    hidden_grad = nt(grad_rows, down_full)
-    gate_pre_grad = (hidden_grad * up_pre * gate_slope).astype(BF16)
-    up_pre_grad = (hidden_grad * gate_act).astype(BF16)
-    row_grad = (nt(gate_pre_grad, gate_full) + nt(up_pre_grad, up_full)).astype(BF16)
-    row_back = swap(row_grad.reshape(devices, CAP, width), ("dp", "seq")).reshape(slots, width)
-
+    early_grads, late_grads = grad_rows[:, :EARLY], grad_rows[:, EARLY:]
+    early_rows, gate_full, up_full, down_full, early_grads, late_grads = (
+        lax.optimization_barrier(
+            (early_rows, gate_full, up_full, down_full, early_grads, late_grads)
+        )
+    )
+
+    def run_expert(slot_rows, grads):
+        blocks = slot_rows.shape[:2]
+        slot_rows, grads = slot_rows.reshape(-1, width), grads.reshape(-1, width)
+        gate_pre = nn(slot_rows, gate_full)
+        up_pre = nn(slot_rows, up_full)
+        gate_sigmoid = jax.nn.sigmoid(gate_pre)
+        gate_act = gate_pre * gate_sigmoid
+        gate_slope = gate_sigmoid * (1.0 + gate_pre * (1.0 - gate_sigmoid))
+        hidden = (gate_act * up_pre).astype(BF16)
+        hidden_grad = nt(grads, down_full)
+        gate_pre_grad = (hidden_grad * up_pre * gate_slope).astype(BF16)
+        up_pre_grad = (hidden_grad * gate_act).astype(BF16)
+        row_grad = (nt(gate_pre_grad, gate_full) + nt(up_pre_grad, up_full)).astype(BF16)
+        return [x.reshape(blocks + (-1,)) for x in (hidden, gate_pre_grad, up_pre_grad, row_grad)]
+
+    *early_terms, early_row_grad = run_expert(early_rows, early_grads)
+    late_rows, early_row_grad = lax.optimization_barrier((late_rows, early_row_grad))
+    early_back = swap(early_row_grad, ("dp", "seq"))
+    *late_terms, late_row_grad = run_expert(late_rows, late_grads)
+    slot_rows, expert_hidden, gate_pre_grad, up_pre_grad = (
+        jnp.concatenate(both, axis=1).reshape(slots, -1)
+        for both in zip([early_rows, *early_terms], [late_rows, *late_terms], strict=True)
+    )
     gate_grad = tn(slot_rows, gate_pre_grad).astype(BF16)
     up_grad = tn(slot_rows, up_pre_grad).astype(BF16)
-    down_grad = tn(expert_hidden, grad_rows).astype(BF16)
+    early_back, late_row_grad, gate_grad, up_grad = lax.optimization_barrier(
+        (early_back, late_row_grad, gate_grad, up_grad)
+    )
+    late_back = swap(late_row_grad, ("dp", "seq"))
+    down_grad = tn(expert_hidden, grad_rows.reshape(slots, width)).astype(BF16)
 
     def to_owners(grad):
         grad = grad.reshape(seq_count, -1, grad.shape[1])
@@ -738,13 +781,14 @@
         whole = in_seq_order(pieces, F32)
         return jnp.sum(whole.reshape((own_experts, sharers) + whole.shape[1:]), axis=1)
 
-    gate_grad_parts, up_grad_parts = to_owners(gate_grad), to_owners(up_grad)
-    row_back, down_grad = lax.optimization_barrier((row_back, down_grad))
-    down_grad_parts = to_owners(down_grad)
+    gate_owned, up_owned = owned_sum(to_owners(gate_grad)), owned_sum(to_owners(up_grad))
     expert_out = nn(expert_hidden, down_full).astype(BF16)
-    expert_out, row_back = lax.optimization_barrier((expert_out, row_back))
+    expert_out, late_back, gate_owned, up_owned, down_grad = lax.optimization_barrier(
+        (expert_out, late_back, gate_owned, up_owned, down_grad)
+    )
     returned = swap(expert_out.reshape(devices, CAP, width), ("dp", "seq")).reshape(slots, width)
-    moe_input_grad = nn(token_hot, row_back)
+    early_back, late_back = early_back.reshape(-1, width), late_back.reshape(-1, width)
+    moe_input_grad = nn(early_hot, early_back) + nn(late_hot, late_back)
     middle_norm_grad, gain_two_grad = norm_back(middle, scale_two, gain_two, moe_input_grad)
     middle_grad = out_grad + middle_norm_grad
     branch_grad = middle_grad.astype(BF16)
@@ -756,7 +800,7 @@
     cosines, sines = cosine_lookup[:, 0], sine_lookup[:, 0]
     projected_grad = attention_back(
         lengths,
-        query_rotated.reshape(rows, q_width),
+        query_flat,
         kv_all,
         attended_grad,
         log_total.reshape(q_heads, rows),
@@ -772,20 +816,24 @@
     lane = lax.broadcasted_iota(jnp.int32, (width, LANES), 1)
     gain_terms = jnp.where(lane == 0, gain_one_grad[:, None], gain_two_grad[:, None])
     gain_terms = jnp.where(lane < 2, gain_terms, 0.0).astype(BF16)
-    projected_grad, down_grad_parts = lax.optimization_barrier((projected_grad, down_grad_parts))
     query_terms = tn(normed, projected_grad).astype(BF16)
-    grad_parts = [gate_grad_parts, up_grad_parts, down_grad_parts]
     if staged:
-        out_owned, gains_owned, owned = staged_scatter(
-            [out_terms, gain_terms, query_terms], [], None, 6, "scatter_attention_grads"
+        out_owned, gains_owned, owned, down_owned = staged_scatter(
+            [out_terms, gain_terms, query_terms],
+            [down_grad.reshape(seq_count, -1, width)],
+            lambda ref, peer: ref.at[peer],
+            6,
+            "scatter_attention_grads",
         )
+        down_owned = down_owned.astype(F32)
     else:
         terms = jnp.concatenate([out_terms, gain_terms, query_terms], axis=1)
         terms = lax.psum_scatter(terms, BOTH, scatter_dimension=0, tiled=True).astype(F32)
         out_owned, gains_owned = terms[:, :width], terms[:, width : width + LANES]
         owned = terms[:, width + LANES :]
+        down_owned = owned_sum(to_owners(down_grad))
     returned, owned = lax.optimization_barrier((returned, owned))
-    expert_grads = [owned_sum(parts) for parts in grad_parts]
+    expert_grads = [gate_owned, up_owned, down_owned]
 
     gate_hot = jnp.sum(jnp.where(hits, gate_rows[:, :, None], 0.0), axis=1).astype(BF16)
     layer_out = middle + nn(gate_hot, returned)

time: 638 us -> 642 us (level)
  local copies, waits for them, and re-layouts: 60.4 us -> 78.4 us
  waiting for transfers between devices: 135 us -> 121 us
  Pallas kernels: 243 us -> 232 us
  matrix products: 98.1 us -> 108 us
    ppermute x18 -> x15, waiting for transfers between devices: 123 us -> 82 us  [seq_permutes(): lax.ppermute(block_for(lax.rem(me + step, count)), 'seq', ring)]
    all_to_all x4 -> x6, waiting for transfers between devices: 11.5 us -> 39.5 us  [swap(): return lax.all_to_all(blocks, axes, split_axis=0, concat_axis=0, tiled=True)]
    pallas_call x1, Pallas kernels: 54.7 us -> 30.7 us  [attention_back(): pl.pallas_call(functools.partial(attention_back_kernel, count, heads, kv_...]
    pallas_call x1, Pallas kernels: 72.4 us -> 90.2 us  [staged_scatter(): pl.pallas_call(functools.partial(scatter_kernel, line, chunks, n, len(ext...]
    dot_general x19 -> x26, matrix products: 90.1 us -> 100 us  [dot(): lax.dot_general(left, right, (contract, ((), ())), preferred_element_type...]
    all_to_all x4 -> x6, starting transfers between devices: 22.6 us -> 31.2 us  [swap(): return lax.all_to_all(blocks, axes, split_axis=0, concat_axis=0, tiled=True)]
    unnamed x122 -> x161, local copies, waits for them, and re-layouts: 9.93 us -> 18.4 us
    dynamic_update_slice x12 -> x8, other arithmetic: 16.6 us -> 8.72 us  [in_seq_order(): lax.dynamic_update_index_in_dim(whole, piece.astype(dtype), place, 0)]
  transfers between devices with their start and end apart: 22 -> 21, of which waited for: 12 -> 12; matrix products, arithmetic and copies ran while one was open for 23% -> 29% of each run, Pallas kernels for 39% -> 37%
where the time goes in v8:
time: 642 us; the launch traced here: 633 us
  Pallas kernels  232 us (36%)
  waiting for transfers between devices  121 us (19%)
  matrix products  108 us (17%)
  local copies, waits for them, and re-layouts  78.4 us (12%)
  starting transfers between devices  53 us (8%)
  other arithmetic  37.3 us (6%)
    dot_general x26, matrix products, dot(): lax.dot_general(left, right, (contract, ((), ())), preferred_element_type...  100 us
    pallas_call x1, Pallas kernels, staged_scatter(): pl.pallas_call(functools.partial(scatter_kernel, line, chunks, n, len(ext...  90.2 us
    ppermute x15, waiting for transfers between devices, seq_permutes(): lax.ppermute(block_for(lax.rem(me + step, count)), 'seq', ring)  82 us
    pallas_call x1, Pallas kernels, staged_gather(): pl.pallas_call(functools.partial(gather_kernel, line, chunks, n, len(extr...  65.3 us
    pallas_call x1, Pallas kernels, seq_spread(): pl.pallas_call(functools.partial(spread_kernel, count, parts), out_shape=...  45.7 us
    all_to_all x6, waiting for transfers between devices, swap(): return lax.all_to_all(blocks, axes, split_axis=0, concat_axis=0, tiled=True)  39.5 us
    all_to_all x6, starting transfers between devices, swap(): return lax.all_to_all(blocks, axes, split_axis=0, concat_axis=0, tiled=True)  31.2 us
    pallas_call x1, Pallas kernels, attention_back(): pl.pallas_call(functools.partial(attention_back_kernel, count, heads, kv_...  30.7 us
  transfers between devices with their start and end apart: 21, of which 12 were waited for; matrix products, arithmetic and copies ran while one was open for 29% of the time, Pallas kernels for 37%

profile of v8, /device:TPU:0, one launch (start us, length us, event | category | flops | bytes accessed | tf_op | source)
XLA Modules:
  0.0 633.2 jit_solution(12464265137268707281)
XLA Ops:
  21.0 65.3 %gather_attention_weights.1 = (bf16[2,2,4,2,48,2048]{5,4,3,2,1,0:T(8,128)(2,1)S(1)}, bf16[2,2,4,2,48,128]{5,4,3,2,1,0:T(8,128)(2,1)S(1)}, bf16[2,2,4,2,48,1536]{5,4,3,2,1,0:T(8,128)(2,1)S(1)}) custom-call(bf16[48,2048]{1,0:T(8,128)(2,1)S(1)} %pad_maximum_fusion.3.refs_0_, bf16[48,128]{1,0:T(8,128)(2,1)S(1)} %maximum_maximum_fusion.refs_1_, ...), custom_call_target="tpu_custom_call" | custom-call | bytes 11403264 | tf_op jit(solution)/shard_map/gather_attention_weights/pallas_call | solution.py:278
  102.6 5.8 all-to-all-start
  111.2 45.7 %gather_keys.1 = bf16[4,256,512]{2,1,0:T(8,128)(2,1)S(1)} custom-call(bf16[256,512]{1,0:T(8,128)(2,1)S(1)} %pad_maximum_fusion.2.source), custom_call_target="tpu_custom_call" | custom-call | bytes 1048576 | tf_op jit(solution)/shard_map/gather_keys/pallas_call | solution.py:435
  178.4 13.7 %while.14 = (s32[]{:T(128)}, bf16[2,256,6,128]{1,3,2,0:T(8,128)(2,1)S(1)}, f32[2,6,256]{2,1,0:T(8,128)}, bf16[2,1024,128]{1,2,0:T(8,128)(2,1)}, s32[]{:T(128)}, ...) while((s32[]{:T(128)}, ...), condition=%wide.region_7.8_spmd.clone.clone, body=%wide.region_4.7_spmd.clone.clone.sunk | while | flops 824704768 | bytes 23888060 | solution.py:709
  200.5 6.9 %collective-permute-done.4 = bf16[384,768]{1,0:T(8,128)(2,1)} collective-permute-done((bf16[384,768]{1,0:T(8,128)(2,1)}, bf16[384,768]{1,0:T(8,128)(2,1)}, u32[]{:S(2)}, u32[]{:S(2)}) %collective-permute-start.4) | collective-permute-done | bytes 589856 | tf_op jit(solution)/shard_map/ppermute | solution.py:583
  209.1 6.2 all-to-all-start.1
  227.4 22.1 %collective-permute-done.6 = bf16[192,1536]{1,0:T(8,128)(2,1)S(1)} collective-permute-done((bf16[192,1536]{1,0:T(8,128)(2,1)S(1)}, bf16[192,1536]{1,0:T(8,128)(2,1)S(1)}, u32[]{:S(2)}, u32[]{:S(2)}) %collective-permute-start.6) | collective-permute-done | bytes 589856 | tf_op jit(solution)/shard_map/ppermute | solution.py:583
  285.9 26.9 %all-to-all-done.2 = bf16[32,24,1536]{2,1,0:T(8,128)(2,1)S(1)} async-done(((bf16[32,24,1536]{2,1,0:T(8,128)(2,1)}), bf16[32,24,1536]{2,1,0:T(8,128)(2,1)S(1)}, u32[]{:S(2)}, u32[]{:S(2)}) %all-to-all-start.2) | async-done | bytes 2359328 | tf_op jit(solution)/shard_map/all_to_all | solution.py:101
  312.9 5.2 fusion.74
  327.6 6.5 %multiply_convert_fusion = (bf16[768,768]{1,0:T(8,128)(2,1)S(1)}, bf16[768,768]{1,0:T(8,128)(2,1)S(1)}, bf16[768,768]{1,0:T(8,128)(2,1)S(1)}) fusion(f32[768,768]{1,0:T(8,128)} %fusion.73, f32[768,768]{1,0:T(8,128)} %fusion.74, bf16[768,1536]{1,0:T(8,128)(2,1)} %bitcast.326, bf16[768,1536]{1,0:T(8,128)(2,1)} %bitcast.51), kind=kOutput, calls=%fused_computation.55 | convolution fusion | flops 1820786688 | bytes 12976128 | tf_op jit(solution)/shard_map/dot_general | solution.py:47
  335.8 6.9 %bitcast_convert_fusion.1 = bf16[1536,768]{1,0:T(8,128)(2,1)} fusion(bf16[32,40,1536]{2,1,0:T(8,128)(2,1)} %constant_dynamic-update-slice_fusion, bf16[32,24,768]{2,1,0:T(8,128)(2,1)S(1)} %bitcast.344, bf16[32,16,768]{2,1,0:T(8,128)(2,1)S(1)} %bitcast.346), kind=kOutput, calls=%fused_computation.36 | convolution fusion | flops 3025010688 | bytes 8257536 | tf_op jit(solution)/shard_map/dot_general | solution.py:47
  348.3 6.8 %bitcast_convert_fusion.2 = bf16[1536,768]{1,0:T(8,128)(2,1)} fusion(bf16[32,40,1536]{2,1,0:T(8,128)(2,1)} %constant_dynamic-update-slice_fusion, bf16[32,24,768]{2,1,0:T(8,128)(2,1)S(1)} %bitcast.343, bf16[32,16,768]{2,1,0:T(8,128)(2,1)S(1)} %bitcast.345), kind=kOutput, calls=%fused_computation.37 | convolution fusion | flops 3025010688 | bytes 8257536 | tf_op jit(solution)/shard_map/dot_general | solution.py:47
  355.1 9.9 %all-to-all-done.3 = bf16[32,16,1536]{2,1,0:T(8,128)(2,1)S(1)} async-done(((bf16[32,16,1536]{2,1,0:T(8,128)(2,1)}), bf16[32,16,1536]{2,1,0:T(8,128)(2,1)S(1)}, u32[]{:S(2)}, u32[]{:S(2)}) %all-to-all-start.3) | async-done | bytes 1572896 | tf_op jit(solution)/shard_map/all_to_all | solution.py:101
  366.2 4.7 all-to-all-start.4
  370.8 6.1 bitcast_convert_fusion
  379.0 6.4 %convolution_convert_fusion.2 = bf16[1280,1536]{1,0:T(8,128)(2,1)} fusion(bf16[1280,768]{1,0:T(8,128)(2,1)S(1)} %bitcast.329, bf16[768,1536]{1,0:T(8,128)(2,1)} %bitcast.51), kind=kOutput, calls=%fused_computation.30 | convolution fusion | flops 3021864960 | bytes 8257536 | tf_op jit(solution)/shard_map/dot_general | solution.py:47
  397.2 14.5 %collective-permute-done.12 = bf16[384,768]{1,0:T(8,128)(2,1)S(1)} collective-permute-done((bf16[384,768]{1,0:T(8,128)(2,1)S(1)}, bf16[384,768]{1,0:T(8,128)(2,1)S(1)}, u32[]{:S(2)}, u32[]{:S(2)}) %collective-permute-start.12) | collective-permute-done | bytes 589856 | tf_op jit(solution)/shard_map/ppermute | solution.py:583
  412.8 12.5 %collective-permute-done.13 = bf16[384,768]{1,0:T(8,128)(2,1)S(1)} collective-permute-done((bf16[384,768]{1,0:T(8,128)(2,1)S(1)}, bf16[384,768]{1,0:T(8,128)(2,1)S(1)}, u32[]{:S(2)}, u32[]{:S(2)}) %collective-permute-start.13) | collective-permute-done | bytes 589856 | tf_op jit(solution)/shard_map/ppermute | solution.py:583
  427.9 13.1 %collective-permute-done.9 = bf16[384,768]{1,0:T(8,128)(2,1)S(1)} collective-permute-done((bf16[384,768]{1,0:T(8,128)(2,1)S(1)}, bf16[384,768]{1,0:T(8,128)(2,1)S(1)}, u32[]{:S(2)}, u32[]{:S(2)}) %collective-permute-start.9) | collective-permute-done | bytes 589856 | tf_op jit(solution)/shard_map/ppermute | solution.py:583
  442.0 8.5 %collective-permute-done.10 = bf16[384,768]{1,0:T(8,128)(2,1)S(1)} collective-permute-done((bf16[384,768]{1,0:T(8,128)(2,1)S(1)}, bf16[384,768]{1,0:T(8,128)(2,1)S(1)}, u32[]{:S(2)}, u32[]{:S(2)}) %collective-permute-start.10) | collective-permute-done | bytes 589856 | tf_op jit(solution)/shard_map/ppermute | solution.py:583
  452.7 5.5 all-to-all-start.5
  489.1 30.7 %attention_backward.1 = bf16[256,2048]{1,0:T(8,128)(2,1)S(1)} custom-call(s32[1]{0:T(128)} %copy.118.refs_0_, bf16[256,1536]{1,0:T(8,128)(2,1)S(1)} %copy-done.2, bf16[1024,512]{1,0:T(8,128)(2,1)S(1)} %bitcast.292, bf16[256,1536]{1,0:T(8,128)(2,1)S(1)} %copy-done.4, f32[12,256]{1,0:T(8,128)S(1)} %copy-done.9, f32[12,256]{1,0:T(8,128)S(1)} %bitcast.295, ...), custom_call_target="tpu_custom_call" | custom-call | flops 4026531840 | bytes 1048576 | tf_op jit(solution)/shard_map/attention_backward/pallas_call | solution.py:555
  520.0 6.4 %fusion.45 = (f32[256]{0:T(256)S(1)}, bf16[1536]{0:T(1024)(128)(2,1)S(1)}, f32[256,1536]{1,0:T(8,128)}) fusion(bf16[1,256,1536]{2,1,0:T(8,128)(2,1)S(1)} %copy-done.17, f32[1536]{0:T(1024)S(1)} %copy-done.54, f32[256]{0:T(256)S(1)} %copy-done.59, bf16[256,2048]{1,0:T(8,128)(2,1)S(1)} %attention_backward.1, bf16[1536,2048]{1,0:T(8,128)(2,1)} %bitcast.297), kind=kOutput, calls=%fused_computation.80 | convolution fusion | flops 1613363456 | bytes 9710592 | tf_op jit(solution)/shard_map/dot_general | solution.py:47
  530.8 90.2 %scatter_attention_grads.1 = (f32[48,1536]{1,0:T(8,128)S(1)}, f32[48,128]{1,0:T(8,128)S(1)}, f32[48,2048]{1,0:T(8,128)S(1)}, bf16[4,192,1536]{2,1,0:T(8,128)(2,1)S(1)}) custom-call(bf16[2,2,4,2,48,1536]{5,4,3,2,1,0:T(8,128)(2,1)S(1)} %bitcast.286, bf16[2,2,4,2,48,128]{5,4,3,2,1,0:T(8,128)(2,1)S(1)} %select_convert_fusion.refs_1_, ...), custom_call_target="tpu_custom_call" | custom-call | bytes 11403264 | tf_op jit(solution)/shard_map/scatter_attention_grads/pallas_call | solution.py:399
  (339 shorter events, 217.5 us)
Async XLA Ops:
  3.8 91.5 %collective-permute-start = (bf16[384,768]{1,0:T(8,128)(2,1)}, bf16[384,768]{1,0:T(8,128)(2,1)}, u32[]{:S(2)}, u32[]{:S(2)}) collective-permute-start(bf16[384,768]{1,0:T(8,128)(2,1)} %get-tuple-element.255), channel_id=1, source_target_pairs={{0,8},{8,16},{16,24},{24,0},{1,9},{9,17},{17,25},{25,1},{2,10},{10... | collective-permute-start | bytes 1769480 | tf_op jit(solution)/shard_map/ppermute | solution.py:583
  6.8 88.5 %collective-permute-start.1 = (bf16[384,768]{1,0:T(8,128)(2,1)}, bf16[384,768]{1,0:T(8,128)(2,1)}, u32[]{:S(2)}, u32[]{:S(2)}) collective-permute-start(bf16[384,768]{1,0:T(8,128)(2,1)} %get-tuple-element.257), channel_id=1, source_target_pairs={{0,16},{8,24},{16,0},{24,8},{1,17},{9,25},{17,1},{25,9},{2,18},{10... | collective-permute-start | bytes 1769480 | tf_op jit(solution)/shard_map/ppermute | solution.py:583
  8.3 87.0 %collective-permute-start.2 = (bf16[384,768]{1,0:T(8,128)(2,1)}, bf16[384,768]{1,0:T(8,128)(2,1)}, u32[]{:S(2)}, u32[]{:S(2)}) collective-permute-start(bf16[384,768]{1,0:T(8,128)(2,1)} %get-tuple-element.254), channel_id=1, source_target_pairs={{0,24},{8,0},{16,8},{24,16},{1,25},{9,1},{17,9},{25,17},{2,26},{10... | collective-permute-start | bytes 1769480 | tf_op jit(solution)/shard_map/ppermute | solution.py:583
  19.1 82.6 %copy-start.39 = (f32[256,64]{1,0:T(8,128)}, f32[256,64]{1,0:T(8,128)S(1)}, u32[]{:S(2)}) copy-start(f32[256,64]{1,0:T(8,128)S(1)} %get-tuple-element.270) | copy-start | bytes 196612
  19.2 82.6 %copy-start.40 = (f32[256,64]{1,0:T(8,128)}, f32[256,64]{1,0:T(8,128)S(1)}, u32[]{:S(2)}) copy-start(f32[256,64]{1,0:T(8,128)S(1)} %get-tuple-element.271) | copy-start | bytes 196612
  19.6 176.7 %copy-start.46 = (pred[256,512]{1,0:T(8,128)(4,1)}, pred[256,512]{1,0:T(8,128)(4,1)S(1)}, u32[]{:S(2)}) copy-start(pred[256,512]{1,0:T(8,128)(4,1)S(1)} %fusion.27) | copy-start | bytes 393220
  102.6 106.5 %all-to-all-start = ((bf16[32,40,1536]{2,1,0:T(8,128)(2,1)}), bf16[32,40,1536]{2,1,0:T(8,128)(2,1)}, u32[]{:S(2)}, u32[]{:S(2)}) async-start(bf16[32,40,1536]{2,1,0:T(8,128)(2,1)} %bitcast.311), calls=%async_computation | async-start | bytes 7864320 | tf_op jit(solution)/shard_map/all_to_all | solution.py:101
  172.1 28.4 %collective-permute-start.3 = (bf16[384,768]{1,0:T(8,128)(2,1)}, bf16[384,768]{1,0:T(8,128)(2,1)}, u32[]{:S(2)}, u32[]{:S(2)}) collective-permute-start(bf16[384,768]{1,0:T(8,128)(2,1)} %get-tuple-element.252), channel_id=1, source_target_pairs={{0,8},{8,16},{16,24},{24,0},{1,9},{9,17},{17,25},{25,1},{2,10},{10... | collective-permute-start | bytes 1769480 | tf_op jit(solution)/shard_map/ppermute | solution.py:583
  175.4 32.0 %collective-permute-start.4 = (bf16[384,768]{1,0:T(8,128)(2,1)}, bf16[384,768]{1,0:T(8,128)(2,1)}, u32[]{:S(2)}, u32[]{:S(2)}) collective-permute-start(bf16[384,768]{1,0:T(8,128)(2,1)} %get-tuple-element.251), channel_id=1, source_target_pairs={{0,16},{8,24},{16,0},{24,8},{1,17},{9,25},{17,1},{25,9},{2,18},{10... | collective-permute-start | bytes 1769480 | tf_op jit(solution)/shard_map/ppermute | solution.py:583
  177.1 32.1 %collective-permute-start.5 = (bf16[384,768]{1,0:T(8,128)(2,1)}, bf16[384,768]{1,0:T(8,128)(2,1)}, u32[]{:S(2)}, u32[]{:S(2)}) collective-permute-start(bf16[384,768]{1,0:T(8,128)(2,1)} %get-tuple-element.250), channel_id=1, source_target_pairs={{0,24},{8,0},{16,8},{24,16},{1,25},{9,1},{17,9},{25,17},{2,26},{10... | collective-permute-start | bytes 1769480 | tf_op jit(solution)/shard_map/ppermute | solution.py:583
  209.1 43.8 %all-to-all-start.1 = ((bf16[32,16,1536]{2,1,0:T(8,128)(2,1)}), bf16[32,16,1536]{2,1,0:T(8,128)(2,1)S(1)}, u32[]{:S(2)}, u32[]{:S(2)}) async-start(bf16[32,16,1536]{2,1,0:T(8,128)(2,1)} %bitcast.307), calls=%async_computation.1 | async-start | bytes 3145728 | tf_op jit(solution)/shard_map/all_to_all | solution.py:101
  219.1 30.4 %collective-permute-start.6 = (bf16[192,1536]{1,0:T(8,128)(2,1)S(1)}, bf16[192,1536]{1,0:T(8,128)(2,1)S(1)}, u32[]{:S(2)}, u32[]{:S(2)}) collective-permute-start(bf16[192,1536]{1,0:T(8,128)(2,1)S(1)} %get-tuple-element.248), channel_id=1, source_target_pairs={{0,8},{8,16},{16,24},{24,0},{1,9},{9,17},{17,25},{25,1},{2,10},{10... | collective-permute-start | bytes 1769480 | tf_op jit(solution)/shard_map/ppermute | solution.py:583
  220.8 40.0 %collective-permute-start.7 = (bf16[192,1536]{1,0:T(8,128)(2,1)}, bf16[192,1536]{1,0:T(8,128)(2,1)}, u32[]{:S(2)}, u32[]{:S(2)}) collective-permute-start(bf16[192,1536]{1,0:T(8,128)(2,1)} %get-tuple-element.247), channel_id=1, source_target_pairs={{0,16},{8,24},{16,0},{24,8},{1,17},{9,25},{17,1},{25,9},{2,18},{10... | collective-permute-start | bytes 1769480 | tf_op jit(solution)/shard_map/ppermute | solution.py:583
  222.3 40.5 %collective-permute-start.8 = (bf16[192,1536]{1,0:T(8,128)(2,1)}, bf16[192,1536]{1,0:T(8,128)(2,1)}, u32[]{:S(2)}, u32[]{:S(2)}) collective-permute-start(bf16[192,1536]{1,0:T(8,128)(2,1)} %get-tuple-element.246), channel_id=1, source_target_pairs={{0,24},{8,0},{16,8},{24,16},{1,25},{9,1},{17,9},{25,17},{2,26},{10... | collective-permute-start | bytes 1769480 | tf_op jit(solution)/shard_map/ppermute | solution.py:583
  254.1 58.8 %all-to-all-start.2 = ((bf16[32,24,1536]{2,1,0:T(8,128)(2,1)}), bf16[32,24,1536]{2,1,0:T(8,128)(2,1)S(1)}, u32[]{:S(2)}, u32[]{:S(2)}) async-start(bf16[32,24,1536]{2,1,0:T(8,128)(2,1)} %bitcast.27), calls=%async_computation.2 | async-start | bytes 4718592 | tf_op jit(solution)/shard_map/all_to_all | solution.py:101
  323.0 42.0 %all-to-all-start.3 = ((bf16[32,16,1536]{2,1,0:T(8,128)(2,1)}), bf16[32,16,1536]{2,1,0:T(8,128)(2,1)S(1)}, u32[]{:S(2)}, u32[]{:S(2)}) async-start(bf16[32,16,1536]{2,1,0:T(8,128)(2,1)} %bitcast.330), calls=%async_computation.3 | async-start | bytes 3145728 | tf_op jit(solution)/shard_map/all_to_all | solution.py:101
  366.2 86.6 %all-to-all-start.4 = ((bf16[32,24,1536]{2,1,0:T(8,128)(2,1)}), bf16[32,24,1536]{2,1,0:T(8,128)(2,1)}, u32[]{:S(2)}, u32[]{:S(2)}) async-start(bf16[32,24,1536]{2,1,0:T(8,128)(2,1)} %bitcast.323), calls=%async_computation.4 | async-start | bytes 4718592 | tf_op jit(solution)/shard_map/all_to_all | solution.py:101
  377.1 34.6 %collective-permute-start.12 = (bf16[384,768]{1,0:T(8,128)(2,1)S(1)}, bf16[384,768]{1,0:T(8,128)(2,1)S(1)}, u32[]{:S(2)}, u32[]{:S(2)}) collective-permute-start(bf16[384,768]{1,0:T(8,128)(2,1)S(1)} %get-tuple-element.242), channel_id=1, source_target_pairs={{0,8},{8,16},{16,24},{24,0},{1,9},{9,17},{17,25},{25,1},{2,10},{10... | collective-permute-start | bytes 1769480 | tf_op jit(solution)/shard_map/ppermute | solution.py:583
  385.5 39.8 %collective-permute-start.13 = (bf16[384,768]{1,0:T(8,128)(2,1)S(1)}, bf16[384,768]{1,0:T(8,128)(2,1)S(1)}, u32[]{:S(2)}, u32[]{:S(2)}) collective-permute-start(bf16[384,768]{1,0:T(8,128)(2,1)S(1)} %get-tuple-element.241), channel_id=1, source_target_pairs={{0,16},{8,24},{16,0},{24,8},{1,17},{9,25},{17,1},{25,9},{2,18},{10... | collective-permute-start | bytes 1769480 | tf_op jit(solution)/shard_map/ppermute | solution.py:583
  390.6 36.2 %collective-permute-start.14 = (bf16[384,768]{1,0:T(8,128)(2,1)S(1)}, bf16[384,768]{1,0:T(8,128)(2,1)S(1)}, u32[]{:S(2)}, u32[]{:S(2)}) collective-permute-start(bf16[384,768]{1,0:T(8,128)(2,1)S(1)} %get-tuple-element.240), channel_id=1, source_target_pairs={{0,24},{8,0},{16,8},{24,16},{1,25},{9,1},{17,9},{25,17},{2,26},{10... | collective-permute-start | bytes 1769480 | tf_op jit(solution)/shard_map/ppermute | solution.py:583
  395.9 45.1 %collective-permute-start.9 = (bf16[384,768]{1,0:T(8,128)(2,1)S(1)}, bf16[384,768]{1,0:T(8,128)(2,1)S(1)}, u32[]{:S(2)}, u32[]{:S(2)}) collective-permute-start(bf16[384,768]{1,0:T(8,128)(2,1)S(1)} %get-tuple-element.245), channel_id=1, source_target_pairs={{0,8},{8,16},{16,24},{24,0},{1,9},{9,17},{17,25},{25,1},{2,10},{10... | collective-permute-start | bytes 1769480 | tf_op jit(solution)/shard_map/ppermute | solution.py:583
  396.4 54.1 %collective-permute-start.10 = (bf16[384,768]{1,0:T(8,128)(2,1)S(1)}, bf16[384,768]{1,0:T(8,128)(2,1)S(1)}, u32[]{:S(2)}, u32[]{:S(2)}) collective-permute-start(bf16[384,768]{1,0:T(8,128)(2,1)S(1)} %get-tuple-element.244), channel_id=1, source_target_pairs={{0,16},{8,24},{16,0},{24,8},{1,17},{9,25},{17,1},{25,9},{2,18},{10... | collective-permute-start | bytes 1769480 | tf_op jit(solution)/shard_map/ppermute | solution.py:583
  411.7 40.0 %collective-permute-start.11 = (bf16[384,768]{1,0:T(8,128)(2,1)S(1)}, bf16[384,768]{1,0:T(8,128)(2,1)S(1)}, u32[]{:S(2)}, u32[]{:S(2)}) collective-permute-start(bf16[384,768]{1,0:T(8,128)(2,1)S(1)} %get-tuple-element.243), channel_id=1, source_target_pairs={{0,24},{8,0},{16,8},{24,16},{1,25},{9,1},{17,9},{25,17},{2,26},{10... | collective-permute-start | bytes 1769480 | tf_op jit(solution)/shard_map/ppermute | solution.py:583
  452.7 173.7 %all-to-all-start.5 = ((bf16[32,40,1536]{2,1,0:T(8,128)(2,1)}), bf16[32,40,1536]{2,1,0:T(8,128)(2,1)}, u32[]{:S(2)}, u32[]{:S(2)}) async-start(bf16[32,40,1536]{2,1,0:T(8,128)(2,1)} %bitcast.310), calls=%async_computation.5 | async-start | bytes 7864320 | tf_op jit(solution)/shard_map/all_to_all | solution.py:101
  (81 other events, 639.5 us)

commit v9 on v8

--- a/solution.py
+++ b/solution.py
@@ -699,8 +699,6 @@
     key_rotated = key_rotated.reshape(rows, kv_width)
     kv_mine = jnp.concatenate([key_rotated, value_matrix_rows], axis=1)
     kv_all = seq_spread(kv_mine, 8, 1, "gather_keys").reshape(extent, 2 * kv_width)
-    kv_all, w_up, w_down = lax.optimization_barrier((kv_all, w_up, w_down))
-    up_parts, down_parts = expert_pieces(w_up), expert_pieces(w_down)
     key_all, value_all = kv_all[:, :kv_width], kv_all[:, kv_width:]
     query_head_groups = query_rotated.reshape(rows, kv_heads, group_size, HEAD_DIM).transpose(
         1, 0, 2, 3
@@ -722,9 +720,12 @@
 
     early_send, late_send = to_experts(early_hot), to_experts(late_hot)
     query_flat = query_rotated.reshape(rows, q_width)
-    early_send, late_send, grad_rows, up_parts, query_flat, attended = lax.optimization_barrier(
-        (early_send, late_send, grad_rows, up_parts, query_flat, attended)
-    )
+    early_send, late_send, grad_rows, query_flat, attended, w_up, w_down = (
+        lax.optimization_barrier(
+            (early_send, late_send, grad_rows, query_flat, attended, w_up, w_down)
+        )
+    )
+    up_parts, down_parts = expert_pieces(w_up), expert_pieces(w_down)
     early_rows = swap(early_send, ("dp", "seq"))
     early_rows, late_send = lax.optimization_barrier((early_rows, late_send))
     late_rows = swap(late_send, ("dp", "seq"))
@@ -750,24 +751,17 @@
         hidden_grad = nt(grads, down_full)
         gate_pre_grad = (hidden_grad * up_pre * gate_slope).astype(BF16)
         up_pre_grad = (hidden_grad * gate_act).astype(BF16)
+        return [x.reshape(blocks + (-1,)) for x in (hidden, gate_pre_grad, up_pre_grad)]
+
+    def row_grads(gate_pre_grad, up_pre_grad):
+        blocks = gate_pre_grad.shape[:2]
+        gate_pre_grad = gate_pre_grad.reshape(-1, hidden_units)
+        up_pre_grad = up_pre_grad.reshape(-1, hidden_units)
         row_grad = (nt(gate_pre_grad, gate_full) + nt(up_pre_grad, up_full)).astype(BF16)
-        return [x.reshape(blocks + (-1,)) for x in (hidden, gate_pre_grad, up_pre_grad, row_grad)]
-
-    *early_terms, early_row_grad = run_expert(early_rows, early_grads)
-    late_rows, early_row_grad = lax.optimization_barrier((late_rows, early_row_grad))
-    early_back = swap(early_row_grad, ("dp", "seq"))
-    *late_terms, late_row_grad = run_expert(late_rows, late_grads)
-    slot_rows, expert_hidden, gate_pre_grad, up_pre_grad = (
-        jnp.concatenate(both, axis=1).reshape(slots, -1)
-        for both in zip([early_rows, *early_terms], [late_rows, *late_terms], strict=True)
-    )
-    gate_grad = tn(slot_rows, gate_pre_grad).astype(BF16)
-    up_grad = tn(slot_rows, up_pre_grad).astype(BF16)
-    early_back, late_row_grad, gate_grad, up_grad = lax.optimization_barrier(
-        (early_back, late_row_grad, gate_grad, up_grad)
-    )
-    late_back = swap(late_row_grad, ("dp", "seq"))
-    down_grad = tn(expert_hidden, grad_rows.reshape(slots, width)).astype(BF16)
+        return row_grad.reshape(blocks + (width,))
+
+    def both_parts(early, late):
+        return jnp.concatenate([early, late], axis=1).reshape(slots, -1)
 
     def to_owners(grad):
         grad = grad.reshape(seq_count, -1, grad.shape[1])
@@ -781,10 +775,31 @@
         whole = in_seq_order(pieces, F32)
         return jnp.sum(whole.reshape((own_experts, sharers) + whole.shape[1:]), axis=1)
 
+    early_hidden, *early_pre_grads = run_expert(early_rows, early_grads)
+    early_row_grad = row_grads(*early_pre_grads)
+    late_rows, early_row_grad = lax.optimization_barrier((late_rows, early_row_grad))
+    early_back = swap(early_row_grad, ("dp", "seq"))
+    late_hidden, *late_pre_grads = run_expert(late_rows, late_grads)
+    expert_hidden = both_parts(early_hidden, late_hidden)
+    down_grad = tn(expert_hidden, grad_rows.reshape(slots, width)).astype(BF16)
+    late_rows, late_pre_grads, down_grad = lax.optimization_barrier(
+        (late_rows, late_pre_grads, down_grad)
+    )
+    down_grad_parts = to_owners(down_grad)
+    late_row_grad = row_grads(*late_pre_grads)
+    early_back, late_row_grad, down_grad_parts = lax.optimization_barrier(
+        (early_back, late_row_grad, down_grad_parts)
+    )
+    late_back = swap(late_row_grad, ("dp", "seq"))
+    slot_rows = both_parts(early_rows, late_rows)
+    gate_pre_grad, up_pre_grad = map(both_parts, early_pre_grads, late_pre_grads)
+    gate_grad = tn(slot_rows, gate_pre_grad).astype(BF16)
+    up_grad = tn(slot_rows, up_pre_grad).astype(BF16)
     gate_owned, up_owned = owned_sum(to_owners(gate_grad)), owned_sum(to_owners(up_grad))
+    down_owned = owned_sum(down_grad_parts)
     expert_out = nn(expert_hidden, down_full).astype(BF16)
-    expert_out, late_back, gate_owned, up_owned, down_grad = lax.optimization_barrier(
-        (expert_out, late_back, gate_owned, up_owned, down_grad)
+    expert_out, late_back, gate_owned, up_owned, down_owned = lax.optimization_barrier(
+        (expert_out, late_back, gate_owned, up_owned, down_owned)
     )
     returned = swap(expert_out.reshape(devices, CAP, width), ("dp", "seq")).reshape(slots, width)
     early_back, late_back = early_back.reshape(-1, width), late_back.reshape(-1, width)
@@ -818,20 +833,14 @@
     gain_terms = jnp.where(lane < 2, gain_terms, 0.0).astype(BF16)
     query_terms = tn(normed, projected_grad).astype(BF16)
     if staged:
-        out_owned, gains_owned, owned, down_owned = staged_scatter(
-            [out_terms, gain_terms, query_terms],
-            [down_grad.reshape(seq_count, -1, width)],
-            lambda ref, peer: ref.at[peer],
-            6,
-            "scatter_attention_grads",
+        out_owned, gains_owned, owned = staged_scatter(
+            [out_terms, gain_terms, query_terms], [], None, 6, "scatter_attention_grads"
         )
-        down_owned = down_owned.astype(F32)
     else:
         terms = jnp.concatenate([out_terms, gain_terms, query_terms], axis=1)
         terms = lax.psum_scatter(terms, BOTH, scatter_dimension=0, tiled=True).astype(F32)
         out_owned, gains_owned = terms[:, :width], terms[:, width : width + LANES]
         owned = terms[:, width + LANES :]
-        down_owned = owned_sum(to_owners(down_grad))
     returned, owned = lax.optimization_barrier((returned, owned))
     expert_grads = [gate_owned, up_owned, down_owned]
 

time: 642 us -> 636 us (level)
  Pallas kernels: 232 us -> 215 us
  local copies, waits for them, and re-layouts: 78.4 us -> 68.2 us
  starting transfers between devices: 53 us -> 61.7 us
  waiting for transfers between devices: 121 us -> 129 us
    ppermute x15 -> x18, waiting for transfers between devices: 82 us -> 104 us  [seq_permutes(): lax.ppermute(block_for(lax.rem(me + step, count)), 'seq', ring)]
    pallas_call x1, Pallas kernels: 90.2 us -> 68.1 us  [staged_scatter(): pl.pallas_call(functools.partial(scatter_kernel, line, chunks, n, len(ext...]
    all_to_all x6, waiting for transfers between devices: 39.5 us -> 24.2 us  [swap(): return lax.all_to_all(blocks, axes, split_axis=0, concat_axis=0, tiled=True)]
    dynamic_update_slice x8 -> x12, other arithmetic: 8.72 us -> 15.6 us  [in_seq_order(): lax.dynamic_update_index_in_dim(whole, piece.astype(dtype), place, 0)]
    unnamed x161 -> x143, local copies, waits for them, and re-layouts: 18.4 us -> 13.1 us
    ppermute x15 -> x18, starting transfers between devices: 21.8 us -> 26.6 us  [seq_permutes(): lax.ppermute(block_for(lax.rem(me + step, count)), 'seq', ring)]
    dynamic_update_slice x11 -> x10, local copies, waits for them, and re-layouts: 11.6 us -> 15.5 us  [in_seq_order(): lax.dynamic_update_index_in_dim(whole, piece.astype(dtype), place, 0)]
  transfers between devices with their start and end apart: 21 -> 24, of which waited for: 12 -> 13; matrix products, arithmetic and copies ran while one was open for 29% -> 29% of each run, Pallas kernels for 37% -> 34%
where the time goes in v9:
time: 636 us; the launch traced here: 627 us
  Pallas kernels  215 us (34%)
  waiting for transfers between devices  129 us (20%)
  matrix products  111 us (17%)
  local copies, waits for them, and re-layouts  68.2 us (11%)
  starting transfers between devices  61.7 us (10%)
  other arithmetic  39 us (6%)
    dot_general x26, matrix products, dot(): lax.dot_general(left, right, (contract, ((), ())), preferred_element_type...  105 us
    ppermute x18, waiting for transfers between devices, seq_permutes(): lax.ppermute(block_for(lax.rem(me + step, count)), 'seq', ring)  104 us
    pallas_call x1, Pallas kernels, staged_scatter(): pl.pallas_call(functools.partial(scatter_kernel, line, chunks, n, len(ext...  68.1 us
    pallas_call x1, Pallas kernels, staged_gather(): pl.pallas_call(functools.partial(gather_kernel, line, chunks, n, len(extr...  65.8 us
    pallas_call x1, Pallas kernels, seq_spread(): pl.pallas_call(functools.partial(spread_kernel, count, parts), out_shape=...  47.9 us
    all_to_all x6, starting transfers between devices, swap(): return lax.all_to_all(blocks, axes, split_axis=0, concat_axis=0, tiled=True)  35.1 us
    pallas_call x1, Pallas kernels, attention_back(): pl.pallas_call(functools.partial(attention_back_kernel, count, heads, kv_...  33.7 us
    ppermute x18, starting transfers between devices, seq_permutes(): lax.ppermute(block_for(lax.rem(me + step, count)), 'seq', ring)  26.6 us
  transfers between devices with their start and end apart: 24, of which 13 were waited for; matrix products, arithmetic and copies ran while one was open for 29% of the time, Pallas kernels for 34%

profile of v9, /device:TPU:0, one launch (start us, length us, event | category | flops | bytes accessed | tf_op | source)
XLA Modules:
  0.0 626.8 jit_solution(1185537252784020952)
XLA Ops:
  20.5 65.8 %gather_attention_weights.1 = (bf16[2,2,4,2,48,2048]{5,4,3,2,1,0:T(8,128)(2,1)S(1)}, bf16[2,2,4,2,48,128]{5,4,3,2,1,0:T(8,128)(2,1)S(1)}, bf16[2,2,4,2,48,1536]{5,4,3,2,1,0:T(8,128)(2,1)S(1)}) custom-call(bf16[48,2048]{1,0:T(8,128)(2,1)S(1)} %pad_maximum_fusion.3.refs_0_, bf16[48,128]{1,0:T(8,128)(2,1)S(1)} %maximum_maximum_fusion.refs_1_, ...), custom_call_target="tpu_custom_call" | custom-call | bytes 11403264 | tf_op jit(solution)/shard_map/gather_attention_weights/pallas_call | solution.py:278
  101.3 5.8 all-to-all-start
  107.5 47.9 %gather_keys.1 = bf16[4,256,512]{2,1,0:T(8,128)(2,1)S(1)} custom-call(bf16[256,512]{1,0:T(8,128)(2,1)S(1)} %pad_maximum_fusion.2.source), custom_call_target="tpu_custom_call" | custom-call | bytes 1048576 | tf_op jit(solution)/shard_map/gather_keys/pallas_call | solution.py:435
  165.0 10.7 %while.14 = (s32[]{:T(128)}, bf16[2,256,6,128]{1,3,2,0:T(8,128)(2,1)S(1)}, f32[2,6,256]{2,1,0:T(8,128)S(1)}, bf16[2,1024,128]{1,2,0:T(8,128)(2,1)}, s32[]{:T(128...) while((s32[]{:T(128)}, ...), condition=%wide.region_7.8_spmd.clone.clone, body=%wide.region_4.7_spmd.clone.clone.sunk | while | flops 824704768 | bytes 23789708 | solution.py:707
  183.7 12.0 %all-to-all-done = bf16[32,40,1536]{2,1,0:T(8,128)(2,1)} async-done(((bf16[32,40,1536]{2,1,0:T(8,128)(2,1)}), bf16[32,40,1536]{2,1,0:T(8,128)(2,1)}, u32[]{:S(2)}, u32[]{:S(2)}) %all-to-all-start) | async-done | bytes 3932192 | tf_op jit(solution)/shard_map/all_to_all | solution.py:101
  195.7 5.7 all-to-all-start.1
  226.8 12.2 %all-to-all-done.1 = bf16[32,16,1536]{2,1,0:T(8,128)(2,1)} async-done(((bf16[32,16,1536]{2,1,0:T(8,128)(2,1)}), bf16[32,16,1536]{2,1,0:T(8,128)(2,1)}, u32[]{:S(2)}, u32[]{:S(2)}) %all-to-all-start.1) | async-done | bytes 1572896 | tf_op jit(solution)/shard_map/all_to_all | solution.py:101
  254.6 19.1 %collective-permute-done.4 = bf16[384,768]{1,0:T(8,128)(2,1)} collective-permute-done((bf16[384,768]{1,0:T(8,128)(2,1)}, bf16[384,768]{1,0:T(8,128)(2,1)}, u32[]{:S(2)}, u32[]{:S(2)}) %collective-permute-start.4) | collective-permute-done | bytes 589856 | tf_op jit(solution)/shard_map/ppermute | solution.py:583
  277.6 17.8 %collective-permute-done.7 = bf16[192,1536]{1,0:T(8,128)(2,1)} collective-permute-done((bf16[192,1536]{1,0:T(8,128)(2,1)}, bf16[192,1536]{1,0:T(8,128)(2,1)}, u32[]{:S(2)}, u32[]{:S(2)}) %collective-permute-start.7) | collective-permute-done | bytes 589856 | tf_op jit(solution)/shard_map/ppermute | solution.py:583
  319.6 5.8 fusion.73
  325.4 5.8 fusion.74
  331.1 9.3 %all-to-all-start.3 = ((bf16[32,16,1536]{2,1,0:T(8,128)(2,1)}), bf16[32,16,1536]{2,1,0:T(8,128)(2,1)}, u32[]{:S(2)}, u32[]{:S(2)}) async-start(bf16[32,16,1536]{2,1,0:T(8,128)(2,1)} %bitcast.339), calls=%async_computation.3 | async-start | bytes 3145728 | tf_op jit(solution)/shard_map/all_to_all | solution.py:101
  340.4 6.4 %multiply_convert_fusion = (bf16[768,768]{1,0:T(8,128)(2,1)S(1)}, bf16[768,768]{1,0:T(8,128)(2,1)S(1)}, bf16[768,768]{1,0:T(8,128)(2,1)S(1)}) fusion(f32[768,768]{1,0:T(8,128)} %fusion.73, f32[768,768]{1,0:T(8,128)} %fusion.74, bf16[768,1536]{1,0:T(8,128)(2,1)} %bitcast.332, bf16[768,1536]{1,0:T(8,128)(2,1)} %bitcast.329), kind=kOutput, calls=%fused_computation.55 | convolution fusion | flops 1820786688 | bytes 12976128 | tf_op jit(solution)/shard_map/dot_general | solution.py:47
  346.9 6.0 bitcast_convert_fusion.2
  378.4 5.2 add_convert_fusion
  390.4 5.0 all-to-all-start.4
  395.4 6.0 bitcast_convert_fusion
  409.7 19.8 %collective-permute-done.13 = bf16[384,768]{1,0:T(8,128)(2,1)} collective-permute-done((bf16[384,768]{1,0:T(8,128)(2,1)}, bf16[384,768]{1,0:T(8,128)(2,1)}, u32[]{:S(2)}, u32[]{:S(2)}) %collective-permute-start.13) | collective-permute-done | bytes 589856 | tf_op jit(solution)/shard_map/ppermute | solution.py:583
  433.8 21.6 %collective-permute-done.15 = bf16[384,768]{1,0:T(8,128)(2,1)S(1)} collective-permute-done((bf16[384,768]{1,0:T(8,128)(2,1)S(1)}, bf16[384,768]{1,0:T(8,128)(2,1)S(1)}, u32[]{:S(2)}, u32[]{:S(2)}) %collective-permute-start.15) | collective-permute-done | bytes 589856 | tf_op jit(solution)/shard_map/ppermute | solution.py:583
  455.5 9.2 %collective-permute-done.16 = bf16[384,768]{1,0:T(8,128)(2,1)S(1)} collective-permute-done((bf16[384,768]{1,0:T(8,128)(2,1)S(1)}, bf16[384,768]{1,0:T(8,128)(2,1)S(1)}, u32[]{:S(2)}, u32[]{:S(2)}) %collective-permute-start.16) | collective-permute-done | bytes 589856 | tf_op jit(solution)/shard_map/ppermute | solution.py:583
  478.9 5.0 all-to-all-start.5
  506.6 33.7 %attention_backward.1 = bf16[256,2048]{1,0:T(8,128)(2,1)S(1)} custom-call(s32[1]{0:T(128)} %copy.122.refs_0_, bf16[256,1536]{1,0:T(8,128)(2,1)S(1)} %copy.75.refs_1_, bf16[1024,512]{1,0:T(8,128)(2,1)S(1)} %bitcast.310, bf16[256,1536]{1,0:T(8,128)(2,1)S(1)} %copy-done.4, f32[12,256]{1,0:T(8,128)S(1)} %reshape.640.refs_4_, f32[12,256]{1,0:T(8,128)S(1)} %bitcast.312, ...), custom_call_target="tpu_custom_call" | custom-call | flops 4026531840 | bytes 1048576 | tf_op jit(solution)/shard_map/attention_backward/pallas_call | solution.py:555
  540.3 6.2 fusion.45
  549.1 68.1 %scatter_attention_grads.1 = (f32[48,1536]{1,0:T(8,128)S(1)}, f32[48,128]{1,0:T(8,128)S(1)}, f32[48,2048]{1,0:T(8,128)S(1)}) custom-call(bf16[2,2,4,2,48,1536]{5,4,3,2,1,0:T(8,128)(2,1)S(1)} %bitcast.304, bf16[2,2,4,2,48,128]{5,4,3,2,1,0:T(8,128)(2,1)S(1)} %select_convert_fusion.refs_1_, bf16[2,2,4,2,48,2048]{5,4,3,2,1,0:T(8,128)(2,1)S(1)} %bitcast.301), custom_call_target="tpu_custom_call" | custom-call | bytes 11403264 | tf_op jit(solution)/shard_map/scatter_attention_grads/pallas_call | solution.py:399
  (323 shorter events, 224.3 us)
Async XLA Ops:
  3.8 91.8 %collective-permute-start = (bf16[384,768]{1,0:T(8,128)(2,1)}, bf16[384,768]{1,0:T(8,128)(2,1)}, u32[]{:S(2)}, u32[]{:S(2)}) collective-permute-start(bf16[384,768]{1,0:T(8,128)(2,1)} %get-tuple-element.259), channel_id=1, source_target_pairs={{0,8},{8,16},{16,24},{24,0},{1,9},{9,17},{17,25},{25,1},{2,10},{10... | collective-permute-start | bytes 1769480 | tf_op jit(solution)/shard_map/ppermute | solution.py:583
  6.8 88.8 %collective-permute-start.1 = (bf16[384,768]{1,0:T(8,128)(2,1)}, bf16[384,768]{1,0:T(8,128)(2,1)}, u32[]{:S(2)}, u32[]{:S(2)}) collective-permute-start(bf16[384,768]{1,0:T(8,128)(2,1)} %get-tuple-element.261), channel_id=1, source_target_pairs={{0,16},{8,24},{16,0},{24,8},{1,17},{9,25},{17,1},{25,9},{2,18},{10... | collective-permute-start | bytes 1769480 | tf_op jit(solution)/shard_map/ppermute | solution.py:583
  8.3 87.2 %collective-permute-start.2 = (bf16[384,768]{1,0:T(8,128)(2,1)}, bf16[384,768]{1,0:T(8,128)(2,1)}, u32[]{:S(2)}, u32[]{:S(2)}) collective-permute-start(bf16[384,768]{1,0:T(8,128)(2,1)} %get-tuple-element.258), channel_id=1, source_target_pairs={{0,24},{8,0},{16,8},{24,16},{1,25},{9,1},{17,9},{25,17},{2,26},{10... | collective-permute-start | bytes 1769480 | tf_op jit(solution)/shard_map/ppermute | solution.py:583
  101.3 94.4 %all-to-all-start = ((bf16[32,40,1536]{2,1,0:T(8,128)(2,1)}), bf16[32,40,1536]{2,1,0:T(8,128)(2,1)}, u32[]{:S(2)}, u32[]{:S(2)}) async-start(bf16[32,40,1536]{2,1,0:T(8,128)(2,1)} %bitcast.324), calls=%async_computation | async-start | bytes 7864320 | tf_op jit(solution)/shard_map/all_to_all | solution.py:101
  195.7 43.3 %all-to-all-start.1 = ((bf16[32,16,1536]{2,1,0:T(8,128)(2,1)}), bf16[32,16,1536]{2,1,0:T(8,128)(2,1)}, u32[]{:S(2)}, u32[]{:S(2)}) async-start(bf16[32,16,1536]{2,1,0:T(8,128)(2,1)} %bitcast.320), calls=%async_computation.1 | async-start | bytes 3145728 | tf_op jit(solution)/shard_map/all_to_all | solution.py:101
  207.3 36.0 %collective-permute-start.6 = (bf16[192,1536]{1,0:T(8,128)(2,1)}, bf16[192,1536]{1,0:T(8,128)(2,1)}, u32[]{:S(2)}, u32[]{:S(2)}) collective-permute-start(bf16[192,1536]{1,0:T(8,128)(2,1)} %get-tuple-element.252), channel_id=1, source_target_pairs={{0,8},{8,16},{16,24},{24,0},{1,9},{9,17},{17,25},{25,1},{2,10},{10... | collective-permute-start | bytes 1769480 | tf_op jit(solution)/shard_map/ppermute | solution.py:583
  214.0 38.7 %collective-permute-start.3 = (bf16[384,768]{1,0:T(8,128)(2,1)}, bf16[384,768]{1,0:T(8,128)(2,1)}, u32[]{:S(2)}, u32[]{:S(2)}) collective-permute-start(bf16[384,768]{1,0:T(8,128)(2,1)} %get-tuple-element.256), channel_id=1, source_target_pairs={{0,8},{8,16},{16,24},{24,0},{1,9},{9,17},{17,25},{25,1},{2,10},{10... | collective-permute-start | bytes 1769480 | tf_op jit(solution)/shard_map/ppermute | solution.py:583
  223.4 50.3 %collective-permute-start.4 = (bf16[384,768]{1,0:T(8,128)(2,1)}, bf16[384,768]{1,0:T(8,128)(2,1)}, u32[]{:S(2)}, u32[]{:S(2)}) collective-permute-start(bf16[384,768]{1,0:T(8,128)(2,1)} %get-tuple-element.255), channel_id=1, source_target_pairs={{0,16},{8,24},{16,0},{24,8},{1,17},{9,25},{17,1},{25,9},{2,18},{10... | collective-permute-start | bytes 1769480 | tf_op jit(solution)/shard_map/ppermute | solution.py:583
  224.7 51.0 %collective-permute-start.5 = (bf16[384,768]{1,0:T(8,128)(2,1)}, bf16[384,768]{1,0:T(8,128)(2,1)}, u32[]{:S(2)}, u32[]{:S(2)}) collective-permute-start(bf16[384,768]{1,0:T(8,128)(2,1)} %get-tuple-element.254), channel_id=1, source_target_pairs={{0,24},{8,0},{16,8},{24,16},{1,25},{9,1},{17,9},{25,17},{2,26},{10... | collective-permute-start | bytes 1769480 | tf_op jit(solution)/shard_map/ppermute | solution.py:583
  226.3 69.1 %collective-permute-start.7 = (bf16[192,1536]{1,0:T(8,128)(2,1)}, bf16[192,1536]{1,0:T(8,128)(2,1)}, u32[]{:S(2)}, u32[]{:S(2)}) collective-permute-start(bf16[192,1536]{1,0:T(8,128)(2,1)} %get-tuple-element.251), channel_id=1, source_target_pairs={{0,16},{8,24},{16,0},{24,8},{1,17},{9,25},{17,1},{25,9},{2,18},{10... | collective-permute-start | bytes 1769480 | tf_op jit(solution)/shard_map/ppermute | solution.py:583
  239.0 80.6 %all-to-all-start.2 = ((bf16[32,24,1536]{2,1,0:T(8,128)(2,1)}), bf16[32,24,1536]{2,1,0:T(8,128)(2,1)}, u32[]{:S(2)}, u32[]{:S(2)}) async-start(bf16[32,24,1536]{2,1,0:T(8,128)(2,1)} %bitcast.318), calls=%async_computation.2 | async-start | bytes 4718592 | tf_op jit(solution)/shard_map/all_to_all | solution.py:101
  243.3 55.5 %collective-permute-start.8 = (bf16[192,1536]{1,0:T(8,128)(2,1)S(1)}, bf16[192,1536]{1,0:T(8,128)(2,1)S(1)}, u32[]{:S(2)}, u32[]{:S(2)}) collective-permute-start(bf16[192,1536]{1,0:T(8,128)(2,1)S(1)} %get-tuple-element.250), channel_id=1, source_target_pairs={{0,24},{8,0},{16,8},{24,16},{1,25},{9,1},{17,9},{25,17},{2,26},{10... | collective-permute-start | bytes 1769480 | tf_op jit(solution)/shard_map/ppermute | solution.py:583
  331.1 59.2 %all-to-all-start.3 = ((bf16[32,16,1536]{2,1,0:T(8,128)(2,1)}), bf16[32,16,1536]{2,1,0:T(8,128)(2,1)}, u32[]{:S(2)}, u32[]{:S(2)}) async-start(bf16[32,16,1536]{2,1,0:T(8,128)(2,1)} %bitcast.339), calls=%async_computation.3 | async-start | bytes 3145728 | tf_op jit(solution)/shard_map/all_to_all | solution.py:101
  353.1 30.4 %collective-permute-start.9 = (bf16[192,1536]{1,0:T(8,128)(2,1)S(1)}, bf16[192,1536]{1,0:T(8,128)(2,1)}, u32[]{:S(2)}, u32[]{:S(2)}) collective-permute-start(bf16[192,1536]{1,0:T(8,128)(2,1)S(1)} %get-tuple-element.248), channel_id=1, source_target_pairs={{0,8},{8,16},{16,24},{24,0},{1,9},{9,17},{17,25},{25,1},{2,10},{10... | collective-permute-start | bytes 1769480 | tf_op jit(solution)/shard_map/ppermute | solution.py:583
  355.1 34.4 %collective-permute-start.10 = (bf16[192,1536]{1,0:T(8,128)(2,1)S(1)}, bf16[192,1536]{1,0:T(8,128)(2,1)}, u32[]{:S(2)}, u32[]{:S(2)}) collective-permute-start(bf16[192,1536]{1,0:T(8,128)(2,1)S(1)} %get-tuple-element.247), channel_id=1, source_target_pairs={{0,16},{8,24},{16,0},{24,8},{1,17},{9,25},{17,1},{25,9},{2,18},{10... | collective-permute-start | bytes 1769480 | tf_op jit(solution)/shard_map/ppermute | solution.py:583
  356.5 33.8 %collective-permute-start.11 = (bf16[192,1536]{1,0:T(8,128)(2,1)S(1)}, bf16[192,1536]{1,0:T(8,128)(2,1)}, u32[]{:S(2)}, u32[]{:S(2)}) collective-permute-start(bf16[192,1536]{1,0:T(8,128)(2,1)S(1)} %get-tuple-element.246), channel_id=1, source_target_pairs={{0,24},{8,0},{16,8},{24,16},{1,25},{9,1},{17,9},{25,17},{2,26},{10... | collective-permute-start | bytes 1769480 | tf_op jit(solution)/shard_map/ppermute | solution.py:583
  364.7 42.8 %collective-permute-start.12 = (bf16[384,768]{1,0:T(8,128)(2,1)}, bf16[384,768]{1,0:T(8,128)(2,1)}, u32[]{:S(2)}, u32[]{:S(2)}) collective-permute-start(bf16[384,768]{1,0:T(8,128)(2,1)} %get-tuple-element.245), channel_id=1, source_target_pairs={{0,8},{8,16},{16,24},{24,0},{1,9},{9,17},{17,25},{25,1},{2,10},{10... | collective-permute-start | bytes 1769480 | tf_op jit(solution)/shard_map/ppermute | solution.py:583
  365.3 64.2 %collective-permute-start.13 = (bf16[384,768]{1,0:T(8,128)(2,1)}, bf16[384,768]{1,0:T(8,128)(2,1)}, u32[]{:S(2)}, u32[]{:S(2)}) collective-permute-start(bf16[384,768]{1,0:T(8,128)(2,1)} %get-tuple-element.244), channel_id=1, source_target_pairs={{0,16},{8,24},{16,0},{24,8},{1,17},{9,25},{17,1},{25,9},{2,18},{10... | collective-permute-start | bytes 1769480 | tf_op jit(solution)/shard_map/ppermute | solution.py:583
  383.6 48.0 %collective-permute-start.14 = (bf16[384,768]{1,0:T(8,128)(2,1)}, bf16[384,768]{1,0:T(8,128)(2,1)}, u32[]{:S(2)}, u32[]{:S(2)}) collective-permute-start(bf16[384,768]{1,0:T(8,128)(2,1)} %get-tuple-element.243), channel_id=1, source_target_pairs={{0,24},{8,0},{16,8},{24,16},{1,25},{9,1},{17,9},{25,17},{2,26},{10... | collective-permute-start | bytes 1769480 | tf_op jit(solution)/shard_map/ppermute | solution.py:583
  390.4 88.5 %all-to-all-start.4 = ((bf16[32,24,1536]{2,1,0:T(8,128)(2,1)}), bf16[32,24,1536]{2,1,0:T(8,128)(2,1)}, u32[]{:S(2)}, u32[]{:S(2)}) async-start(bf16[32,24,1536]{2,1,0:T(8,128)(2,1)} %bitcast.331), calls=%async_computation.4 | async-start | bytes 4718592 | tf_op jit(solution)/shard_map/all_to_all | solution.py:101
  401.9 53.5 %collective-permute-start.15 = (bf16[384,768]{1,0:T(8,128)(2,1)S(1)}, bf16[384,768]{1,0:T(8,128)(2,1)S(1)}, u32[]{:S(2)}, u32[]{:S(2)}) collective-permute-start(bf16[384,768]{1,0:T(8,128)(2,1)S(1)} %get-tuple-element.242), channel_id=1, source_target_pairs={{0,8},{8,16},{16,24},{24,0},{1,9},{9,17},{17,25},{25,1},{2,10},{10... | collective-permute-start | bytes 1769480 | tf_op jit(solution)/shard_map/ppermute | solution.py:583
  403.8 60.8 %collective-permute-start.16 = (bf16[384,768]{1,0:T(8,128)(2,1)S(1)}, bf16[384,768]{1,0:T(8,128)(2,1)S(1)}, u32[]{:S(2)}, u32[]{:S(2)}) collective-permute-start(bf16[384,768]{1,0:T(8,128)(2,1)S(1)} %get-tuple-element.241), channel_id=1, source_target_pairs={{0,16},{8,24},{16,0},{24,8},{1,17},{9,25},{17,1},{25,9},{2,18},{10... | collective-permute-start | bytes 1769480 | tf_op jit(solution)/shard_map/ppermute | solution.py:583
  407.5 59.8 %collective-permute-start.17 = (bf16[384,768]{1,0:T(8,128)(2,1)S(1)}, bf16[384,768]{1,0:T(8,128)(2,1)S(1)}, u32[]{:S(2)}, u32[]{:S(2)}) collective-permute-start(bf16[384,768]{1,0:T(8,128)(2,1)S(1)} %get-tuple-element.240), channel_id=1, source_target_pairs={{0,24},{8,0},{16,8},{24,16},{1,25},{9,1},{17,9},{25,17},{2,26},{10... | collective-permute-start | bytes 1769480 | tf_op jit(solution)/shard_map/ppermute | solution.py:583
  478.9 140.8 %all-to-all-start.5 = ((bf16[32,40,1536]{2,1,0:T(8,128)(2,1)}), bf16[32,40,1536]{2,1,0:T(8,128)(2,1)}, u32[]{:S(2)}, u32[]{:S(2)}) async-start(bf16[32,40,1536]{2,1,0:T(8,128)(2,1)} %bitcast.323), calls=%async_computation.5 | async-start | bytes 7864320 | tf_op jit(solution)/shard_map/all_to_all | solution.py:101
  (71 other events, 1297.2 us)

commit v10 on v9

--- a/solution.py
+++ b/solution.py
@@ -30,19 +30,6 @@
     return (jnp.cos(angles)[:, None, :], jnp.sin(angles)[:, None, :])
 
 
-def apply_rotary(values, cosine_lookup, sine_lookup):
-    half_dim = values.shape[-1] // 2
-    lower_half = values[..., :half_dim]
-    upper_half = values[..., half_dim:]
-    return jnp.concatenate(
-        [
-            lower_half * cosine_lookup - upper_half * sine_lookup,
-            upper_half * cosine_lookup + lower_half * sine_lookup,
-        ],
-        axis=-1,
-    )
-
-
 def dot(left, right, contract):
     return lax.dot_general(left, right, (contract, ((), ())), preferred_element_type=F32)
 
@@ -68,33 +55,11 @@
     return pair_routes, place, live & (place < CAP)
 
 
-def masked_scores(query_group, key_head, query_pos, key_pos, length, score_scale):
-    scores = (
-        jnp.einsum("qgd,kd->gqk", query_group, key_head, preferred_element_type=F32) * score_scale
-    )
-    key_mask = (key_pos[None, :] <= query_pos[:, None]) & (key_pos[None, :] < length)
-    return jnp.where(key_mask[None], scores, NEG_FILL)
-
-
-def head_forward(query_group, key_head, value_head, query_pos, key_pos, length, score_scale):
-    scores = masked_scores(query_group, key_head, query_pos, key_pos, length, score_scale)
-    row_max = jnp.max(scores, axis=-1, keepdims=True)
-    exp_scores = jnp.exp(scores - row_max)
-    exp_total = jnp.sum(exp_scores, axis=-1, keepdims=True)
-    attn_probs = (exp_scores / exp_total).astype(BF16)
-    head_out = jnp.einsum("gqk,kd->qgd", attn_probs, value_head, preferred_element_type=F32)
-    return (head_out, (row_max + jnp.log(exp_total))[..., 0])
-
-
 def norm_back(values, scale_rows, gain_vec, incoming):
     weighted = incoming * gain_vec
     inner_mean = jnp.mean(weighted * values, axis=-1, keepdims=True)
     values_grad = scale_rows * weighted - values * scale_rows * scale_rows * scale_rows * inner_mean
     return (values_grad, jnp.sum(incoming * values * scale_rows, axis=0))
-
-
-def split_heads(gathered, kv_heads):
-    return gathered.reshape(gathered.shape[0], kv_heads, HEAD_DIM).transpose(1, 0, 2)
 
 
 def swap(blocks, axes):
@@ -419,42 +384,143 @@
     )(*[x.reshape(2, 2, line, 2, rows, x.shape[1]) for x in arrays], *extras)
 
 
-def spread_kernel(count, parts, source, target, *sems):
-    me = lax.axis_index("seq")
-    greet([{"seq": lax.rem(me + step, count)} for step in range(1, count)])
-    size = source.shape[0] // parts
-    pieces = [pl.ds(part * size, size) for part in range(parts)]
-    sources = [source.at[piece] for piece in pieces]
-    targets = [target.at[:, piece] for piece in pieces]
-    for copy in start_exchange(count, sources, targets, lambda ref, peer: ref, sems):
-        copy.wait()
-
-
-def seq_spread(array, parts, collective_id, name):
-    count = lax.axis_size("seq")
-    return pl.pallas_call(
-        functools.partial(spread_kernel, count, parts),
-        out_shape=jax.ShapeDtypeStruct((count,) + array.shape, BF16),
-        in_specs=[pl.BlockSpec(memory_space=pl.ANY)],
-        out_specs=pl.BlockSpec(memory_space=pl.ANY),
-        scratch_shapes=exchange_sems(parts, count),
-        compiler_params=pltpu.CompilerParams(
-            collective_id=collective_id, vmem_limit_bytes=4 << 20
-        ),
-        cost_estimate=pl.CostEstimate(
-            flops=0, bytes_accessed=2 * count * array.size, transcendentals=0
-        ),
-        name=name,
-    )(array)
-
-
 def rotate(values, cosines, sines):
     return values * cosines + pltpu.roll(values, HEAD_DIM // 2, 1) * sines
 
 
+def attention_kernel(count, heads, kv_heads, *refs):
+    length_ref, projected_ref, cos_ref, sin_ref = refs[:4]
+    attended_ref, lse_ref, q_ref, kv_ref = refs[4:8]
+    max_ref, sum_ref, acc_ref, send, recv = refs[8:]
+    me = lax.axis_index("seq")
+    rows, kv_width = q_ref.shape[0], kv_heads * HEAD_DIM
+    q_width, group, scale = heads * HEAD_DIM, heads // kv_heads, 1.0 / math.sqrt(HEAD_DIM)
+    greet([{"seq": lax.rem(me + step, count)} for step in range(1, count)])
+    cosines, sines = cos_ref[...], sin_ref[...]
+    for g in range(kv_heads):
+        cols = slice(g * HEAD_DIM, (g + 1) * HEAD_DIM)
+        keys = projected_ref[:, q_width + g * HEAD_DIM : q_width + (g + 1) * HEAD_DIM]
+        kv_ref[me, :, cols] = rotate(keys, cosines, sines).astype(BF16)
+    kv_ref[me, :, kv_width:] = projected_ref[:, q_width + kv_width :].astype(BF16)
+
+    def to_later(peer):
+        return pltpu.make_async_remote_copy(
+            src_ref=kv_ref.at[me],
+            dst_ref=kv_ref.at[me],
+            send_sem=send.at[peer],
+            recv_sem=recv.at[me],
+            device_id={"seq": peer},
+            device_id_type=MESH_IDS,
+        )
+
+    def start(peer, carry):
+        to_later(peer).start()
+        return carry
+
+    lax.fori_loop(me + 1, count, start, 0)
+
+    def one_query(h, carry):
+        cols = pl.ds(pl.multiple_of(h * HEAD_DIM, HEAD_DIM), HEAD_DIM)
+        q_ref[:, cols] = rotate(projected_ref[:, cols], cosines, sines).astype(BF16)
+        return carry
+
+    lax.fori_loop(0, heads, one_query, 0)
+    max_ref[...] = jnp.full_like(max_ref, NEG_FILL)
+    sum_ref[...] = jnp.zeros_like(sum_ref)
+    acc_ref[...] = jnp.zeros_like(acc_ref)
+    length = length_ref[0]
+    query_pos = me * rows + lax.broadcasted_iota(jnp.int32, (rows, rows), 1)
+    key_local = lax.broadcasted_iota(jnp.int32, (rows, rows), 0)
+
+    def key_block(j):
+        key_pos = j * rows + key_local
+        mask = (key_pos <= query_pos) & (key_pos < length)
+        for g in range(kv_heads):
+            key_cols = slice(g * HEAD_DIM, (g + 1) * HEAD_DIM)
+            value_cols = slice(kv_width + g * HEAD_DIM, kv_width + (g + 1) * HEAD_DIM)
+
+            def one_head(i, carry):
+                h = g * group + i
+                cols = pl.ds(pl.multiple_of(h * HEAD_DIM, HEAD_DIM), HEAD_DIM)
+                row = pl.ds(h, 1)
+                keys, values = kv_ref[j, :, key_cols], kv_ref[j, :, value_cols]
+                scores = jnp.where(mask, nt(keys, q_ref[:, cols]) * scale, NEG_FILL)
+                before = max_ref[row, :]
+                top = jnp.maximum(before, jnp.max(scores, axis=0, keepdims=True))
+                shrink = jnp.exp(before - top)
+                weights = jnp.exp(scores - top)
+                max_ref[row, :] = top
+                sum_ref[row, :] = sum_ref[row, :] * shrink + jnp.sum(weights, axis=0, keepdims=True)
+                acc_ref[h] = acc_ref[h] * shrink + tn(values, weights.astype(BF16))
+                return carry
+
+            lax.fori_loop(0, group, one_head, 0, unroll=2)
+
+    key_block(me)
+
+    def earlier_block(j, carry):
+        pltpu.make_async_remote_copy(
+            src_ref=kv_ref.at[j],
+            dst_ref=kv_ref.at[j],
+            send_sem=send.at[j],
+            recv_sem=recv.at[j],
+            device_id={"seq": j},
+            device_id_type=MESH_IDS,
+        ).wait_recv()
+        key_block(j)
+        return carry
+
+    lax.fori_loop(0, me, earlier_block, 0)
+    lse_ref[...] = max_ref[...] + jnp.log(sum_ref[...])
+
+    def finish(h, carry):
+        cols = pl.ds(pl.multiple_of(h * HEAD_DIM, HEAD_DIM), HEAD_DIM)
+        attended_ref[:, cols] = (acc_ref[h] / sum_ref[pl.ds(h, 1), :]).T.astype(BF16)
+        return carry
+
+    lax.fori_loop(0, heads, finish, 0)
+
+    def sent(peer, carry):
+        to_later(peer).wait_send()
+        return carry
+
+    lax.fori_loop(me + 1, count, sent, 0)
+
+
+def attention(length, projected, cosines, sines, q_width, collective_id):
+    count = lax.axis_size("seq")
+    rows = projected.shape[0]
+    kv_width = (projected.shape[1] - q_width) // 2
+    heads, kv_heads = q_width // HEAD_DIM, kv_width // HEAD_DIM
+    vmem = pl.BlockSpec(memory_space=pltpu.VMEM)
+    return pl.pallas_call(
+        functools.partial(attention_kernel, count, heads, kv_heads),
+        out_shape=[
+            jax.ShapeDtypeStruct((rows, q_width), BF16),
+            jax.ShapeDtypeStruct((heads, rows), F32),
+            jax.ShapeDtypeStruct((rows, q_width), BF16),
+            jax.ShapeDtypeStruct((count, rows, 2 * kv_width), BF16),
+        ],
+        in_specs=[pl.BlockSpec(memory_space=pltpu.SMEM)] + [vmem] * 3,
+        out_specs=[vmem] * 4,
+        scratch_shapes=[
+            pltpu.VMEM((heads, rows), F32),
+            pltpu.VMEM((heads, rows), F32),
+            pltpu.VMEM((heads, HEAD_DIM, rows), F32),
+            pltpu.SemaphoreType.DMA((count,)),
+            pltpu.SemaphoreType.DMA((count,)),
+        ],
+        compiler_params=pltpu.CompilerParams(
+            collective_id=collective_id, vmem_limit_bytes=30 << 20
+        ),
+        cost_estimate=pl.CostEstimate(flops=0, bytes_accessed=1 << 20, transcendentals=0),
+        name="attention_forward",
+    )(length, projected, cosines, sines)
+
+
 def attention_back_kernel(count, heads, kv_heads, *refs):
-    length_ref, q_ref, kv_ref, grad_ref, lse_ref, delta_ref, cos_ref, sin_ref, out_ref = refs[:9]
-    dq_ref, part_ref, leaving, arriving, send, recv = refs[9:]
+    length_ref, q_ref, kv_ref, grad_ref, lse_ref, attended_ref, cos_ref, sin_ref = refs[:8]
+    out_ref, delta_ref, dq_ref, part_ref, leaving, arriving, send, recv = refs[8:]
     me = lax.axis_index("seq")
     rows, kv_width = q_ref.shape[0], kv_heads * HEAD_DIM
     group, scale = heads // kv_heads, 1.0 / math.sqrt(HEAD_DIM)
@@ -463,6 +529,13 @@
     query_pos = me * rows + lax.broadcasted_iota(jnp.int32, (rows, rows), 1)
     key_local = lax.broadcasted_iota(jnp.int32, (rows, rows), 0)
     dq_ref[...] = jnp.zeros_like(dq_ref)
+    ones = jnp.ones((8, HEAD_DIM), BF16)
+    for h in range(heads):
+        cols = slice(h * HEAD_DIM, (h + 1) * HEAD_DIM)
+        terms = grad_ref[:, cols].astype(F32) * attended_ref[:, cols].astype(F32)
+        high = terms.astype(BF16)
+        low = (terms - high.astype(F32)).astype(BF16)
+        delta_ref[h : h + 1, :] = (nt(ones, high) + nt(ones, low))[:1]
 
     def key_block(j):
         key_pos = j * rows + key_local
@@ -546,7 +619,7 @@
     lax.fori_loop(0, me, sent, 0)
 
 
-def attention_back(length, queries, kv_all, grads, lse, delta, cosines, sines, collective_id):
+def attention_back(length, queries, kv_all, grads, lse, attended, cosines, sines, collective_id):
     count = lax.axis_size("seq")
     rows, q_width = queries.shape
     kv_width = kv_all.shape[1] // 2
@@ -558,6 +631,7 @@
         in_specs=[pl.BlockSpec(memory_space=pltpu.SMEM)] + [vmem] * 7,
         out_specs=vmem,
         scratch_shapes=[
+            pltpu.VMEM((heads, rows), F32),
             pltpu.VMEM((rows, q_width), F32),
             pltpu.VMEM((rows, 2 * kv_width), F32),
             pltpu.VMEM((count, rows, 2 * kv_width), BF16),
@@ -572,7 +646,7 @@
             flops=10 * count * rows * rows * q_width, bytes_accessed=1 << 20, transcendentals=0
         ),
         name="attention_backward",
-    )(length, queries, kv_all, grads, lse, delta, cosines, sines)
+    )(length, queries, kv_all, grads, lse, attended, cosines, sines)
 
 
 def seq_permutes(block_for):
@@ -621,15 +695,10 @@
     my_seq = lax.axis_index("seq")
     extent = rows * seq_count
     query_pos = my_seq * rows + jnp.arange(rows, dtype=jnp.int32)
-    key_pos = jnp.arange(extent, dtype=jnp.int32)
     length = lengths[0]
     is_valid = query_pos < length
-    score_scale = 1.0 / math.sqrt(HEAD_DIM)
     q_width = w_query.shape[1]
     kv_width = key_projection.shape[1]
-    q_heads = q_width // HEAD_DIM
-    kv_heads = kv_width // HEAD_DIM
-    group_size = q_heads // kv_heads
     cosine_lookup, sine_lookup = rope_angles(query_pos, HEAD_DIM)
 
     gain_block = jnp.concatenate(
@@ -687,30 +756,15 @@
     scale_one = lax.rsqrt(jnp.mean(inputs * inputs, axis=-1, keepdims=True) + EPSILON)
     normed = (inputs * scale_one * gain_one).astype(BF16)
     projected = nn(normed, packed_full)
-    query_rows = projected[:, :q_width]
-    key_matrix_rows = projected[:, q_width : q_width + kv_width]
-    value_matrix_rows = projected[:, q_width + kv_width : q_width + 2 * kv_width].astype(BF16)
-    query_rotated = apply_rotary(
-        query_rows.reshape(rows, q_heads, HEAD_DIM), cosine_lookup, sine_lookup
-    ).astype(BF16)
-    key_rotated = apply_rotary(
-        key_matrix_rows.reshape(rows, kv_heads, HEAD_DIM), cosine_lookup, sine_lookup
-    ).astype(BF16)
-    key_rotated = key_rotated.reshape(rows, kv_width)
-    kv_mine = jnp.concatenate([key_rotated, value_matrix_rows], axis=1)
-    kv_all = seq_spread(kv_mine, 8, 1, "gather_keys").reshape(extent, 2 * kv_width)
-    key_all, value_all = kv_all[:, :kv_width], kv_all[:, kv_width:]
-    query_head_groups = query_rotated.reshape(rows, kv_heads, group_size, HEAD_DIM).transpose(
-        1, 0, 2, 3
-    )
-    key_heads, value_heads = split_heads(key_all, kv_heads), split_heads(value_all, kv_heads)
-    attended, log_total = lax.map(
-        lambda operands: head_forward(
-            operands[0], operands[1], operands[2], query_pos, key_pos, length, score_scale
-        ),
-        (query_head_groups, key_heads, value_heads),
-    )
-    attended = attended.transpose(1, 0, 2, 3).reshape(rows, q_width).astype(BF16)
+    cosines, sines = cosine_lookup[:, 0], sine_lookup[:, 0]
+    cosines = jnp.concatenate([cosines, cosines], axis=1)
+    sines = jnp.concatenate([-sines, sines], axis=1)
+    attended, log_total, query_flat, kv_all = attention(
+        lengths, projected, cosines, sines, q_width, 1
+    )
+    kv_all = kv_all.reshape(extent, 2 * kv_width)
+    attended, w_up = lax.optimization_barrier((attended, w_up))
+    up_parts = expert_pieces(w_up)
     middle = inputs + nn(attended, out_full)
     scale_two = lax.rsqrt(jnp.mean(middle * middle, axis=-1, keepdims=True) + EPSILON)
     moe_input = (middle * scale_two * gain_two).astype(BF16)
@@ -719,13 +773,10 @@
         return tn(hot, moe_input).astype(BF16).reshape(devices, -1, width)
 
     early_send, late_send = to_experts(early_hot), to_experts(late_hot)
-    query_flat = query_rotated.reshape(rows, q_width)
-    early_send, late_send, grad_rows, query_flat, attended, w_up, w_down = (
-        lax.optimization_barrier(
-            (early_send, late_send, grad_rows, query_flat, attended, w_up, w_down)
-        )
-    )
-    up_parts, down_parts = expert_pieces(w_up), expert_pieces(w_down)
+    early_send, late_send, grad_rows, query_flat, attended, w_down = lax.optimization_barrier(
+        (early_send, late_send, grad_rows, query_flat, attended, w_down)
+    )
+    down_parts = expert_pieces(w_down)
     early_rows = swap(early_send, ("dp", "seq"))
     early_rows, late_send = lax.optimization_barrier((early_rows, late_send))
     late_rows = swap(late_send, ("dp", "seq"))
@@ -787,19 +838,22 @@
     )
     down_grad_parts = to_owners(down_grad)
     late_row_grad = row_grads(*late_pre_grads)
-    early_back, late_row_grad, down_grad_parts = lax.optimization_barrier(
-        (early_back, late_row_grad, down_grad_parts)
+    late_hidden = expert_hidden
+    early_back, late_row_grad, down_grad_parts, late_pre_grads, late_hidden = (
+        lax.optimization_barrier(
+            (early_back, late_row_grad, down_grad_parts, late_pre_grads, late_hidden)
+        )
     )
     late_back = swap(late_row_grad, ("dp", "seq"))
     slot_rows = both_parts(early_rows, late_rows)
     gate_pre_grad, up_pre_grad = map(both_parts, early_pre_grads, late_pre_grads)
     gate_grad = tn(slot_rows, gate_pre_grad).astype(BF16)
     up_grad = tn(slot_rows, up_pre_grad).astype(BF16)
-    gate_owned, up_owned = owned_sum(to_owners(gate_grad)), owned_sum(to_owners(up_grad))
+    gate_owned, up_grad_parts = owned_sum(to_owners(gate_grad)), to_owners(up_grad)
     down_owned = owned_sum(down_grad_parts)
-    expert_out = nn(expert_hidden, down_full).astype(BF16)
-    expert_out, late_back, gate_owned, up_owned, down_owned = lax.optimization_barrier(
-        (expert_out, late_back, gate_owned, up_owned, down_owned)
+    expert_out = nn(late_hidden, down_full).astype(BF16)
+    expert_out, late_back, gate_owned, down_owned, up_grad = lax.optimization_barrier(
+        (expert_out, late_back, gate_owned, down_owned, up_grad)
     )
     returned = swap(expert_out.reshape(devices, CAP, width), ("dp", "seq")).reshape(slots, width)
     early_back, late_back = early_back.reshape(-1, width), late_back.reshape(-1, width)
@@ -809,19 +863,16 @@
     branch_grad = middle_grad.astype(BF16)
     out_terms = tn(attended, branch_grad).astype(BF16)
     attended_grad = nt(branch_grad, out_full).astype(BF16)
-    attended_grad, out_terms = lax.optimization_barrier((attended_grad, out_terms))
-    delta = attended_grad.astype(F32) * attended.astype(F32)
-    delta = jnp.sum(delta.reshape(rows, q_heads, HEAD_DIM), axis=-1).T
-    cosines, sines = cosine_lookup[:, 0], sine_lookup[:, 0]
+    attended_grad, up_grad_parts = lax.optimization_barrier((attended_grad, up_grad_parts))
     projected_grad = attention_back(
         lengths,
         query_flat,
         kv_all,
         attended_grad,
-        log_total.reshape(q_heads, rows),
-        delta,
-        jnp.concatenate([cosines, cosines], axis=1),
-        jnp.concatenate([-sines, sines], axis=1),
+        log_total,
+        attended,
+        cosines,
+        sines,
         4,
     )
     normed_grad = nt(projected_grad, packed_full)
@@ -842,7 +893,7 @@
         out_owned, gains_owned = terms[:, :width], terms[:, width : width + LANES]
         owned = terms[:, width + LANES :]
     returned, owned = lax.optimization_barrier((returned, owned))
-    expert_grads = [gate_owned, up_owned, down_owned]
+    expert_grads = [gate_owned, owned_sum(up_grad_parts), down_owned]
 
     gate_hot = jnp.sum(jnp.where(hits, gate_rows[:, :, None], 0.0), axis=1).astype(BF16)
     layer_out = middle + nn(gate_hot, returned)

time: 636 us -> 642 us (level)
  waiting for transfers between devices: 129 us -> 173 us
  other arithmetic: 39 us -> 23.1 us
  Pallas kernels: 215 us -> 203 us
  matrix products: 111 us -> 103 us
  local copies, waits for them, and re-layouts: 68.2 us -> 60.8 us
    ppermute x18, waiting for transfers between devices: 104 us -> 128 us  [seq_permutes(): lax.ppermute(block_for(lax.rem(me + step, count)), 'seq', ring)]
    all_to_all x6, waiting for transfers between devices: 24.2 us -> 44.8 us  [swap(): return lax.all_to_all(blocks, axes, split_axis=0, concat_axis=0, tiled=True)]
    pallas_call x1, Pallas kernels: 33.7 us -> 24.4 us  [attention_back(): pl.pallas_call(functools.partial(attention_back_kernel, count, heads, kv_...]
    pallas_call x1, Pallas kernels: 47.9 us -> 40.2 us  [attention(): pl.pallas_call(functools.partial(attention_kernel, count, heads, kv_heads...]
    unnamed x143 -> x131, local copies, waits for them, and re-layouts: 13.1 us -> 17.4 us
  transfers between devices with their start and end apart: 24 -> 24, of which waited for: 13 -> 12; matrix products, arithmetic and copies ran while one was open for 29% -> 24% of each run, Pallas kernels for 34% -> 32%
where the time goes in v10:
time: 642 us; the launch traced here: 633 us
  Pallas kernels  203 us (32%)
  waiting for transfers between devices  173 us (27%)
  matrix products  103 us (16%)
  starting transfers between devices  67.3 us (10%)
  local copies, waits for them, and re-layouts  60.8 us (9%)
  other arithmetic  23.1 us (4%)
    ppermute x18, waiting for transfers between devices, seq_permutes(): lax.ppermute(block_for(lax.rem(me + step, count)), 'seq', ring)  128 us
    dot_general x26, matrix products, dot(): lax.dot_general(left, right, (contract, ((), ())), preferred_element_type...  103 us
    pallas_call x1, Pallas kernels, staged_gather(): pl.pallas_call(functools.partial(gather_kernel, line, chunks, n, len(extr...  71.7 us
    pallas_call x1, Pallas kernels, staged_scatter(): pl.pallas_call(functools.partial(scatter_kernel, line, chunks, n, len(ext...  66.3 us
    all_to_all x6, waiting for transfers between devices, swap(): return lax.all_to_all(blocks, axes, split_axis=0, concat_axis=0, tiled=True)  44.8 us
    pallas_call x1, Pallas kernels, attention(): pl.pallas_call(functools.partial(attention_kernel, count, heads, kv_heads...  40.2 us
    all_to_all x6, starting transfers between devices, swap(): return lax.all_to_all(blocks, axes, split_axis=0, concat_axis=0, tiled=True)  34.9 us
    ppermute x18, starting transfers between devices, seq_permutes(): lax.ppermute(block_for(lax.rem(me + step, count)), 'seq', ring)  32.5 us
  transfers between devices with their start and end apart: 24, of which 12 were waited for; matrix products, arithmetic and copies ran while one was open for 24% of the time, Pallas kernels for 32%

profile of v10, /device:TPU:0, one launch (start us, length us, event | category | flops | bytes accessed | tf_op | source)
XLA Modules:
  0.0 632.7 jit_solution(14379004922182052101)
XLA Ops:
  14.5 71.7 %gather_attention_weights.1 = (bf16[2,2,4,2,48,2048]{5,4,3,2,1,0:T(8,128)(2,1)S(1)}, bf16[2,2,4,2,48,128]{5,4,3,2,1,0:T(8,128)(2,1)S(1)}, bf16[2,2,4,2,48,1536]{5,4,3,2,1,0:T(8,128)(2,1)S(1)}) custom-call(bf16[48,2048]{1,0:T(8,128)(2,1)S(1)} %pad_maximum_fusion.1.refs_0_, bf16[48,128]{1,0:T(8,128)(2,1)S(1)} %maximum_maximum_fusion.refs_1_, ...), custom_call_target="tpu_custom_call" | custom-call | bytes 11403264 | tf_op jit(solution)/shard_map/gather_attention_weights/pallas_call | solution.py:243
  97.0 5.6 all-to-all-start
  110.9 40.2 %attention_forward.1 = (bf16[256,1536]{1,0:T(8,128)(2,1)S(1)}, f32[12,256]{1,0:T(8,128)S(1)}, bf16[256,1536]{1,0:T(8,128)(2,1)S(1)}, bf16[4,256,512]{2,1,0:T(8,128)(2,1)S(1)}) custom-call(s32[1]{0:T(128)} %copy.74.refs_0_, f32[256,2048]{1,0:T(8,128)S(1)} %fusion.30.refs_1_, f32[256,128]{1,0:T(8,128)S(1)} %get-tuple-element.182.refs_2_.refs_6_, ...), custom_call_target="tpu_custom_call" | custom-call | bytes 1048576 | tf_op jit(solution)/shard_map/attention_forward/pallas_call | solution.py:496
  156.9 33.8 %all-to-all-done = bf16[32,40,1536]{2,1,0:T(8,128)(2,1)} async-done(((bf16[32,40,1536]{2,1,0:T(8,128)(2,1)}), bf16[32,40,1536]{2,1,0:T(8,128)(2,1)}, u32[]{:S(2)}, u32[]{:S(2)}) %all-to-all-start) | async-done | bytes 3932192 | tf_op jit(solution)/shard_map/all_to_all | solution.py:66
  190.7 6.1 all-to-all-start.1
  215.8 15.1 %collective-permute-done.3 = bf16[384,768]{1,0:T(8,128)(2,1)S(1)} collective-permute-done((bf16[384,768]{1,0:T(8,128)(2,1)S(1)}, bf16[384,768]{1,0:T(8,128)(2,1)S(1)}, u32[]{:S(2)}, u32[]{:S(2)}) %collective-permute-start.3) | collective-permute-done | bytes 589856 | tf_op jit(solution)/shard_map/ppermute | solution.py:657
  231.7 10.4 %collective-permute-done.4 = bf16[384,768]{1,0:T(8,128)(2,1)S(1)} collective-permute-done((bf16[384,768]{1,0:T(8,128)(2,1)S(1)}, bf16[384,768]{1,0:T(8,128)(2,1)S(1)}, u32[]{:S(2)}, u32[]{:S(2)}) %collective-permute-start.4) | collective-permute-done | bytes 589856 | tf_op jit(solution)/shard_map/ppermute | solution.py:657
  251.0 6.2 all-to-all-start.2
  259.3 21.1 %collective-permute-done.7 = bf16[192,1536]{1,0:T(8,128)(2,1)} collective-permute-done((bf16[192,1536]{1,0:T(8,128)(2,1)S(1)}, bf16[192,1536]{1,0:T(8,128)(2,1)}, u32[]{:S(2)}, u32[]{:S(2)}) %collective-permute-start.7) | collective-permute-done | bytes 589856 | tf_op jit(solution)/shard_map/ppermute | solution.py:657
  306.6 5.2 fusion.52
  311.8 5.8 fusion.53
  317.6 8.3 %all-to-all-start.3 = ((bf16[32,16,1536]{2,1,0:T(8,128)(2,1)}), bf16[32,16,1536]{2,1,0:T(8,128)(2,1)}, u32[]{:S(2)}, u32[]{:S(2)}) async-start(bf16[32,16,1536]{2,1,0:T(8,128)(2,1)} %bitcast.253), calls=%async_computation.3 | async-start | bytes 3145728 | tf_op jit(solution)/shard_map/all_to_all | solution.py:66
  325.8 6.4 %multiply_convert_fusion = (bf16[768,768]{1,0:T(8,128)(2,1)S(1)}, bf16[768,768]{1,0:T(8,128)(2,1)S(1)}, bf16[768,768]{1,0:T(8,128)(2,1)S(1)}) fusion(f32[768,768]{1,0:T(8,128)} %fusion.53, f32[768,768]{1,0:T(8,128)} %fusion.52, bf16[768,1536]{1,0:T(8,128)(2,1)} %bitcast.42, bf16[1536,768]{1,0:T(8,128)(2,1)} %bitcast.30), kind=kOutput, calls=%fused_computation.29 | convolution fusion | flops 1820786688 | bytes 12976128 | tf_op jit(solution)/shard_map/dot_general | solution.py:34
  332.3 6.5 %bitcast_convert_fusion.2 = bf16[768,1536]{1,0:T(8,128)(2,1)S(1)} fusion(bf16[32,40,1536]{2,1,0:T(8,128)(2,1)} %all-to-all-done, bf16[32,24,768]{2,1,0:T(8,128)(2,1)S(1)} %bitcast.255, bf16[32,16,768]{2,1,0:T(8,128)(2,1)S(1)} %bitcast.257), kind=kOutput, calls=%fused_computation.11 | convolution fusion | flops 3025010688 | bytes 8257536 | tf_op jit(solution)/shard_map/dot_general | solution.py:34
  342.2 9.1 %collective-permute-start.9 = (bf16[192,1536]{1,0:T(8,128)(2,1)S(1)}, bf16[192,1536]{1,0:T(8,128)(2,1)}, u32[]{:S(2)}, u32[]{:S(2)}) collective-permute-start(bf16[192,1536]{1,0:T(8,128)(2,1)S(1)} %get-tuple-element.156), channel_id=1, source_target_pairs={{0,8},{8,16},{16,24},{24,0},{1,9},{9,17},{17,25},{25,1},{2,10},{10... | collective-permute-start | bytes 1769480 | tf_op jit(solution)/shard_map/ppermute | solution.py:657
  365.5 9.4 %collective-permute-done.9 = bf16[192,1536]{1,0:T(8,128)(2,1)} collective-permute-done((bf16[192,1536]{1,0:T(8,128)(2,1)S(1)}, bf16[192,1536]{1,0:T(8,128)(2,1)}, u32[]{:S(2)}, u32[]{:S(2)}) %collective-permute-start.9) | collective-permute-done | bytes 589856 | tf_op jit(solution)/shard_map/ppermute | solution.py:657
  374.9 6.0 bitcast_convert_fusion.1
  394.2 6.5 %convolution_convert_fusion.2 = bf16[1280,1536]{1,0:T(8,128)(2,1)} fusion(bf16[1280,768]{1,0:T(8,128)(2,1)S(1)} %bitcast.252, bf16[768,1536]{1,0:T(8,128)(2,1)} %bitcast.37), kind=kOutput, calls=%fused_computation.4 | convolution fusion | flops 3021864960 | bytes 8257536 | tf_op jit(solution)/shard_map/dot_general | solution.py:34
  413.5 17.5 %collective-permute-done.13 = bf16[384,768]{1,0:T(8,128)(2,1)} collective-permute-done((bf16[384,768]{1,0:T(8,128)(2,1)}, bf16[384,768]{1,0:T(8,128)(2,1)}, u32[]{:S(2)}, u32[]{:S(2)}) %collective-permute-start.13) | collective-permute-done | bytes 589856 | tf_op jit(solution)/shard_map/ppermute | solution.py:657
  435.2 10.9 %all-to-all-done.4 = bf16[32,24,1536]{2,1,0:T(8,128)(2,1)} async-done(((bf16[32,24,1536]{2,1,0:T(8,128)(2,1)}), bf16[32,24,1536]{2,1,0:T(8,128)(2,1)}, u32[]{:S(2)}, u32[]{:S(2)}) %all-to-all-start.4) | async-done | bytes 2359328 | tf_op jit(solution)/shard_map/all_to_all | solution.py:66
  464.6 42.4 %collective-permute-done.15 = bf16[384,768]{1,0:T(8,128)(2,1)S(1)} collective-permute-done((bf16[384,768]{1,0:T(8,128)(2,1)S(1)}, bf16[384,768]{1,0:T(8,128)(2,1)S(1)}, u32[]{:S(2)}, u32[]{:S(2)}) %collective-permute-start.15) | collective-permute-done | bytes 589856 | tf_op jit(solution)/shard_map/ppermute | solution.py:657
  507.1 7.9 %collective-permute-done.16 = bf16[384,768]{1,0:T(8,128)(2,1)S(1)} collective-permute-done((bf16[384,768]{1,0:T(8,128)(2,1)S(1)}, bf16[384,768]{1,0:T(8,128)(2,1)S(1)}, u32[]{:S(2)}, u32[]{:S(2)}) %collective-permute-start.16) | collective-permute-done | bytes 589856 | tf_op jit(solution)/shard_map/ppermute | solution.py:657
  519.0 24.4 %attention_backward.1 = bf16[256,2048]{1,0:T(8,128)(2,1)S(1)} custom-call(s32[1]{0:T(128)} %copy.74.refs_0_, bf16[256,1536]{1,0:T(8,128)(2,1)S(1)} %copy-done.4, bf16[1024,512]{1,0:T(8,128)(2,1)S(1)} %bitcast.241, bf16[256,1536]{1,0:T(8,128)(2,1)S(1)} %convolution_convert_fusion.5.refs_3_, f32[12,256]{1,0:T(8,128)S(1)} %get-tuple-element.119.refs_4_, ...), custom_call_target="tpu_custom_call" | custom-call | flops 4026531840 | bytes 1048576 | tf_op jit(solution)/shard_map/attention_backward/pallas_call | solution.py:628
  552.3 66.3 %scatter_attention_grads.1 = (f32[48,1536]{1,0:T(8,128)S(1)}, f32[48,128]{1,0:T(8,128)S(1)}, f32[48,2048]{1,0:T(8,128)S(1)}) custom-call(bf16[2,2,4,2,48,1536]{5,4,3,2,1,0:T(8,128)(2,1)S(1)} %bitcast.229, bf16[2,2,4,2,48,128]{5,4,3,2,1,0:T(8,128)(2,1)S(1)} %select_convert_fusion.refs_1_, bf16[2,2,4,2,48,2048]{5,4,3,2,1,0:T(8,128)(2,1)S(1)} %bitcast.228), custom_call_target="tpu_custom_call" | custom-call | bytes 11403264 | tf_op jit(solution)/shard_map/scatter_attention_grads/pallas_call | solution.py:364
  (268 shorter events, 187.2 us)
Async XLA Ops:
  3.7 92.5 %collective-permute-start = (bf16[384,768]{1,0:T(8,128)(2,1)}, bf16[384,768]{1,0:T(8,128)(2,1)S(1)}, u32[]{:S(2)}, u32[]{:S(2)}) collective-permute-start(bf16[384,768]{1,0:T(8,128)(2,1)} %get-tuple-element.167), channel_id=1, source_target_pairs={{0,8},{8,16},{16,24},{24,0},{1,9},{9,17},{17,25},{25,1},{2,10},{10... | collective-permute-start | bytes 1769480 | tf_op jit(solution)/shard_map/ppermute | solution.py:657
  6.6 89.5 %collective-permute-start.1 = (bf16[384,768]{1,0:T(8,128)(2,1)}, bf16[384,768]{1,0:T(8,128)(2,1)}, u32[]{:S(2)}, u32[]{:S(2)}) collective-permute-start(bf16[384,768]{1,0:T(8,128)(2,1)} %get-tuple-element.169), channel_id=1, source_target_pairs={{0,16},{8,24},{16,0},{24,8},{1,17},{9,25},{17,1},{25,9},{2,18},{10... | collective-permute-start | bytes 1769480 | tf_op jit(solution)/shard_map/ppermute | solution.py:657
  8.2 88.0 %collective-permute-start.2 = (bf16[384,768]{1,0:T(8,128)(2,1)}, bf16[384,768]{1,0:T(8,128)(2,1)}, u32[]{:S(2)}, u32[]{:S(2)}) collective-permute-start(bf16[384,768]{1,0:T(8,128)(2,1)} %get-tuple-element.166), channel_id=1, source_target_pairs={{0,24},{8,0},{16,8},{24,16},{1,25},{9,1},{17,9},{25,17},{2,26},{10... | collective-permute-start | bytes 1769480 | tf_op jit(solution)/shard_map/ppermute | solution.py:657
  97.0 93.7 %all-to-all-start = ((bf16[32,40,1536]{2,1,0:T(8,128)(2,1)}), bf16[32,40,1536]{2,1,0:T(8,128)(2,1)}, u32[]{:S(2)}, u32[]{:S(2)}) async-start(bf16[32,40,1536]{2,1,0:T(8,128)(2,1)} %bitcast.245), calls=%async_computation | async-start | bytes 7864320 | tf_op jit(solution)/shard_map/all_to_all | solution.py:66
  190.7 60.3 %all-to-all-start.1 = ((bf16[32,16,1536]{2,1,0:T(8,128)(2,1)}), bf16[32,16,1536]{2,1,0:T(8,128)(2,1)}, u32[]{:S(2)}, u32[]{:S(2)}) async-start(bf16[32,16,1536]{2,1,0:T(8,128)(2,1)} %bitcast.243), calls=%async_computation.1 | async-start | bytes 3145728 | tf_op jit(solution)/shard_map/all_to_all | solution.py:66
  200.4 30.4 %collective-permute-start.3 = (bf16[384,768]{1,0:T(8,128)(2,1)S(1)}, bf16[384,768]{1,0:T(8,128)(2,1)S(1)}, u32[]{:S(2)}, u32[]{:S(2)}) collective-permute-start(bf16[384,768]{1,0:T(8,128)(2,1)S(1)} %get-tuple-element.164), channel_id=1, source_target_pairs={{0,8},{8,16},{16,24},{24,0},{1,9},{9,17},{17,25},{25,1},{2,10},{10... | collective-permute-start | bytes 1769480 | tf_op jit(solution)/shard_map/ppermute | solution.py:657
  202.1 40.0 %collective-permute-start.4 = (bf16[384,768]{1,0:T(8,128)(2,1)S(1)}, bf16[384,768]{1,0:T(8,128)(2,1)S(1)}, u32[]{:S(2)}, u32[]{:S(2)}) collective-permute-start(bf16[384,768]{1,0:T(8,128)(2,1)S(1)} %get-tuple-element.163), channel_id=1, source_target_pairs={{0,16},{8,24},{16,0},{24,8},{1,17},{9,25},{17,1},{25,9},{2,18},{10... | collective-permute-start | bytes 1769480 | tf_op jit(solution)/shard_map/ppermute | solution.py:657
  203.6 39.7 %collective-permute-start.5 = (bf16[384,768]{1,0:T(8,128)(2,1)S(1)}, bf16[384,768]{1,0:T(8,128)(2,1)S(1)}, u32[]{:S(2)}, u32[]{:S(2)}) collective-permute-start(bf16[384,768]{1,0:T(8,128)(2,1)S(1)} %get-tuple-element.162), channel_id=1, source_target_pairs={{0,24},{8,0},{16,8},{24,16},{1,25},{9,1},{17,9},{25,17},{2,26},{10... | collective-permute-start | bytes 1769480 | tf_op jit(solution)/shard_map/ppermute | solution.py:657
  215.2 42.2 %collective-permute-start.6 = (bf16[192,1536]{1,0:T(8,128)(2,1)}, bf16[192,1536]{1,0:T(8,128)(2,1)}, u32[]{:S(2)}, u32[]{:S(2)}) collective-permute-start(bf16[192,1536]{1,0:T(8,128)(2,1)} %get-tuple-element.160), channel_id=1, source_target_pairs={{0,8},{8,16},{16,24},{24,0},{1,9},{9,17},{17,25},{25,1},{2,10},{10... | collective-permute-start | bytes 1769480 | tf_op jit(solution)/shard_map/ppermute | solution.py:657
  243.0 37.4 %collective-permute-start.7 = (bf16[192,1536]{1,0:T(8,128)(2,1)S(1)}, bf16[192,1536]{1,0:T(8,128)(2,1)}, u32[]{:S(2)}, u32[]{:S(2)}) collective-permute-start(bf16[192,1536]{1,0:T(8,128)(2,1)S(1)} %get-tuple-element.159), channel_id=1, source_target_pairs={{0,16},{8,24},{16,0},{24,8},{1,17},{9,25},{17,1},{25,9},{2,18},{10... | collective-permute-start | bytes 1769480 | tf_op jit(solution)/shard_map/ppermute | solution.py:657
  250.1 32.2 %collective-permute-start.8 = (bf16[192,1536]{1,0:T(8,128)(2,1)S(1)}, bf16[192,1536]{1,0:T(8,128)(2,1)}, u32[]{:S(2)}, u32[]{:S(2)}) collective-permute-start(bf16[192,1536]{1,0:T(8,128)(2,1)S(1)} %get-tuple-element.158), channel_id=1, source_target_pairs={{0,24},{8,0},{16,8},{24,16},{1,25},{9,1},{17,9},{25,17},{2,26},{10... | collective-permute-start | bytes 1769480 | tf_op jit(solution)/shard_map/ppermute | solution.py:657
  251.0 60.8 %all-to-all-start.2 = ((bf16[32,24,1536]{2,1,0:T(8,128)(2,1)}), bf16[32,24,1536]{2,1,0:T(8,128)(2,1)}, u32[]{:S(2)}, u32[]{:S(2)}) async-start(bf16[32,24,1536]{2,1,0:T(8,128)(2,1)} %bitcast.242), calls=%async_computation.2 | async-start | bytes 4718592 | tf_op jit(solution)/shard_map/all_to_all | solution.py:66
  317.6 57.4 %all-to-all-start.3 = ((bf16[32,16,1536]{2,1,0:T(8,128)(2,1)}), bf16[32,16,1536]{2,1,0:T(8,128)(2,1)}, u32[]{:S(2)}, u32[]{:S(2)}) async-start(bf16[32,16,1536]{2,1,0:T(8,128)(2,1)} %bitcast.253), calls=%async_computation.3 | async-start | bytes 3145728 | tf_op jit(solution)/shard_map/all_to_all | solution.py:66
  338.9 25.8 %collective-permute-start.10 = (bf16[192,1536]{1,0:T(8,128)(2,1)S(1)}, bf16[192,1536]{1,0:T(8,128)(2,1)S(1)}, u32[]{:S(2)}, u32[]{:S(2)}) collective-permute-start(bf16[192,1536]{1,0:T(8,128)(2,1)S(1)} %get-tuple-element.155), channel_id=1, source_target_pairs={{0,16},{8,24},{16,0},{24,8},{1,17},{9,25},{17,1},{25,9},{2,18},{10... | collective-permute-start | bytes 1769480 | tf_op jit(solution)/shard_map/ppermute | solution.py:657
  340.7 24.0 %collective-permute-start.11 = (bf16[192,1536]{1,0:T(8,128)(2,1)S(1)}, bf16[192,1536]{1,0:T(8,128)(2,1)S(1)}, u32[]{:S(2)}, u32[]{:S(2)}) collective-permute-start(bf16[192,1536]{1,0:T(8,128)(2,1)S(1)} %get-tuple-element.154), channel_id=1, source_target_pairs={{0,24},{8,0},{16,8},{24,16},{1,25},{9,1},{17,9},{25,17},{2,26},{10... | collective-permute-start | bytes 1769480 | tf_op jit(solution)/shard_map/ppermute | solution.py:657
  342.2 32.7 %collective-permute-start.9 = (bf16[192,1536]{1,0:T(8,128)(2,1)S(1)}, bf16[192,1536]{1,0:T(8,128)(2,1)}, u32[]{:S(2)}, u32[]{:S(2)}) collective-permute-start(bf16[192,1536]{1,0:T(8,128)(2,1)S(1)} %get-tuple-element.156), channel_id=1, source_target_pairs={{0,8},{8,16},{16,24},{24,0},{1,9},{9,17},{17,25},{25,1},{2,10},{10... | collective-permute-start | bytes 1769480 | tf_op jit(solution)/shard_map/ppermute | solution.py:657
  383.5 27.8 %collective-permute-start.12 = (bf16[384,768]{1,0:T(8,128)(2,1)}, bf16[384,768]{1,0:T(8,128)(2,1)}, u32[]{:S(2)}, u32[]{:S(2)}) collective-permute-start(bf16[384,768]{1,0:T(8,128)(2,1)} %get-tuple-element.153), channel_id=1, source_target_pairs={{0,8},{8,16},{16,24},{24,0},{1,9},{9,17},{17,25},{25,1},{2,10},{10... | collective-permute-start | bytes 1769480 | tf_op jit(solution)/shard_map/ppermute | solution.py:657
  384.1 46.9 %collective-permute-start.13 = (bf16[384,768]{1,0:T(8,128)(2,1)}, bf16[384,768]{1,0:T(8,128)(2,1)}, u32[]{:S(2)}, u32[]{:S(2)}) collective-permute-start(bf16[384,768]{1,0:T(8,128)(2,1)} %get-tuple-element.152), channel_id=1, source_target_pairs={{0,16},{8,24},{16,0},{24,8},{1,17},{9,25},{17,1},{25,9},{2,18},{10... | collective-permute-start | bytes 1769480 | tf_op jit(solution)/shard_map/ppermute | solution.py:657
  386.2 46.9 %collective-permute-start.14 = (bf16[384,768]{1,0:T(8,128)(2,1)}, bf16[384,768]{1,0:T(8,128)(2,1)}, u32[]{:S(2)}, u32[]{:S(2)}) collective-permute-start(bf16[384,768]{1,0:T(8,128)(2,1)} %get-tuple-element.151), channel_id=1, source_target_pairs={{0,24},{8,0},{16,8},{24,16},{1,25},{9,1},{17,9},{25,17},{2,26},{10... | collective-permute-start | bytes 1769480 | tf_op jit(solution)/shard_map/ppermute | solution.py:657
  386.9 59.2 %all-to-all-start.4 = ((bf16[32,24,1536]{2,1,0:T(8,128)(2,1)}), bf16[32,24,1536]{2,1,0:T(8,128)(2,1)}, u32[]{:S(2)}, u32[]{:S(2)}) async-start(bf16[32,24,1536]{2,1,0:T(8,128)(2,1)} %bitcast.246), calls=%async_computation.4 | async-start | bytes 4718592 | tf_op jit(solution)/shard_map/all_to_all | solution.py:66
  446.2 179.5 %all-to-all-start.5 = ((bf16[32,40,1536]{2,1,0:T(8,128)(2,1)}), bf16[32,40,1536]{2,1,0:T(8,128)(2,1)}, u32[]{:S(2)}, u32[]{:S(2)}) async-start(bf16[32,40,1536]{2,1,0:T(8,128)(2,1)} %bitcast.244), calls=%async_computation.5 | async-start | bytes 7864320 | tf_op jit(solution)/shard_map/all_to_all | solution.py:66
  452.8 54.2 %collective-permute-start.15 = (bf16[384,768]{1,0:T(8,128)(2,1)S(1)}, bf16[384,768]{1,0:T(8,128)(2,1)S(1)}, u32[]{:S(2)}, u32[]{:S(2)}) collective-permute-start(bf16[384,768]{1,0:T(8,128)(2,1)S(1)} %get-tuple-element.149), channel_id=1, source_target_pairs={{0,8},{8,16},{16,24},{24,0},{1,9},{9,17},{17,25},{25,1},{2,10},{10... | collective-permute-start | bytes 1769480 | tf_op jit(solution)/shard_map/ppermute | solution.py:657
  454.5 60.4 %collective-permute-start.16 = (bf16[384,768]{1,0:T(8,128)(2,1)S(1)}, bf16[384,768]{1,0:T(8,128)(2,1)S(1)}, u32[]{:S(2)}, u32[]{:S(2)}) collective-permute-start(bf16[384,768]{1,0:T(8,128)(2,1)S(1)} %get-tuple-element.148), channel_id=1, source_target_pairs={{0,16},{8,24},{16,0},{24,8},{1,17},{9,25},{17,1},{25,9},{2,18},{10... | collective-permute-start | bytes 1769480 | tf_op jit(solution)/shard_map/ppermute | solution.py:657
  456.0 63.0 %collective-permute-start.17 = (bf16[384,768]{1,0:T(8,128)(2,1)S(1)}, bf16[384,768]{1,0:T(8,128)(2,1)S(1)}, u32[]{:S(2)}, u32[]{:S(2)}) collective-permute-start(bf16[384,768]{1,0:T(8,128)(2,1)S(1)} %get-tuple-element.147), channel_id=1, source_target_pairs={{0,24},{8,0},{16,8},{24,16},{1,25},{9,1},{17,9},{25,17},{2,26},{10... | collective-permute-start | bytes 1769480 | tf_op jit(solution)/shard_map/ppermute | solution.py:657
  (64 other events, 812.7 us)

commit v11 on v10

--- a/solution.py
+++ b/solution.py
@@ -647,6 +647,29 @@
         ),
         name="attention_backward",
     )(length, queries, kv_all, grads, lse, attended, cosines, sines)
+
+
+def weight_grad_kernel(n, left_ref, *refs):
+    for right_ref, out_ref in zip(refs[:n], refs[n:], strict=True):
+        out_ref[...] = tn(left_ref[...], right_ref[...]).astype(BF16)
+
+
+def weight_grads(left, rights, name):
+    total, columns = left.shape
+    tile = 256
+    return pl.pallas_call(
+        functools.partial(weight_grad_kernel, len(rights)),
+        grid=(columns // tile,),
+        out_shape=[jax.ShapeDtypeStruct((columns, r.shape[1]), BF16) for r in rights],
+        in_specs=[pl.BlockSpec((total, tile), lambda i: (0, i))]
+        + [
+            pl.BlockSpec(r.shape, lambda i: (0, 0), pipeline_mode=pl.Buffered(1)) for r in rights
+        ],
+        out_specs=[pl.BlockSpec((tile, r.shape[1]), lambda i: (i, 0)) for r in rights],
+        compiler_params=pltpu.CompilerParams(vmem_limit_bytes=48 << 20),
+        cost_estimate=pl.CostEstimate(flops=0, bytes_accessed=1 << 20, transcendentals=0),
+        name=name,
+    )(left, *rights)
 
 
 def seq_permutes(block_for):
@@ -773,8 +796,11 @@
         return tn(hot, moe_input).astype(BF16).reshape(devices, -1, width)
 
     early_send, late_send = to_experts(early_hot), to_experts(late_hot)
-    early_send, late_send, grad_rows, query_flat, attended, w_down = lax.optimization_barrier(
-        (early_send, late_send, grad_rows, query_flat, attended, w_down)
+    early_send, late_send, grad_rows, up_parts, w_down = lax.optimization_barrier(
+        (early_send, late_send, grad_rows, up_parts, w_down)
+    )
+    early_grads, late_grads, w_down = lax.optimization_barrier(
+        (grad_rows[:, :EARLY], grad_rows[:, EARLY:], w_down)
     )
     down_parts = expert_pieces(w_down)
     early_rows = swap(early_send, ("dp", "seq"))
@@ -783,7 +809,6 @@
     gate_full = in_seq_order(gate_parts, BF16).reshape(width, hidden_units)
     up_full = in_seq_order(up_parts, BF16).reshape(width, hidden_units)
     down_full = in_seq_order(down_parts, BF16).reshape(hidden_units, width)
-    early_grads, late_grads = grad_rows[:, :EARLY], grad_rows[:, EARLY:]
     early_rows, gate_full, up_full, down_full, early_grads, late_grads = (
         lax.optimization_barrier(
             (early_rows, gate_full, up_full, down_full, early_grads, late_grads)
@@ -832,28 +857,26 @@
     early_back = swap(early_row_grad, ("dp", "seq"))
     late_hidden, *late_pre_grads = run_expert(late_rows, late_grads)
     expert_hidden = both_parts(early_hidden, late_hidden)
-    down_grad = tn(expert_hidden, grad_rows.reshape(slots, width)).astype(BF16)
+    (down_grad,) = weight_grads(expert_hidden, [grad_rows.reshape(slots, width)], "down_grads")
     late_rows, late_pre_grads, down_grad = lax.optimization_barrier(
         (late_rows, late_pre_grads, down_grad)
     )
     down_grad_parts = to_owners(down_grad)
-    late_row_grad = row_grads(*late_pre_grads)
-    late_hidden = expert_hidden
-    early_back, late_row_grad, down_grad_parts, late_pre_grads, late_hidden = (
-        lax.optimization_barrier(
-            (early_back, late_row_grad, down_grad_parts, late_pre_grads, late_hidden)
-        )
-    )
-    late_back = swap(late_row_grad, ("dp", "seq"))
     slot_rows = both_parts(early_rows, late_rows)
     gate_pre_grad, up_pre_grad = map(both_parts, early_pre_grads, late_pre_grads)
-    gate_grad = tn(slot_rows, gate_pre_grad).astype(BF16)
-    up_grad = tn(slot_rows, up_pre_grad).astype(BF16)
-    gate_owned, up_grad_parts = owned_sum(to_owners(gate_grad)), to_owners(up_grad)
+    gate_grad, up_grad = weight_grads(slot_rows, [gate_pre_grad, up_pre_grad], "gate_up_grads")
+    late_row_grad = row_grads(*late_pre_grads)
+    early_back, late_row_grad, down_grad_parts, gate_grad, up_grad, expert_hidden = (
+        lax.optimization_barrier(
+            (early_back, late_row_grad, down_grad_parts, gate_grad, up_grad, expert_hidden)
+        )
+    )
+    late_back = swap(late_row_grad, ("dp", "seq"))
+    gate_owned, up_owned = owned_sum(to_owners(gate_grad)), owned_sum(to_owners(up_grad))
     down_owned = owned_sum(down_grad_parts)
-    expert_out = nn(late_hidden, down_full).astype(BF16)
-    expert_out, late_back, gate_owned, down_owned, up_grad = lax.optimization_barrier(
-        (expert_out, late_back, gate_owned, down_owned, up_grad)
+    expert_out = nn(expert_hidden, down_full).astype(BF16)
+    expert_out, late_back, gate_owned, up_owned, down_owned = lax.optimization_barrier(
+        (expert_out, late_back, gate_owned, up_owned, down_owned)
     )
     returned = swap(expert_out.reshape(devices, CAP, width), ("dp", "seq")).reshape(slots, width)
     early_back, late_back = early_back.reshape(-1, width), late_back.reshape(-1, width)
@@ -863,7 +886,6 @@
     branch_grad = middle_grad.astype(BF16)
     out_terms = tn(attended, branch_grad).astype(BF16)
     attended_grad = nt(branch_grad, out_full).astype(BF16)
-    attended_grad, up_grad_parts = lax.optimization_barrier((attended_grad, up_grad_parts))
     projected_grad = attention_back(
         lengths,
         query_flat,
@@ -893,7 +915,7 @@
         out_owned, gains_owned = terms[:, :width], terms[:, width : width + LANES]
         owned = terms[:, width + LANES :]
     returned, owned = lax.optimization_barrier((returned, owned))
-    expert_grads = [gate_owned, owned_sum(up_grad_parts), down_owned]
+    expert_grads = [gate_owned, up_owned, down_owned]
 
     gate_hot = jnp.sum(jnp.where(hits, gate_rows[:, :, None], 0.0), axis=1).astype(BF16)
     layer_out = middle + nn(gate_hot, returned)

time: 642 us -> 603 us (0.939)
  waiting for transfers between devices: 173 us -> 119 us
  Pallas kernels: 203 us -> 236 us
  matrix products: 103 us -> 79.2 us
    ppermute x18, waiting for transfers between devices: 128 us -> 90 us  [seq_permutes(): lax.ppermute(block_for(lax.rem(me + step, count)), 'seq', ring)]
    dot_general x26 -> x23, matrix products: 103 us -> 79.2 us  [dot(): lax.dot_general(left, right, (contract, ((), ())), preferred_element_type...]
    all_to_all x6, waiting for transfers between devices: 44.8 us -> 29.3 us  [swap(): return lax.all_to_all(blocks, axes, split_axis=0, concat_axis=0, tiled=True)]
    pallas_call x0 -> x2, Pallas kernels: none -> 15.1 us  [weight_grads(): pl.pallas_call(functools.partial(weight_grad_kernel, len(rights)), grid=(...]
    pallas_call x1, Pallas kernels: 66.3 us -> 77.7 us  [staged_scatter(): pl.pallas_call(functools.partial(scatter_kernel, line, chunks, n, len(ext...]
    ppermute x18, starting transfers between devices: 32.5 us -> 40.3 us  [seq_permutes(): lax.ppermute(block_for(lax.rem(me + step, count)), 'seq', ring)]
    unnamed x131 -> x142, local copies, waits for them, and re-layouts: 17.4 us -> 13.9 us
    dynamic_update_slice x10 -> x11, local copies, waits for them, and re-layouts: 14.3 us -> 16 us  [in_seq_order(): lax.dynamic_update_index_in_dim(whole, piece.astype(dtype), place, 0)]
  transfers between devices with their start and end apart: 24 -> 24, of which waited for: 12 -> 14; matrix products, arithmetic and copies ran while one was open for 24% -> 24% of each run, Pallas kernels for 32% -> 40%
where the time goes in v11:
time: 603 us; the launch traced here: 593 us
  Pallas kernels  236 us (39%)
  waiting for transfers between devices  119 us (20%)
  matrix products  79.2 us (13%)
  starting transfers between devices  70.3 us (12%)
  local copies, waits for them, and re-layouts  57.6 us (10%)
  other arithmetic  27.7 us (5%)
    ppermute x18, waiting for transfers between devices, seq_permutes(): lax.ppermute(block_for(lax.rem(me + step, count)), 'seq', ring)  90 us
    dot_general x23, matrix products, dot(): lax.dot_general(left, right, (contract, ((), ())), preferred_element_type...  79.2 us
    pallas_call x1, Pallas kernels, staged_scatter(): pl.pallas_call(functools.partial(scatter_kernel, line, chunks, n, len(ext...  77.7 us
    pallas_call x1, Pallas kernels, staged_gather(): pl.pallas_call(functools.partial(gather_kernel, line, chunks, n, len(extr...  72.3 us
    pallas_call x1, Pallas kernels, attention(): pl.pallas_call(functools.partial(attention_kernel, count, heads, kv_heads...  41.7 us
    ppermute x18, starting transfers between devices, seq_permutes(): lax.ppermute(block_for(lax.rem(me + step, count)), 'seq', ring)  40.3 us
    all_to_all x6, starting transfers between devices, swap(): return lax.all_to_all(blocks, axes, split_axis=0, concat_axis=0, tiled=True)  29.9 us
    pallas_call x1, Pallas kernels, attention_back(): pl.pallas_call(functools.partial(attention_back_kernel, count, heads, kv_...  29.4 us
  transfers between devices with their start and end apart: 24, of which 14 were waited for; matrix products, arithmetic and copies ran while one was open for 24% of the time, Pallas kernels for 40%

profile of v11, /device:TPU:0, one launch (start us, length us, event | category | flops | bytes accessed | tf_op | source)
XLA Modules:
  0.0 593.2 jit_solution(1423817498015694305)
XLA Ops:
  13.8 72.3 %gather_attention_weights.1 = (bf16[2,2,4,2,48,2048]{5,4,3,2,1,0:T(8,128)(2,1)S(1)}, bf16[2,2,4,2,48,128]{5,4,3,2,1,0:T(8,128)(2,1)S(1)}, bf16[2,2,4,2,48,1536]{5,4,3,2,1,0:T(8,128)(2,1)S(1)}) custom-call(bf16[48,2048]{1,0:T(8,128)(2,1)S(1)} %pad_maximum_fusion.4.refs_0_, bf16[48,128]{1,0:T(8,128)(2,1)S(1)} %maximum_maximum_fusion.refs_1_, ...), custom_call_target="tpu_custom_call" | custom-call | bytes 11403264 | tf_op jit(solution)/shard_map/gather_attention_weights/pallas_call | solution.py:243
  97.0 5.6 all-to-all-start
  109.6 41.7 %attention_forward.1 = (bf16[256,1536]{1,0:T(8,128)(2,1)S(1)}, f32[12,256]{1,0:T(8,128)S(1)}, bf16[256,1536]{1,0:T(8,128)(2,1)S(1)}, bf16[4,256,512]{2,1,0:T(8,128)(2,1)S(1)}) custom-call(s32[1]{0:T(128)} %copy.73.refs_0_, f32[256,2048]{1,0:T(8,128)S(1)} %fusion.24.refs_1_, f32[256,128]{1,0:T(8,128)S(1)} %get-tuple-element.187.refs_2_.refs_6_, ...), custom_call_target="tpu_custom_call" | custom-call | bytes 1048576 | tf_op jit(solution)/shard_map/attention_forward/pallas_call | solution.py:496
  152.7 18.8 %collective-permute-start.4 = (bf16[384,768]{1,0:T(8,128)(2,1)S(1)}, bf16[384,768]{1,0:T(8,128)(2,1)S(1)}, u32[]{:S(2)}, u32[]{:S(2)}) collective-permute-start(bf16[384,768]{1,0:T(8,128)(2,1)S(1)} %get-tuple-element.168), channel_id=1, source_target_pairs={{0,16},{8,24},{16,0},{24,8},{1,17},{9,25},{17,1},{25,9},{2,18},{10... | collective-permute-start | bytes 1769480 | tf_op jit(solution)/shard_map/ppermute | solution.py:680
  177.3 14.6 %collective-permute-done.3 = bf16[384,768]{1,0:T(8,128)(2,1)S(1)} collective-permute-done((bf16[384,768]{1,0:T(8,128)(2,1)S(1)}, bf16[384,768]{1,0:T(8,128)(2,1)S(1)}, u32[]{:S(2)}, u32[]{:S(2)}) %collective-permute-start.3) | collective-permute-done | bytes 589856 | tf_op jit(solution)/shard_map/ppermute | solution.py:680
  192.7 9.1 %collective-permute-done.4 = bf16[384,768]{1,0:T(8,128)(2,1)S(1)} collective-permute-done((bf16[384,768]{1,0:T(8,128)(2,1)S(1)}, bf16[384,768]{1,0:T(8,128)(2,1)S(1)}, u32[]{:S(2)}, u32[]{:S(2)}) %collective-permute-start.4) | collective-permute-done | bytes 589856 | tf_op jit(solution)/shard_map/ppermute | solution.py:680
  202.7 5.1 all-to-all-start.1
  232.7 12.7 %all-to-all-done.1 = bf16[32,16,1536]{2,1,0:T(8,128)(2,1)S(1)} async-done(((bf16[32,16,1536]{2,1,0:T(8,128)(2,1)}), bf16[32,16,1536]{2,1,0:T(8,128)(2,1)S(1)}, u32[]{:S(2)}, u32[]{:S(2)}) %all-to-all-start.1) | async-done | bytes 1572896 | tf_op jit(solution)/shard_map/all_to_all | solution.py:66
  260.7 5.2 collective-permute-done.8
  288.4 16.6 %all-to-all-done.2 = bf16[32,24,1536]{2,1,0:T(8,128)(2,1)S(1)} async-done(((bf16[32,24,1536]{2,1,0:T(8,128)(2,1)}), bf16[32,24,1536]{2,1,0:T(8,128)(2,1)S(1)}, u32[]{:S(2)}, u32[]{:S(2)}) %all-to-all-start.2) | async-done | bytes 2359328 | tf_op jit(solution)/shard_map/all_to_all | solution.py:66
  305.0 4.9 all-to-all-start.3
  318.2 5.9 down_grads.1
  334.5 9.2 %gate_up_grads.1 = (bf16[1536,768]{1,0:T(8,128)(2,1)}, bf16[1536,768]{1,0:T(8,128)(2,1)}) custom-call(bf16[1280,1536]{1,0:T(8,128)(2,1)} %bitcast.239, bf16[1280,768]{1,0:T(8,128)(2,1)S(1)} %bitcast.227, bf16[1280,768]{1,0:T(8,128)(2,1)S(1)} %bitcast.228), custom_call_target="tpu_custom_call" | custom-call | bytes 1048576 | tf_op jit(solution)/shard_map/gate_up_grads/pallas_call | solution.py:660
  347.4 5.1 add_convert_fusion
  352.5 7.8 %collective-permute-done.10 = bf16[192,1536]{1,0:T(8,128)(2,1)} collective-permute-done((bf16[192,1536]{1,0:T(8,128)(2,1)S(1)}, bf16[192,1536]{1,0:T(8,128)(2,1)}, u32[]{:S(2)}, u32[]{:S(2)}) %collective-permute-start.10) | collective-permute-done | bytes 589856 | tf_op jit(solution)/shard_map/ppermute | solution.py:680
  360.6 4.8 all-to-all-start.4
  376.0 4.8 convolution_convert_fusion.2
  392.0 14.4 %collective-permute-done.12 = bf16[384,768]{1,0:T(8,128)(2,1)S(1)} collective-permute-done((bf16[384,768]{1,0:T(8,128)(2,1)S(1)}, bf16[384,768]{1,0:T(8,128)(2,1)S(1)}, u32[]{:S(2)}, u32[]{:S(2)}) %collective-permute-start.12) | collective-permute-done | bytes 589856 | tf_op jit(solution)/shard_map/ppermute | solution.py:680
  407.5 11.7 %collective-permute-done.13 = bf16[384,768]{1,0:T(8,128)(2,1)S(1)} collective-permute-done((bf16[384,768]{1,0:T(8,128)(2,1)S(1)}, bf16[384,768]{1,0:T(8,128)(2,1)S(1)}, u32[]{:S(2)}, u32[]{:S(2)}) %collective-permute-start.13) | collective-permute-done | bytes 589856 | tf_op jit(solution)/shard_map/ppermute | solution.py:680
  422.5 13.1 %collective-permute-done.15 = bf16[384,768]{1,0:T(8,128)(2,1)S(1)} collective-permute-done((bf16[384,768]{1,0:T(8,128)(2,1)S(1)}, bf16[384,768]{1,0:T(8,128)(2,1)S(1)}, u32[]{:S(2)}, u32[]{:S(2)}) %collective-permute-start.15) | collective-permute-done | bytes 589856 | tf_op jit(solution)/shard_map/ppermute | solution.py:680
  436.7 7.3 %collective-permute-done.16 = bf16[384,768]{1,0:T(8,128)(2,1)S(1)} collective-permute-done((bf16[384,768]{1,0:T(8,128)(2,1)S(1)}, bf16[384,768]{1,0:T(8,128)(2,1)S(1)}, u32[]{:S(2)}, u32[]{:S(2)}) %collective-permute-start.16) | collective-permute-done | bytes 589856 | tf_op jit(solution)/shard_map/ppermute | solution.py:680
  447.3 5.5 all-to-all-start.5
  467.8 29.4 %attention_backward.1 = bf16[256,2048]{1,0:T(8,128)(2,1)S(1)} custom-call(s32[1]{0:T(128)} %copy.73.refs_0_, bf16[256,1536]{1,0:T(8,128)(2,1)S(1)} %copy-done.6, bf16[1024,512]{1,0:T(8,128)(2,1)S(1)} %bitcast.238, bf16[256,1536]{1,0:T(8,128)(2,1)S(1)} %convolution_convert_fusion.5.refs_3_, f32[12,256]{1,0:T(8,128)S(1)} %get-tuple-element.128.refs_4_, ...), custom_call_target="tpu_custom_call" | custom-call | flops 4026531840 | bytes 1048576 | tf_op jit(solution)/shard_map/attention_backward/pallas_call | solution.py:628
  505.9 77.7 %scatter_attention_grads.1 = (f32[48,1536]{1,0:T(8,128)S(1)}, f32[48,128]{1,0:T(8,128)S(1)}, f32[48,2048]{1,0:T(8,128)S(1)}) custom-call(bf16[2,2,4,2,48,1536]{5,4,3,2,1,0:T(8,128)(2,1)S(1)} %bitcast.223, bf16[2,2,4,2,48,128]{5,4,3,2,1,0:T(8,128)(2,1)S(1)} %select_convert_fusion.refs_1_, bf16[2,2,4,2,48,2048]{5,4,3,2,1,0:T(8,128)(2,1)S(1)} %bitcast.222), custom_call_target="tpu_custom_call" | custom-call | bytes 11403264 | tf_op jit(solution)/shard_map/scatter_attention_grads/pallas_call | solution.py:364
  (280 shorter events, 187.0 us)
Async XLA Ops:
  3.7 92.4 %collective-permute-start = (bf16[384,768]{1,0:T(8,128)(2,1)}, bf16[384,768]{1,0:T(8,128)(2,1)S(1)}, u32[]{:S(2)}, u32[]{:S(2)}) collective-permute-start(bf16[384,768]{1,0:T(8,128)(2,1)} %get-tuple-element.172), channel_id=1, source_target_pairs={{0,8},{8,16},{16,24},{24,0},{1,9},{9,17},{17,25},{25,1},{2,10},{10... | collective-permute-start | bytes 1769480 | tf_op jit(solution)/shard_map/ppermute | solution.py:680
  6.6 89.5 %collective-permute-start.1 = (bf16[384,768]{1,0:T(8,128)(2,1)}, bf16[384,768]{1,0:T(8,128)(2,1)}, u32[]{:S(2)}, u32[]{:S(2)}) collective-permute-start(bf16[384,768]{1,0:T(8,128)(2,1)} %get-tuple-element.174), channel_id=1, source_target_pairs={{0,16},{8,24},{16,0},{24,8},{1,17},{9,25},{17,1},{25,9},{2,18},{10... | collective-permute-start | bytes 1769480 | tf_op jit(solution)/shard_map/ppermute | solution.py:680
  8.2 88.0 %collective-permute-start.2 = (bf16[384,768]{1,0:T(8,128)(2,1)}, bf16[384,768]{1,0:T(8,128)(2,1)}, u32[]{:S(2)}, u32[]{:S(2)}) collective-permute-start(bf16[384,768]{1,0:T(8,128)(2,1)} %get-tuple-element.171), channel_id=1, source_target_pairs={{0,24},{8,0},{16,8},{24,16},{1,25},{9,1},{17,9},{25,17},{2,26},{10... | collective-permute-start | bytes 1769480 | tf_op jit(solution)/shard_map/ppermute | solution.py:680
  97.0 105.7 %all-to-all-start = ((bf16[32,40,1536]{2,1,0:T(8,128)(2,1)}), bf16[32,40,1536]{2,1,0:T(8,128)(2,1)}, u32[]{:S(2)}, u32[]{:S(2)}) async-start(bf16[32,40,1536]{2,1,0:T(8,128)(2,1)} %bitcast.245), calls=%async_computation | async-start | bytes 7864320 | tf_op jit(solution)/shard_map/all_to_all | solution.py:66
  152.7 39.2 %collective-permute-start.3 = (bf16[384,768]{1,0:T(8,128)(2,1)S(1)}, bf16[384,768]{1,0:T(8,128)(2,1)S(1)}, u32[]{:S(2)}, u32[]{:S(2)}) collective-permute-start(bf16[384,768]{1,0:T(8,128)(2,1)S(1)} %get-tuple-element.169), channel_id=1, source_target_pairs={{0,8},{8,16},{16,24},{24,0},{1,9},{9,17},{17,25},{25,1},{2,10},{10... | collective-permute-start | bytes 1769480 | tf_op jit(solution)/shard_map/ppermute | solution.py:680
  152.7 49.1 %collective-permute-start.4 = (bf16[384,768]{1,0:T(8,128)(2,1)S(1)}, bf16[384,768]{1,0:T(8,128)(2,1)S(1)}, u32[]{:S(2)}, u32[]{:S(2)}) collective-permute-start(bf16[384,768]{1,0:T(8,128)(2,1)S(1)} %get-tuple-element.168), channel_id=1, source_target_pairs={{0,16},{8,24},{16,0},{24,8},{1,17},{9,25},{17,1},{25,9},{2,18},{10... | collective-permute-start | bytes 1769480 | tf_op jit(solution)/shard_map/ppermute | solution.py:680
  171.6 31.1 %collective-permute-start.5 = (bf16[384,768]{1,0:T(8,128)(2,1)S(1)}, bf16[384,768]{1,0:T(8,128)(2,1)}, u32[]{:S(2)}, u32[]{:S(2)}) collective-permute-start(bf16[384,768]{1,0:T(8,128)(2,1)S(1)} %get-tuple-element.167), channel_id=1, source_target_pairs={{0,24},{8,0},{16,8},{24,16},{1,25},{9,1},{17,9},{25,17},{2,26},{10... | collective-permute-start | bytes 1769480 | tf_op jit(solution)/shard_map/ppermute | solution.py:680
  202.7 42.7 %all-to-all-start.1 = ((bf16[32,16,1536]{2,1,0:T(8,128)(2,1)}), bf16[32,16,1536]{2,1,0:T(8,128)(2,1)S(1)}, u32[]{:S(2)}, u32[]{:S(2)}) async-start(bf16[32,16,1536]{2,1,0:T(8,128)(2,1)} %bitcast.16), calls=%async_computation.1 | async-start | bytes 3145728 | tf_op jit(solution)/shard_map/all_to_all | solution.py:66
  223.8 28.9 %collective-permute-start.6 = (bf16[192,1536]{1,0:T(8,128)(2,1)}, bf16[192,1536]{1,0:T(8,128)(2,1)}, u32[]{:S(2)}, u32[]{:S(2)}) collective-permute-start(bf16[192,1536]{1,0:T(8,128)(2,1)} %get-tuple-element.165), channel_id=1, source_target_pairs={{0,8},{8,16},{16,24},{24,0},{1,9},{9,17},{17,25},{25,1},{2,10},{10... | collective-permute-start | bytes 1769480 | tf_op jit(solution)/shard_map/ppermute | solution.py:680
  225.6 33.2 %collective-permute-start.7 = (bf16[192,1536]{1,0:T(8,128)(2,1)}, bf16[192,1536]{1,0:T(8,128)(2,1)}, u32[]{:S(2)}, u32[]{:S(2)}) collective-permute-start(bf16[192,1536]{1,0:T(8,128)(2,1)} %get-tuple-element.164), channel_id=1, source_target_pairs={{0,16},{8,24},{16,0},{24,8},{1,17},{9,25},{17,1},{25,9},{2,18},{10... | collective-permute-start | bytes 1769480 | tf_op jit(solution)/shard_map/ppermute | solution.py:680
  227.1 38.9 %collective-permute-start.8 = (bf16[192,1536]{1,0:T(8,128)(2,1)}, bf16[192,1536]{1,0:T(8,128)(2,1)}, u32[]{:S(2)}, u32[]{:S(2)}) collective-permute-start(bf16[192,1536]{1,0:T(8,128)(2,1)} %get-tuple-element.163), channel_id=1, source_target_pairs={{0,24},{8,0},{16,8},{24,16},{1,25},{9,1},{17,9},{25,17},{2,26},{10... | collective-permute-start | bytes 1769480 | tf_op jit(solution)/shard_map/ppermute | solution.py:680
  246.5 58.5 %all-to-all-start.2 = ((bf16[32,24,1536]{2,1,0:T(8,128)(2,1)}), bf16[32,24,1536]{2,1,0:T(8,128)(2,1)S(1)}, u32[]{:S(2)}, u32[]{:S(2)}) async-start(bf16[32,24,1536]{2,1,0:T(8,128)(2,1)} %bitcast.17), calls=%async_computation.2 | async-start | bytes 4718592 | tf_op jit(solution)/shard_map/all_to_all | solution.py:66
  305.0 55.6 %all-to-all-start.3 = ((bf16[32,16,1536]{2,1,0:T(8,128)(2,1)}), bf16[32,16,1536]{2,1,0:T(8,128)(2,1)}, u32[]{:S(2)}, u32[]{:S(2)}) async-start(bf16[32,16,1536]{2,1,0:T(8,128)(2,1)} %bitcast.255), calls=%async_computation.3 | async-start | bytes 3145728 | tf_op jit(solution)/shard_map/all_to_all | solution.py:66
  325.3 27.2 %collective-permute-start.9 = (bf16[192,1536]{1,0:T(8,128)(2,1)}, bf16[192,1536]{1,0:T(8,128)(2,1)}, u32[]{:S(2)}, u32[]{:S(2)}) collective-permute-start(bf16[192,1536]{1,0:T(8,128)(2,1)} %get-tuple-element.161), channel_id=1, source_target_pairs={{0,8},{8,16},{16,24},{24,0},{1,9},{9,17},{17,25},{25,1},{2,10},{10... | collective-permute-start | bytes 1769480 | tf_op jit(solution)/shard_map/ppermute | solution.py:680
  327.1 33.1 %collective-permute-start.10 = (bf16[192,1536]{1,0:T(8,128)(2,1)S(1)}, bf16[192,1536]{1,0:T(8,128)(2,1)}, u32[]{:S(2)}, u32[]{:S(2)}) collective-permute-start(bf16[192,1536]{1,0:T(8,128)(2,1)S(1)} %get-tuple-element.160), channel_id=1, source_target_pairs={{0,16},{8,24},{16,0},{24,8},{1,17},{9,25},{17,1},{25,9},{2,18},{10... | collective-permute-start | bytes 1769480 | tf_op jit(solution)/shard_map/ppermute | solution.py:680
  328.6 32.0 %collective-permute-start.11 = (bf16[192,1536]{1,0:T(8,128)(2,1)S(1)}, bf16[192,1536]{1,0:T(8,128)(2,1)}, u32[]{:S(2)}, u32[]{:S(2)}) collective-permute-start(bf16[192,1536]{1,0:T(8,128)(2,1)S(1)} %get-tuple-element.159), channel_id=1, source_target_pairs={{0,24},{8,0},{16,8},{24,16},{1,25},{9,1},{17,9},{25,17},{2,26},{10... | collective-permute-start | bytes 1769480 | tf_op jit(solution)/shard_map/ppermute | solution.py:680
  360.6 86.7 %all-to-all-start.4 = ((bf16[32,24,1536]{2,1,0:T(8,128)(2,1)}), bf16[32,24,1536]{2,1,0:T(8,128)(2,1)}, u32[]{:S(2)}, u32[]{:S(2)}) async-start(bf16[32,24,1536]{2,1,0:T(8,128)(2,1)} %bitcast.249), calls=%async_computation.4 | async-start | bytes 4718592 | tf_op jit(solution)/shard_map/all_to_all | solution.py:66
  367.1 39.3 %collective-permute-start.12 = (bf16[384,768]{1,0:T(8,128)(2,1)S(1)}, bf16[384,768]{1,0:T(8,128)(2,1)S(1)}, u32[]{:S(2)}, u32[]{:S(2)}) collective-permute-start(bf16[384,768]{1,0:T(8,128)(2,1)S(1)} %get-tuple-element.158), channel_id=1, source_target_pairs={{0,8},{8,16},{16,24},{24,0},{1,9},{9,17},{17,25},{25,1},{2,10},{10... | collective-permute-start | bytes 1769480 | tf_op jit(solution)/shard_map/ppermute | solution.py:680
  368.9 50.3 %collective-permute-start.13 = (bf16[384,768]{1,0:T(8,128)(2,1)S(1)}, bf16[384,768]{1,0:T(8,128)(2,1)S(1)}, u32[]{:S(2)}, u32[]{:S(2)}) collective-permute-start(bf16[384,768]{1,0:T(8,128)(2,1)S(1)} %get-tuple-element.157), channel_id=1, source_target_pairs={{0,16},{8,24},{16,0},{24,8},{1,17},{9,25},{17,1},{25,9},{2,18},{10... | collective-permute-start | bytes 1769480 | tf_op jit(solution)/shard_map/ppermute | solution.py:680
  370.3 51.1 %collective-permute-start.14 = (bf16[384,768]{1,0:T(8,128)(2,1)S(1)}, bf16[384,768]{1,0:T(8,128)(2,1)S(1)}, u32[]{:S(2)}, u32[]{:S(2)}) collective-permute-start(bf16[384,768]{1,0:T(8,128)(2,1)S(1)} %get-tuple-element.156), channel_id=1, source_target_pairs={{0,24},{8,0},{16,8},{24,16},{1,25},{9,1},{17,9},{25,17},{2,26},{10... | collective-permute-start | bytes 1769480 | tf_op jit(solution)/shard_map/ppermute | solution.py:680
  371.9 63.7 %collective-permute-start.15 = (bf16[384,768]{1,0:T(8,128)(2,1)S(1)}, bf16[384,768]{1,0:T(8,128)(2,1)S(1)}, u32[]{:S(2)}, u32[]{:S(2)}) collective-permute-start(bf16[384,768]{1,0:T(8,128)(2,1)S(1)} %get-tuple-element.155), channel_id=1, source_target_pairs={{0,8},{8,16},{16,24},{24,0},{1,9},{9,17},{17,25},{25,1},{2,10},{10... | collective-permute-start | bytes 1769480 | tf_op jit(solution)/shard_map/ppermute | solution.py:680
  391.5 52.5 %collective-permute-start.16 = (bf16[384,768]{1,0:T(8,128)(2,1)S(1)}, bf16[384,768]{1,0:T(8,128)(2,1)S(1)}, u32[]{:S(2)}, u32[]{:S(2)}) collective-permute-start(bf16[384,768]{1,0:T(8,128)(2,1)S(1)} %get-tuple-element.154), channel_id=1, source_target_pairs={{0,16},{8,24},{16,0},{24,8},{1,17},{9,25},{17,1},{25,9},{2,18},{10... | collective-permute-start | bytes 1769480 | tf_op jit(solution)/shard_map/ppermute | solution.py:680
  406.4 39.9 %collective-permute-start.17 = (bf16[384,768]{1,0:T(8,128)(2,1)S(1)}, bf16[384,768]{1,0:T(8,128)(2,1)S(1)}, u32[]{:S(2)}, u32[]{:S(2)}) collective-permute-start(bf16[384,768]{1,0:T(8,128)(2,1)S(1)} %get-tuple-element.153), channel_id=1, source_target_pairs={{0,24},{8,0},{16,8},{24,16},{1,25},{9,1},{17,9},{25,17},{2,26},{10... | collective-permute-start | bytes 1769480 | tf_op jit(solution)/shard_map/ppermute | solution.py:680
  447.3 138.7 %all-to-all-start.5 = ((bf16[32,40,1536]{2,1,0:T(8,128)(2,1)}), bf16[32,40,1536]{2,1,0:T(8,128)(2,1)}, u32[]{:S(2)}, u32[]{:S(2)}) async-start(bf16[32,40,1536]{2,1,0:T(8,128)(2,1)} %bitcast.244), calls=%async_computation.5 | async-start | bytes 7864320 | tf_op jit(solution)/shard_map/all_to_all | solution.py:66
  (70 other events, 1170.3 us)

commit v12 on v11

--- a/solution.py
+++ b/solution.py
@@ -12,7 +12,7 @@
 EXPERTS = 32
 TOP = 4
 CAP = 40
-EARLY = 16
+EARLY = 24
 
 EPSILON = 1e-06
 ROPE_BASE = 10000.0
@@ -649,27 +649,28 @@
     )(length, queries, kv_all, grads, lse, attended, cosines, sines)
 
 
-def weight_grad_kernel(n, left_ref, *refs):
-    for right_ref, out_ref in zip(refs[:n], refs[n:], strict=True):
-        out_ref[...] = tn(left_ref[...], right_ref[...]).astype(BF16)
-
-
-def weight_grads(left, rights, name):
-    total, columns = left.shape
-    tile = 256
+def weight_grad_kernel(n, *refs):
+    lefts, rights, outs = refs[:2], refs[2 : 2 + 2 * n], refs[2 + 2 * n :]
+    for k, out_ref in enumerate(outs):
+        early, late = rights[2 * k : 2 * k + 2]
+        total = tn(lefts[0][...], early[...]) + tn(lefts[1][...], late[...])
+        out_ref[...] = total.astype(BF16)
+
+
+def weight_grads(lefts, rights, name):
+    columns, tile = lefts[0].shape[1], 256
+    flat = [part for pair in rights for part in pair]
     return pl.pallas_call(
         functools.partial(weight_grad_kernel, len(rights)),
         grid=(columns // tile,),
-        out_shape=[jax.ShapeDtypeStruct((columns, r.shape[1]), BF16) for r in rights],
-        in_specs=[pl.BlockSpec((total, tile), lambda i: (0, i))]
-        + [
-            pl.BlockSpec(r.shape, lambda i: (0, 0), pipeline_mode=pl.Buffered(1)) for r in rights
-        ],
-        out_specs=[pl.BlockSpec((tile, r.shape[1]), lambda i: (i, 0)) for r in rights],
+        out_shape=[jax.ShapeDtypeStruct((columns, r[0].shape[1]), BF16) for r in rights],
+        in_specs=[pl.BlockSpec((x.shape[0], tile), lambda i: (0, i)) for x in lefts]
+        + [pl.BlockSpec(r.shape, lambda i: (0, 0), pipeline_mode=pl.Buffered(1)) for r in flat],
+        out_specs=[pl.BlockSpec((tile, r[0].shape[1]), lambda i: (i, 0)) for r in rights],
         compiler_params=pltpu.CompilerParams(vmem_limit_bytes=48 << 20),
         cost_estimate=pl.CostEstimate(flops=0, bytes_accessed=1 << 20, transcendentals=0),
         name=name,
-    )(left, *rights)
+    )(*lefts, *flat)
 
 
 def seq_permutes(block_for):
@@ -778,7 +779,8 @@
     inputs = hidden_in[0].astype(F32)
     scale_one = lax.rsqrt(jnp.mean(inputs * inputs, axis=-1, keepdims=True) + EPSILON)
     normed = (inputs * scale_one * gain_one).astype(BF16)
-    projected = nn(normed, packed_full)
+    projected, w_up = lax.optimization_barrier((nn(normed, packed_full), w_up))
+    up_parts = expert_pieces(w_up)
     cosines, sines = cosine_lookup[:, 0], sine_lookup[:, 0]
     cosines = jnp.concatenate([cosines, cosines], axis=1)
     sines = jnp.concatenate([-sines, sines], axis=1)
@@ -786,8 +788,6 @@
         lengths, projected, cosines, sines, q_width, 1
     )
     kv_all = kv_all.reshape(extent, 2 * kv_width)
-    attended, w_up = lax.optimization_barrier((attended, w_up))
-    up_parts = expert_pieces(w_up)
     middle = inputs + nn(attended, out_full)
     scale_two = lax.rsqrt(jnp.mean(middle * middle, axis=-1, keepdims=True) + EPSILON)
     moe_input = (middle * scale_two * gain_two).astype(BF16)
@@ -856,21 +856,29 @@
     late_rows, early_row_grad = lax.optimization_barrier((late_rows, early_row_grad))
     early_back = swap(early_row_grad, ("dp", "seq"))
     late_hidden, *late_pre_grads = run_expert(late_rows, late_grads)
-    expert_hidden = both_parts(early_hidden, late_hidden)
-    (down_grad,) = weight_grads(expert_hidden, [grad_rows.reshape(slots, width)], "down_grads")
+
+    def flat(*parts):
+        return [part.reshape(-1, part.shape[-1]) for part in parts]
+
+    (down_grad,) = weight_grads(
+        flat(early_hidden, late_hidden), [flat(early_grads, late_grads)], "down_grads"
+    )
     late_rows, late_pre_grads, down_grad = lax.optimization_barrier(
         (late_rows, late_pre_grads, down_grad)
     )
     down_grad_parts = to_owners(down_grad)
-    slot_rows = both_parts(early_rows, late_rows)
-    gate_pre_grad, up_pre_grad = map(both_parts, early_pre_grads, late_pre_grads)
-    gate_grad, up_grad = weight_grads(slot_rows, [gate_pre_grad, up_pre_grad], "gate_up_grads")
+    gate_grad, up_grad = weight_grads(
+        flat(early_rows, late_rows),
+        [flat(*pair) for pair in zip(early_pre_grads, late_pre_grads, strict=True)],
+        "gate_up_grads",
+    )
     late_row_grad = row_grads(*late_pre_grads)
-    early_back, late_row_grad, down_grad_parts, gate_grad, up_grad, expert_hidden = (
+    early_back, late_row_grad, down_grad_parts, gate_grad, up_grad, late_hidden = (
         lax.optimization_barrier(
-            (early_back, late_row_grad, down_grad_parts, gate_grad, up_grad, expert_hidden)
+            (early_back, late_row_grad, down_grad_parts, gate_grad, up_grad, late_hidden)
         )
     )
+    expert_hidden = both_parts(early_hidden, late_hidden)
     late_back = swap(late_row_grad, ("dp", "seq"))
     gate_owned, up_owned = owned_sum(to_owners(gate_grad)), owned_sum(to_owners(up_grad))
     down_owned = owned_sum(down_grad_parts)

time: 603 us -> 611 us (1.013)
  Pallas kernels: 236 us -> 265 us
  local copies, waits for them, and re-layouts: 57.6 us -> 46.1 us
  waiting for transfers between devices: 119 us -> 109 us
  other arithmetic: 27.7 us -> 21.1 us
    pallas_call x1, Pallas kernels: 41.7 us -> 68.1 us  [attention(): pl.pallas_call(functools.partial(attention_kernel, count, heads, kv_heads...]
    all_to_all x6, starting transfers between devices: 29.9 us -> 50.2 us  [swap(): return lax.all_to_all(blocks, axes, split_axis=0, concat_axis=0, tiled=True)]
    ppermute x18, starting transfers between devices: 40.3 us -> 25.9 us  [seq_permutes(): lax.ppermute(block_for(lax.rem(me + step, count)), 'seq', ring)]
    all_to_all x6, waiting for transfers between devices: 29.3 us -> 15.6 us  [swap(): return lax.all_to_all(blocks, axes, split_axis=0, concat_axis=0, tiled=True)]
    unnamed x142 -> x134, local copies, waits for them, and re-layouts: 13.9 us -> 11 us
  transfers between devices with their start and end apart: 24 -> 24, of which waited for: 14 -> 13; matrix products, arithmetic and copies ran while one was open for 24% -> 21% of each run, Pallas kernels for 40% -> 44%
where the time goes in v12:
time: 611 us; the launch traced here: 601 us
  Pallas kernels  265 us (43%)
  waiting for transfers between devices  109 us (18%)
  matrix products  81.5 us (13%)
  starting transfers between devices  76.1 us (12%)
  local copies, waits for them, and re-layouts  46.1 us (8%)
  other arithmetic  21.1 us (3%)
    ppermute x18, waiting for transfers between devices, seq_permutes(): lax.ppermute(block_for(lax.rem(me + step, count)), 'seq', ring)  93.1 us
    dot_general x23, matrix products, dot(): lax.dot_general(left, right, (contract, ((), ())), preferred_element_type...  81.5 us
    pallas_call x1, Pallas kernels, staged_scatter(): pl.pallas_call(functools.partial(scatter_kernel, line, chunks, n, len(ext...  77.3 us
    pallas_call x1, Pallas kernels, staged_gather(): pl.pallas_call(functools.partial(gather_kernel, line, chunks, n, len(extr...  71.4 us
    pallas_call x1, Pallas kernels, attention(): pl.pallas_call(functools.partial(attention_kernel, count, heads, kv_heads...  68.1 us
    all_to_all x6, starting transfers between devices, swap(): return lax.all_to_all(blocks, axes, split_axis=0, concat_axis=0, tiled=True)  50.2 us
    pallas_call x1, Pallas kernels, attention_back(): pl.pallas_call(functools.partial(attention_back_kernel, count, heads, kv_...  33.2 us
    ppermute x18, starting transfers between devices, seq_permutes(): lax.ppermute(block_for(lax.rem(me + step, count)), 'seq', ring)  25.9 us
  transfers between devices with their start and end apart: 24, of which 13 were waited for; matrix products, arithmetic and copies ran while one was open for 21% of the time, Pallas kernels for 44%

profile of v12, /device:TPU:0, one launch (start us, length us, event | category | flops | bytes accessed | tf_op | source)
XLA Modules:
  0.0 601.5 jit_solution(10016513204285617714)
XLA Ops:
  14.7 71.4 %gather_attention_weights.1 = (bf16[2,2,4,2,48,2048]{5,4,3,2,1,0:T(8,128)(2,1)S(1)}, bf16[2,2,4,2,48,128]{5,4,3,2,1,0:T(8,128)(2,1)S(1)}, bf16[2,2,4,2,48,1536]{5,4,3,2,1,0:T(8,128)(2,1)S(1)}) custom-call(bf16[48,2048]{1,0:T(8,128)(2,1)S(1)} %pad_maximum_fusion.1.refs_0_, bf16[48,128]{1,0:T(8,128)(2,1)S(1)} %maximum_maximum_fusion.refs_1_, ...), custom_call_target="tpu_custom_call" | custom-call | bytes 11403264 | tf_op jit(solution)/shard_map/gather_attention_weights/pallas_call | solution.py:243
  96.9 5.6 all-to-all-start
  105.0 4.8 fusion.24.refs_1_
  114.6 68.1 %attention_forward.1 = (bf16[256,1536]{1,0:T(8,128)(2,1)S(1)}, f32[12,256]{1,0:T(8,128)S(1)}, bf16[256,1536]{1,0:T(8,128)(2,1)S(1)}, bf16[4,256,512]{2,1,0:T(8,128)(2,1)S(1)}) custom-call(s32[1]{0:T(128)} %copy.73.refs_0_, f32[256,2048]{1,0:T(8,128)S(1)} %fusion.24.refs_1_, f32[256,128]{1,0:T(8,128)S(1)} %get-tuple-element.187.refs_2_.refs_6_, ...), custom_call_target="tpu_custom_call" | custom-call | bytes 1048576 | tf_op jit(solution)/shard_map/attention_forward/pallas_call | solution.py:496
  192.3 24.1 %all-to-all-start.1 = ((bf16[32,24,1536]{2,1,0:T(8,128)(2,1)}), bf16[32,24,1536]{2,1,0:T(8,128)(2,1)}, u32[]{:S(2)}, u32[]{:S(2)}) async-start(bf16[32,24,1536]{2,1,0:T(8,128)(2,1)} %bitcast.16), calls=%async_computation.1 | async-start | bytes 4718592 | tf_op jit(solution)/shard_map/all_to_all | solution.py:66
  240.7 16.7 %collective-permute-done.6 = bf16[192,1536]{1,0:T(8,128)(2,1)S(1)} collective-permute-done((bf16[192,1536]{1,0:T(8,128)(2,1)S(1)}, bf16[192,1536]{1,0:T(8,128)(2,1)S(1)}, u32[]{:S(2)}, u32[]{:S(2)}) %collective-permute-start.6) | collective-permute-done | bytes 589856 | tf_op jit(solution)/shard_map/ppermute | solution.py:681
  258.3 12.7 %collective-permute-done.7 = bf16[192,1536]{1,0:T(8,128)(2,1)S(1)} collective-permute-done((bf16[192,1536]{1,0:T(8,128)(2,1)S(1)}, bf16[192,1536]{1,0:T(8,128)(2,1)S(1)}, u32[]{:S(2)}, u32[]{:S(2)}) %collective-permute-start.7) | collective-permute-done | bytes 589856 | tf_op jit(solution)/shard_map/ppermute | solution.py:681
  273.8 5.7 all-to-all-start.2
  287.8 6.1 %multiply_convert_fusion.2 = (bf16[768,768]{1,0:T(8,128)(2,1)}, bf16[768,768]{1,0:T(8,128)(2,1)S(1)}, bf16[768,768]{1,0:T(8,128)(2,1)S(1)}) fusion(f32[768,768]{1,0:T(8,128)S(1)} %fusion.41, f32[768,768]{1,0:T(8,128)S(1)} %fusion.42, bf16[768,1536]{1,0:T(8,128)(2,1)} %bitcast.40.refs_0_, bf16[1536,768]{1,0:T(8,128)(2,1)} %bitcast.32), kind=kOutput, calls=%fused_computation.28 | convolution fusion | flops 1820786688 | bytes 12976128 | tf_op jit(solution)/shard_map/dot_general | solution.py:34
  298.4 5.2 add_convert_fusion
  303.6 13.4 %all-to-all-done.2 = bf16[32,16,1536]{2,1,0:T(8,128)(2,1)S(1)} async-done(((bf16[32,16,1536]{2,1,0:T(8,128)(2,1)}), bf16[32,16,1536]{2,1,0:T(8,128)(2,1)S(1)}, u32[]{:S(2)}, u32[]{:S(2)}) %all-to-all-start.2) | async-done | bytes 1572896 | tf_op jit(solution)/shard_map/all_to_all | solution.py:66
  330.9 5.6 down_grads.1
  345.6 9.5 %gate_up_grads.1 = (bf16[1536,768]{1,0:T(8,128)(2,1)}, bf16[1536,768]{1,0:T(8,128)(2,1)}) custom-call(bf16[768,1536]{1,0:T(8,128)(2,1)} %bitcast.40.refs_0_, bf16[512,1536]{1,0:T(8,128)(2,1)S(1)} %bitcast.224, bf16[768,768]{1,0:T(8,128)(2,1)S(1)} %copy-done.7, bf16[512,768]{1,0:T(8,128)(2,1)S(1)} %get-tuple-element.151, bf16[768,768]{1,0:T(8,128)(2,1)S(1)} %copy-done.9, ...), custom_call_target="tpu_custom_call" | custom-call | bytes 1048576 | tf_op jit(solution)/shard_map/gate_up_grads/pallas_call | solution.py:663
  359.4 6.3 %collective-permute-done.9 = bf16[192,1536]{1,0:T(8,128)(2,1)} collective-permute-done((bf16[192,1536]{1,0:T(8,128)(2,1)S(1)}, bf16[192,1536]{1,0:T(8,128)(2,1)}, u32[]{:S(2)}, u32[]{:S(2)}) %collective-permute-start.9) | collective-permute-done | bytes 589856 | tf_op jit(solution)/shard_map/ppermute | solution.py:681
  365.6 12.3 %collective-permute-done.10 = bf16[192,1536]{1,0:T(8,128)(2,1)} collective-permute-done((bf16[192,1536]{1,0:T(8,128)(2,1)S(1)}, bf16[192,1536]{1,0:T(8,128)(2,1)}, u32[]{:S(2)}, u32[]{:S(2)}) %collective-permute-start.10) | collective-permute-done | bytes 589856 | tf_op jit(solution)/shard_map/ppermute | solution.py:681
  379.1 5.0 all-to-all-start.4
  395.0 6.4 %convolution_convert_fusion.2 = bf16[1280,1536]{1,0:T(8,128)(2,1)} fusion(bf16[1280,768]{1,0:T(8,128)(2,1)S(1)} %bitcast.248, bf16[768,1536]{1,0:T(8,128)(2,1)} %bitcast.39), kind=kOutput, calls=%fused_computation.4 | convolution fusion | flops 3021864960 | bytes 8257536 | tf_op jit(solution)/shard_map/dot_general | solution.py:34
  410.2 8.0 %collective-permute-done.12 = bf16[384,768]{1,0:T(8,128)(2,1)S(1)} collective-permute-done((bf16[384,768]{1,0:T(8,128)(2,1)S(1)}, bf16[384,768]{1,0:T(8,128)(2,1)S(1)}, u32[]{:S(2)}, u32[]{:S(2)}) %collective-permute-start.12) | collective-permute-done | bytes 589856 | tf_op jit(solution)/shard_map/ppermute | solution.py:681
  418.3 10.9 %collective-permute-done.13 = bf16[384,768]{1,0:T(8,128)(2,1)S(1)} collective-permute-done((bf16[384,768]{1,0:T(8,128)(2,1)S(1)}, bf16[384,768]{1,0:T(8,128)(2,1)S(1)}, u32[]{:S(2)}, u32[]{:S(2)}) %collective-permute-start.13) | collective-permute-done | bytes 589856 | tf_op jit(solution)/shard_map/ppermute | solution.py:681
  430.7 13.8 %collective-permute-done.15 = bf16[384,768]{1,0:T(8,128)(2,1)S(1)} collective-permute-done((bf16[384,768]{1,0:T(8,128)(2,1)S(1)}, bf16[384,768]{1,0:T(8,128)(2,1)S(1)}, u32[]{:S(2)}, u32[]{:S(2)}) %collective-permute-start.15) | collective-permute-done | bytes 589856 | tf_op jit(solution)/shard_map/ppermute | solution.py:681
  445.7 8.7 %collective-permute-done.16 = bf16[384,768]{1,0:T(8,128)(2,1)S(1)} collective-permute-done((bf16[384,768]{1,0:T(8,128)(2,1)S(1)}, bf16[384,768]{1,0:T(8,128)(2,1)S(1)}, u32[]{:S(2)}, u32[]{:S(2)}) %collective-permute-start.16) | collective-permute-done | bytes 589856 | tf_op jit(solution)/shard_map/ppermute | solution.py:681
  456.6 5.6 all-to-all-start.5
  472.8 33.2 %attention_backward.1 = bf16[256,2048]{1,0:T(8,128)(2,1)S(1)} custom-call(s32[1]{0:T(128)} %copy.73.refs_0_, bf16[256,1536]{1,0:T(8,128)(2,1)S(1)} %copy-done.16, bf16[1024,512]{1,0:T(8,128)(2,1)S(1)} %bitcast.236, bf16[256,1536]{1,0:T(8,128)(2,1)S(1)} %convolution_convert_fusion.5.refs_3_, f32[12,256]{1,0:T(8,128)S(1)} %get-tuple-element.128.refs_4_, ...), custom_call_target="tpu_custom_call" | custom-call | flops 4026531840 | bytes 1048576 | tf_op jit(solution)/shard_map/attention_backward/pallas_call | solution.py:628
  514.7 77.3 %scatter_attention_grads.1 = (f32[48,1536]{1,0:T(8,128)S(1)}, f32[48,128]{1,0:T(8,128)S(1)}, f32[48,2048]{1,0:T(8,128)S(1)}) custom-call(bf16[2,2,4,2,48,1536]{5,4,3,2,1,0:T(8,128)(2,1)S(1)} %bitcast.218, bf16[2,2,4,2,48,128]{5,4,3,2,1,0:T(8,128)(2,1)S(1)} %select_convert_fusion.refs_1_, bf16[2,2,4,2,48,2048]{5,4,3,2,1,0:T(8,128)(2,1)S(1)} %bitcast.217), custom_call_target="tpu_custom_call" | custom-call | bytes 11403264 | tf_op jit(solution)/shard_map/scatter_attention_grads/pallas_call | solution.py:364
  (269 shorter events, 162.1 us)
Async XLA Ops:
  3.7 92.4 %collective-permute-start = (bf16[384,768]{1,0:T(8,128)(2,1)}, bf16[384,768]{1,0:T(8,128)(2,1)S(1)}, u32[]{:S(2)}, u32[]{:S(2)}) collective-permute-start(bf16[384,768]{1,0:T(8,128)(2,1)} %get-tuple-element.172), channel_id=1, source_target_pairs={{0,8},{8,16},{16,24},{24,0},{1,9},{9,17},{17,25},{25,1},{2,10},{10... | collective-permute-start | bytes 1769480 | tf_op jit(solution)/shard_map/ppermute | solution.py:681
  6.6 89.5 %collective-permute-start.1 = (bf16[384,768]{1,0:T(8,128)(2,1)}, bf16[384,768]{1,0:T(8,128)(2,1)S(1)}, u32[]{:S(2)}, u32[]{:S(2)}) collective-permute-start(bf16[384,768]{1,0:T(8,128)(2,1)} %get-tuple-element.174), channel_id=1, source_target_pairs={{0,16},{8,24},{16,0},{24,8},{1,17},{9,25},{17,1},{25,9},{2,18},{10... | collective-permute-start | bytes 1769480 | tf_op jit(solution)/shard_map/ppermute | solution.py:681
  8.1 88.0 %collective-permute-start.2 = (bf16[384,768]{1,0:T(8,128)(2,1)}, bf16[384,768]{1,0:T(8,128)(2,1)}, u32[]{:S(2)}, u32[]{:S(2)}) collective-permute-start(bf16[384,768]{1,0:T(8,128)(2,1)} %get-tuple-element.171), channel_id=1, source_target_pairs={{0,24},{8,0},{16,8},{24,16},{1,25},{9,1},{17,9},{25,17},{2,26},{10... | collective-permute-start | bytes 1769480 | tf_op jit(solution)/shard_map/ppermute | solution.py:681
  96.9 95.4 %all-to-all-start = ((bf16[32,40,1536]{2,1,0:T(8,128)(2,1)}), bf16[32,40,1536]{2,1,0:T(8,128)(2,1)}, u32[]{:S(2)}, u32[]{:S(2)}) async-start(bf16[32,40,1536]{2,1,0:T(8,128)(2,1)} %bitcast.242), calls=%async_computation | async-start | bytes 7864320 | tf_op jit(solution)/shard_map/all_to_all | solution.py:66
  110.0 78.5 %collective-permute-start.3 = (bf16[384,768]{1,0:T(8,128)(2,1)S(1)}, bf16[384,768]{1,0:T(8,128)(2,1)S(1)}, u32[]{:S(2)}, u32[]{:S(2)}) collective-permute-start(bf16[384,768]{1,0:T(8,128)(2,1)S(1)} %get-tuple-element.169), channel_id=1, source_target_pairs={{0,8},{8,16},{16,24},{24,0},{1,9},{9,17},{17,25},{25,1},{2,10},{10... | collective-permute-start | bytes 1769480 | tf_op jit(solution)/shard_map/ppermute | solution.py:681
  111.7 77.6 %collective-permute-start.4 = (bf16[384,768]{1,0:T(8,128)(2,1)S(1)}, bf16[384,768]{1,0:T(8,128)(2,1)S(1)}, u32[]{:S(2)}, u32[]{:S(2)}) collective-permute-start(bf16[384,768]{1,0:T(8,128)(2,1)S(1)} %get-tuple-element.168), channel_id=1, source_target_pairs={{0,16},{8,24},{16,0},{24,8},{1,17},{9,25},{17,1},{25,9},{2,18},{10... | collective-permute-start | bytes 1769480 | tf_op jit(solution)/shard_map/ppermute | solution.py:681
  113.2 77.0 %collective-permute-start.5 = (bf16[384,768]{1,0:T(8,128)(2,1)S(1)}, bf16[384,768]{1,0:T(8,128)(2,1)}, u32[]{:S(2)}, u32[]{:S(2)}) collective-permute-start(bf16[384,768]{1,0:T(8,128)(2,1)S(1)} %get-tuple-element.167), channel_id=1, source_target_pairs={{0,24},{8,0},{16,8},{24,16},{1,25},{9,1},{17,9},{25,17},{2,26},{10... | collective-permute-start | bytes 1769480 | tf_op jit(solution)/shard_map/ppermute | solution.py:681
  192.3 81.5 %all-to-all-start.1 = ((bf16[32,24,1536]{2,1,0:T(8,128)(2,1)}), bf16[32,24,1536]{2,1,0:T(8,128)(2,1)}, u32[]{:S(2)}, u32[]{:S(2)}) async-start(bf16[32,24,1536]{2,1,0:T(8,128)(2,1)} %bitcast.16), calls=%async_computation.1 | async-start | bytes 4718592 | tf_op jit(solution)/shard_map/all_to_all | solution.py:66
  230.0 27.4 %collective-permute-start.6 = (bf16[192,1536]{1,0:T(8,128)(2,1)S(1)}, bf16[192,1536]{1,0:T(8,128)(2,1)S(1)}, u32[]{:S(2)}, u32[]{:S(2)}) collective-permute-start(bf16[192,1536]{1,0:T(8,128)(2,1)S(1)} %get-tuple-element.165), channel_id=1, source_target_pairs={{0,8},{8,16},{16,24},{24,0},{1,9},{9,17},{17,25},{25,1},{2,10},{10... | collective-permute-start | bytes 1769480 | tf_op jit(solution)/shard_map/ppermute | solution.py:681
  231.7 39.3 %collective-permute-start.7 = (bf16[192,1536]{1,0:T(8,128)(2,1)S(1)}, bf16[192,1536]{1,0:T(8,128)(2,1)S(1)}, u32[]{:S(2)}, u32[]{:S(2)}) collective-permute-start(bf16[192,1536]{1,0:T(8,128)(2,1)S(1)} %get-tuple-element.164), channel_id=1, source_target_pairs={{0,16},{8,24},{16,0},{24,8},{1,17},{9,25},{17,1},{25,9},{2,18},{10... | collective-permute-start | bytes 1769480 | tf_op jit(solution)/shard_map/ppermute | solution.py:681
  233.2 39.8 %collective-permute-start.8 = (bf16[192,1536]{1,0:T(8,128)(2,1)S(1)}, bf16[192,1536]{1,0:T(8,128)(2,1)S(1)}, u32[]{:S(2)}, u32[]{:S(2)}) collective-permute-start(bf16[192,1536]{1,0:T(8,128)(2,1)S(1)} %get-tuple-element.163), channel_id=1, source_target_pairs={{0,24},{8,0},{16,8},{24,16},{1,25},{9,1},{17,9},{25,17},{2,26},{10... | collective-permute-start | bytes 1769480 | tf_op jit(solution)/shard_map/ppermute | solution.py:681
  273.8 43.2 %all-to-all-start.2 = ((bf16[32,16,1536]{2,1,0:T(8,128)(2,1)}), bf16[32,16,1536]{2,1,0:T(8,128)(2,1)S(1)}, u32[]{:S(2)}, u32[]{:S(2)}) async-start(bf16[32,16,1536]{2,1,0:T(8,128)(2,1)} %bitcast.239), calls=%async_computation.2 | async-start | bytes 3145728 | tf_op jit(solution)/shard_map/all_to_all | solution.py:66
  317.0 62.1 %all-to-all-start.3 = ((bf16[32,24,1536]{2,1,0:T(8,128)(2,1)}), bf16[32,24,1536]{2,1,0:T(8,128)(2,1)}, u32[]{:S(2)}, u32[]{:S(2)}) async-start(bf16[32,24,1536]{2,1,0:T(8,128)(2,1)} %bitcast.247), calls=%async_computation.3 | async-start | bytes 4718592 | tf_op jit(solution)/shard_map/all_to_all | solution.py:66
  337.6 28.0 %collective-permute-start.9 = (bf16[192,1536]{1,0:T(8,128)(2,1)S(1)}, bf16[192,1536]{1,0:T(8,128)(2,1)}, u32[]{:S(2)}, u32[]{:S(2)}) collective-permute-start(bf16[192,1536]{1,0:T(8,128)(2,1)S(1)} %get-tuple-element.161), channel_id=1, source_target_pairs={{0,8},{8,16},{16,24},{24,0},{1,9},{9,17},{17,25},{25,1},{2,10},{10... | collective-permute-start | bytes 1769480 | tf_op jit(solution)/shard_map/ppermute | solution.py:681
  339.3 38.7 %collective-permute-start.10 = (bf16[192,1536]{1,0:T(8,128)(2,1)S(1)}, bf16[192,1536]{1,0:T(8,128)(2,1)}, u32[]{:S(2)}, u32[]{:S(2)}) collective-permute-start(bf16[192,1536]{1,0:T(8,128)(2,1)S(1)} %get-tuple-element.160), channel_id=1, source_target_pairs={{0,16},{8,24},{16,0},{24,8},{1,17},{9,25},{17,1},{25,9},{2,18},{10... | collective-permute-start | bytes 1769480 | tf_op jit(solution)/shard_map/ppermute | solution.py:681
  340.8 38.4 %collective-permute-start.11 = (bf16[192,1536]{1,0:T(8,128)(2,1)S(1)}, bf16[192,1536]{1,0:T(8,128)(2,1)}, u32[]{:S(2)}, u32[]{:S(2)}) collective-permute-start(bf16[192,1536]{1,0:T(8,128)(2,1)S(1)} %get-tuple-element.159), channel_id=1, source_target_pairs={{0,24},{8,0},{16,8},{24,16},{1,25},{9,1},{17,9},{25,17},{2,26},{10... | collective-permute-start | bytes 1769480 | tf_op jit(solution)/shard_map/ppermute | solution.py:681
  379.1 77.5 %all-to-all-start.4 = ((bf16[32,16,1536]{2,1,0:T(8,128)(2,1)}), bf16[32,16,1536]{2,1,0:T(8,128)(2,1)S(1)}, u32[]{:S(2)}, u32[]{:S(2)}) async-start(bf16[32,16,1536]{2,1,0:T(8,128)(2,1)} %bitcast.50), calls=%async_computation.4 | async-start | bytes 3145728 | tf_op jit(solution)/shard_map/all_to_all | solution.py:66
  385.8 32.4 %collective-permute-start.12 = (bf16[384,768]{1,0:T(8,128)(2,1)S(1)}, bf16[384,768]{1,0:T(8,128)(2,1)S(1)}, u32[]{:S(2)}, u32[]{:S(2)}) collective-permute-start(bf16[384,768]{1,0:T(8,128)(2,1)S(1)} %get-tuple-element.158), channel_id=1, source_target_pairs={{0,8},{8,16},{16,24},{24,0},{1,9},{9,17},{17,25},{25,1},{2,10},{10... | collective-permute-start | bytes 1769480 | tf_op jit(solution)/shard_map/ppermute | solution.py:681
  387.6 41.5 %collective-permute-start.13 = (bf16[384,768]{1,0:T(8,128)(2,1)S(1)}, bf16[384,768]{1,0:T(8,128)(2,1)S(1)}, u32[]{:S(2)}, u32[]{:S(2)}) collective-permute-start(bf16[384,768]{1,0:T(8,128)(2,1)S(1)} %get-tuple-element.157), channel_id=1, source_target_pairs={{0,16},{8,24},{16,0},{24,8},{1,17},{9,25},{17,1},{25,9},{2,18},{10... | collective-permute-start | bytes 1769480 | tf_op jit(solution)/shard_map/ppermute | solution.py:681
  389.1 41.5 %collective-permute-start.14 = (bf16[384,768]{1,0:T(8,128)(2,1)S(1)}, bf16[384,768]{1,0:T(8,128)(2,1)S(1)}, u32[]{:S(2)}, u32[]{:S(2)}) collective-permute-start(bf16[384,768]{1,0:T(8,128)(2,1)S(1)} %get-tuple-element.156), channel_id=1, source_target_pairs={{0,24},{8,0},{16,8},{24,16},{1,25},{9,1},{17,9},{25,17},{2,26},{10... | collective-permute-start | bytes 1769480 | tf_op jit(solution)/shard_map/ppermute | solution.py:681
  390.7 53.9 %collective-permute-start.15 = (bf16[384,768]{1,0:T(8,128)(2,1)S(1)}, bf16[384,768]{1,0:T(8,128)(2,1)S(1)}, u32[]{:S(2)}, u32[]{:S(2)}) collective-permute-start(bf16[384,768]{1,0:T(8,128)(2,1)S(1)} %get-tuple-element.155), channel_id=1, source_target_pairs={{0,8},{8,16},{16,24},{24,0},{1,9},{9,17},{17,25},{25,1},{2,10},{10... | collective-permute-start | bytes 1769480 | tf_op jit(solution)/shard_map/ppermute | solution.py:681
  409.6 44.7 %collective-permute-start.16 = (bf16[384,768]{1,0:T(8,128)(2,1)S(1)}, bf16[384,768]{1,0:T(8,128)(2,1)S(1)}, u32[]{:S(2)}, u32[]{:S(2)}) collective-permute-start(bf16[384,768]{1,0:T(8,128)(2,1)S(1)} %get-tuple-element.154), channel_id=1, source_target_pairs={{0,16},{8,24},{16,0},{24,8},{1,17},{9,25},{17,1},{25,9},{2,18},{10... | collective-permute-start | bytes 1769480 | tf_op jit(solution)/shard_map/ppermute | solution.py:681
  418.2 37.3 %collective-permute-start.17 = (bf16[384,768]{1,0:T(8,128)(2,1)S(1)}, bf16[384,768]{1,0:T(8,128)(2,1)S(1)}, u32[]{:S(2)}, u32[]{:S(2)}) collective-permute-start(bf16[384,768]{1,0:T(8,128)(2,1)S(1)} %get-tuple-element.153), channel_id=1, source_target_pairs={{0,24},{8,0},{16,8},{24,16},{1,25},{9,1},{17,9},{25,17},{2,26},{10... | collective-permute-start | bytes 1769480 | tf_op jit(solution)/shard_map/ppermute | solution.py:681
  456.6 137.8 %all-to-all-start.5 = ((bf16[32,40,1536]{2,1,0:T(8,128)(2,1)}), bf16[32,40,1536]{2,1,0:T(8,128)(2,1)}, u32[]{:S(2)}, u32[]{:S(2)}) async-start(bf16[32,40,1536]{2,1,0:T(8,128)(2,1)} %bitcast.241), calls=%async_computation.5 | async-start | bytes 7864320 | tf_op jit(solution)/shard_map/all_to_all | solution.py:66
  (66 other events, 1160.9 us)

commit v13 on v12

--- a/solution.py
+++ b/solution.py
@@ -245,7 +245,7 @@
         out_shape=[jax.ShapeDtypeStruct(shape + (x.shape[1],), BF16) for x in arrays]
         + [jax.ShapeDtypeStruct((seq_count,) + x.shape[1:], BF16) for x in extras],
         in_specs=[pl.BlockSpec(memory_space=pl.ANY)] * count,
-        out_specs=[pl.BlockSpec(memory_space=pl.ANY)] * count,
+        out_specs=[pl.BlockSpec(memory_space=pltpu.HBM)] * count,
         scratch_shapes=[
             pltpu.SemaphoreType.DMA((m, 2 + line)),
             pltpu.SemaphoreType.DMA((m, 2 + line)),
@@ -779,8 +779,7 @@
     inputs = hidden_in[0].astype(F32)
     scale_one = lax.rsqrt(jnp.mean(inputs * inputs, axis=-1, keepdims=True) + EPSILON)
     normed = (inputs * scale_one * gain_one).astype(BF16)
-    projected, w_up = lax.optimization_barrier((nn(normed, packed_full), w_up))
-    up_parts = expert_pieces(w_up)
+    projected = nn(normed, packed_full)
     cosines, sines = cosine_lookup[:, 0], sine_lookup[:, 0]
     cosines = jnp.concatenate([cosines, cosines], axis=1)
     sines = jnp.concatenate([-sines, sines], axis=1)
@@ -788,6 +787,8 @@
         lengths, projected, cosines, sines, q_width, 1
     )
     kv_all = kv_all.reshape(extent, 2 * kv_width)
+    attended, w_up = lax.optimization_barrier((attended, w_up))
+    up_parts = expert_pieces(w_up)
     middle = inputs + nn(attended, out_full)
     scale_two = lax.rsqrt(jnp.mean(middle * middle, axis=-1, keepdims=True) + EPSILON)
     moe_input = (middle * scale_two * gain_two).astype(BF16)
@@ -860,28 +861,28 @@
     def flat(*parts):
         return [part.reshape(-1, part.shape[-1]) for part in parts]
 
-    (down_grad,) = weight_grads(
-        flat(early_hidden, late_hidden), [flat(early_grads, late_grads)], "down_grads"
-    )
-    late_rows, late_pre_grads, down_grad = lax.optimization_barrier(
-        (late_rows, late_pre_grads, down_grad)
-    )
-    down_grad_parts = to_owners(down_grad)
     gate_grad, up_grad = weight_grads(
         flat(early_rows, late_rows),
         [flat(*pair) for pair in zip(early_pre_grads, late_pre_grads, strict=True)],
         "gate_up_grads",
     )
+    late_pre_grads, late_hidden, gate_grad, up_grad = lax.optimization_barrier(
+        (late_pre_grads, late_hidden, gate_grad, up_grad)
+    )
+    gate_grad_parts, up_grad_parts = to_owners(gate_grad), to_owners(up_grad)
     late_row_grad = row_grads(*late_pre_grads)
-    early_back, late_row_grad, down_grad_parts, gate_grad, up_grad, late_hidden = (
+    (down_grad,) = weight_grads(
+        flat(early_hidden, late_hidden), [flat(early_grads, late_grads)], "down_grads"
+    )
+    early_back, late_row_grad, gate_grad_parts, up_grad_parts, down_grad, late_hidden = (
         lax.optimization_barrier(
-            (early_back, late_row_grad, down_grad_parts, gate_grad, up_grad, late_hidden)
+            (early_back, late_row_grad, gate_grad_parts, up_grad_parts, down_grad, late_hidden)
         )
     )
     expert_hidden = both_parts(early_hidden, late_hidden)
     late_back = swap(late_row_grad, ("dp", "seq"))
-    gate_owned, up_owned = owned_sum(to_owners(gate_grad)), owned_sum(to_owners(up_grad))
-    down_owned = owned_sum(down_grad_parts)
+    down_owned = owned_sum(to_owners(down_grad))
+    gate_owned, up_owned = owned_sum(gate_grad_parts), owned_sum(up_grad_parts)
     expert_out = nn(expert_hidden, down_full).astype(BF16)
     expert_out, late_back, gate_owned, up_owned, down_owned = lax.optimization_barrier(
         (expert_out, late_back, gate_owned, up_owned, down_owned)

time: 611 us -> 608 us (level)
  Pallas kernels: 265 us -> 240 us
  waiting for transfers between devices: 109 us -> 124 us
    pallas_call x1, Pallas kernels: 68.1 us -> 41.1 us  [attention(): pl.pallas_call(functools.partial(attention_kernel, count, heads, kv_heads...]
    ppermute x18, waiting for transfers between devices: 93.1 us -> 111 us  [seq_permutes(): lax.ppermute(block_for(lax.rem(me + step, count)), 'seq', ring)]
    all_to_all x6, starting transfers between devices: 50.2 us -> 33.3 us  [swap(): return lax.all_to_all(blocks, axes, split_axis=0, concat_axis=0, tiled=True)]
    ppermute x18, starting transfers between devices: 25.9 us -> 40 us  [seq_permutes(): lax.ppermute(block_for(lax.rem(me + step, count)), 'seq', ring)]
    dynamic_update_slice x12 -> x11, other arithmetic: 9.43 us -> 13.6 us  [in_seq_order(): lax.dynamic_update_index_in_dim(whole, piece.astype(dtype), place, 0)]
  transfers between devices with their start and end apart: 24 -> 24, of which waited for: 13 -> 11; matrix products, arithmetic and copies ran while one was open for 21% -> 23% of each run, Pallas kernels for 44% -> 40%
where the time goes in v13:
time: 608 us; the launch traced here: 598 us
  Pallas kernels  240 us (39%)
  waiting for transfers between devices  124 us (20%)
  matrix products  83.7 us (14%)
  starting transfers between devices  73.3 us (12%)
  local copies, waits for them, and re-layouts  50 us (8%)
  other arithmetic  24.7 us (4%)
    ppermute x18, waiting for transfers between devices, seq_permutes(): lax.ppermute(block_for(lax.rem(me + step, count)), 'seq', ring)  111 us
    dot_general x23, matrix products, dot(): lax.dot_general(left, right, (contract, ((), ())), preferred_element_type...  83.7 us
    pallas_call x1, Pallas kernels, staged_scatter(): pl.pallas_call(functools.partial(scatter_kernel, line, chunks, n, len(ext...  75.8 us
    pallas_call x1, Pallas kernels, staged_gather(): pl.pallas_call(functools.partial(gather_kernel, line, chunks, n, len(extr...  71.6 us
    pallas_call x1, Pallas kernels, attention(): pl.pallas_call(functools.partial(attention_kernel, count, heads, kv_heads...  41.1 us
    ppermute x18, starting transfers between devices, seq_permutes(): lax.ppermute(block_for(lax.rem(me + step, count)), 'seq', ring)  40 us
    pallas_call x1, Pallas kernels, attention_back(): pl.pallas_call(functools.partial(attention_back_kernel, count, heads, kv_...  35.9 us
    all_to_all x6, starting transfers between devices, swap(): return lax.all_to_all(blocks, axes, split_axis=0, concat_axis=0, tiled=True)  33.3 us
  transfers between devices with their start and end apart: 24, of which 11 were waited for; matrix products, arithmetic and copies ran while one was open for 23% of the time, Pallas kernels for 40%

profile of v13, /device:TPU:0, one launch (start us, length us, event | category | flops | bytes accessed | tf_op | source)
XLA Modules:
  0.0 598.1 jit_solution(10652190643662164955)
XLA Ops:
  14.5 71.6 %gather_attention_weights.1 = (bf16[2,2,4,2,48,2048]{5,4,3,2,1,0:T(8,128)(2,1)S(1)}, bf16[2,2,4,2,48,128]{5,4,3,2,1,0:T(8,128)(2,1)S(1)}, bf16[2,2,4,2,48,1536]{5,4,3,2,1,0:T(8,128)(2,1)S(1)}) custom-call(bf16[48,2048]{1,0:T(8,128)(2,1)S(1)} %pad_maximum_fusion.1.refs_0_, bf16[48,128]{1,0:T(8,128)(2,1)S(1)} %maximum_maximum_fusion.refs_1_, ...), custom_call_target="tpu_custom_call" | custom-call | bytes 11403264 | tf_op jit(solution)/shard_map/gather_attention_weights/pallas_call | solution.py:243
  97.1 5.6 all-to-all-start
  110.2 41.1 %attention_forward.1 = (bf16[256,1536]{1,0:T(8,128)(2,1)S(1)}, f32[12,256]{1,0:T(8,128)S(1)}, bf16[256,1536]{1,0:T(8,128)(2,1)S(1)}, bf16[4,256,512]{2,1,0:T(8,128)(2,1)S(1)}) custom-call(s32[1]{0:T(128)} %copy.73.refs_0_, f32[256,2048]{1,0:T(8,128)S(1)} %fusion.24.refs_1_, f32[256,128]{1,0:T(8,128)S(1)} %pad_maximum_fusion.2.refs_2_.refs_6_, ...), custom_call_target="tpu_custom_call" | custom-call | bytes 1048576 | tf_op jit(solution)/shard_map/attention_forward/pallas_call | solution.py:496
  152.6 18.8 %collective-permute-start.4 = (bf16[384,768]{1,0:T(8,128)(2,1)S(1)}, bf16[384,768]{1,0:T(8,128)(2,1)S(1)}, u32[]{:S(2)}, u32[]{:S(2)}) collective-permute-start(bf16[384,768]{1,0:T(8,128)(2,1)S(1)} %get-tuple-element.177), channel_id=1, source_target_pairs={{0,16},{8,24},{16,0},{24,8},{1,17},{9,25},{17,1},{25,9},{2,18},{10... | collective-permute-start | bytes 1769480 | tf_op jit(solution)/shard_map/ppermute | solution.py:681
  179.5 12.2 %collective-permute-done.3 = bf16[384,768]{1,0:T(8,128)(2,1)S(1)} collective-permute-done((bf16[384,768]{1,0:T(8,128)(2,1)S(1)}, bf16[384,768]{1,0:T(8,128)(2,1)S(1)}, u32[]{:S(2)}, u32[]{:S(2)}) %collective-permute-start.3) | collective-permute-done | bytes 589856 | tf_op jit(solution)/shard_map/ppermute | solution.py:681
  192.5 9.2 %collective-permute-done.4 = bf16[384,768]{1,0:T(8,128)(2,1)S(1)} collective-permute-done((bf16[384,768]{1,0:T(8,128)(2,1)S(1)}, bf16[384,768]{1,0:T(8,128)(2,1)S(1)}, u32[]{:S(2)}, u32[]{:S(2)}) %collective-permute-start.4) | collective-permute-done | bytes 589856 | tf_op jit(solution)/shard_map/ppermute | solution.py:681
  202.5 5.2 all-to-all-start.1
  232.1 16.8 %collective-permute-done.6 = bf16[192,1536]{1,0:T(8,128)(2,1)S(1)} collective-permute-done((bf16[192,1536]{1,0:T(8,128)(2,1)S(1)}, bf16[192,1536]{1,0:T(8,128)(2,1)S(1)}, u32[]{:S(2)}, u32[]{:S(2)}) %collective-permute-start.6) | collective-permute-done | bytes 589856 | tf_op jit(solution)/shard_map/ppermute | solution.py:681
  249.8 12.6 %collective-permute-done.7 = bf16[192,1536]{1,0:T(8,128)(2,1)S(1)} collective-permute-done((bf16[192,1536]{1,0:T(8,128)(2,1)S(1)}, bf16[192,1536]{1,0:T(8,128)(2,1)S(1)}, u32[]{:S(2)}, u32[]{:S(2)}) %collective-permute-start.7) | collective-permute-done | bytes 589856 | tf_op jit(solution)/shard_map/ppermute | solution.py:681
  265.2 5.7 all-to-all-start.2
  279.1 6.1 %multiply_convert_fusion.2 = (bf16[768,768]{1,0:T(8,128)(2,1)}, bf16[768,768]{1,0:T(8,128)(2,1)S(1)}, bf16[768,768]{1,0:T(8,128)(2,1)S(1)}) fusion(f32[768,768]{1,0:T(8,128)S(1)} %fusion.41, f32[768,768]{1,0:T(8,128)S(1)} %fusion.42, bf16[768,1536]{1,0:T(8,128)(2,1)} %bitcast.40.refs_0_, bf16[1536,768]{1,0:T(8,128)(2,1)} %bitcast.32), kind=kOutput, calls=%fused_computation.28 | convolution fusion | flops 1820786688 | bytes 12976128 | tf_op jit(solution)/shard_map/dot_general | solution.py:34
  295.0 13.4 %all-to-all-done.2 = bf16[32,16,1536]{2,1,0:T(8,128)(2,1)S(1)} async-done(((bf16[32,16,1536]{2,1,0:T(8,128)(2,1)}), bf16[32,16,1536]{2,1,0:T(8,128)(2,1)S(1)}, u32[]{:S(2)}, u32[]{:S(2)}) %all-to-all-start.2) | async-done | bytes 1572896 | tf_op jit(solution)/shard_map/all_to_all | solution.py:66
  322.4 9.8 %gate_up_grads.1 = (bf16[1536,768]{1,0:T(8,128)(2,1)}, bf16[1536,768]{1,0:T(8,128)(2,1)}) custom-call(bf16[768,1536]{1,0:T(8,128)(2,1)} %bitcast.40.refs_0_, bf16[512,1536]{1,0:T(8,128)(2,1)S(1)} %bitcast.230, bf16[768,768]{1,0:T(8,128)(2,1)S(1)} %copy-done.8, bf16[512,768]{1,0:T(8,128)(2,1)S(1)} %get-tuple-element.159.refs_3_, ...), custom_call_target="tpu_custom_call" | custom-call | bytes 1048576 | tf_op jit(solution)/shard_map/gate_up_grads/pallas_call | solution.py:663
  341.8 18.7 %collective-permute-done.9 = bf16[384,768]{1,0:T(8,128)(2,1)S(1)} collective-permute-done((bf16[384,768]{1,0:T(8,128)(2,1)S(1)}, bf16[384,768]{1,0:T(8,128)(2,1)S(1)}, u32[]{:S(2)}, u32[]{:S(2)}) %collective-permute-start.9) | collective-permute-done | bytes 589856 | tf_op jit(solution)/shard_map/ppermute | solution.py:681
  364.6 5.4 down_grads.1
  374.3 13.1 %collective-permute-done.12 = bf16[384,768]{1,0:T(8,128)(2,1)S(1)} collective-permute-done((bf16[384,768]{1,0:T(8,128)(2,1)S(1)}, bf16[384,768]{1,0:T(8,128)(2,1)S(1)}, u32[]{:S(2)}, u32[]{:S(2)}) %collective-permute-start.12) | collective-permute-done | bytes 589856 | tf_op jit(solution)/shard_map/ppermute | solution.py:681
  387.4 11.2 %collective-permute-done.13 = bf16[384,768]{1,0:T(8,128)(2,1)} collective-permute-done((bf16[384,768]{1,0:T(8,128)(2,1)S(1)}, bf16[384,768]{1,0:T(8,128)(2,1)}, u32[]{:S(2)}, u32[]{:S(2)}) %collective-permute-start.13) | collective-permute-done | bytes 589856 | tf_op jit(solution)/shard_map/ppermute | solution.py:681
  398.6 7.0 %all-to-all-start.4 = ((bf16[32,16,1536]{2,1,0:T(8,128)(2,1)}), bf16[32,16,1536]{2,1,0:T(8,128)(2,1)}, u32[]{:S(2)}, u32[]{:S(2)}) async-start(bf16[32,16,1536]{2,1,0:T(8,128)(2,1)} %bitcast.250), calls=%async_computation.4 | async-start | bytes 3145728 | tf_op jit(solution)/shard_map/all_to_all | solution.py:66
  420.4 6.4 %convolution_convert_fusion.2 = bf16[1280,1536]{1,0:T(8,128)(2,1)} fusion(bf16[1280,768]{1,0:T(8,128)(2,1)S(1)} %bitcast.249, bf16[768,1536]{1,0:T(8,128)(2,1)} %bitcast.39), kind=kOutput, calls=%fused_computation.4 | convolution fusion | flops 3021864960 | bytes 8257536 | tf_op jit(solution)/shard_map/dot_general | solution.py:34
  433.9 5.8 collective-permute-done.15
  440.8 9.7 %collective-permute-done.16 = bf16[192,1536]{1,0:T(8,128)(2,1)S(1)} collective-permute-done((bf16[192,1536]{1,0:T(8,128)(2,1)S(1)}, bf16[192,1536]{1,0:T(8,128)(2,1)S(1)}, u32[]{:S(2)}, u32[]{:S(2)}) %collective-permute-start.16) | collective-permute-done | bytes 589856 | tf_op jit(solution)/shard_map/ppermute | solution.py:681
  452.9 5.5 all-to-all-start.5
  469.7 35.9 %attention_backward.1 = bf16[256,2048]{1,0:T(8,128)(2,1)S(1)} custom-call(s32[1]{0:T(128)} %copy.73.refs_0_, bf16[256,1536]{1,0:T(8,128)(2,1)S(1)} %copy-done.21, bf16[1024,512]{1,0:T(8,128)(2,1)S(1)} %bitcast.240, bf16[256,1536]{1,0:T(8,128)(2,1)S(1)} %convolution_convert_fusion.5.refs_3_, f32[12,256]{1,0:T(8,128)S(1)} %get-tuple-element.136.refs_4_, ...), custom_call_target="tpu_custom_call" | custom-call | flops 4026531840 | bytes 1048576 | tf_op jit(solution)/shard_map/attention_backward/pallas_call | solution.py:628
  513.0 75.8 %scatter_attention_grads.1 = (f32[48,1536]{1,0:T(8,128)S(1)}, f32[48,128]{1,0:T(8,128)S(1)}, f32[48,2048]{1,0:T(8,128)S(1)}) custom-call(bf16[2,2,4,2,48,1536]{5,4,3,2,1,0:T(8,128)(2,1)S(1)} %bitcast.223, bf16[2,2,4,2,48,128]{5,4,3,2,1,0:T(8,128)(2,1)S(1)} %select_convert_fusion.refs_1_, bf16[2,2,4,2,48,2048]{5,4,3,2,1,0:T(8,128)(2,1)S(1)} %bitcast.222), custom_call_target="tpu_custom_call" | custom-call | bytes 11403264 | tf_op jit(solution)/shard_map/scatter_attention_grads/pallas_call | solution.py:364
  (286 shorter events, 172.4 us)
Async XLA Ops:
  3.6 92.4 %collective-permute-start = (bf16[384,768]{1,0:T(8,128)(2,1)}, bf16[384,768]{1,0:T(8,128)(2,1)S(1)}, u32[]{:S(2)}, u32[]{:S(2)}) collective-permute-start(bf16[384,768]{1,0:T(8,128)(2,1)} %get-tuple-element.181), channel_id=1, source_target_pairs={{0,8},{8,16},{16,24},{24,0},{1,9},{9,17},{17,25},{25,1},{2,10},{10... | collective-permute-start | bytes 1769480 | tf_op jit(solution)/shard_map/ppermute | solution.py:681
  6.6 89.5 %collective-permute-start.1 = (bf16[384,768]{1,0:T(8,128)(2,1)}, bf16[384,768]{1,0:T(8,128)(2,1)S(1)}, u32[]{:S(2)}, u32[]{:S(2)}) collective-permute-start(bf16[384,768]{1,0:T(8,128)(2,1)} %get-tuple-element.183), channel_id=1, source_target_pairs={{0,16},{8,24},{16,0},{24,8},{1,17},{9,25},{17,1},{25,9},{2,18},{10... | collective-permute-start | bytes 1769480 | tf_op jit(solution)/shard_map/ppermute | solution.py:681
  8.1 88.0 %collective-permute-start.2 = (bf16[384,768]{1,0:T(8,128)(2,1)}, bf16[384,768]{1,0:T(8,128)(2,1)}, u32[]{:S(2)}, u32[]{:S(2)}) collective-permute-start(bf16[384,768]{1,0:T(8,128)(2,1)} %get-tuple-element.180), channel_id=1, source_target_pairs={{0,24},{8,0},{16,8},{24,16},{1,25},{9,1},{17,9},{25,17},{2,26},{10... | collective-permute-start | bytes 1769480 | tf_op jit(solution)/shard_map/ppermute | solution.py:681
  97.1 105.4 %all-to-all-start = ((bf16[32,40,1536]{2,1,0:T(8,128)(2,1)}), bf16[32,40,1536]{2,1,0:T(8,128)(2,1)}, u32[]{:S(2)}, u32[]{:S(2)}) async-start(bf16[32,40,1536]{2,1,0:T(8,128)(2,1)} %bitcast.245), calls=%async_computation | async-start | bytes 7864320 | tf_op jit(solution)/shard_map/all_to_all | solution.py:66
  152.6 39.1 %collective-permute-start.3 = (bf16[384,768]{1,0:T(8,128)(2,1)S(1)}, bf16[384,768]{1,0:T(8,128)(2,1)S(1)}, u32[]{:S(2)}, u32[]{:S(2)}) collective-permute-start(bf16[384,768]{1,0:T(8,128)(2,1)S(1)} %get-tuple-element.178), channel_id=1, source_target_pairs={{0,8},{8,16},{16,24},{24,0},{1,9},{9,17},{17,25},{25,1},{2,10},{10... | collective-permute-start | bytes 1769480 | tf_op jit(solution)/shard_map/ppermute | solution.py:681
  152.6 49.1 %collective-permute-start.4 = (bf16[384,768]{1,0:T(8,128)(2,1)S(1)}, bf16[384,768]{1,0:T(8,128)(2,1)S(1)}, u32[]{:S(2)}, u32[]{:S(2)}) collective-permute-start(bf16[384,768]{1,0:T(8,128)(2,1)S(1)} %get-tuple-element.177), channel_id=1, source_target_pairs={{0,16},{8,24},{16,0},{24,8},{1,17},{9,25},{17,1},{25,9},{2,18},{10... | collective-permute-start | bytes 1769480 | tf_op jit(solution)/shard_map/ppermute | solution.py:681
  171.4 31.1 %collective-permute-start.5 = (bf16[384,768]{1,0:T(8,128)(2,1)S(1)}, bf16[384,768]{1,0:T(8,128)(2,1)}, u32[]{:S(2)}, u32[]{:S(2)}) collective-permute-start(bf16[384,768]{1,0:T(8,128)(2,1)S(1)} %get-tuple-element.176), channel_id=1, source_target_pairs={{0,24},{8,0},{16,8},{24,16},{1,25},{9,1},{17,9},{25,17},{2,26},{10... | collective-permute-start | bytes 1769480 | tf_op jit(solution)/shard_map/ppermute | solution.py:681
  202.5 62.7 %all-to-all-start.1 = ((bf16[32,24,1536]{2,1,0:T(8,128)(2,1)}), bf16[32,24,1536]{2,1,0:T(8,128)(2,1)}, u32[]{:S(2)}, u32[]{:S(2)}) async-start(bf16[32,24,1536]{2,1,0:T(8,128)(2,1)} %bitcast.16), calls=%async_computation.1 | async-start | bytes 4718592 | tf_op jit(solution)/shard_map/all_to_all | solution.py:66
  221.5 27.5 %collective-permute-start.6 = (bf16[192,1536]{1,0:T(8,128)(2,1)S(1)}, bf16[192,1536]{1,0:T(8,128)(2,1)S(1)}, u32[]{:S(2)}, u32[]{:S(2)}) collective-permute-start(bf16[192,1536]{1,0:T(8,128)(2,1)S(1)} %get-tuple-element.174), channel_id=1, source_target_pairs={{0,8},{8,16},{16,24},{24,0},{1,9},{9,17},{17,25},{25,1},{2,10},{10... | collective-permute-start | bytes 1769480 | tf_op jit(solution)/shard_map/ppermute | solution.py:681
  223.2 39.3 %collective-permute-start.7 = (bf16[192,1536]{1,0:T(8,128)(2,1)S(1)}, bf16[192,1536]{1,0:T(8,128)(2,1)S(1)}, u32[]{:S(2)}, u32[]{:S(2)}) collective-permute-start(bf16[192,1536]{1,0:T(8,128)(2,1)S(1)} %get-tuple-element.173), channel_id=1, source_target_pairs={{0,16},{8,24},{16,0},{24,8},{1,17},{9,25},{17,1},{25,9},{2,18},{10... | collective-permute-start | bytes 1769480 | tf_op jit(solution)/shard_map/ppermute | solution.py:681
  224.6 39.7 %collective-permute-start.8 = (bf16[192,1536]{1,0:T(8,128)(2,1)S(1)}, bf16[192,1536]{1,0:T(8,128)(2,1)S(1)}, u32[]{:S(2)}, u32[]{:S(2)}) collective-permute-start(bf16[192,1536]{1,0:T(8,128)(2,1)S(1)} %get-tuple-element.172), channel_id=1, source_target_pairs={{0,24},{8,0},{16,8},{24,16},{1,25},{9,1},{17,9},{25,17},{2,26},{10... | collective-permute-start | bytes 1769480 | tf_op jit(solution)/shard_map/ppermute | solution.py:681
  265.2 43.2 %all-to-all-start.2 = ((bf16[32,16,1536]{2,1,0:T(8,128)(2,1)}), bf16[32,16,1536]{2,1,0:T(8,128)(2,1)S(1)}, u32[]{:S(2)}, u32[]{:S(2)}) async-start(bf16[32,16,1536]{2,1,0:T(8,128)(2,1)} %bitcast.243), calls=%async_computation.2 | async-start | bytes 3145728 | tf_op jit(solution)/shard_map/all_to_all | solution.py:66
  308.4 90.2 %all-to-all-start.3 = ((bf16[32,24,1536]{2,1,0:T(8,128)(2,1)}), bf16[32,24,1536]{2,1,0:T(8,128)(2,1)}, u32[]{:S(2)}, u32[]{:S(2)}) async-start(bf16[32,24,1536]{2,1,0:T(8,128)(2,1)} %bitcast.246), calls=%async_computation.3 | async-start | bytes 4718592 | tf_op jit(solution)/shard_map/all_to_all | solution.py:66
  334.9 25.6 %collective-permute-start.9 = (bf16[384,768]{1,0:T(8,128)(2,1)S(1)}, bf16[384,768]{1,0:T(8,128)(2,1)S(1)}, u32[]{:S(2)}, u32[]{:S(2)}) collective-permute-start(bf16[384,768]{1,0:T(8,128)(2,1)S(1)} %get-tuple-element.170), channel_id=1, source_target_pairs={{0,8},{8,16},{16,24},{24,0},{1,9},{9,17},{17,25},{25,1},{2,10},{10... | collective-permute-start | bytes 1769480 | tf_op jit(solution)/shard_map/ppermute | solution.py:681
  336.6 37.7 %collective-permute-start.10 = (bf16[384,768]{1,0:T(8,128)(2,1)S(1)}, bf16[384,768]{1,0:T(8,128)(2,1)}, u32[]{:S(2)}, u32[]{:S(2)}) collective-permute-start(bf16[384,768]{1,0:T(8,128)(2,1)S(1)} %get-tuple-element.169), channel_id=1, source_target_pairs={{0,16},{8,24},{16,0},{24,8},{1,17},{9,25},{17,1},{25,9},{2,18},{10... | collective-permute-start | bytes 1769480 | tf_op jit(solution)/shard_map/ppermute | solution.py:681
  338.1 36.2 %collective-permute-start.11 = (bf16[384,768]{1,0:T(8,128)(2,1)S(1)}, bf16[384,768]{1,0:T(8,128)(2,1)}, u32[]{:S(2)}, u32[]{:S(2)}) collective-permute-start(bf16[384,768]{1,0:T(8,128)(2,1)S(1)} %get-tuple-element.168), channel_id=1, source_target_pairs={{0,24},{8,0},{16,8},{24,16},{1,25},{9,1},{17,9},{25,17},{2,26},{10... | collective-permute-start | bytes 1769480 | tf_op jit(solution)/shard_map/ppermute | solution.py:681
  340.6 46.8 %collective-permute-start.12 = (bf16[384,768]{1,0:T(8,128)(2,1)S(1)}, bf16[384,768]{1,0:T(8,128)(2,1)S(1)}, u32[]{:S(2)}, u32[]{:S(2)}) collective-permute-start(bf16[384,768]{1,0:T(8,128)(2,1)S(1)} %get-tuple-element.166), channel_id=1, source_target_pairs={{0,8},{8,16},{16,24},{24,0},{1,9},{9,17},{17,25},{25,1},{2,10},{10... | collective-permute-start | bytes 1769480 | tf_op jit(solution)/shard_map/ppermute | solution.py:681
  341.2 57.4 %collective-permute-start.13 = (bf16[384,768]{1,0:T(8,128)(2,1)S(1)}, bf16[384,768]{1,0:T(8,128)(2,1)}, u32[]{:S(2)}, u32[]{:S(2)}) collective-permute-start(bf16[384,768]{1,0:T(8,128)(2,1)S(1)} %get-tuple-element.165), channel_id=1, source_target_pairs={{0,16},{8,24},{16,0},{24,8},{1,17},{9,25},{17,1},{25,9},{2,18},{10... | collective-permute-start | bytes 1769480 | tf_op jit(solution)/shard_map/ppermute | solution.py:681
  360.5 38.1 %collective-permute-start.14 = (bf16[384,768]{1,0:T(8,128)(2,1)S(1)}, bf16[384,768]{1,0:T(8,128)(2,1)}, u32[]{:S(2)}, u32[]{:S(2)}) collective-permute-start(bf16[384,768]{1,0:T(8,128)(2,1)S(1)} %get-tuple-element.164), channel_id=1, source_target_pairs={{0,24},{8,0},{16,8},{24,16},{1,25},{9,1},{17,9},{25,17},{2,26},{10... | collective-permute-start | bytes 1769480 | tf_op jit(solution)/shard_map/ppermute | solution.py:681
  398.6 54.2 %all-to-all-start.4 = ((bf16[32,16,1536]{2,1,0:T(8,128)(2,1)}), bf16[32,16,1536]{2,1,0:T(8,128)(2,1)}, u32[]{:S(2)}, u32[]{:S(2)}) async-start(bf16[32,16,1536]{2,1,0:T(8,128)(2,1)} %bitcast.250), calls=%async_computation.4 | async-start | bytes 3145728 | tf_op jit(solution)/shard_map/all_to_all | solution.py:66
  405.8 33.9 %collective-permute-start.15 = (bf16[192,1536]{1,0:T(8,128)(2,1)S(1)}, bf16[192,1536]{1,0:T(8,128)(2,1)S(1)}, u32[]{:S(2)}, u32[]{:S(2)}) collective-permute-start(bf16[192,1536]{1,0:T(8,128)(2,1)S(1)} %get-tuple-element.163), channel_id=1, source_target_pairs={{0,8},{8,16},{16,24},{24,0},{1,9},{9,17},{17,25},{25,1},{2,10},{10... | collective-permute-start | bytes 1769480 | tf_op jit(solution)/shard_map/ppermute | solution.py:681
  407.6 43.0 %collective-permute-start.16 = (bf16[192,1536]{1,0:T(8,128)(2,1)S(1)}, bf16[192,1536]{1,0:T(8,128)(2,1)S(1)}, u32[]{:S(2)}, u32[]{:S(2)}) collective-permute-start(bf16[192,1536]{1,0:T(8,128)(2,1)S(1)} %get-tuple-element.162), channel_id=1, source_target_pairs={{0,16},{8,24},{16,0},{24,8},{1,17},{9,25},{17,1},{25,9},{2,18},{10... | collective-permute-start | bytes 1769480 | tf_op jit(solution)/shard_map/ppermute | solution.py:681
  409.0 42.7 %collective-permute-start.17 = (bf16[192,1536]{1,0:T(8,128)(2,1)S(1)}, bf16[192,1536]{1,0:T(8,128)(2,1)S(1)}, u32[]{:S(2)}, u32[]{:S(2)}) collective-permute-start(bf16[192,1536]{1,0:T(8,128)(2,1)S(1)} %get-tuple-element.161), channel_id=1, source_target_pairs={{0,24},{8,0},{16,8},{24,16},{1,25},{9,1},{17,9},{25,17},{2,26},{10... | collective-permute-start | bytes 1769480 | tf_op jit(solution)/shard_map/ppermute | solution.py:681
  452.9 138.3 %all-to-all-start.5 = ((bf16[32,40,1536]{2,1,0:T(8,128)(2,1)}), bf16[32,40,1536]{2,1,0:T(8,128)(2,1)}, u32[]{:S(2)}, u32[]{:S(2)}) async-start(bf16[32,40,1536]{2,1,0:T(8,128)(2,1)} %bitcast.244), calls=%async_computation.5 | async-start | bytes 7864320 | tf_op jit(solution)/shard_map/all_to_all | solution.py:66
  (75 other events, 1263.3 us)

commit v14 on v13

--- a/solution.py
+++ b/solution.py
@@ -245,7 +245,7 @@
         out_shape=[jax.ShapeDtypeStruct(shape + (x.shape[1],), BF16) for x in arrays]
         + [jax.ShapeDtypeStruct((seq_count,) + x.shape[1:], BF16) for x in extras],
         in_specs=[pl.BlockSpec(memory_space=pl.ANY)] * count,
-        out_specs=[pl.BlockSpec(memory_space=pltpu.HBM)] * count,
+        out_specs=[pl.BlockSpec(memory_space=pl.ANY)] * count,
         scratch_shapes=[
             pltpu.SemaphoreType.DMA((m, 2 + line)),
             pltpu.SemaphoreType.DMA((m, 2 + line)),
@@ -253,7 +253,7 @@
         ]
         + (exchange_sems(len(extras), seq_count) if extras else []),
         compiler_params=pltpu.CompilerParams(
-            collective_id=collective_id, vmem_limit_bytes=4 << 20
+            collective_id=collective_id, vmem_limit_bytes=56 << 20
         ),
         cost_estimate=pl.CostEstimate(flops=0, bytes_accessed=size, transcendentals=0),
         name=name,
@@ -869,23 +869,20 @@
     late_pre_grads, late_hidden, gate_grad, up_grad = lax.optimization_barrier(
         (late_pre_grads, late_hidden, gate_grad, up_grad)
     )
-    gate_grad_parts, up_grad_parts = to_owners(gate_grad), to_owners(up_grad)
+    gate_grad_parts = to_owners(gate_grad)
     late_row_grad = row_grads(*late_pre_grads)
+    early_back, late_row_grad, gate_grad_parts, up_grad, late_hidden = lax.optimization_barrier(
+        (early_back, late_row_grad, gate_grad_parts, up_grad, late_hidden)
+    )
+    expert_hidden = both_parts(early_hidden, late_hidden)
+    late_back = swap(late_row_grad, ("dp", "seq"))
+    gate_owned, up_owned = owned_sum(gate_grad_parts), owned_sum(to_owners(up_grad))
     (down_grad,) = weight_grads(
         flat(early_hidden, late_hidden), [flat(early_grads, late_grads)], "down_grads"
     )
-    early_back, late_row_grad, gate_grad_parts, up_grad_parts, down_grad, late_hidden = (
-        lax.optimization_barrier(
-            (early_back, late_row_grad, gate_grad_parts, up_grad_parts, down_grad, late_hidden)
-        )
-    )
-    expert_hidden = both_parts(early_hidden, late_hidden)
-    late_back = swap(late_row_grad, ("dp", "seq"))
-    down_owned = owned_sum(to_owners(down_grad))
-    gate_owned, up_owned = owned_sum(gate_grad_parts), owned_sum(up_grad_parts)
     expert_out = nn(expert_hidden, down_full).astype(BF16)
-    expert_out, late_back, gate_owned, up_owned, down_owned = lax.optimization_barrier(
-        (expert_out, late_back, gate_owned, up_owned, down_owned)
+    expert_out, late_back, gate_owned, up_owned, down_grad = lax.optimization_barrier(
+        (expert_out, late_back, gate_owned, up_owned, down_grad)
     )
     returned = swap(expert_out.reshape(devices, CAP, width), ("dp", "seq")).reshape(slots, width)
     early_back, late_back = early_back.reshape(-1, width), late_back.reshape(-1, width)
@@ -915,14 +912,21 @@
     gain_terms = jnp.where(lane < 2, gain_terms, 0.0).astype(BF16)
     query_terms = tn(normed, projected_grad).astype(BF16)
     if staged:
-        out_owned, gains_owned, owned = staged_scatter(
-            [out_terms, gain_terms, query_terms], [], None, 6, "scatter_attention_grads"
+        out_owned, gains_owned, owned, down_owned = staged_scatter(
+            [out_terms, gain_terms, query_terms],
+            [down_grad.reshape(seq_count, -1, width)],
+            lambda ref, peer: ref.at[peer],
+            6,
+            "scatter_attention_grads",
         )
+        down_owned = down_owned.reshape((own_experts, sharers) + down_owned.shape[1:])
+        down_owned = jnp.sum(down_owned.astype(F32), axis=1)
     else:
         terms = jnp.concatenate([out_terms, gain_terms, query_terms], axis=1)
         terms = lax.psum_scatter(terms, BOTH, scatter_dimension=0, tiled=True).astype(F32)
         out_owned, gains_owned = terms[:, :width], terms[:, width : width + LANES]
         owned = terms[:, width + LANES :]
+        down_owned = owned_sum(to_owners(down_grad))
     returned, owned = lax.optimization_barrier((returned, owned))
     expert_grads = [gate_owned, up_owned, down_owned]
 

time: 608 us -> 600 us (0.987)
  Pallas kernels: 240 us -> 259 us
  waiting for transfers between devices: 124 us -> 105 us
  local copies, waits for them, and re-layouts: 50 us -> 42.2 us
    pallas_call x1, Pallas kernels: 75.8 us -> 98 us  [staged_scatter(): pl.pallas_call(functools.partial(scatter_kernel, line, chunks, n, len(ext...]
    ppermute x18 -> x15, waiting for transfers between devices: 111 us -> 92.2 us  [seq_permutes(): lax.ppermute(block_for(lax.rem(me + step, count)), 'seq', ring)]
    unnamed x152 -> x128, local copies, waits for them, and re-layouts: 11.4 us -> 4.62 us
    ppermute x18 -> x15, starting transfers between devices: 40 us -> 37.9 us  [seq_permutes(): lax.ppermute(block_for(lax.rem(me + step, count)), 'seq', ring)]
    dynamic_update_slice x11 -> x8, other arithmetic: 13.6 us -> 11.9 us  [in_seq_order(): lax.dynamic_update_index_in_dim(whole, piece.astype(dtype), place, 0)]
  transfers between devices with their start and end apart: 24 -> 21, of which waited for: 11 -> 10; matrix products, arithmetic and copies ran while one was open for 23% -> 24% of each run, Pallas kernels for 40% -> 44%
where the time goes in v14:
time: 600 us; the launch traced here: 590 us
  Pallas kernels  259 us (43%)
  waiting for transfers between devices  105 us (18%)
  matrix products  85.5 us (14%)
  starting transfers between devices  70.2 us (12%)
  local copies, waits for them, and re-layouts  42.2 us (7%)
  other arithmetic  25.7 us (4%)
    pallas_call x1, Pallas kernels, staged_scatter(): pl.pallas_call(functools.partial(scatter_kernel, line, chunks, n, len(ext...  98 us
    ppermute x15, waiting for transfers between devices, seq_permutes(): lax.ppermute(block_for(lax.rem(me + step, count)), 'seq', ring)  92.2 us
    dot_general x23, matrix products, dot(): lax.dot_general(left, right, (contract, ((), ())), preferred_element_type...  85.5 us
    pallas_call x1, Pallas kernels, staged_gather(): pl.pallas_call(functools.partial(gather_kernel, line, chunks, n, len(extr...  71.5 us
    pallas_call x1, Pallas kernels, attention(): pl.pallas_call(functools.partial(attention_kernel, count, heads, kv_heads...  40.8 us
    ppermute x15, starting transfers between devices, seq_permutes(): lax.ppermute(block_for(lax.rem(me + step, count)), 'seq', ring)  37.9 us
    pallas_call x1, Pallas kernels, attention_back(): pl.pallas_call(functools.partial(attention_back_kernel, count, heads, kv_...  33 us
    all_to_all x6, starting transfers between devices, swap(): return lax.all_to_all(blocks, axes, split_axis=0, concat_axis=0, tiled=True)  32.2 us
  transfers between devices with their start and end apart: 21, of which 10 were waited for; matrix products, arithmetic and copies ran while one was open for 24% of the time, Pallas kernels for 44%

profile of v14, /device:TPU:0, one launch (start us, length us, event | category | flops | bytes accessed | tf_op | source)
XLA Modules:
  0.0 590.1 jit_solution(7948751273950391579)
XLA Ops:
  15.1 71.5 %gather_attention_weights.1 = (bf16[2,2,4,2,48,2048]{5,4,3,2,1,0:T(8,128)(2,1)}, bf16[2,2,4,2,48,128]{5,4,3,2,1,0:T(8,128)(2,1)}, bf16[2,2,4,2,48,1536]{5,4,3,2,1,0:T(8,128)(2,1)}) custom-call(bf16[48,2048]{1,0:T(8,128)(2,1)} %pad_maximum_fusion.1.refs_0_, bf16[48,128]{1,0:T(8,128)(2,1)} %maximum_maximum_fusion.refs_1_, bf16[48,1536]{1,0:T(8,128)(2,1)} %refs_2_.1), custom_call_target="tpu_custom_call" | custom-call | bytes 11403264 | tf_op jit(solution)/shard_map/gather_attention_weights/pallas_call | solution.py:243
  92.7 5.6 all-to-all-start
  101.5 4.6 fusion.24.refs_1_
  106.1 40.8 %attention_forward.1 = (bf16[256,1536]{1,0:T(8,128)(2,1)S(1)}, f32[12,256]{1,0:T(8,128)S(1)}, bf16[256,1536]{1,0:T(8,128)(2,1)S(1)}, bf16[4,256,512]{2,1,0:T(8,128)(2,1)S(1)}) custom-call(s32[1]{0:T(128)} %copy.69.refs_0_, f32[256,2048]{1,0:T(8,128)S(1)} %fusion.24.refs_1_, f32[256,128]{1,0:T(8,128)S(1)} %get-tuple-element.186.refs_2_.refs_6_, ...), custom_call_target="tpu_custom_call" | custom-call | bytes 1048576 | tf_op jit(solution)/shard_map/attention_forward/pallas_call | solution.py:496
  148.2 18.8 %collective-permute-start.4 = (bf16[384,768]{1,0:T(8,128)(2,1)S(1)}, bf16[384,768]{1,0:T(8,128)(2,1)S(1)}, u32[]{:S(2)}, u32[]{:S(2)}) collective-permute-start(bf16[384,768]{1,0:T(8,128)(2,1)S(1)} %get-tuple-element.167), channel_id=1, source_target_pairs={{0,16},{8,24},{16,0},{24,8},{1,17},{9,25},{17,1},{25,9},{2,18},{10... | collective-permute-start | bytes 1769480 | tf_op jit(solution)/shard_map/ppermute | solution.py:681
  175.1 12.2 %collective-permute-done.3 = bf16[384,768]{1,0:T(8,128)(2,1)S(1)} collective-permute-done((bf16[384,768]{1,0:T(8,128)(2,1)S(1)}, bf16[384,768]{1,0:T(8,128)(2,1)S(1)}, u32[]{:S(2)}, u32[]{:S(2)}) %collective-permute-start.3) | collective-permute-done | bytes 589856 | tf_op jit(solution)/shard_map/ppermute | solution.py:681
  188.1 9.2 %collective-permute-done.4 = bf16[384,768]{1,0:T(8,128)(2,1)S(1)} collective-permute-done((bf16[384,768]{1,0:T(8,128)(2,1)S(1)}, bf16[384,768]{1,0:T(8,128)(2,1)S(1)}, u32[]{:S(2)}, u32[]{:S(2)}) %collective-permute-start.4) | collective-permute-done | bytes 589856 | tf_op jit(solution)/shard_map/ppermute | solution.py:681
  198.1 5.3 all-to-all-start.1
  227.7 16.8 %collective-permute-done.6 = bf16[192,1536]{1,0:T(8,128)(2,1)S(1)} collective-permute-done((bf16[192,1536]{1,0:T(8,128)(2,1)S(1)}, bf16[192,1536]{1,0:T(8,128)(2,1)S(1)}, u32[]{:S(2)}, u32[]{:S(2)}) %collective-permute-start.6) | collective-permute-done | bytes 589856 | tf_op jit(solution)/shard_map/ppermute | solution.py:681
  245.3 12.7 %collective-permute-done.7 = bf16[192,1536]{1,0:T(8,128)(2,1)S(1)} collective-permute-done((bf16[192,1536]{1,0:T(8,128)(2,1)S(1)}, bf16[192,1536]{1,0:T(8,128)(2,1)S(1)}, u32[]{:S(2)}, u32[]{:S(2)}) %collective-permute-start.7) | collective-permute-done | bytes 589856 | tf_op jit(solution)/shard_map/ppermute | solution.py:681
  260.8 5.7 all-to-all-start.2
  275.3 6.1 %multiply_convert_fusion.2 = (bf16[768,768]{1,0:T(8,128)(2,1)}, bf16[768,768]{1,0:T(8,128)(2,1)S(1)}, bf16[768,768]{1,0:T(8,128)(2,1)S(1)}) fusion(f32[768,768]{1,0:T(8,128)S(1)} %fusion.41, f32[768,768]{1,0:T(8,128)S(1)} %fusion.42, bf16[768,1536]{1,0:T(8,128)(2,1)} %bitcast.40.refs_0_, bf16[1536,768]{1,0:T(8,128)(2,1)} %bitcast.32), kind=kOutput, calls=%fused_computation.28 | convolution fusion | flops 1820786688 | bytes 12976128 | tf_op jit(solution)/shard_map/dot_general | solution.py:34
  285.9 5.1 add_convert_fusion
  291.0 13.0 %all-to-all-done.2 = bf16[32,16,1536]{2,1,0:T(8,128)(2,1)S(1)} async-done(((bf16[32,16,1536]{2,1,0:T(8,128)(2,1)}), bf16[32,16,1536]{2,1,0:T(8,128)(2,1)S(1)}, u32[]{:S(2)}, u32[]{:S(2)}) %all-to-all-start.2) | async-done | bytes 1572896 | tf_op jit(solution)/shard_map/all_to_all | solution.py:66
  318.0 9.8 %gate_up_grads.1 = (bf16[1536,768]{1,0:T(8,128)(2,1)}, bf16[1536,768]{1,0:T(8,128)(2,1)}) custom-call(bf16[768,1536]{1,0:T(8,128)(2,1)} %bitcast.40.refs_0_, bf16[512,1536]{1,0:T(8,128)(2,1)S(1)} %bitcast.209, bf16[768,768]{1,0:T(8,128)(2,1)S(1)} %copy-done.8, bf16[512,768]{1,0:T(8,128)(2,1)S(1)} %get-tuple-element.153.refs_3_, ...), custom_call_target="tpu_custom_call" | custom-call | bytes 1048576 | tf_op jit(solution)/shard_map/gate_up_grads/pallas_call | solution.py:663
  341.5 11.6 %collective-permute-done.10 = bf16[384,768]{1,0:T(8,128)(2,1)} collective-permute-done((bf16[384,768]{1,0:T(8,128)(2,1)S(1)}, bf16[384,768]{1,0:T(8,128)(2,1)}, u32[]{:S(2)}, u32[]{:S(2)}) %collective-permute-start.10) | collective-permute-done | bytes 589856 | tf_op jit(solution)/shard_map/ppermute | solution.py:681
  353.2 15.5 %collective-permute-done.9 = bf16[384,768]{1,0:T(8,128)(2,1)} collective-permute-done((bf16[384,768]{1,0:T(8,128)(2,1)S(1)}, bf16[384,768]{1,0:T(8,128)(2,1)}, u32[]{:S(2)}, u32[]{:S(2)}) %collective-permute-start.9) | collective-permute-done | bytes 589856 | tf_op jit(solution)/shard_map/ppermute | solution.py:681
  368.7 5.9 all-to-all-start.4
  385.4 6.4 %convolution_convert_fusion.2 = bf16[1280,1536]{1,0:T(8,128)(2,1)} fusion(bf16[1280,768]{1,0:T(8,128)(2,1)S(1)} %bitcast.222, bf16[768,1536]{1,0:T(8,128)(2,1)} %bitcast.39), kind=kOutput, calls=%fused_computation.4 | convolution fusion | flops 3021864960 | bytes 8257536 | tf_op jit(solution)/shard_map/dot_general | solution.py:34
  399.8 5.4 down_grads.1
  409.7 9.8 %collective-permute-done.13 = bf16[384,768]{1,0:T(8,128)(2,1)S(1)} collective-permute-done((bf16[384,768]{1,0:T(8,128)(2,1)S(1)}, bf16[384,768]{1,0:T(8,128)(2,1)S(1)}, u32[]{:S(2)}, u32[]{:S(2)}) %collective-permute-start.13) | collective-permute-done | bytes 589856 | tf_op jit(solution)/shard_map/ppermute | solution.py:681
  421.6 5.6 all-to-all-start.5
  437.9 33.0 %attention_backward.1 = bf16[256,2048]{1,0:T(8,128)(2,1)S(1)} custom-call(s32[1]{0:T(128)} %copy.69.refs_0_, bf16[256,1536]{1,0:T(8,128)(2,1)S(1)} %copy-done.16, bf16[1024,512]{1,0:T(8,128)(2,1)S(1)} %bitcast.212, bf16[256,1536]{1,0:T(8,128)(2,1)S(1)} %convolution_convert_fusion.5.refs_3_, f32[12,256]{1,0:T(8,128)S(1)} %get-tuple-element.129.refs_4_, ...), custom_call_target="tpu_custom_call" | custom-call | flops 4026531840 | bytes 1048576 | tf_op jit(solution)/shard_map/attention_backward/pallas_call | solution.py:628
  479.9 98.0 %scatter_attention_grads.1 = (f32[48,1536]{1,0:T(8,128)S(1)}, f32[48,128]{1,0:T(8,128)S(1)}, f32[48,2048]{1,0:T(8,128)S(1)}, bf16[4,192,1536]{2,1,0:T(8,128)(2,1)S(1)}) custom-call(bf16[2,2,4,2,48,1536]{5,4,3,2,1,0:T(8,128)(2,1)S(1)} %bitcast.203, bf16[2,2,4,2,48,128]{5,4,3,2,1,0:T(8,128)(2,1)S(1)} %select_convert_fusion.refs_1_, ...), custom_call_target="tpu_custom_call" | custom-call | bytes 11403264 | tf_op jit(solution)/shard_map/scatter_attention_grads/pallas_call | solution.py:364
  (251 shorter events, 159.0 us)
Async XLA Ops:
  3.7 82.9 %copy-start.55 = (f32[1,256,4]{1,2,0:T(4,128)S(1)}, f32[1,256,4]{1,2,0:T(4,128)}, u32[]{:S(2)}) copy-start(f32[1,256,4]{1,2,0:T(4,128)} %param.18) | copy-start | bytes 12292
  3.7 84.9 %copy-start.33 = (bf16[1,256,1536]{2,1,0:T(8,128)(2,1)S(1)}, bf16[1,256,1536]{2,1,0:T(8,128)(2,1)}, u32[]{:S(2)}) copy-start(bf16[1,256,1536]{2,1,0:T(8,128)(2,1)} %param.29) | copy-start | bytes 2359300
  3.7 88.2 %collective-permute-start = (bf16[384,768]{1,0:T(8,128)(2,1)}, bf16[384,768]{1,0:T(8,128)(2,1)S(1)}, u32[]{:S(2)}, u32[]{:S(2)}) collective-permute-start(bf16[384,768]{1,0:T(8,128)(2,1)} %get-tuple-element.171), channel_id=1, source_target_pairs={{0,8},{8,16},{16,24},{24,0},{1,9},{9,17},{17,25},{25,1},{2,10},{10... | collective-permute-start | bytes 1769480 | tf_op jit(solution)/shard_map/ppermute | solution.py:681
  6.6 85.2 %collective-permute-start.1 = (bf16[384,768]{1,0:T(8,128)(2,1)}, bf16[384,768]{1,0:T(8,128)(2,1)S(1)}, u32[]{:S(2)}, u32[]{:S(2)}) collective-permute-start(bf16[384,768]{1,0:T(8,128)(2,1)} %get-tuple-element.173), channel_id=1, source_target_pairs={{0,16},{8,24},{16,0},{24,8},{1,17},{9,25},{17,1},{25,9},{2,18},{10... | collective-permute-start | bytes 1769480 | tf_op jit(solution)/shard_map/ppermute | solution.py:681
  8.1 83.7 %collective-permute-start.2 = (bf16[384,768]{1,0:T(8,128)(2,1)}, bf16[384,768]{1,0:T(8,128)(2,1)}, u32[]{:S(2)}, u32[]{:S(2)}) collective-permute-start(bf16[384,768]{1,0:T(8,128)(2,1)} %get-tuple-element.170), channel_id=1, source_target_pairs={{0,24},{8,0},{16,8},{24,16},{1,25},{9,1},{17,9},{25,17},{2,26},{10... | collective-permute-start | bytes 1769480 | tf_op jit(solution)/shard_map/ppermute | solution.py:681
  92.7 105.4 %all-to-all-start = ((bf16[32,40,1536]{2,1,0:T(8,128)(2,1)}), bf16[32,40,1536]{2,1,0:T(8,128)(2,1)}, u32[]{:S(2)}, u32[]{:S(2)}) async-start(bf16[32,40,1536]{2,1,0:T(8,128)(2,1)} %bitcast.217), calls=%async_computation | async-start | bytes 7864320 | tf_op jit(solution)/shard_map/all_to_all | solution.py:66
  148.2 39.1 %collective-permute-start.3 = (bf16[384,768]{1,0:T(8,128)(2,1)S(1)}, bf16[384,768]{1,0:T(8,128)(2,1)S(1)}, u32[]{:S(2)}, u32[]{:S(2)}) collective-permute-start(bf16[384,768]{1,0:T(8,128)(2,1)S(1)} %get-tuple-element.168), channel_id=1, source_target_pairs={{0,8},{8,16},{16,24},{24,0},{1,9},{9,17},{17,25},{25,1},{2,10},{10... | collective-permute-start | bytes 1769480 | tf_op jit(solution)/shard_map/ppermute | solution.py:681
  148.2 49.1 %collective-permute-start.4 = (bf16[384,768]{1,0:T(8,128)(2,1)S(1)}, bf16[384,768]{1,0:T(8,128)(2,1)S(1)}, u32[]{:S(2)}, u32[]{:S(2)}) collective-permute-start(bf16[384,768]{1,0:T(8,128)(2,1)S(1)} %get-tuple-element.167), channel_id=1, source_target_pairs={{0,16},{8,24},{16,0},{24,8},{1,17},{9,25},{17,1},{25,9},{2,18},{10... | collective-permute-start | bytes 1769480 | tf_op jit(solution)/shard_map/ppermute | solution.py:681
  167.0 31.1 %collective-permute-start.5 = (bf16[384,768]{1,0:T(8,128)(2,1)S(1)}, bf16[384,768]{1,0:T(8,128)(2,1)}, u32[]{:S(2)}, u32[]{:S(2)}) collective-permute-start(bf16[384,768]{1,0:T(8,128)(2,1)S(1)} %get-tuple-element.166), channel_id=1, source_target_pairs={{0,24},{8,0},{16,8},{24,16},{1,25},{9,1},{17,9},{25,17},{2,26},{10... | collective-permute-start | bytes 1769480 | tf_op jit(solution)/shard_map/ppermute | solution.py:681
  198.1 62.7 %all-to-all-start.1 = ((bf16[32,24,1536]{2,1,0:T(8,128)(2,1)}), bf16[32,24,1536]{2,1,0:T(8,128)(2,1)}, u32[]{:S(2)}, u32[]{:S(2)}) async-start(bf16[32,24,1536]{2,1,0:T(8,128)(2,1)} %bitcast.16), calls=%async_computation.1 | async-start | bytes 4718592 | tf_op jit(solution)/shard_map/all_to_all | solution.py:66
  214.3 93.9 %copy-start = (bf16[32,16,1536]{2,1,0:T(8,128)(2,1)}, bf16[32,16,1536]{2,1,0:T(8,128)(2,1)S(1)}, u32[]{:S(2)}) copy-start(bf16[32,16,1536]{2,1,0:T(8,128)(2,1)S(1)} %slice.30) | copy-start | bytes 4718596
  217.0 27.4 %collective-permute-start.6 = (bf16[192,1536]{1,0:T(8,128)(2,1)S(1)}, bf16[192,1536]{1,0:T(8,128)(2,1)S(1)}, u32[]{:S(2)}, u32[]{:S(2)}) collective-permute-start(bf16[192,1536]{1,0:T(8,128)(2,1)S(1)} %get-tuple-element.164), channel_id=1, source_target_pairs={{0,8},{8,16},{16,24},{24,0},{1,9},{9,17},{17,25},{25,1},{2,10},{10... | collective-permute-start | bytes 1769480 | tf_op jit(solution)/shard_map/ppermute | solution.py:681
  218.7 39.3 %collective-permute-start.7 = (bf16[192,1536]{1,0:T(8,128)(2,1)S(1)}, bf16[192,1536]{1,0:T(8,128)(2,1)S(1)}, u32[]{:S(2)}, u32[]{:S(2)}) collective-permute-start(bf16[192,1536]{1,0:T(8,128)(2,1)S(1)} %get-tuple-element.163), channel_id=1, source_target_pairs={{0,16},{8,24},{16,0},{24,8},{1,17},{9,25},{17,1},{25,9},{2,18},{10... | collective-permute-start | bytes 1769480 | tf_op jit(solution)/shard_map/ppermute | solution.py:681
  220.2 39.7 %collective-permute-start.8 = (bf16[192,1536]{1,0:T(8,128)(2,1)S(1)}, bf16[192,1536]{1,0:T(8,128)(2,1)S(1)}, u32[]{:S(2)}, u32[]{:S(2)}) collective-permute-start(bf16[192,1536]{1,0:T(8,128)(2,1)S(1)} %get-tuple-element.162), channel_id=1, source_target_pairs={{0,24},{8,0},{16,8},{24,16},{1,25},{9,1},{17,9},{25,17},{2,26},{10... | collective-permute-start | bytes 1769480 | tf_op jit(solution)/shard_map/ppermute | solution.py:681
  260.8 43.2 %all-to-all-start.2 = ((bf16[32,16,1536]{2,1,0:T(8,128)(2,1)}), bf16[32,16,1536]{2,1,0:T(8,128)(2,1)S(1)}, u32[]{:S(2)}, u32[]{:S(2)}) async-start(bf16[32,16,1536]{2,1,0:T(8,128)(2,1)} %bitcast.215), calls=%async_computation.2 | async-start | bytes 3145728 | tf_op jit(solution)/shard_map/all_to_all | solution.py:66
  304.0 64.7 %all-to-all-start.3 = ((bf16[32,24,1536]{2,1,0:T(8,128)(2,1)}), bf16[32,24,1536]{2,1,0:T(8,128)(2,1)}, u32[]{:S(2)}, u32[]{:S(2)}) async-start(bf16[32,24,1536]{2,1,0:T(8,128)(2,1)} %bitcast.220), calls=%async_computation.3 | async-start | bytes 4718592 | tf_op jit(solution)/shard_map/all_to_all | solution.py:66
  330.4 22.8 %collective-permute-start.10 = (bf16[384,768]{1,0:T(8,128)(2,1)S(1)}, bf16[384,768]{1,0:T(8,128)(2,1)}, u32[]{:S(2)}, u32[]{:S(2)}) collective-permute-start(bf16[384,768]{1,0:T(8,128)(2,1)S(1)} %get-tuple-element.159), channel_id=1, source_target_pairs={{0,16},{8,24},{16,0},{24,8},{1,17},{9,25},{17,1},{25,9},{2,18},{10... | collective-permute-start | bytes 1769480 | tf_op jit(solution)/shard_map/ppermute | solution.py:681
  332.1 21.1 %collective-permute-start.11 = (bf16[384,768]{1,0:T(8,128)(2,1)S(1)}, bf16[384,768]{1,0:T(8,128)(2,1)}, u32[]{:S(2)}, u32[]{:S(2)}) collective-permute-start(bf16[384,768]{1,0:T(8,128)(2,1)S(1)} %get-tuple-element.158), channel_id=1, source_target_pairs={{0,24},{8,0},{16,8},{24,16},{1,25},{9,1},{17,9},{25,17},{2,26},{10... | collective-permute-start | bytes 1769480 | tf_op jit(solution)/shard_map/ppermute | solution.py:681
  333.5 35.2 %collective-permute-start.9 = (bf16[384,768]{1,0:T(8,128)(2,1)S(1)}, bf16[384,768]{1,0:T(8,128)(2,1)}, u32[]{:S(2)}, u32[]{:S(2)}) collective-permute-start(bf16[384,768]{1,0:T(8,128)(2,1)S(1)} %get-tuple-element.160), channel_id=1, source_target_pairs={{0,8},{8,16},{16,24},{24,0},{1,9},{9,17},{17,25},{25,1},{2,10},{10... | collective-permute-start | bytes 1769480 | tf_op jit(solution)/shard_map/ppermute | solution.py:681
  368.7 53.0 %all-to-all-start.4 = ((bf16[32,16,1536]{2,1,0:T(8,128)(2,1)}), bf16[32,16,1536]{2,1,0:T(8,128)(2,1)}, u32[]{:S(2)}, u32[]{:S(2)}) async-start(bf16[32,16,1536]{2,1,0:T(8,128)(2,1)} %bitcast.223), calls=%async_computation.4 | async-start | bytes 3145728 | tf_op jit(solution)/shard_map/all_to_all | solution.py:66
  374.7 33.8 %collective-permute-start.12 = (bf16[384,768]{1,0:T(8,128)(2,1)S(1)}, bf16[384,768]{1,0:T(8,128)(2,1)S(1)}, u32[]{:S(2)}, u32[]{:S(2)}) collective-permute-start(bf16[384,768]{1,0:T(8,128)(2,1)S(1)} %get-tuple-element.157), channel_id=1, source_target_pairs={{0,8},{8,16},{16,24},{24,0},{1,9},{9,17},{17,25},{25,1},{2,10},{10... | collective-permute-start | bytes 1769480 | tf_op jit(solution)/shard_map/ppermute | solution.py:681
  376.5 43.0 %collective-permute-start.13 = (bf16[384,768]{1,0:T(8,128)(2,1)S(1)}, bf16[384,768]{1,0:T(8,128)(2,1)S(1)}, u32[]{:S(2)}, u32[]{:S(2)}) collective-permute-start(bf16[384,768]{1,0:T(8,128)(2,1)S(1)} %get-tuple-element.156), channel_id=1, source_target_pairs={{0,16},{8,24},{16,0},{24,8},{1,17},{9,25},{17,1},{25,9},{2,18},{10... | collective-permute-start | bytes 1769480 | tf_op jit(solution)/shard_map/ppermute | solution.py:681
  377.9 42.6 %collective-permute-start.14 = (bf16[384,768]{1,0:T(8,128)(2,1)S(1)}, bf16[384,768]{1,0:T(8,128)(2,1)S(1)}, u32[]{:S(2)}, u32[]{:S(2)}) collective-permute-start(bf16[384,768]{1,0:T(8,128)(2,1)S(1)} %get-tuple-element.155), channel_id=1, source_target_pairs={{0,24},{8,0},{16,8},{24,16},{1,25},{9,1},{17,9},{25,17},{2,26},{10... | collective-permute-start | bytes 1769480 | tf_op jit(solution)/shard_map/ppermute | solution.py:681
  421.6 161.5 %all-to-all-start.5 = ((bf16[32,40,1536]{2,1,0:T(8,128)(2,1)}), bf16[32,40,1536]{2,1,0:T(8,128)(2,1)}, u32[]{:S(2)}, u32[]{:S(2)}) async-start(bf16[32,40,1536]{2,1,0:T(8,128)(2,1)} %bitcast.216), calls=%async_computation.5 | async-start | bytes 7864320 | tf_op jit(solution)/shard_map/all_to_all | solution.py:66
  (60 other events, 779.8 us)

commit v15 on v14

--- a/solution.py
+++ b/solution.py
@@ -12,7 +12,7 @@
 EXPERTS = 32
 TOP = 4
 CAP = 40
-EARLY = 24
+EARLY = 16
 
 EPSILON = 1e-06
 ROPE_BASE = 10000.0
@@ -232,7 +232,7 @@
         copy.wait()
 
 
-def staged_gather(arrays, extras, block_of, collective_id, name, parts=6):
+def staged_gather(arrays, extras, block_of, collective_id, name, parts=8):
     seq_count, line = lax.axis_size("seq"), lax.axis_size("dp") // 2
     rows, n = arrays[0].shape[0], len(arrays)
     chunks = column_chunks([x.shape[1] for x in arrays], parts)
@@ -353,7 +353,7 @@
         copy.wait()
 
 
-def staged_scatter(arrays, extras, block_of, collective_id, name, parts=6):
+def staged_scatter(arrays, extras, block_of, collective_id, name, parts=8):
     seq_count, line = lax.axis_size("seq"), lax.axis_size("dp") // 2
     rows, n = arrays[0].shape[0] // (2 * line * seq_count), len(arrays)
     chunks = column_chunks([x.shape[1] for x in arrays], parts)

time: 600 us -> 607 us (1.012)
  Pallas kernels: 259 us -> 266 us
    all_to_all x6, waiting for transfers between devices: 13 us -> 41 us  [swap(): return lax.all_to_all(blocks, axes, split_axis=0, concat_axis=0, tiled=True)]
    ppermute x15, waiting for transfers between devices: 92.2 us -> 69.3 us  [seq_permutes(): lax.ppermute(block_for(lax.rem(me + step, count)), 'seq', ring)]
    pallas_call x1, Pallas kernels: 98 us -> 105 us  [staged_scatter(): pl.pallas_call(functools.partial(scatter_kernel, line, chunks, n, len(ext...]
  transfers between devices with their start and end apart: 21 -> 21, of which waited for: 10 -> 12; matrix products, arithmetic and copies ran while one was open for 24% -> 23% of each run, Pallas kernels for 44% -> 44%
where the time goes in v15:
time: 607 us; the launch traced here: 598 us
  Pallas kernels  266 us (44%)
  waiting for transfers between devices  110 us (18%)
  matrix products  79.5 us (13%)
  starting transfers between devices  69 us (11%)
  local copies, waits for them, and re-layouts  44.3 us (7%)
  other arithmetic  25.7 us (4%)
    pallas_call x1, Pallas kernels, staged_scatter(): pl.pallas_call(functools.partial(scatter_kernel, line, chunks, n, len(ext...  105 us
    dot_general x23, matrix products, dot(): lax.dot_general(left, right, (contract, ((), ())), preferred_element_type...  79.5 us
    pallas_call x1, Pallas kernels, staged_gather(): pl.pallas_call(functools.partial(gather_kernel, line, chunks, n, len(extr...  72 us
    ppermute x15, waiting for transfers between devices, seq_permutes(): lax.ppermute(block_for(lax.rem(me + step, count)), 'seq', ring)  69.3 us
    all_to_all x6, waiting for transfers between devices, swap(): return lax.all_to_all(blocks, axes, split_axis=0, concat_axis=0, tiled=True)  41 us
    pallas_call x1, Pallas kernels, attention(): pl.pallas_call(functools.partial(attention_kernel, count, heads, kv_heads...  40.4 us
    ppermute x15, starting transfers between devices, seq_permutes(): lax.ppermute(block_for(lax.rem(me + step, count)), 'seq', ring)  38.3 us
    pallas_call x1, Pallas kernels, attention_back(): pl.pallas_call(functools.partial(attention_back_kernel, count, heads, kv_...  34 us
  transfers between devices with their start and end apart: 21, of which 12 were waited for; matrix products, arithmetic and copies ran while one was open for 23% of the time, Pallas kernels for 44%

profile of v15, /device:TPU:0, one launch (start us, length us, event | category | flops | bytes accessed | tf_op | source)
XLA Modules:
  0.0 597.7 jit_solution(15685086150399550969)
XLA Ops:
  15.1 72.0 %gather_attention_weights.1 = (bf16[2,2,4,2,48,2048]{5,4,3,2,1,0:T(8,128)(2,1)}, bf16[2,2,4,2,48,128]{5,4,3,2,1,0:T(8,128)(2,1)}, bf16[2,2,4,2,48,1536]{5,4,3,2,1,0:T(8,128)(2,1)}) custom-call(bf16[48,2048]{1,0:T(8,128)(2,1)} %pad_maximum_fusion.1.refs_0_, bf16[48,128]{1,0:T(8,128)(2,1)} %maximum_maximum_fusion.refs_1_, bf16[48,1536]{1,0:T(8,128)(2,1)} %refs_2_.1), custom_call_target="tpu_custom_call" | custom-call | bytes 11403264 | tf_op jit(solution)/shard_map/gather_attention_weights/pallas_call | solution.py:243
  93.1 5.7 all-to-all-start
  101.9 4.6 fusion.24.refs_1_
  106.6 40.4 %attention_forward.1 = (bf16[256,1536]{1,0:T(8,128)(2,1)S(1)}, f32[12,256]{1,0:T(8,128)S(1)}, bf16[256,1536]{1,0:T(8,128)(2,1)S(1)}, bf16[4,256,512]{2,1,0:T(8,128)(2,1)S(1)}) custom-call(s32[1]{0:T(128)} %copy.69.refs_0_, f32[256,2048]{1,0:T(8,128)S(1)} %fusion.24.refs_1_, f32[256,128]{1,0:T(8,128)S(1)} %get-tuple-element.186.refs_2_.refs_6_, ...), custom_call_target="tpu_custom_call" | custom-call | bytes 1048576 | tf_op jit(solution)/shard_map/attention_forward/pallas_call | solution.py:496
  148.5 18.8 %collective-permute-start.4 = (bf16[384,768]{1,0:T(8,128)(2,1)S(1)}, bf16[384,768]{1,0:T(8,128)(2,1)}, u32[]{:S(2)}, u32[]{:S(2)}) collective-permute-start(bf16[384,768]{1,0:T(8,128)(2,1)S(1)} %get-tuple-element.167), channel_id=1, source_target_pairs={{0,16},{8,24},{16,0},{24,8},{1,17},{9,25},{17,1},{25,9},{2,18},{10... | collective-permute-start | bytes 1769480 | tf_op jit(solution)/shard_map/ppermute | solution.py:681
  175.3 12.3 %collective-permute-done.3 = bf16[384,768]{1,0:T(8,128)(2,1)S(1)} collective-permute-done((bf16[384,768]{1,0:T(8,128)(2,1)S(1)}, bf16[384,768]{1,0:T(8,128)(2,1)S(1)}, u32[]{:S(2)}, u32[]{:S(2)}) %collective-permute-start.3) | collective-permute-done | bytes 589856 | tf_op jit(solution)/shard_map/ppermute | solution.py:681
  187.6 10.1 %collective-permute-done.4 = bf16[384,768]{1,0:T(8,128)(2,1)} collective-permute-done((bf16[384,768]{1,0:T(8,128)(2,1)S(1)}, bf16[384,768]{1,0:T(8,128)(2,1)}, u32[]{:S(2)}, u32[]{:S(2)}) %collective-permute-start.4) | collective-permute-done | bytes 589856 | tf_op jit(solution)/shard_map/ppermute | solution.py:681
  197.7 5.9 all-to-all-start.1
  223.4 17.8 %all-to-all-done.1 = bf16[32,16,1536]{2,1,0:T(8,128)(2,1)S(1)} async-done(((bf16[32,16,1536]{2,1,0:T(8,128)(2,1)}), bf16[32,16,1536]{2,1,0:T(8,128)(2,1)S(1)}, u32[]{:S(2)}, u32[]{:S(2)}) %all-to-all-start.1) | async-done | bytes 1572896 | tf_op jit(solution)/shard_map/all_to_all | solution.py:66
  253.7 4.9 collective-permute-done.8
  276.5 23.3 %all-to-all-done.2 = bf16[32,24,1536]{2,1,0:T(8,128)(2,1)} async-done(((bf16[32,24,1536]{2,1,0:T(8,128)(2,1)}), bf16[32,24,1536]{2,1,0:T(8,128)(2,1)}, u32[]{:S(2)}, u32[]{:S(2)}) %all-to-all-start.2) | async-done | bytes 2359328 | tf_op jit(solution)/shard_map/all_to_all | solution.py:66
  299.7 4.9 all-to-all-start.3
  313.4 5.1 multiply_convert_fusion
  318.5 9.6 %gate_up_grads.1 = (bf16[1536,768]{1,0:T(8,128)(2,1)}, bf16[1536,768]{1,0:T(8,128)(2,1)}) custom-call(bf16[512,1536]{1,0:T(8,128)(2,1)S(1)} %bitcast.209, bf16[768,1536]{1,0:T(8,128)(2,1)} %bitcast.45.refs_1_, bf16[512,768]{1,0:T(8,128)(2,1)S(1)} %copy-done.10, bf16[768,768]{1,0:T(8,128)(2,1)S(1)} %get-tuple-element.150.refs_3_, ...), custom_call_target="tpu_custom_call" | custom-call | bytes 1048576 | tf_op jit(solution)/shard_map/gate_up_grads/pallas_call | solution.py:663
  337.5 5.1 add_convert_fusion
  342.6 5.0 collective-permute-done.10
  349.9 12.0 %collective-permute-done.9 = bf16[384,768]{1,0:T(8,128)(2,1)} collective-permute-done((bf16[384,768]{1,0:T(8,128)(2,1)S(1)}, bf16[384,768]{1,0:T(8,128)(2,1)}, u32[]{:S(2)}, u32[]{:S(2)}) %collective-permute-start.9) | collective-permute-done | bytes 589856 | tf_op jit(solution)/shard_map/ppermute | solution.py:681
  379.1 4.8 convolution_convert_fusion.2
  391.9 5.4 down_grads.1
  397.4 10.2 %collective-permute-done.12 = bf16[384,768]{1,0:T(8,128)(2,1)S(1)} collective-permute-done((bf16[384,768]{1,0:T(8,128)(2,1)S(1)}, bf16[384,768]{1,0:T(8,128)(2,1)S(1)}, u32[]{:S(2)}, u32[]{:S(2)}) %collective-permute-start.12) | collective-permute-done | bytes 589856 | tf_op jit(solution)/shard_map/ppermute | solution.py:681
  408.7 11.2 %collective-permute-done.13 = bf16[384,768]{1,0:T(8,128)(2,1)S(1)} collective-permute-done((bf16[384,768]{1,0:T(8,128)(2,1)S(1)}, bf16[384,768]{1,0:T(8,128)(2,1)S(1)}, u32[]{:S(2)}, u32[]{:S(2)}) %collective-permute-start.13) | collective-permute-done | bytes 589856 | tf_op jit(solution)/shard_map/ppermute | solution.py:681
  423.2 5.5 all-to-all-start.5
  437.9 34.0 %attention_backward.1 = bf16[256,2048]{1,0:T(8,128)(2,1)S(1)} custom-call(s32[1]{0:T(128)} %copy.69.refs_0_, bf16[256,1536]{1,0:T(8,128)(2,1)S(1)} %copy-done.16, bf16[1024,512]{1,0:T(8,128)(2,1)S(1)} %bitcast.212, bf16[256,1536]{1,0:T(8,128)(2,1)S(1)} %convolution_convert_fusion.5.refs_3_, f32[12,256]{1,0:T(8,128)S(1)} %get-tuple-element.129.refs_4_, ...), custom_call_target="tpu_custom_call" | custom-call | flops 4026531840 | bytes 1048576 | tf_op jit(solution)/shard_map/attention_backward/pallas_call | solution.py:628
  480.9 104.6 %scatter_attention_grads.1 = (f32[48,1536]{1,0:T(8,128)S(1)}, f32[48,128]{1,0:T(8,128)S(1)}, f32[48,2048]{1,0:T(8,128)S(1)}, bf16[4,192,1536]{2,1,0:T(8,128)(2,1)S(1)}) custom-call(bf16[2,2,4,2,48,1536]{5,4,3,2,1,0:T(8,128)(2,1)S(1)} %bitcast.203, bf16[2,2,4,2,48,128]{5,4,3,2,1,0:T(8,128)(2,1)S(1)} %select_convert_fusion.refs_1_, ...), custom_call_target="tpu_custom_call" | custom-call | bytes 11403264 | tf_op jit(solution)/shard_map/scatter_attention_grads/pallas_call | solution.py:364
  (258 shorter events, 161.9 us)
Async XLA Ops:
  3.7 83.4 %copy-start.56 = (f32[1,256,4]{1,2,0:T(4,128)S(1)}, f32[1,256,4]{1,2,0:T(4,128)}, u32[]{:S(2)}) copy-start(f32[1,256,4]{1,2,0:T(4,128)} %param.18) | copy-start | bytes 12292
  3.7 85.3 %copy-start.36 = (bf16[1,256,1536]{2,1,0:T(8,128)(2,1)S(1)}, bf16[1,256,1536]{2,1,0:T(8,128)(2,1)}, u32[]{:S(2)}) copy-start(bf16[1,256,1536]{2,1,0:T(8,128)(2,1)} %param.29) | copy-start | bytes 2359300
  3.7 88.6 %collective-permute-start = (bf16[384,768]{1,0:T(8,128)(2,1)}, bf16[384,768]{1,0:T(8,128)(2,1)S(1)}, u32[]{:S(2)}, u32[]{:S(2)}) collective-permute-start(bf16[384,768]{1,0:T(8,128)(2,1)} %get-tuple-element.171), channel_id=1, source_target_pairs={{0,8},{8,16},{16,24},{24,0},{1,9},{9,17},{17,25},{25,1},{2,10},{10... | collective-permute-start | bytes 1769480 | tf_op jit(solution)/shard_map/ppermute | solution.py:681
  6.6 85.7 %collective-permute-start.1 = (bf16[384,768]{1,0:T(8,128)(2,1)}, bf16[384,768]{1,0:T(8,128)(2,1)S(1)}, u32[]{:S(2)}, u32[]{:S(2)}) collective-permute-start(bf16[384,768]{1,0:T(8,128)(2,1)} %get-tuple-element.173), channel_id=1, source_target_pairs={{0,16},{8,24},{16,0},{24,8},{1,17},{9,25},{17,1},{25,9},{2,18},{10... | collective-permute-start | bytes 1769480 | tf_op jit(solution)/shard_map/ppermute | solution.py:681
  8.1 84.2 %collective-permute-start.2 = (bf16[384,768]{1,0:T(8,128)(2,1)}, bf16[384,768]{1,0:T(8,128)(2,1)}, u32[]{:S(2)}, u32[]{:S(2)}) collective-permute-start(bf16[384,768]{1,0:T(8,128)(2,1)} %get-tuple-element.170), channel_id=1, source_target_pairs={{0,24},{8,0},{16,8},{24,16},{1,25},{9,1},{17,9},{25,17},{2,26},{10... | collective-permute-start | bytes 1769480 | tf_op jit(solution)/shard_map/ppermute | solution.py:681
  10.2 82.0 %copy-start.54 = (pred[256]{0:T(512)(128)(4,1)}, pred[256]{0:T(512)(128)(4,1)S(1)}, u32[]{:S(2)}) copy-start(pred[256]{0:T(512)(128)(4,1)S(1)} %fusion.38) | copy-start | bytes 772
  93.1 104.6 %all-to-all-start = ((bf16[32,40,1536]{2,1,0:T(8,128)(2,1)}), bf16[32,40,1536]{2,1,0:T(8,128)(2,1)}, u32[]{:S(2)}, u32[]{:S(2)}) async-start(bf16[32,40,1536]{2,1,0:T(8,128)(2,1)} %bitcast.217), calls=%async_computation | async-start | bytes 7864320 | tf_op jit(solution)/shard_map/all_to_all | solution.py:66
  148.5 39.1 %collective-permute-start.3 = (bf16[384,768]{1,0:T(8,128)(2,1)S(1)}, bf16[384,768]{1,0:T(8,128)(2,1)S(1)}, u32[]{:S(2)}, u32[]{:S(2)}) collective-permute-start(bf16[384,768]{1,0:T(8,128)(2,1)S(1)} %get-tuple-element.168), channel_id=1, source_target_pairs={{0,8},{8,16},{16,24},{24,0},{1,9},{9,17},{17,25},{25,1},{2,10},{10... | collective-permute-start | bytes 1769480 | tf_op jit(solution)/shard_map/ppermute | solution.py:681
  148.5 49.2 %collective-permute-start.4 = (bf16[384,768]{1,0:T(8,128)(2,1)S(1)}, bf16[384,768]{1,0:T(8,128)(2,1)}, u32[]{:S(2)}, u32[]{:S(2)}) collective-permute-start(bf16[384,768]{1,0:T(8,128)(2,1)S(1)} %get-tuple-element.167), channel_id=1, source_target_pairs={{0,16},{8,24},{16,0},{24,8},{1,17},{9,25},{17,1},{25,9},{2,18},{10... | collective-permute-start | bytes 1769480 | tf_op jit(solution)/shard_map/ppermute | solution.py:681
  167.3 30.4 %collective-permute-start.5 = (bf16[384,768]{1,0:T(8,128)(2,1)S(1)}, bf16[384,768]{1,0:T(8,128)(2,1)}, u32[]{:S(2)}, u32[]{:S(2)}) collective-permute-start(bf16[384,768]{1,0:T(8,128)(2,1)S(1)} %get-tuple-element.166), channel_id=1, source_target_pairs={{0,24},{8,0},{16,8},{24,16},{1,25},{9,1},{17,9},{25,17},{2,26},{10... | collective-permute-start | bytes 1769480 | tf_op jit(solution)/shard_map/ppermute | solution.py:681
  197.7 43.4 %all-to-all-start.1 = ((bf16[32,16,1536]{2,1,0:T(8,128)(2,1)}), bf16[32,16,1536]{2,1,0:T(8,128)(2,1)S(1)}, u32[]{:S(2)}, u32[]{:S(2)}) async-start(bf16[32,16,1536]{2,1,0:T(8,128)(2,1)} %bitcast.16), calls=%async_computation.1 | async-start | bytes 3145728 | tf_op jit(solution)/shard_map/all_to_all | solution.py:66
  216.3 35.1 %collective-permute-start.6 = (bf16[192,1536]{1,0:T(8,128)(2,1)}, bf16[192,1536]{1,0:T(8,128)(2,1)}, u32[]{:S(2)}, u32[]{:S(2)}) collective-permute-start(bf16[192,1536]{1,0:T(8,128)(2,1)} %get-tuple-element.164), channel_id=1, source_target_pairs={{0,8},{8,16},{16,24},{24,0},{1,9},{9,17},{17,25},{25,1},{2,10},{10... | collective-permute-start | bytes 1769480 | tf_op jit(solution)/shard_map/ppermute | solution.py:681
  218.0 34.6 %collective-permute-start.7 = (bf16[192,1536]{1,0:T(8,128)(2,1)}, bf16[192,1536]{1,0:T(8,128)(2,1)}, u32[]{:S(2)}, u32[]{:S(2)}) collective-permute-start(bf16[192,1536]{1,0:T(8,128)(2,1)} %get-tuple-element.163), channel_id=1, source_target_pairs={{0,16},{8,24},{16,0},{24,8},{1,17},{9,25},{17,1},{25,9},{2,18},{10... | collective-permute-start | bytes 1769480 | tf_op jit(solution)/shard_map/ppermute | solution.py:681
  219.5 39.1 %collective-permute-start.8 = (bf16[192,1536]{1,0:T(8,128)(2,1)}, bf16[192,1536]{1,0:T(8,128)(2,1)}, u32[]{:S(2)}, u32[]{:S(2)}) collective-permute-start(bf16[192,1536]{1,0:T(8,128)(2,1)} %get-tuple-element.162), channel_id=1, source_target_pairs={{0,24},{8,0},{16,8},{24,16},{1,25},{9,1},{17,9},{25,17},{2,26},{10... | collective-permute-start | bytes 1769480 | tf_op jit(solution)/shard_map/ppermute | solution.py:681
  241.1 58.6 %all-to-all-start.2 = ((bf16[32,24,1536]{2,1,0:T(8,128)(2,1)}), bf16[32,24,1536]{2,1,0:T(8,128)(2,1)}, u32[]{:S(2)}, u32[]{:S(2)}) async-start(bf16[32,24,1536]{2,1,0:T(8,128)(2,1)} %bitcast.213), calls=%async_computation.2 | async-start | bytes 4718592 | tf_op jit(solution)/shard_map/all_to_all | solution.py:66
  299.7 62.2 %all-to-all-start.3 = ((bf16[32,16,1536]{2,1,0:T(8,128)(2,1)}), bf16[32,16,1536]{2,1,0:T(8,128)(2,1)}, u32[]{:S(2)}, u32[]{:S(2)}) async-start(bf16[32,16,1536]{2,1,0:T(8,128)(2,1)} %bitcast.43), calls=%async_computation.3 | async-start | bytes 3145728 | tf_op jit(solution)/shard_map/all_to_all | solution.py:66
  329.8 17.8 %collective-permute-start.10 = (bf16[384,768]{1,0:T(8,128)(2,1)S(1)}, bf16[384,768]{1,0:T(8,128)(2,1)S(1)}, u32[]{:S(2)}, u32[]{:S(2)}) collective-permute-start(bf16[384,768]{1,0:T(8,128)(2,1)S(1)} %get-tuple-element.159), channel_id=1, source_target_pairs={{0,16},{8,24},{16,0},{24,8},{1,17},{9,25},{17,1},{25,9},{2,18},{10... | collective-permute-start | bytes 1769480 | tf_op jit(solution)/shard_map/ppermute | solution.py:681
  331.8 18.2 %collective-permute-start.11 = (bf16[384,768]{1,0:T(8,128)(2,1)S(1)}, bf16[384,768]{1,0:T(8,128)(2,1)}, u32[]{:S(2)}, u32[]{:S(2)}) collective-permute-start(bf16[384,768]{1,0:T(8,128)(2,1)S(1)} %get-tuple-element.158), channel_id=1, source_target_pairs={{0,24},{8,0},{16,8},{24,16},{1,25},{9,1},{17,9},{25,17},{2,26},{10... | collective-permute-start | bytes 1769480 | tf_op jit(solution)/shard_map/ppermute | solution.py:681
  333.2 28.7 %collective-permute-start.9 = (bf16[384,768]{1,0:T(8,128)(2,1)S(1)}, bf16[384,768]{1,0:T(8,128)(2,1)}, u32[]{:S(2)}, u32[]{:S(2)}) collective-permute-start(bf16[384,768]{1,0:T(8,128)(2,1)S(1)} %get-tuple-element.160), channel_id=1, source_target_pairs={{0,8},{8,16},{16,24},{24,0},{1,9},{9,17},{17,25},{25,1},{2,10},{10... | collective-permute-start | bytes 1769480 | tf_op jit(solution)/shard_map/ppermute | solution.py:681
  362.0 61.2 %all-to-all-start.4 = ((bf16[32,24,1536]{2,1,0:T(8,128)(2,1)}), bf16[32,24,1536]{2,1,0:T(8,128)(2,1)}, u32[]{:S(2)}, u32[]{:S(2)}) async-start(bf16[32,24,1536]{2,1,0:T(8,128)(2,1)} %bitcast.221), calls=%async_computation.4 | async-start | bytes 4718592 | tf_op jit(solution)/shard_map/all_to_all | solution.py:66
  368.2 39.4 %collective-permute-start.12 = (bf16[384,768]{1,0:T(8,128)(2,1)S(1)}, bf16[384,768]{1,0:T(8,128)(2,1)S(1)}, u32[]{:S(2)}, u32[]{:S(2)}) collective-permute-start(bf16[384,768]{1,0:T(8,128)(2,1)S(1)} %get-tuple-element.157), channel_id=1, source_target_pairs={{0,8},{8,16},{16,24},{24,0},{1,9},{9,17},{17,25},{25,1},{2,10},{10... | collective-permute-start | bytes 1769480 | tf_op jit(solution)/shard_map/ppermute | solution.py:681
  370.0 49.9 %collective-permute-start.13 = (bf16[384,768]{1,0:T(8,128)(2,1)S(1)}, bf16[384,768]{1,0:T(8,128)(2,1)S(1)}, u32[]{:S(2)}, u32[]{:S(2)}) collective-permute-start(bf16[384,768]{1,0:T(8,128)(2,1)S(1)} %get-tuple-element.156), channel_id=1, source_target_pairs={{0,16},{8,24},{16,0},{24,8},{1,17},{9,25},{17,1},{25,9},{2,18},{10... | collective-permute-start | bytes 1769480 | tf_op jit(solution)/shard_map/ppermute | solution.py:681
  371.4 50.7 %collective-permute-start.14 = (bf16[384,768]{1,0:T(8,128)(2,1)S(1)}, bf16[384,768]{1,0:T(8,128)(2,1)S(1)}, u32[]{:S(2)}, u32[]{:S(2)}) collective-permute-start(bf16[384,768]{1,0:T(8,128)(2,1)S(1)} %get-tuple-element.155), channel_id=1, source_target_pairs={{0,24},{8,0},{16,8},{24,16},{1,25},{9,1},{17,9},{25,17},{2,26},{10... | collective-permute-start | bytes 1769480 | tf_op jit(solution)/shard_map/ppermute | solution.py:681
  423.2 167.5 %all-to-all-start.5 = ((bf16[32,40,1536]{2,1,0:T(8,128)(2,1)}), bf16[32,40,1536]{2,1,0:T(8,128)(2,1)}, u32[]{:S(2)}, u32[]{:S(2)}) async-start(bf16[32,40,1536]{2,1,0:T(8,128)(2,1)} %bitcast.216), calls=%async_computation.5 | async-start | bytes 7864320 | tf_op jit(solution)/shard_map/all_to_all | solution.py:66
  (63 other events, 734.8 us)

commit v16 on v14

--- a/solution.py
+++ b/solution.py
@@ -263,12 +263,14 @@
 
 def scatter_kernel(line, chunks, n, extras, block_of, *refs):
     m = len(chunks)
-    sources, more_sources = refs[:n], refs[n : n + extras]
-    refs = refs[n + extras :]
+    lefts, rights, more_sources = refs[:n], refs[n : 2 * n], refs[2 * n : 2 * n + extras]
+    refs = refs[2 * n + extras :]
     targets, more_targets = refs[:n], refs[n : n + extras]
     scratch = refs[n + extras :]
-    owns, ins1, accs2, ins2, accs3, ins3, ins4 = (scratch[m * s : m * (s + 1)] for s in range(7))
-    send, recv, local, *more_sems = scratch[7 * m :]
+    terms, owns, ins1, accs2, ins2, accs3, ins3, ins4 = (
+        scratch[m * s : m * (s + 1)] for s in range(8)
+    )
+    send, recv, *more_sems = scratch[8 * m :]
     sems = (send, recv)
     a, b, z, c = torus_place()
     greet(torus_peers(line))
@@ -290,21 +292,25 @@
 
     def send_core(i):
         k, first, size = chunks[i]
-        cols = pl.ds(first, size)
-        keep = pltpu.make_async_copy(sources[k].at[:, :, :, c, :, cols], owns[i], local.at[i])
-        keep.start()
-        swap_core = remote(
-            sources[k].at[:, :, :, 1 - c, :, cols], ins1[i], sems, i, 0, torus_id(a, b, z, 1 - c)
-        )
-        between_cores[i] = (keep, start(swap_core))
-
-    def send_first(i):
-        keep, copy = between_cores[i]
-        keep.wait()
-        copy.wait_recv()
+        right = rights[k][:, first : first + size]
+        rows = terms[i].shape[4]
         for p in range(2):
             for q in range(2):
-                add_lines(owns[i].at[p, q], owns[i].at[p, q], ins1[i].at[p, q])
+                start_row = (2 * p + q) * 2 * line * rows
+                left = lefts[k][:, start_row : start_row + 2 * line * rows]
+                product = tn(left, right).astype(BF16)
+                for block in range(2 * line):
+                    terms[i][p, q, block // 2, block % 2] = product[block * rows : (block + 1) * rows]
+        swap_core = remote(
+            terms[i].at[:, :, :, 1 - c], ins1[i], sems, i, 0, torus_id(a, b, z, 1 - c)
+        )
+        between_cores[i] = start(swap_core)
+
+    def send_first(i):
+        between_cores[i].wait_recv()
+        for p in range(2):
+            for q in range(2):
+                add_lines(owns[i].at[p, q], terms[i].at[p, q, :, c], ins1[i].at[p, q])
         if i % 2 == 0:
             block, peer = owns[i].at[:, 1 - b], torus_id(a, 1 - b, z, c)
         else:
@@ -353,35 +359,36 @@
         copy.wait()
 
 
-def staged_scatter(arrays, extras, block_of, collective_id, name, parts=6):
+def staged_scatter(products, extras, block_of, collective_id, name, parts=6):
     seq_count, line = lax.axis_size("seq"), lax.axis_size("dp") // 2
-    rows, n = arrays[0].shape[0] // (2 * line * seq_count), len(arrays)
-    chunks = column_chunks([x.shape[1] for x in arrays], parts)
+    lefts, rights = zip(*products, strict=True)
+    rows, n = lefts[0].shape[1] // (2 * line * seq_count), len(products)
+    widths = [x.shape[1] for x in rights]
+    chunks = column_chunks(widths, parts)
     m = len(chunks)
-    leads = [(2, 2, line), (2, 2, line), (2, line), (2, line), (line,), (line,), (line,)]
-    size = sum(x.shape[1] for x in arrays) * rows * 64
-    anywhere = pl.BlockSpec(memory_space=pl.ANY)
+    leads = [(2, 2, line, 2), (2, 2, line), (2, 2, line), (2, line), (2, line)] + [(line,)] * 3
+    size = sum(widths) * rows * 64
+    anywhere, vmem = pl.BlockSpec(memory_space=pl.ANY), pl.BlockSpec(memory_space=pltpu.VMEM)
     return pl.pallas_call(
         functools.partial(scatter_kernel, line, chunks, n, len(extras), block_of),
-        out_shape=[jax.ShapeDtypeStruct((rows, x.shape[1]), F32) for x in arrays]
+        out_shape=[jax.ShapeDtypeStruct((rows, w), F32) for w in widths]
         + [jax.ShapeDtypeStruct((seq_count,) + x.shape[1:], BF16) for x in extras],
-        in_specs=[anywhere] * (n + len(extras)),
-        out_specs=[pl.BlockSpec(memory_space=pltpu.VMEM)] * n + [anywhere] * len(extras),
+        in_specs=[vmem] * (2 * n) + [anywhere] * len(extras),
+        out_specs=[vmem] * n + [anywhere] * len(extras),
         scratch_shapes=[
             pltpu.VMEM(lead + (rows, width), BF16) for lead in leads for _, _, width in chunks
         ]
         + [
             pltpu.SemaphoreType.DMA((m, 2 + line)),
             pltpu.SemaphoreType.DMA((m, 2 + line)),
-            pltpu.SemaphoreType.DMA((m,)),
         ]
         + (exchange_sems(len(extras), seq_count) if extras else []),
         compiler_params=pltpu.CompilerParams(
-            collective_id=collective_id, vmem_limit_bytes=36 << 20
+            collective_id=collective_id, vmem_limit_bytes=56 << 20
         ),
         cost_estimate=pl.CostEstimate(flops=0, bytes_accessed=size, transcendentals=0),
         name=name,
-    )(*[x.reshape(2, 2, line, 2, rows, x.shape[1]) for x in arrays], *extras)
+    )(*lefts, *rights, *extras)
 
 
 def rotate(values, cosines, sines):
@@ -890,7 +897,6 @@
     middle_norm_grad, gain_two_grad = norm_back(middle, scale_two, gain_two, moe_input_grad)
     middle_grad = out_grad + middle_norm_grad
     branch_grad = middle_grad.astype(BF16)
-    out_terms = tn(attended, branch_grad).astype(BF16)
     attended_grad = nt(branch_grad, out_full).astype(BF16)
     projected_grad = attention_back(
         lengths,
@@ -907,13 +913,14 @@
     input_norm_grad, gain_one_grad = norm_back(inputs, scale_one, gain_one, normed_grad)
     input_grad = middle_grad + input_norm_grad
 
-    lane = lax.broadcasted_iota(jnp.int32, (width, LANES), 1)
-    gain_terms = jnp.where(lane == 0, gain_one_grad[:, None], gain_two_grad[:, None])
-    gain_terms = jnp.where(lane < 2, gain_terms, 0.0).astype(BF16)
-    query_terms = tn(normed, projected_grad).astype(BF16)
+    gain_rows = jnp.pad(
+        jnp.stack([gain_one_grad, gain_two_grad]).astype(BF16), ((0, 14), (0, 0))
+    )
+    gain_places = jnp.eye(16, LANES, dtype=BF16)
+    products = [(attended, branch_grad), (gain_rows, gain_places), (normed, projected_grad)]
     if staged:
         out_owned, gains_owned, owned, down_owned = staged_scatter(
-            [out_terms, gain_terms, query_terms],
+            products,
             [down_grad.reshape(seq_count, -1, width)],
             lambda ref, peer: ref.at[peer],
             6,
@@ -922,7 +929,7 @@
         down_owned = down_owned.reshape((own_experts, sharers) + down_owned.shape[1:])
         down_owned = jnp.sum(down_owned.astype(F32), axis=1)
     else:
-        terms = jnp.concatenate([out_terms, gain_terms, query_terms], axis=1)
+        terms = jnp.concatenate([tn(*pair).astype(BF16) for pair in products], axis=1)
         terms = lax.psum_scatter(terms, BOTH, scatter_dimension=0, tiled=True).astype(F32)
         out_owned, gains_owned = terms[:, :width], terms[:, width : width + LANES]
         owned = terms[:, width + LANES :]

time: 600 us -> 601 us (level)
  matrix products: 85.5 us -> 76.8 us
  starting transfers between devices: 70.2 us -> 78.4 us
    dot_general x23 -> x21, matrix products: 85.5 us -> 76.8 us  [dot(): lax.dot_general(left, right, (contract, ((), ())), preferred_element_type...]
    ppermute x15, starting transfers between devices: 37.9 us -> 46.2 us  [seq_permutes(): lax.ppermute(block_for(lax.rem(me + step, count)), 'seq', ring)]
    pallas_call x1, Pallas kernels: 98 us -> 105 us  [staged_scatter(): pl.pallas_call(functools.partial(scatter_kernel, line, chunks, n, len(ext...]
  transfers between devices with their start and end apart: 21 -> 21, of which waited for: 10 -> 10; matrix products, arithmetic and copies ran while one was open for 24% -> 22% of each run, Pallas kernels for 44% -> 45%
where the time goes in v16:
time: 601 us; the launch traced here: 592 us
  Pallas kernels  265 us (44%)
  waiting for transfers between devices  101 us (17%)
  starting transfers between devices  78.4 us (13%)
  matrix products  76.8 us (13%)
  local copies, waits for them, and re-layouts  44.5 us (7%)
  other arithmetic  23.8 us (4%)
    pallas_call x1, Pallas kernels, staged_scatter(): pl.pallas_call(functools.partial(scatter_kernel, line, chunks, n, len(ext...  105 us
    ppermute x15, waiting for transfers between devices, seq_permutes(): lax.ppermute(block_for(lax.rem(me + step, count)), 'seq', ring)  87.8 us
    dot_general x21, matrix products, dot(): lax.dot_general(left, right, (contract, ((), ())), preferred_element_type...  76.8 us
    pallas_call x1, Pallas kernels, staged_gather(): pl.pallas_call(functools.partial(gather_kernel, line, chunks, n, len(extr...  71.5 us
    ppermute x15, starting transfers between devices, seq_permutes(): lax.ppermute(block_for(lax.rem(me + step, count)), 'seq', ring)  46.2 us
    pallas_call x1, Pallas kernels, attention(): pl.pallas_call(functools.partial(attention_kernel, count, heads, kv_heads...  39.8 us
    pallas_call x1, Pallas kernels, attention_back(): pl.pallas_call(functools.partial(attention_back_kernel, count, heads, kv_...  33.8 us
    all_to_all x6, starting transfers between devices, swap(): return lax.all_to_all(blocks, axes, split_axis=0, concat_axis=0, tiled=True)  32.2 us
  transfers between devices with their start and end apart: 21, of which 10 were waited for; matrix products, arithmetic and copies ran while one was open for 22% of the time, Pallas kernels for 45%

profile of v16, /device:TPU:0, one launch (start us, length us, event | category | flops | bytes accessed | tf_op | source)
XLA Modules:
  0.0 592.1 jit_solution(13307884601072218376)
XLA Ops:
  15.1 71.5 %gather_attention_weights.1 = (bf16[2,2,4,2,48,2048]{5,4,3,2,1,0:T(8,128)(2,1)}, bf16[2,2,4,2,48,128]{5,4,3,2,1,0:T(8,128)(2,1)}, bf16[2,2,4,2,48,1536]{5,4,3,2,1,0:T(8,128)(2,1)}) custom-call(bf16[48,2048]{1,0:T(8,128)(2,1)} %pad_maximum_fusion.1.refs_0_, bf16[48,128]{1,0:T(8,128)(2,1)} %maximum_maximum_fusion.refs_1_, bf16[48,1536]{1,0:T(8,128)(2,1)} %refs_2_.1), custom_call_target="tpu_custom_call" | custom-call | bytes 11403264 | tf_op jit(solution)/shard_map/gather_attention_weights/pallas_call | solution.py:243
  92.7 5.6 all-to-all-start
  106.8 39.8 %attention_forward.1 = (bf16[256,1536]{1,0:T(8,128)(2,1)S(1)}, f32[12,256]{1,0:T(8,128)S(1)}, bf16[256,1536]{1,0:T(8,128)(2,1)S(1)}, bf16[4,256,512]{2,1,0:T(8,128)(2,1)S(1)}) custom-call(s32[1]{0:T(128)} %copy.69.refs_0_, f32[256,2048]{1,0:T(8,128)S(1)} %fusion.41.refs_1_, f32[256,128]{1,0:T(8,128)S(1)} %get-tuple-element.188.refs_2_.refs_6_, ...), custom_call_target="tpu_custom_call" | custom-call | bytes 1048576 | tf_op jit(solution)/shard_map/attention_forward/pallas_call | solution.py:503
  147.9 18.8 %collective-permute-start.4 = (bf16[384,768]{1,0:T(8,128)(2,1)S(1)}, bf16[384,768]{1,0:T(8,128)(2,1)S(1)}, u32[]{:S(2)}, u32[]{:S(2)}) collective-permute-start(bf16[384,768]{1,0:T(8,128)(2,1)S(1)} %get-tuple-element.169), channel_id=1, source_target_pairs={{0,16},{8,24},{16,0},{24,8},{1,17},{9,25},{17,1},{25,9},{2,18},{10... | collective-permute-start | bytes 1769480 | tf_op jit(solution)/shard_map/ppermute | solution.py:688
  172.4 14.6 %collective-permute-done.3 = bf16[384,768]{1,0:T(8,128)(2,1)S(1)} collective-permute-done((bf16[384,768]{1,0:T(8,128)(2,1)S(1)}, bf16[384,768]{1,0:T(8,128)(2,1)S(1)}, u32[]{:S(2)}, u32[]{:S(2)}) %collective-permute-start.3) | collective-permute-done | bytes 589856 | tf_op jit(solution)/shard_map/ppermute | solution.py:688
  187.8 9.2 %collective-permute-done.4 = bf16[384,768]{1,0:T(8,128)(2,1)S(1)} collective-permute-done((bf16[384,768]{1,0:T(8,128)(2,1)S(1)}, bf16[384,768]{1,0:T(8,128)(2,1)S(1)}, u32[]{:S(2)}, u32[]{:S(2)}) %collective-permute-start.4) | collective-permute-done | bytes 589856 | tf_op jit(solution)/shard_map/ppermute | solution.py:688
  197.8 5.4 all-to-all-start.1
  227.4 16.7 %collective-permute-done.6 = bf16[192,1536]{1,0:T(8,128)(2,1)S(1)} collective-permute-done((bf16[192,1536]{1,0:T(8,128)(2,1)S(1)}, bf16[192,1536]{1,0:T(8,128)(2,1)S(1)}, u32[]{:S(2)}, u32[]{:S(2)}) %collective-permute-start.6) | collective-permute-done | bytes 589856 | tf_op jit(solution)/shard_map/ppermute | solution.py:688
  245.0 12.8 %collective-permute-done.7 = bf16[192,1536]{1,0:T(8,128)(2,1)S(1)} collective-permute-done((bf16[192,1536]{1,0:T(8,128)(2,1)S(1)}, bf16[192,1536]{1,0:T(8,128)(2,1)S(1)}, u32[]{:S(2)}, u32[]{:S(2)}) %collective-permute-start.7) | collective-permute-done | bytes 589856 | tf_op jit(solution)/shard_map/ppermute | solution.py:688
  260.5 5.7 all-to-all-start.2
  275.0 6.1 %multiply_convert_fusion.2 = (bf16[768,768]{1,0:T(8,128)(2,1)}, bf16[768,768]{1,0:T(8,128)(2,1)S(1)}, bf16[768,768]{1,0:T(8,128)(2,1)S(1)}) fusion(f32[768,768]{1,0:T(8,128)S(1)} %fusion.42, f32[768,768]{1,0:T(8,128)S(1)} %fusion.43, bf16[768,1536]{1,0:T(8,128)(2,1)} %bitcast.40.refs_0_, bf16[1536,768]{1,0:T(8,128)(2,1)} %bitcast.32), kind=kOutput, calls=%fused_computation.26 | convolution fusion | flops 1820786688 | bytes 12976128 | tf_op jit(solution)/shard_map/dot_general | solution.py:34
  285.7 5.2 add_convert_fusion
  290.9 12.8 %all-to-all-done.2 = bf16[32,16,1536]{2,1,0:T(8,128)(2,1)S(1)} async-done(((bf16[32,16,1536]{2,1,0:T(8,128)(2,1)}), bf16[32,16,1536]{2,1,0:T(8,128)(2,1)S(1)}, u32[]{:S(2)}, u32[]{:S(2)}) %all-to-all-start.2) | async-done | bytes 1572896 | tf_op jit(solution)/shard_map/all_to_all | solution.py:66
  318.6 9.5 %gate_up_grads.1 = (bf16[1536,768]{1,0:T(8,128)(2,1)}, bf16[1536,768]{1,0:T(8,128)(2,1)}) custom-call(bf16[768,1536]{1,0:T(8,128)(2,1)} %bitcast.40.refs_0_, bf16[512,1536]{1,0:T(8,128)(2,1)S(1)} %bitcast.204, bf16[768,768]{1,0:T(8,128)(2,1)S(1)} %copy-done.4, bf16[512,768]{1,0:T(8,128)(2,1)S(1)} %get-tuple-element.155.refs_3_, ...), custom_call_target="tpu_custom_call" | custom-call | bytes 1048576 | tf_op jit(solution)/shard_map/gate_up_grads/pallas_call | solution.py:670
  333.8 8.9 %collective-permute-start.9 = (bf16[384,768]{1,0:T(8,128)(2,1)S(1)}, bf16[384,768]{1,0:T(8,128)(2,1)}, u32[]{:S(2)}, u32[]{:S(2)}) collective-permute-start(bf16[384,768]{1,0:T(8,128)(2,1)S(1)} %get-tuple-element.162), channel_id=1, source_target_pairs={{0,8},{8,16},{16,24},{24,0},{1,9},{9,17},{17,25},{25,1},{2,10},{10... | collective-permute-start | bytes 1769480 | tf_op jit(solution)/shard_map/ppermute | solution.py:688
  353.0 15.9 %collective-permute-done.9 = bf16[384,768]{1,0:T(8,128)(2,1)} collective-permute-done((bf16[384,768]{1,0:T(8,128)(2,1)S(1)}, bf16[384,768]{1,0:T(8,128)(2,1)}, u32[]{:S(2)}, u32[]{:S(2)}) %collective-permute-start.9) | collective-permute-done | bytes 589856 | tf_op jit(solution)/shard_map/ppermute | solution.py:688
  368.9 5.7 all-to-all-start.4
  383.5 6.4 %convolution_convert_fusion = bf16[1280,1536]{1,0:T(8,128)(2,1)} fusion(bf16[1280,768]{1,0:T(8,128)(2,1)S(1)} %bitcast.218, bf16[768,1536]{1,0:T(8,128)(2,1)} %bitcast.39), kind=kOutput, calls=%fused_computation.2 | convolution fusion | flops 3021864960 | bytes 8257536 | tf_op jit(solution)/shard_map/dot_general | solution.py:34
  395.9 5.4 down_grads.1
  402.7 6.1 %collective-permute-done.12 = bf16[384,768]{1,0:T(8,128)(2,1)} collective-permute-done((bf16[384,768]{1,0:T(8,128)(2,1)S(1)}, bf16[384,768]{1,0:T(8,128)(2,1)}, u32[]{:S(2)}, u32[]{:S(2)}) %collective-permute-start.12) | collective-permute-done | bytes 589856 | tf_op jit(solution)/shard_map/ppermute | solution.py:688
  410.9 8.6 %collective-permute-done.13 = bf16[384,768]{1,0:T(8,128)(2,1)S(1)} collective-permute-done((bf16[384,768]{1,0:T(8,128)(2,1)S(1)}, bf16[384,768]{1,0:T(8,128)(2,1)S(1)}, u32[]{:S(2)}, u32[]{:S(2)}) %collective-permute-start.13) | collective-permute-done | bytes 589856 | tf_op jit(solution)/shard_map/ppermute | solution.py:688
  421.7 5.6 all-to-all-start.5
  436.4 33.8 %attention_backward.1.refs_5_ = bf16[256,2048]{1,0:T(8,128)(2,1)S(1)} custom-call(s32[1]{0:T(128)} %copy.69.refs_0_, bf16[256,1536]{1,0:T(8,128)(2,1)S(1)} %copy-done.13, bf16[1024,512]{1,0:T(8,128)(2,1)S(1)} %bitcast.207, bf16[256,1536]{1,0:T(8,128)(2,1)S(1)} %convolution_convert_fusion.3.refs_3_, f32[12,256]{1,0:T(8,128)S(1)} %get-tuple-element.129.refs_4_, ...), custom_call_target="tpu_custom_call" | custom-call | flops 4026531840 | bytes 1048576 | tf_op jit(solution)/shard_map/attention_backward/pallas_call | solution.py:635
  473.1 105.1 %scatter_attention_grads.1 = (f32[48,1536]{1,0:T(8,128)}, f32[48,128]{1,0:T(8,128)}, f32[48,2048]{1,0:T(8,128)}, bf16[4,192,1536]{2,1,0:T(8,128)(2,1)}) custom-call(bf16[256,1536]{1,0:T(8,128)(2,1)} %copy-done.8, bf16[16,1536]{1,0:T(8,128)(2,1)} %fusion.31.refs_1_, bf16[256,1536]{1,0:T(8,128)(2,1)} %copy-done.20, bf16[256,1536]{1,0:T(8,128)(2,1)} %copy-done.19, ...), custom_call_target="tpu_custom_call" | custom-call | bytes 11403264 | tf_op jit(solution)/shard_map/scatter_attention_grads/pallas_call | solution.py:372
  (253 shorter events, 154.1 us)
Async XLA Ops:
  3.7 82.9 %copy-start.56 = (f32[1,256,4]{1,2,0:T(4,128)S(1)}, f32[1,256,4]{1,2,0:T(4,128)}, u32[]{:S(2)}) copy-start(f32[1,256,4]{1,2,0:T(4,128)} %param.18) | copy-start | bytes 12292
  3.7 84.9 %copy-start.27 = (bf16[1,256,1536]{2,1,0:T(8,128)(2,1)S(1)}, bf16[1,256,1536]{2,1,0:T(8,128)(2,1)}, u32[]{:S(2)}) copy-start(bf16[1,256,1536]{2,1,0:T(8,128)(2,1)} %param.29) | copy-start | bytes 2359300
  3.7 88.2 %collective-permute-start = (bf16[384,768]{1,0:T(8,128)(2,1)}, bf16[384,768]{1,0:T(8,128)(2,1)S(1)}, u32[]{:S(2)}, u32[]{:S(2)}) collective-permute-start(bf16[384,768]{1,0:T(8,128)(2,1)} %get-tuple-element.173), channel_id=1, source_target_pairs={{0,8},{8,16},{16,24},{24,0},{1,9},{9,17},{17,25},{25,1},{2,10},{10... | collective-permute-start | bytes 1769480 | tf_op jit(solution)/shard_map/ppermute | solution.py:688
  6.6 85.2 %collective-permute-start.1 = (bf16[384,768]{1,0:T(8,128)(2,1)}, bf16[384,768]{1,0:T(8,128)(2,1)S(1)}, u32[]{:S(2)}, u32[]{:S(2)}) collective-permute-start(bf16[384,768]{1,0:T(8,128)(2,1)} %get-tuple-element.175), channel_id=1, source_target_pairs={{0,16},{8,24},{16,0},{24,8},{1,17},{9,25},{17,1},{25,9},{2,18},{10... | collective-permute-start | bytes 1769480 | tf_op jit(solution)/shard_map/ppermute | solution.py:688
  8.1 83.7 %collective-permute-start.2 = (bf16[384,768]{1,0:T(8,128)(2,1)}, bf16[384,768]{1,0:T(8,128)(2,1)}, u32[]{:S(2)}, u32[]{:S(2)}) collective-permute-start(bf16[384,768]{1,0:T(8,128)(2,1)} %get-tuple-element.172), channel_id=1, source_target_pairs={{0,24},{8,0},{16,8},{24,16},{1,25},{9,1},{17,9},{25,17},{2,26},{10... | collective-permute-start | bytes 1769480 | tf_op jit(solution)/shard_map/ppermute | solution.py:688
  10.2 81.6 %copy-start.54 = (pred[256]{0:T(512)(128)(4,1)}, pred[256]{0:T(512)(128)(4,1)S(1)}, u32[]{:S(2)}) copy-start(pred[256]{0:T(512)(128)(4,1)S(1)} %fusion.37) | copy-start | bytes 772
  92.7 105.1 %all-to-all-start = ((bf16[32,40,1536]{2,1,0:T(8,128)(2,1)}), bf16[32,40,1536]{2,1,0:T(8,128)(2,1)}, u32[]{:S(2)}, u32[]{:S(2)}) async-start(bf16[32,40,1536]{2,1,0:T(8,128)(2,1)} %bitcast.213), calls=%async_computation | async-start | bytes 7864320 | tf_op jit(solution)/shard_map/all_to_all | solution.py:66
  147.9 39.1 %collective-permute-start.3 = (bf16[384,768]{1,0:T(8,128)(2,1)S(1)}, bf16[384,768]{1,0:T(8,128)(2,1)S(1)}, u32[]{:S(2)}, u32[]{:S(2)}) collective-permute-start(bf16[384,768]{1,0:T(8,128)(2,1)S(1)} %get-tuple-element.170), channel_id=1, source_target_pairs={{0,8},{8,16},{16,24},{24,0},{1,9},{9,17},{17,25},{25,1},{2,10},{10... | collective-permute-start | bytes 1769480 | tf_op jit(solution)/shard_map/ppermute | solution.py:688
  147.9 49.1 %collective-permute-start.4 = (bf16[384,768]{1,0:T(8,128)(2,1)S(1)}, bf16[384,768]{1,0:T(8,128)(2,1)S(1)}, u32[]{:S(2)}, u32[]{:S(2)}) collective-permute-start(bf16[384,768]{1,0:T(8,128)(2,1)S(1)} %get-tuple-element.169), channel_id=1, source_target_pairs={{0,16},{8,24},{16,0},{24,8},{1,17},{9,25},{17,1},{25,9},{2,18},{10... | collective-permute-start | bytes 1769480 | tf_op jit(solution)/shard_map/ppermute | solution.py:688
  166.7 31.1 %collective-permute-start.5 = (bf16[384,768]{1,0:T(8,128)(2,1)S(1)}, bf16[384,768]{1,0:T(8,128)(2,1)}, u32[]{:S(2)}, u32[]{:S(2)}) collective-permute-start(bf16[384,768]{1,0:T(8,128)(2,1)S(1)} %get-tuple-element.168), channel_id=1, source_target_pairs={{0,24},{8,0},{16,8},{24,16},{1,25},{9,1},{17,9},{25,17},{2,26},{10... | collective-permute-start | bytes 1769480 | tf_op jit(solution)/shard_map/ppermute | solution.py:688
  197.8 62.7 %all-to-all-start.1 = ((bf16[32,24,1536]{2,1,0:T(8,128)(2,1)}), bf16[32,24,1536]{2,1,0:T(8,128)(2,1)}, u32[]{:S(2)}, u32[]{:S(2)}) async-start(bf16[32,24,1536]{2,1,0:T(8,128)(2,1)} %bitcast.16), calls=%async_computation.1 | async-start | bytes 4718592 | tf_op jit(solution)/shard_map/all_to_all | solution.py:66
  216.7 27.4 %collective-permute-start.6 = (bf16[192,1536]{1,0:T(8,128)(2,1)S(1)}, bf16[192,1536]{1,0:T(8,128)(2,1)S(1)}, u32[]{:S(2)}, u32[]{:S(2)}) collective-permute-start(bf16[192,1536]{1,0:T(8,128)(2,1)S(1)} %get-tuple-element.166), channel_id=1, source_target_pairs={{0,8},{8,16},{16,24},{24,0},{1,9},{9,17},{17,25},{25,1},{2,10},{10... | collective-permute-start | bytes 1769480 | tf_op jit(solution)/shard_map/ppermute | solution.py:688
  218.4 39.3 %collective-permute-start.7 = (bf16[192,1536]{1,0:T(8,128)(2,1)S(1)}, bf16[192,1536]{1,0:T(8,128)(2,1)S(1)}, u32[]{:S(2)}, u32[]{:S(2)}) collective-permute-start(bf16[192,1536]{1,0:T(8,128)(2,1)S(1)} %get-tuple-element.165), channel_id=1, source_target_pairs={{0,16},{8,24},{16,0},{24,8},{1,17},{9,25},{17,1},{25,9},{2,18},{10... | collective-permute-start | bytes 1769480 | tf_op jit(solution)/shard_map/ppermute | solution.py:688
  219.9 39.8 %collective-permute-start.8 = (bf16[192,1536]{1,0:T(8,128)(2,1)S(1)}, bf16[192,1536]{1,0:T(8,128)(2,1)S(1)}, u32[]{:S(2)}, u32[]{:S(2)}) collective-permute-start(bf16[192,1536]{1,0:T(8,128)(2,1)S(1)} %get-tuple-element.164), channel_id=1, source_target_pairs={{0,24},{8,0},{16,8},{24,16},{1,25},{9,1},{17,9},{25,17},{2,26},{10... | collective-permute-start | bytes 1769480 | tf_op jit(solution)/shard_map/ppermute | solution.py:688
  260.5 43.2 %all-to-all-start.2 = ((bf16[32,16,1536]{2,1,0:T(8,128)(2,1)}), bf16[32,16,1536]{2,1,0:T(8,128)(2,1)S(1)}, u32[]{:S(2)}, u32[]{:S(2)}) async-start(bf16[32,16,1536]{2,1,0:T(8,128)(2,1)} %bitcast.210), calls=%async_computation.2 | async-start | bytes 3145728 | tf_op jit(solution)/shard_map/all_to_all | solution.py:66
  303.7 65.1 %all-to-all-start.3 = ((bf16[32,24,1536]{2,1,0:T(8,128)(2,1)}), bf16[32,24,1536]{2,1,0:T(8,128)(2,1)}, u32[]{:S(2)}, u32[]{:S(2)}) async-start(bf16[32,24,1536]{2,1,0:T(8,128)(2,1)} %bitcast.216), calls=%async_computation.3 | async-start | bytes 4718592 | tf_op jit(solution)/shard_map/all_to_all | solution.py:66
  330.7 22.3 %collective-permute-start.10 = (bf16[384,768]{1,0:T(8,128)(2,1)S(1)}, bf16[384,768]{1,0:T(8,128)(2,1)S(1)}, u32[]{:S(2)}, u32[]{:S(2)}) collective-permute-start(bf16[384,768]{1,0:T(8,128)(2,1)S(1)} %get-tuple-element.161), channel_id=1, source_target_pairs={{0,16},{8,24},{16,0},{24,8},{1,17},{9,25},{17,1},{25,9},{2,18},{10... | collective-permute-start | bytes 1769480 | tf_op jit(solution)/shard_map/ppermute | solution.py:688
  332.4 20.6 %collective-permute-start.11 = (bf16[384,768]{1,0:T(8,128)(2,1)S(1)}, bf16[384,768]{1,0:T(8,128)(2,1)S(1)}, u32[]{:S(2)}, u32[]{:S(2)}) collective-permute-start(bf16[384,768]{1,0:T(8,128)(2,1)S(1)} %get-tuple-element.160), channel_id=1, source_target_pairs={{0,24},{8,0},{16,8},{24,16},{1,25},{9,1},{17,9},{25,17},{2,26},{10... | collective-permute-start | bytes 1769480 | tf_op jit(solution)/shard_map/ppermute | solution.py:688
  333.8 35.0 %collective-permute-start.9 = (bf16[384,768]{1,0:T(8,128)(2,1)S(1)}, bf16[384,768]{1,0:T(8,128)(2,1)}, u32[]{:S(2)}, u32[]{:S(2)}) collective-permute-start(bf16[384,768]{1,0:T(8,128)(2,1)S(1)} %get-tuple-element.162), channel_id=1, source_target_pairs={{0,8},{8,16},{16,24},{24,0},{1,9},{9,17},{17,25},{25,1},{2,10},{10... | collective-permute-start | bytes 1769480 | tf_op jit(solution)/shard_map/ppermute | solution.py:688
  368.9 52.9 %all-to-all-start.4 = ((bf16[32,16,1536]{2,1,0:T(8,128)(2,1)}), bf16[32,16,1536]{2,1,0:T(8,128)(2,1)S(1)}, u32[]{:S(2)}, u32[]{:S(2)}) async-start(bf16[32,16,1536]{2,1,0:T(8,128)(2,1)} %bitcast.219), calls=%async_computation.4 | async-start | bytes 3145728 | tf_op jit(solution)/shard_map/all_to_all | solution.py:66
  376.3 32.5 %collective-permute-start.12 = (bf16[384,768]{1,0:T(8,128)(2,1)S(1)}, bf16[384,768]{1,0:T(8,128)(2,1)}, u32[]{:S(2)}, u32[]{:S(2)}) collective-permute-start(bf16[384,768]{1,0:T(8,128)(2,1)S(1)} %get-tuple-element.159), channel_id=1, source_target_pairs={{0,8},{8,16},{16,24},{24,0},{1,9},{9,17},{17,25},{25,1},{2,10},{10... | collective-permute-start | bytes 1769480 | tf_op jit(solution)/shard_map/ppermute | solution.py:688
  378.1 41.5 %collective-permute-start.13 = (bf16[384,768]{1,0:T(8,128)(2,1)S(1)}, bf16[384,768]{1,0:T(8,128)(2,1)S(1)}, u32[]{:S(2)}, u32[]{:S(2)}) collective-permute-start(bf16[384,768]{1,0:T(8,128)(2,1)S(1)} %get-tuple-element.158), channel_id=1, source_target_pairs={{0,16},{8,24},{16,0},{24,8},{1,17},{9,25},{17,1},{25,9},{2,18},{10... | collective-permute-start | bytes 1769480 | tf_op jit(solution)/shard_map/ppermute | solution.py:688
  379.5 41.1 %collective-permute-start.14 = (bf16[384,768]{1,0:T(8,128)(2,1)S(1)}, bf16[384,768]{1,0:T(8,128)(2,1)S(1)}, u32[]{:S(2)}, u32[]{:S(2)}) collective-permute-start(bf16[384,768]{1,0:T(8,128)(2,1)S(1)} %get-tuple-element.157), channel_id=1, source_target_pairs={{0,24},{8,0},{16,8},{24,16},{1,25},{9,1},{17,9},{25,17},{2,26},{10... | collective-permute-start | bytes 1769480 | tf_op jit(solution)/shard_map/ppermute | solution.py:688
  421.7 163.4 %all-to-all-start.5 = ((bf16[32,40,1536]{2,1,0:T(8,128)(2,1)}), bf16[32,40,1536]{2,1,0:T(8,128)(2,1)}, u32[]{:S(2)}, u32[]{:S(2)}) async-start(bf16[32,40,1536]{2,1,0:T(8,128)(2,1)} %bitcast.212), calls=%async_computation.5 | async-start | bytes 7864320 | tf_op jit(solution)/shard_map/all_to_all | solution.py:66
  (61 other events, 768.2 us)

commit v17 on v14

--- a/solution.py
+++ b/solution.py
@@ -797,9 +797,11 @@
         return tn(hot, moe_input).astype(BF16).reshape(devices, -1, width)
 
     early_send, late_send = to_experts(early_hot), to_experts(late_hot)
+    *up_parts, last_up = up_parts
     early_send, late_send, grad_rows, up_parts, w_down = lax.optimization_barrier(
         (early_send, late_send, grad_rows, up_parts, w_down)
     )
+    up_parts = [*up_parts, last_up]
     early_grads, late_grads, w_down = lax.optimization_barrier(
         (grad_rows[:, :EARLY], grad_rows[:, EARLY:], w_down)
     )
@@ -871,9 +873,11 @@
     )
     gate_grad_parts = to_owners(gate_grad)
     late_row_grad = row_grads(*late_pre_grads)
+    *gate_grad_parts, last_gate = gate_grad_parts
     early_back, late_row_grad, gate_grad_parts, up_grad, late_hidden = lax.optimization_barrier(
         (early_back, late_row_grad, gate_grad_parts, up_grad, late_hidden)
     )
+    gate_grad_parts = [*gate_grad_parts, last_gate]
     expert_hidden = both_parts(early_hidden, late_hidden)
     late_back = swap(late_row_grad, ("dp", "seq"))
     gate_owned, up_owned = owned_sum(gate_grad_parts), owned_sum(to_owners(up_grad))

time: 600 us -> 621 us (1.035)
  waiting for transfers between devices: 105 us -> 118 us
  starting transfers between devices: 70.2 us -> 80.2 us
    ppermute x15, waiting for transfers between devices: 92.2 us -> 105 us  [seq_permutes(): lax.ppermute(block_for(lax.rem(me + step, count)), 'seq', ring)]
    ppermute x15, starting transfers between devices: 37.9 us -> 48.7 us  [seq_permutes(): lax.ppermute(block_for(lax.rem(me + step, count)), 'seq', ring)]
  transfers between devices with their start and end apart: 21 -> 21, of which waited for: 10 -> 10; matrix products, arithmetic and copies ran while one was open for 24% -> 23% of each run, Pallas kernels for 44% -> 42%
where the time goes in v17:
time: 621 us; the launch traced here: 611 us
  Pallas kernels  258 us (42%)
  waiting for transfers between devices  118 us (19%)
  matrix products  85.5 us (14%)
  starting transfers between devices  80.2 us (13%)
  local copies, waits for them, and re-layouts  41.8 us (7%)
  other arithmetic  24.6 us (4%)
    ppermute x15, waiting for transfers between devices, seq_permutes(): lax.ppermute(block_for(lax.rem(me + step, count)), 'seq', ring)  105 us
    pallas_call x1, Pallas kernels, staged_scatter(): pl.pallas_call(functools.partial(scatter_kernel, line, chunks, n, len(ext...  98 us
    dot_general x23, matrix products, dot(): lax.dot_general(left, right, (contract, ((), ())), preferred_element_type...  85.5 us
    pallas_call x1, Pallas kernels, staged_gather(): pl.pallas_call(functools.partial(gather_kernel, line, chunks, n, len(extr...  71.5 us
    ppermute x15, starting transfers between devices, seq_permutes(): lax.ppermute(block_for(lax.rem(me + step, count)), 'seq', ring)  48.7 us
    pallas_call x1, Pallas kernels, attention(): pl.pallas_call(functools.partial(attention_kernel, count, heads, kv_heads...  40.7 us
    pallas_call x1, Pallas kernels, attention_back(): pl.pallas_call(functools.partial(attention_back_kernel, count, heads, kv_...  33 us
    all_to_all x6, starting transfers between devices, swap(): return lax.all_to_all(blocks, axes, split_axis=0, concat_axis=0, tiled=True)  31.5 us
  transfers between devices with their start and end apart: 21, of which 10 were waited for; matrix products, arithmetic and copies ran while one was open for 23% of the time, Pallas kernels for 42%

profile of v17, /device:TPU:0, one launch (start us, length us, event | category | flops | bytes accessed | tf_op | source)
XLA Modules:
  0.0 611.3 jit_solution(15688105350818374800)
XLA Ops:
  15.1 71.5 %gather_attention_weights.1 = (bf16[2,2,4,2,48,2048]{5,4,3,2,1,0:T(8,128)(2,1)}, bf16[2,2,4,2,48,128]{5,4,3,2,1,0:T(8,128)(2,1)}, bf16[2,2,4,2,48,1536]{5,4,3,2,1,0:T(8,128)(2,1)}) custom-call(bf16[48,2048]{1,0:T(8,128)(2,1)} %pad_maximum_fusion.1.refs_0_, bf16[48,128]{1,0:T(8,128)(2,1)} %maximum_maximum_fusion.refs_1_, bf16[48,1536]{1,0:T(8,128)(2,1)} %refs_2_.1), custom_call_target="tpu_custom_call" | custom-call | bytes 11403264 | tf_op jit(solution)/shard_map/gather_attention_weights/pallas_call | solution.py:243
  92.6 5.6 all-to-all-start
  106.1 40.7 %attention_forward.1 = (bf16[256,1536]{1,0:T(8,128)(2,1)S(1)}, f32[12,256]{1,0:T(8,128)S(1)}, bf16[256,1536]{1,0:T(8,128)(2,1)S(1)}, bf16[4,256,512]{2,1,0:T(8,128)(2,1)S(1)}) custom-call(s32[1]{0:T(128)} %copy.69.refs_0_, f32[256,2048]{1,0:T(8,128)S(1)} %fusion.24.refs_1_, f32[256,128]{1,0:T(8,128)S(1)} %get-tuple-element.182.refs_2_.refs_6_, ...), custom_call_target="tpu_custom_call" | custom-call | bytes 1048576 | tf_op jit(solution)/shard_map/attention_forward/pallas_call | solution.py:496
  148.2 18.8 %collective-permute-start.4 = (bf16[384,768]{1,0:T(8,128)(2,1)S(1)}, bf16[384,768]{1,0:T(8,128)(2,1)}, u32[]{:S(2)}, u32[]{:S(2)}) collective-permute-start(bf16[384,768]{1,0:T(8,128)(2,1)S(1)} %get-tuple-element.163), channel_id=1, source_target_pairs={{0,16},{8,24},{16,0},{24,8},{1,17},{9,25},{17,1},{25,9},{2,18},{10... | collective-permute-start | bytes 1769480 | tf_op jit(solution)/shard_map/ppermute | solution.py:681
  175.1 11.1 %collective-permute-done.3 = bf16[384,768]{1,0:T(8,128)(2,1)S(1)} collective-permute-done((bf16[384,768]{1,0:T(8,128)(2,1)S(1)}, bf16[384,768]{1,0:T(8,128)(2,1)S(1)}, u32[]{:S(2)}, u32[]{:S(2)}) %collective-permute-start.3) | collective-permute-done | bytes 589856 | tf_op jit(solution)/shard_map/ppermute | solution.py:681
  187.0 10.5 %collective-permute-done.4 = bf16[384,768]{1,0:T(8,128)(2,1)} collective-permute-done((bf16[384,768]{1,0:T(8,128)(2,1)S(1)}, bf16[384,768]{1,0:T(8,128)(2,1)}, u32[]{:S(2)}, u32[]{:S(2)}) %collective-permute-start.4) | collective-permute-done | bytes 589856 | tf_op jit(solution)/shard_map/ppermute | solution.py:681
  227.2 12.7 %collective-permute-done.5 = bf16[384,768]{1,0:T(8,128)(2,1)S(1)} collective-permute-done((bf16[384,768]{1,0:T(8,128)(2,1)}, bf16[384,768]{1,0:T(8,128)(2,1)S(1)}, u32[]{:S(2)}, u32[]{:S(2)}) %collective-permute-start.5) | collective-permute-done | bytes 589856 | tf_op jit(solution)/shard_map/ppermute | solution.py:681
  240.8 17.4 %collective-permute-done.6 = bf16[192,1536]{1,0:T(8,128)(2,1)S(1)} collective-permute-done((bf16[192,1536]{1,0:T(8,128)(2,1)S(1)}, bf16[192,1536]{1,0:T(8,128)(2,1)S(1)}, u32[]{:S(2)}, u32[]{:S(2)}) %collective-permute-start.6) | collective-permute-done | bytes 589856 | tf_op jit(solution)/shard_map/ppermute | solution.py:681
  259.9 9.9 %collective-permute-done.8 = bf16[192,1536]{1,0:T(8,128)(2,1)S(1)} collective-permute-done((bf16[192,1536]{1,0:T(8,128)(2,1)S(1)}, bf16[192,1536]{1,0:T(8,128)(2,1)S(1)}, u32[]{:S(2)}, u32[]{:S(2)}) %collective-permute-start.8) | collective-permute-done | bytes 589856 | tf_op jit(solution)/shard_map/ppermute | solution.py:681
  270.6 6.2 %all-to-all-start.2 = ((bf16[32,16,1536]{2,1,0:T(8,128)(2,1)}), bf16[32,16,1536]{2,1,0:T(8,128)(2,1)S(1)}, u32[]{:S(2)}, u32[]{:S(2)}) async-start(bf16[32,16,1536]{2,1,0:T(8,128)(2,1)} %bitcast.215), calls=%async_computation.2 | async-start | bytes 3145728 | tf_op jit(solution)/shard_map/all_to_all | solution.py:66
  285.6 6.1 multiply_convert_fusion.2
  296.2 5.1 add_convert_fusion
  301.3 13.0 %all-to-all-done.2 = bf16[32,16,1536]{2,1,0:T(8,128)(2,1)S(1)} async-done(((bf16[32,16,1536]{2,1,0:T(8,128)(2,1)}), bf16[32,16,1536]{2,1,0:T(8,128)(2,1)S(1)}, u32[]{:S(2)}, u32[]{:S(2)}) %all-to-all-start.2) | async-done | bytes 1572896 | tf_op jit(solution)/shard_map/all_to_all | solution.py:66
  328.3 9.8 %gate_up_grads.1 = (bf16[1536,768]{1,0:T(8,128)(2,1)}, bf16[1536,768]{1,0:T(8,128)(2,1)}) custom-call(bf16[768,1536]{1,0:T(8,128)(2,1)} %bitcast.40.refs_0_, bf16[512,1536]{1,0:T(8,128)(2,1)S(1)} %bitcast.209, bf16[768,768]{1,0:T(8,128)(2,1)S(1)} %copy-done.8, bf16[512,768]{1,0:T(8,128)(2,1)S(1)} %get-tuple-element.149.refs_3_, ...), custom_call_target="tpu_custom_call" | custom-call | bytes 1048576 | tf_op jit(solution)/shard_map/gate_up_grads/pallas_call | solution.py:663
  342.6 9.9 %collective-permute-start.9 = (bf16[384,768]{1,0:T(8,128)(2,1)S(1)}, bf16[384,768]{1,0:T(8,128)(2,1)}, u32[]{:S(2)}, u32[]{:S(2)}) collective-permute-start(bf16[384,768]{1,0:T(8,128)(2,1)S(1)} %get-tuple-element.156), channel_id=1, source_target_pairs={{0,8},{8,16},{16,24},{24,0},{1,9},{9,17},{17,25},{25,1},{2,10},{10... | collective-permute-start | bytes 1769480 | tf_op jit(solution)/shard_map/ppermute | solution.py:681
  359.8 18.7 %collective-permute-done.10 = bf16[384,768]{1,0:T(8,128)(2,1)} collective-permute-done((bf16[384,768]{1,0:T(8,128)(2,1)S(1)}, bf16[384,768]{1,0:T(8,128)(2,1)}, u32[]{:S(2)}, u32[]{:S(2)}) %collective-permute-start.10) | collective-permute-done | bytes 589856 | tf_op jit(solution)/shard_map/ppermute | solution.py:681
  389.5 6.4 %convolution_convert_fusion.2 = bf16[1280,1536]{1,0:T(8,128)(2,1)} fusion(bf16[1280,768]{1,0:T(8,128)(2,1)S(1)} %bitcast.222, bf16[768,1536]{1,0:T(8,128)(2,1)} %bitcast.39), kind=kOutput, calls=%fused_computation.4 | convolution fusion | flops 3021864960 | bytes 8257536 | tf_op jit(solution)/shard_map/dot_general | solution.py:34
  403.9 10.1 %collective-permute-done.11 = bf16[384,768]{1,0:T(8,128)(2,1)S(1)} collective-permute-done((bf16[384,768]{1,0:T(8,128)(2,1)}, bf16[384,768]{1,0:T(8,128)(2,1)S(1)}, u32[]{:S(2)}, u32[]{:S(2)}) %collective-permute-start.11) | collective-permute-done | bytes 589856 | tf_op jit(solution)/shard_map/ppermute | solution.py:681
  418.8 5.4 down_grads.1
  424.2 5.6 collective-permute-done.12
  432.0 9.2 %collective-permute-done.14 = bf16[384,768]{1,0:T(8,128)(2,1)S(1)} collective-permute-done((bf16[384,768]{1,0:T(8,128)(2,1)S(1)}, bf16[384,768]{1,0:T(8,128)(2,1)S(1)}, u32[]{:S(2)}, u32[]{:S(2)}) %collective-permute-start.14) | collective-permute-done | bytes 589856 | tf_op jit(solution)/shard_map/ppermute | solution.py:681
  442.3 6.2 %all-to-all-start.5 = ((bf16[32,40,1536]{2,1,0:T(8,128)(2,1)}), bf16[32,40,1536]{2,1,0:T(8,128)(2,1)}, u32[]{:S(2)}, u32[]{:S(2)}) async-start(bf16[32,40,1536]{2,1,0:T(8,128)(2,1)} %bitcast.216), calls=%async_computation.5 | async-start | bytes 7864320 | tf_op jit(solution)/shard_map/all_to_all | solution.py:66
  459.2 33.0 %attention_backward.1 = bf16[256,2048]{1,0:T(8,128)(2,1)S(1)} custom-call(s32[1]{0:T(128)} %copy.69.refs_0_, bf16[256,1536]{1,0:T(8,128)(2,1)S(1)} %copy-done.16, bf16[1024,512]{1,0:T(8,128)(2,1)S(1)} %bitcast.212, bf16[256,1536]{1,0:T(8,128)(2,1)S(1)} %convolution_convert_fusion.5.refs_3_, f32[12,256]{1,0:T(8,128)S(1)} %get-tuple-element.125.refs_4_, ...), custom_call_target="tpu_custom_call" | custom-call | flops 4026531840 | bytes 1048576 | tf_op jit(solution)/shard_map/attention_backward/pallas_call | solution.py:628
  501.2 98.0 %scatter_attention_grads.1 = (f32[48,1536]{1,0:T(8,128)S(1)}, f32[48,128]{1,0:T(8,128)S(1)}, f32[48,2048]{1,0:T(8,128)S(1)}, bf16[4,192,1536]{2,1,0:T(8,128)(2,1)S(1)}) custom-call(bf16[2,2,4,2,48,1536]{5,4,3,2,1,0:T(8,128)(2,1)S(1)} %bitcast.203, bf16[2,2,4,2,48,128]{5,4,3,2,1,0:T(8,128)(2,1)S(1)} %select_convert_fusion.refs_1_, ...), custom_call_target="tpu_custom_call" | custom-call | bytes 11403264 | tf_op jit(solution)/shard_map/scatter_attention_grads/pallas_call | solution.py:364
  (247 shorter events, 167.8 us)
Async XLA Ops:
  3.7 82.9 %copy-start.53 = (f32[1,256,4]{1,2,0:T(4,128)S(1)}, f32[1,256,4]{1,2,0:T(4,128)}, u32[]{:S(2)}) copy-start(f32[1,256,4]{1,2,0:T(4,128)} %param.18) | copy-start | bytes 12292
  3.7 84.9 %copy-start.33 = (bf16[1,256,1536]{2,1,0:T(8,128)(2,1)S(1)}, bf16[1,256,1536]{2,1,0:T(8,128)(2,1)}, u32[]{:S(2)}) copy-start(bf16[1,256,1536]{2,1,0:T(8,128)(2,1)} %param.29) | copy-start | bytes 2359300
  3.7 88.1 %collective-permute-start = (bf16[384,768]{1,0:T(8,128)(2,1)}, bf16[384,768]{1,0:T(8,128)(2,1)S(1)}, u32[]{:S(2)}, u32[]{:S(2)}) collective-permute-start(bf16[384,768]{1,0:T(8,128)(2,1)} %get-tuple-element.167), channel_id=1, source_target_pairs={{0,8},{8,16},{16,24},{24,0},{1,9},{9,17},{17,25},{25,1},{2,10},{10... | collective-permute-start | bytes 1769480 | tf_op jit(solution)/shard_map/ppermute | solution.py:681
  6.6 85.2 %collective-permute-start.1 = (bf16[384,768]{1,0:T(8,128)(2,1)}, bf16[384,768]{1,0:T(8,128)(2,1)S(1)}, u32[]{:S(2)}, u32[]{:S(2)}) collective-permute-start(bf16[384,768]{1,0:T(8,128)(2,1)} %get-tuple-element.169), channel_id=1, source_target_pairs={{0,16},{8,24},{16,0},{24,8},{1,17},{9,25},{17,1},{25,9},{2,18},{10... | collective-permute-start | bytes 1769480 | tf_op jit(solution)/shard_map/ppermute | solution.py:681
  8.1 83.7 %collective-permute-start.2 = (bf16[384,768]{1,0:T(8,128)(2,1)}, bf16[384,768]{1,0:T(8,128)(2,1)}, u32[]{:S(2)}, u32[]{:S(2)}) collective-permute-start(bf16[384,768]{1,0:T(8,128)(2,1)} %get-tuple-element.166), channel_id=1, source_target_pairs={{0,24},{8,0},{16,8},{24,16},{1,25},{9,1},{17,9},{25,17},{2,26},{10... | collective-permute-start | bytes 1769480 | tf_op jit(solution)/shard_map/ppermute | solution.py:681
  92.6 104.8 %all-to-all-start = ((bf16[32,40,1536]{2,1,0:T(8,128)(2,1)}), bf16[32,40,1536]{2,1,0:T(8,128)(2,1)}, u32[]{:S(2)}, u32[]{:S(2)}) async-start(bf16[32,40,1536]{2,1,0:T(8,128)(2,1)} %bitcast.217), calls=%async_computation | async-start | bytes 7864320 | tf_op jit(solution)/shard_map/all_to_all | solution.py:66
  148.2 38.0 %collective-permute-start.3 = (bf16[384,768]{1,0:T(8,128)(2,1)S(1)}, bf16[384,768]{1,0:T(8,128)(2,1)S(1)}, u32[]{:S(2)}, u32[]{:S(2)}) collective-permute-start(bf16[384,768]{1,0:T(8,128)(2,1)S(1)} %get-tuple-element.164), channel_id=1, source_target_pairs={{0,8},{8,16},{16,24},{24,0},{1,9},{9,17},{17,25},{25,1},{2,10},{10... | collective-permute-start | bytes 1769480 | tf_op jit(solution)/shard_map/ppermute | solution.py:681
  148.2 49.2 %collective-permute-start.4 = (bf16[384,768]{1,0:T(8,128)(2,1)S(1)}, bf16[384,768]{1,0:T(8,128)(2,1)}, u32[]{:S(2)}, u32[]{:S(2)}) collective-permute-start(bf16[384,768]{1,0:T(8,128)(2,1)S(1)} %get-tuple-element.163), channel_id=1, source_target_pairs={{0,16},{8,24},{16,0},{24,8},{1,17},{9,25},{17,1},{25,9},{2,18},{10... | collective-permute-start | bytes 1769480 | tf_op jit(solution)/shard_map/ppermute | solution.py:681
  197.5 73.1 %all-to-all-start.1 = ((bf16[32,24,1536]{2,1,0:T(8,128)(2,1)}), bf16[32,24,1536]{2,1,0:T(8,128)(2,1)}, u32[]{:S(2)}, u32[]{:S(2)}) async-start(bf16[32,24,1536]{2,1,0:T(8,128)(2,1)} %bitcast.16), calls=%async_computation.1 | async-start | bytes 4718592 | tf_op jit(solution)/shard_map/all_to_all | solution.py:66
  202.3 37.7 %collective-permute-start.5 = (bf16[384,768]{1,0:T(8,128)(2,1)}, bf16[384,768]{1,0:T(8,128)(2,1)S(1)}, u32[]{:S(2)}, u32[]{:S(2)}) collective-permute-start(bf16[384,768]{1,0:T(8,128)(2,1)} %get-tuple-element.162), channel_id=1, source_target_pairs={{0,24},{8,0},{16,8},{24,16},{1,25},{9,1},{17,9},{25,17},{2,26},{10... | collective-permute-start | bytes 1769480 | tf_op jit(solution)/shard_map/ppermute | solution.py:681
  215.8 102.7 %copy-start = (bf16[32,16,1536]{2,1,0:T(8,128)(2,1)}, bf16[32,16,1536]{2,1,0:T(8,128)(2,1)S(1)}, u32[]{:S(2)}) copy-start(bf16[32,16,1536]{2,1,0:T(8,128)(2,1)S(1)} %slice.30) | copy-start | bytes 4718596
  218.6 39.6 %collective-permute-start.6 = (bf16[192,1536]{1,0:T(8,128)(2,1)S(1)}, bf16[192,1536]{1,0:T(8,128)(2,1)S(1)}, u32[]{:S(2)}, u32[]{:S(2)}) collective-permute-start(bf16[192,1536]{1,0:T(8,128)(2,1)S(1)} %get-tuple-element.160), channel_id=1, source_target_pairs={{0,8},{8,16},{16,24},{24,0},{1,9},{9,17},{17,25},{25,1},{2,10},{10... | collective-permute-start | bytes 1769480 | tf_op jit(solution)/shard_map/ppermute | solution.py:681
  218.6 40.5 %collective-permute-start.7 = (bf16[192,1536]{1,0:T(8,128)(2,1)S(1)}, bf16[192,1536]{1,0:T(8,128)(2,1)S(1)}, u32[]{:S(2)}, u32[]{:S(2)}) collective-permute-start(bf16[192,1536]{1,0:T(8,128)(2,1)S(1)} %get-tuple-element.159), channel_id=1, source_target_pairs={{0,16},{8,24},{16,0},{24,8},{1,17},{9,25},{17,1},{25,9},{2,18},{10... | collective-permute-start | bytes 1769480 | tf_op jit(solution)/shard_map/ppermute | solution.py:681
  219.7 50.1 %collective-permute-start.8 = (bf16[192,1536]{1,0:T(8,128)(2,1)S(1)}, bf16[192,1536]{1,0:T(8,128)(2,1)S(1)}, u32[]{:S(2)}, u32[]{:S(2)}) collective-permute-start(bf16[192,1536]{1,0:T(8,128)(2,1)S(1)} %get-tuple-element.158), channel_id=1, source_target_pairs={{0,24},{8,0},{16,8},{24,16},{1,25},{9,1},{17,9},{25,17},{2,26},{10... | collective-permute-start | bytes 1769480 | tf_op jit(solution)/shard_map/ppermute | solution.py:681
  270.6 43.7 %all-to-all-start.2 = ((bf16[32,16,1536]{2,1,0:T(8,128)(2,1)}), bf16[32,16,1536]{2,1,0:T(8,128)(2,1)S(1)}, u32[]{:S(2)}, u32[]{:S(2)}) async-start(bf16[32,16,1536]{2,1,0:T(8,128)(2,1)} %bitcast.215), calls=%async_computation.2 | async-start | bytes 3145728 | tf_op jit(solution)/shard_map/all_to_all | solution.py:66
  314.3 64.3 %all-to-all-start.3 = ((bf16[32,24,1536]{2,1,0:T(8,128)(2,1)}), bf16[32,24,1536]{2,1,0:T(8,128)(2,1)}, u32[]{:S(2)}, u32[]{:S(2)}) async-start(bf16[32,24,1536]{2,1,0:T(8,128)(2,1)} %bitcast.220), calls=%async_computation.3 | async-start | bytes 4718592 | tf_op jit(solution)/shard_map/all_to_all | solution.py:66
  340.9 37.7 %collective-permute-start.10 = (bf16[384,768]{1,0:T(8,128)(2,1)S(1)}, bf16[384,768]{1,0:T(8,128)(2,1)}, u32[]{:S(2)}, u32[]{:S(2)}) collective-permute-start(bf16[384,768]{1,0:T(8,128)(2,1)S(1)} %get-tuple-element.155), channel_id=1, source_target_pairs={{0,16},{8,24},{16,0},{24,8},{1,17},{9,25},{17,1},{25,9},{2,18},{10... | collective-permute-start | bytes 1769480 | tf_op jit(solution)/shard_map/ppermute | solution.py:681
  342.6 36.0 %collective-permute-start.9 = (bf16[384,768]{1,0:T(8,128)(2,1)S(1)}, bf16[384,768]{1,0:T(8,128)(2,1)}, u32[]{:S(2)}, u32[]{:S(2)}) collective-permute-start(bf16[384,768]{1,0:T(8,128)(2,1)S(1)} %get-tuple-element.156), channel_id=1, source_target_pairs={{0,8},{8,16},{16,24},{24,0},{1,9},{9,17},{17,25},{25,1},{2,10},{10... | collective-permute-start | bytes 1769480 | tf_op jit(solution)/shard_map/ppermute | solution.py:681
  378.6 63.7 %all-to-all-start.4 = ((bf16[32,16,1536]{2,1,0:T(8,128)(2,1)}), bf16[32,16,1536]{2,1,0:T(8,128)(2,1)}, u32[]{:S(2)}, u32[]{:S(2)}) async-start(bf16[32,16,1536]{2,1,0:T(8,128)(2,1)} %bitcast.223), calls=%async_computation.4 | async-start | bytes 3145728 | tf_op jit(solution)/shard_map/all_to_all | solution.py:66
  383.1 30.9 %collective-permute-start.11 = (bf16[384,768]{1,0:T(8,128)(2,1)}, bf16[384,768]{1,0:T(8,128)(2,1)S(1)}, u32[]{:S(2)}, u32[]{:S(2)}) collective-permute-start(bf16[384,768]{1,0:T(8,128)(2,1)} %get-tuple-element.154), channel_id=1, source_target_pairs={{0,24},{8,0},{16,8},{24,16},{1,25},{9,1},{17,9},{25,17},{2,26},{10... | collective-permute-start | bytes 1769480 | tf_op jit(solution)/shard_map/ppermute | solution.py:681
  385.8 43.9 %collective-permute-start.12 = (bf16[384,768]{1,0:T(8,128)(2,1)S(1)}, bf16[384,768]{1,0:T(8,128)(2,1)S(1)}, u32[]{:S(2)}, u32[]{:S(2)}) collective-permute-start(bf16[384,768]{1,0:T(8,128)(2,1)S(1)} %get-tuple-element.153), channel_id=1, source_target_pairs={{0,8},{8,16},{16,24},{24,0},{1,9},{9,17},{17,25},{25,1},{2,10},{10... | collective-permute-start | bytes 1769480 | tf_op jit(solution)/shard_map/ppermute | solution.py:681
  385.9 45.0 %collective-permute-start.13 = (bf16[384,768]{1,0:T(8,128)(2,1)S(1)}, bf16[384,768]{1,0:T(8,128)(2,1)S(1)}, u32[]{:S(2)}, u32[]{:S(2)}) collective-permute-start(bf16[384,768]{1,0:T(8,128)(2,1)S(1)} %get-tuple-element.152), channel_id=1, source_target_pairs={{0,16},{8,24},{16,0},{24,8},{1,17},{9,25},{17,1},{25,9},{2,18},{10... | collective-permute-start | bytes 1769480 | tf_op jit(solution)/shard_map/ppermute | solution.py:681
  387.0 54.2 %collective-permute-start.14 = (bf16[384,768]{1,0:T(8,128)(2,1)S(1)}, bf16[384,768]{1,0:T(8,128)(2,1)S(1)}, u32[]{:S(2)}, u32[]{:S(2)}) collective-permute-start(bf16[384,768]{1,0:T(8,128)(2,1)S(1)} %get-tuple-element.151), channel_id=1, source_target_pairs={{0,24},{8,0},{16,8},{24,16},{1,25},{9,1},{17,9},{25,17},{2,26},{10... | collective-permute-start | bytes 1769480 | tf_op jit(solution)/shard_map/ppermute | solution.py:681
  442.3 162.1 %all-to-all-start.5 = ((bf16[32,40,1536]{2,1,0:T(8,128)(2,1)}), bf16[32,40,1536]{2,1,0:T(8,128)(2,1)}, u32[]{:S(2)}, u32[]{:S(2)}) async-start(bf16[32,40,1536]{2,1,0:T(8,128)(2,1)} %bitcast.216), calls=%async_computation.5 | async-start | bytes 7864320 | tf_op jit(solution)/shard_map/all_to_all | solution.py:66
  (58 other events, 770.6 us)

commit v18 on v14

--- a/solution.py
+++ b/solution.py
@@ -101,6 +101,16 @@
             if end > first:
                 chunks.append((k, first * LANES, (end - first) * LANES))
     return chunks
+
+
+def first_links(chunks):
+    loads, choices = [0, 0], []
+    for _, _, size in chunks:
+        link = int(loads[0] > loads[1])
+        loads[link] += 2 * size
+        loads[1 - link] += size
+        choices.append(link == 0)
+    return choices
 
 
 def remote(src, dst, sems, i, j, device_id):
@@ -165,6 +175,7 @@
     send, recv, local, *more_sems = refs[n + extras :]
     sems = (send, recv)
     a, b, z, c = torus_place()
+    over_b = first_links(chunks)
     greet(torus_peers(line))
     more = start_exchange(4, more_sources, more_targets, block_of, more_sems) if extras else []
     sent = []
@@ -204,14 +215,14 @@
         for copy in copies:
             copy.wait_recv()
         block = targets[k].at[a, b, :, c, :, pl.ds(first, size)]
-        peer = torus_id(a, 1 - b, z, c) if i % 2 == 0 else torus_id(1 - a, b, z, c)
+        peer = torus_id(a, 1 - b, z, c) if over_b[i] else torus_id(1 - a, b, z, c)
         first_hop[i] = start(remote(block, block, sems, i, 1, peer))
 
     def send_second(i):
         k, first, size = chunks[i]
         first_hop[i].wait_recv()
         cols = pl.ds(first, size)
-        if i % 2 == 0:
+        if over_b[i]:
             block, peer = targets[k].at[a, :, :, c, :, cols], torus_id(1 - a, b, z, c)
         else:
             block, peer = targets[k].at[:, b, :, c, :, cols], torus_id(a, 1 - b, z, c)
@@ -271,6 +282,7 @@
     send, recv, local, *more_sems = scratch[7 * m :]
     sems = (send, recv)
     a, b, z, c = torus_place()
+    over_b = first_links(chunks)
     greet(torus_peers(line))
     sent = []
 
@@ -305,7 +317,7 @@
         for p in range(2):
             for q in range(2):
                 add_lines(owns[i].at[p, q], owns[i].at[p, q], ins1[i].at[p, q])
-        if i % 2 == 0:
+        if over_b[i]:
             block, peer = owns[i].at[:, 1 - b], torus_id(a, 1 - b, z, c)
         else:
             block, peer = owns[i].at[1 - a], torus_id(1 - a, b, z, c)
@@ -314,9 +326,9 @@
     def send_second(i):
         first_hop[i].wait_recv()
         for p in range(2):
-            mine = owns[i].at[p, b] if i % 2 == 0 else owns[i].at[a, p]
+            mine = owns[i].at[p, b] if over_b[i] else owns[i].at[a, p]
             add_lines(accs2[i].at[p], mine, ins2[i].at[p])
-        if i % 2 == 0:
+        if over_b[i]:
             block, peer = accs2[i].at[1 - a], torus_id(1 - a, b, z, c)
         else:
             block, peer = accs2[i].at[1 - b], torus_id(a, 1 - b, z, c)
@@ -324,7 +336,7 @@
 
     def send_line(i):
         second_hop[i].wait_recv()
-        add_lines(accs3[i], accs2[i].at[a if i % 2 == 0 else b], ins3[i])
+        add_lines(accs3[i], accs2[i].at[a if over_b[i] else b], ins3[i])
         copies = []
         for step in range(1, line):
             to = lax.rem(z + step, line)

time: 600 us -> 597 us (level)
  no operation moved by 1% of the time
where the time goes in v18:
time: 597 us; the launch traced here: 588 us
  Pallas kernels  256 us (43%)
  waiting for transfers between devices  105 us (18%)
  matrix products  85.5 us (14%)
  starting transfers between devices  69.7 us (12%)
  local copies, waits for them, and re-layouts  42.2 us (7%)
  other arithmetic  25.7 us (4%)
    pallas_call x1, Pallas kernels, staged_scatter(): pl.pallas_call(functools.partial(scatter_kernel, line, chunks, n, len(ext...  98.2 us
    ppermute x15, waiting for transfers between devices, seq_permutes(): lax.ppermute(block_for(lax.rem(me + step, count)), 'seq', ring)  92.2 us
    dot_general x23, matrix products, dot(): lax.dot_general(left, right, (contract, ((), ())), preferred_element_type...  85.5 us
    pallas_call x1, Pallas kernels, staged_gather(): pl.pallas_call(functools.partial(gather_kernel, line, chunks, n, len(extr...  69.3 us
    pallas_call x1, Pallas kernels, attention(): pl.pallas_call(functools.partial(attention_kernel, count, heads, kv_heads...  40.8 us
    ppermute x15, starting transfers between devices, seq_permutes(): lax.ppermute(block_for(lax.rem(me + step, count)), 'seq', ring)  37.9 us
    pallas_call x1, Pallas kernels, attention_back(): pl.pallas_call(functools.partial(attention_back_kernel, count, heads, kv_...  33 us
    all_to_all x6, starting transfers between devices, swap(): return lax.all_to_all(blocks, axes, split_axis=0, concat_axis=0, tiled=True)  31.7 us
  transfers between devices with their start and end apart: 21, of which 10 were waited for; matrix products, arithmetic and copies ran while one was open for 24% of the time, Pallas kernels for 44%

profile of v18, /device:TPU:0, one launch (start us, length us, event | category | flops | bytes accessed | tf_op | source)
XLA Modules:
  0.0 587.5 jit_solution(7907748297457028430)
XLA Ops:
  15.1 69.3 %gather_attention_weights.1 = (bf16[2,2,4,2,48,2048]{5,4,3,2,1,0:T(8,128)(2,1)}, bf16[2,2,4,2,48,128]{5,4,3,2,1,0:T(8,128)(2,1)}, bf16[2,2,4,2,48,1536]{5,4,3,2,1,0:T(8,128)(2,1)}) custom-call(bf16[48,2048]{1,0:T(8,128)(2,1)} %pad_maximum_fusion.1.refs_0_, bf16[48,128]{1,0:T(8,128)(2,1)} %maximum_maximum_fusion.refs_1_, bf16[48,1536]{1,0:T(8,128)(2,1)} %refs_2_.1), custom_call_target="tpu_custom_call" | custom-call | bytes 11403264 | tf_op jit(solution)/shard_map/gather_attention_weights/pallas_call | solution.py:254
  90.4 5.1 all-to-all-start
  98.7 4.6 fusion.24.refs_1_
  103.4 40.8 %attention_forward.1 = (bf16[256,1536]{1,0:T(8,128)(2,1)S(1)}, f32[12,256]{1,0:T(8,128)S(1)}, bf16[256,1536]{1,0:T(8,128)(2,1)S(1)}, bf16[4,256,512]{2,1,0:T(8,128)(2,1)S(1)}) custom-call(s32[1]{0:T(128)} %copy.69.refs_0_, f32[256,2048]{1,0:T(8,128)S(1)} %fusion.24.refs_1_, f32[256,128]{1,0:T(8,128)S(1)} %get-tuple-element.186.refs_2_.refs_6_, ...), custom_call_target="tpu_custom_call" | custom-call | bytes 1048576 | tf_op jit(solution)/shard_map/attention_forward/pallas_call | solution.py:508
  145.4 18.8 %collective-permute-start.4 = (bf16[384,768]{1,0:T(8,128)(2,1)S(1)}, bf16[384,768]{1,0:T(8,128)(2,1)S(1)}, u32[]{:S(2)}, u32[]{:S(2)}) collective-permute-start(bf16[384,768]{1,0:T(8,128)(2,1)S(1)} %get-tuple-element.167), channel_id=1, source_target_pairs={{0,16},{8,24},{16,0},{24,8},{1,17},{9,25},{17,1},{25,9},{2,18},{10... | collective-permute-start | bytes 1769480 | tf_op jit(solution)/shard_map/ppermute | solution.py:693
  172.4 12.2 %collective-permute-done.3 = bf16[384,768]{1,0:T(8,128)(2,1)S(1)} collective-permute-done((bf16[384,768]{1,0:T(8,128)(2,1)S(1)}, bf16[384,768]{1,0:T(8,128)(2,1)S(1)}, u32[]{:S(2)}, u32[]{:S(2)}) %collective-permute-start.3) | collective-permute-done | bytes 589856 | tf_op jit(solution)/shard_map/ppermute | solution.py:693
  185.4 9.2 %collective-permute-done.4 = bf16[384,768]{1,0:T(8,128)(2,1)S(1)} collective-permute-done((bf16[384,768]{1,0:T(8,128)(2,1)S(1)}, bf16[384,768]{1,0:T(8,128)(2,1)S(1)}, u32[]{:S(2)}, u32[]{:S(2)}) %collective-permute-start.4) | collective-permute-done | bytes 589856 | tf_op jit(solution)/shard_map/ppermute | solution.py:693
  195.4 5.3 all-to-all-start.1
  225.0 16.8 %collective-permute-done.6 = bf16[192,1536]{1,0:T(8,128)(2,1)S(1)} collective-permute-done((bf16[192,1536]{1,0:T(8,128)(2,1)S(1)}, bf16[192,1536]{1,0:T(8,128)(2,1)S(1)}, u32[]{:S(2)}, u32[]{:S(2)}) %collective-permute-start.6) | collective-permute-done | bytes 589856 | tf_op jit(solution)/shard_map/ppermute | solution.py:693
  242.6 12.7 %collective-permute-done.7 = bf16[192,1536]{1,0:T(8,128)(2,1)S(1)} collective-permute-done((bf16[192,1536]{1,0:T(8,128)(2,1)S(1)}, bf16[192,1536]{1,0:T(8,128)(2,1)S(1)}, u32[]{:S(2)}, u32[]{:S(2)}) %collective-permute-start.7) | collective-permute-done | bytes 589856 | tf_op jit(solution)/shard_map/ppermute | solution.py:693
  258.1 5.7 all-to-all-start.2
  272.5 6.1 %multiply_convert_fusion.2 = (bf16[768,768]{1,0:T(8,128)(2,1)}, bf16[768,768]{1,0:T(8,128)(2,1)S(1)}, bf16[768,768]{1,0:T(8,128)(2,1)S(1)}) fusion(f32[768,768]{1,0:T(8,128)S(1)} %fusion.41, f32[768,768]{1,0:T(8,128)S(1)} %fusion.42, bf16[768,1536]{1,0:T(8,128)(2,1)} %bitcast.40.refs_0_, bf16[1536,768]{1,0:T(8,128)(2,1)} %bitcast.32), kind=kOutput, calls=%fused_computation.28 | convolution fusion | flops 1820786688 | bytes 12976128 | tf_op jit(solution)/shard_map/dot_general | solution.py:34
  283.2 5.1 add_convert_fusion
  288.3 13.0 %all-to-all-done.2 = bf16[32,16,1536]{2,1,0:T(8,128)(2,1)S(1)} async-done(((bf16[32,16,1536]{2,1,0:T(8,128)(2,1)}), bf16[32,16,1536]{2,1,0:T(8,128)(2,1)S(1)}, u32[]{:S(2)}, u32[]{:S(2)}) %all-to-all-start.2) | async-done | bytes 1572896 | tf_op jit(solution)/shard_map/all_to_all | solution.py:66
  315.3 9.8 %gate_up_grads.1 = (bf16[1536,768]{1,0:T(8,128)(2,1)}, bf16[1536,768]{1,0:T(8,128)(2,1)}) custom-call(bf16[768,1536]{1,0:T(8,128)(2,1)} %bitcast.40.refs_0_, bf16[512,1536]{1,0:T(8,128)(2,1)S(1)} %bitcast.209, bf16[768,768]{1,0:T(8,128)(2,1)S(1)} %copy-done.8, bf16[512,768]{1,0:T(8,128)(2,1)S(1)} %get-tuple-element.153.refs_3_, ...), custom_call_target="tpu_custom_call" | custom-call | bytes 1048576 | tf_op jit(solution)/shard_map/gate_up_grads/pallas_call | solution.py:675
  338.8 11.6 %collective-permute-done.10 = bf16[384,768]{1,0:T(8,128)(2,1)} collective-permute-done((bf16[384,768]{1,0:T(8,128)(2,1)S(1)}, bf16[384,768]{1,0:T(8,128)(2,1)}, u32[]{:S(2)}, u32[]{:S(2)}) %collective-permute-start.10) | collective-permute-done | bytes 589856 | tf_op jit(solution)/shard_map/ppermute | solution.py:693
  350.4 15.5 %collective-permute-done.9 = bf16[384,768]{1,0:T(8,128)(2,1)} collective-permute-done((bf16[384,768]{1,0:T(8,128)(2,1)S(1)}, bf16[384,768]{1,0:T(8,128)(2,1)}, u32[]{:S(2)}, u32[]{:S(2)}) %collective-permute-start.9) | collective-permute-done | bytes 589856 | tf_op jit(solution)/shard_map/ppermute | solution.py:693
  366.0 5.9 all-to-all-start.4
  382.7 6.4 %convolution_convert_fusion.2 = bf16[1280,1536]{1,0:T(8,128)(2,1)} fusion(bf16[1280,768]{1,0:T(8,128)(2,1)S(1)} %bitcast.222, bf16[768,1536]{1,0:T(8,128)(2,1)} %bitcast.39), kind=kOutput, calls=%fused_computation.4 | convolution fusion | flops 3021864960 | bytes 8257536 | tf_op jit(solution)/shard_map/dot_general | solution.py:34
  397.1 5.4 down_grads.1
  406.9 9.8 %collective-permute-done.13 = bf16[384,768]{1,0:T(8,128)(2,1)S(1)} collective-permute-done((bf16[384,768]{1,0:T(8,128)(2,1)S(1)}, bf16[384,768]{1,0:T(8,128)(2,1)S(1)}, u32[]{:S(2)}, u32[]{:S(2)}) %collective-permute-start.13) | collective-permute-done | bytes 589856 | tf_op jit(solution)/shard_map/ppermute | solution.py:693
  418.9 5.6 all-to-all-start.5
  435.1 33.0 %attention_backward.1 = bf16[256,2048]{1,0:T(8,128)(2,1)S(1)} custom-call(s32[1]{0:T(128)} %copy.69.refs_0_, bf16[256,1536]{1,0:T(8,128)(2,1)S(1)} %copy-done.16, bf16[1024,512]{1,0:T(8,128)(2,1)S(1)} %bitcast.212, bf16[256,1536]{1,0:T(8,128)(2,1)S(1)} %convolution_convert_fusion.5.refs_3_, f32[12,256]{1,0:T(8,128)S(1)} %get-tuple-element.129.refs_4_, ...), custom_call_target="tpu_custom_call" | custom-call | flops 4026531840 | bytes 1048576 | tf_op jit(solution)/shard_map/attention_backward/pallas_call | solution.py:640
  477.1 98.2 %scatter_attention_grads.1 = (f32[48,1536]{1,0:T(8,128)S(1)}, f32[48,128]{1,0:T(8,128)S(1)}, f32[48,2048]{1,0:T(8,128)S(1)}, bf16[4,192,1536]{2,1,0:T(8,128)(2,1)S(1)}) custom-call(bf16[2,2,4,2,48,1536]{5,4,3,2,1,0:T(8,128)(2,1)S(1)} %bitcast.203, bf16[2,2,4,2,48,128]{5,4,3,2,1,0:T(8,128)(2,1)S(1)} %select_convert_fusion.refs_1_, ...), custom_call_target="tpu_custom_call" | custom-call | bytes 11403264 | tf_op jit(solution)/shard_map/scatter_attention_grads/pallas_call | solution.py:376
  (251 shorter events, 159.0 us)
Async XLA Ops:
  3.7 80.7 %copy-start.55 = (f32[1,256,4]{1,2,0:T(4,128)S(1)}, f32[1,256,4]{1,2,0:T(4,128)}, u32[]{:S(2)}) copy-start(f32[1,256,4]{1,2,0:T(4,128)} %param.18) | copy-start | bytes 12292
  3.7 82.7 %copy-start.33 = (bf16[1,256,1536]{2,1,0:T(8,128)(2,1)S(1)}, bf16[1,256,1536]{2,1,0:T(8,128)(2,1)}, u32[]{:S(2)}) copy-start(bf16[1,256,1536]{2,1,0:T(8,128)(2,1)} %param.29) | copy-start | bytes 2359300
  3.7 85.9 %collective-permute-start = (bf16[384,768]{1,0:T(8,128)(2,1)}, bf16[384,768]{1,0:T(8,128)(2,1)S(1)}, u32[]{:S(2)}, u32[]{:S(2)}) collective-permute-start(bf16[384,768]{1,0:T(8,128)(2,1)} %get-tuple-element.171), channel_id=1, source_target_pairs={{0,8},{8,16},{16,24},{24,0},{1,9},{9,17},{17,25},{25,1},{2,10},{10... | collective-permute-start | bytes 1769480 | tf_op jit(solution)/shard_map/ppermute | solution.py:693
  6.6 83.0 %collective-permute-start.1 = (bf16[384,768]{1,0:T(8,128)(2,1)}, bf16[384,768]{1,0:T(8,128)(2,1)S(1)}, u32[]{:S(2)}, u32[]{:S(2)}) collective-permute-start(bf16[384,768]{1,0:T(8,128)(2,1)} %get-tuple-element.173), channel_id=1, source_target_pairs={{0,16},{8,24},{16,0},{24,8},{1,17},{9,25},{17,1},{25,9},{2,18},{10... | collective-permute-start | bytes 1769480 | tf_op jit(solution)/shard_map/ppermute | solution.py:693
  8.1 81.5 %collective-permute-start.2 = (bf16[384,768]{1,0:T(8,128)(2,1)}, bf16[384,768]{1,0:T(8,128)(2,1)}, u32[]{:S(2)}, u32[]{:S(2)}) collective-permute-start(bf16[384,768]{1,0:T(8,128)(2,1)} %get-tuple-element.170), channel_id=1, source_target_pairs={{0,24},{8,0},{16,8},{24,16},{1,25},{9,1},{17,9},{25,17},{2,26},{10... | collective-permute-start | bytes 1769480 | tf_op jit(solution)/shard_map/ppermute | solution.py:693
  90.4 104.9 %all-to-all-start = ((bf16[32,40,1536]{2,1,0:T(8,128)(2,1)}), bf16[32,40,1536]{2,1,0:T(8,128)(2,1)}, u32[]{:S(2)}, u32[]{:S(2)}) async-start(bf16[32,40,1536]{2,1,0:T(8,128)(2,1)} %bitcast.217), calls=%async_computation | async-start | bytes 7864320 | tf_op jit(solution)/shard_map/all_to_all | solution.py:66
  145.4 39.1 %collective-permute-start.3 = (bf16[384,768]{1,0:T(8,128)(2,1)S(1)}, bf16[384,768]{1,0:T(8,128)(2,1)S(1)}, u32[]{:S(2)}, u32[]{:S(2)}) collective-permute-start(bf16[384,768]{1,0:T(8,128)(2,1)S(1)} %get-tuple-element.168), channel_id=1, source_target_pairs={{0,8},{8,16},{16,24},{24,0},{1,9},{9,17},{17,25},{25,1},{2,10},{10... | collective-permute-start | bytes 1769480 | tf_op jit(solution)/shard_map/ppermute | solution.py:693
  145.4 49.1 %collective-permute-start.4 = (bf16[384,768]{1,0:T(8,128)(2,1)S(1)}, bf16[384,768]{1,0:T(8,128)(2,1)S(1)}, u32[]{:S(2)}, u32[]{:S(2)}) collective-permute-start(bf16[384,768]{1,0:T(8,128)(2,1)S(1)} %get-tuple-element.167), channel_id=1, source_target_pairs={{0,16},{8,24},{16,0},{24,8},{1,17},{9,25},{17,1},{25,9},{2,18},{10... | collective-permute-start | bytes 1769480 | tf_op jit(solution)/shard_map/ppermute | solution.py:693
  164.3 31.1 %collective-permute-start.5 = (bf16[384,768]{1,0:T(8,128)(2,1)S(1)}, bf16[384,768]{1,0:T(8,128)(2,1)}, u32[]{:S(2)}, u32[]{:S(2)}) collective-permute-start(bf16[384,768]{1,0:T(8,128)(2,1)S(1)} %get-tuple-element.166), channel_id=1, source_target_pairs={{0,24},{8,0},{16,8},{24,16},{1,25},{9,1},{17,9},{25,17},{2,26},{10... | collective-permute-start | bytes 1769480 | tf_op jit(solution)/shard_map/ppermute | solution.py:693
  195.4 62.7 %all-to-all-start.1 = ((bf16[32,24,1536]{2,1,0:T(8,128)(2,1)}), bf16[32,24,1536]{2,1,0:T(8,128)(2,1)}, u32[]{:S(2)}, u32[]{:S(2)}) async-start(bf16[32,24,1536]{2,1,0:T(8,128)(2,1)} %bitcast.16), calls=%async_computation.1 | async-start | bytes 4718592 | tf_op jit(solution)/shard_map/all_to_all | solution.py:66
  211.6 93.9 %copy-start = (bf16[32,16,1536]{2,1,0:T(8,128)(2,1)}, bf16[32,16,1536]{2,1,0:T(8,128)(2,1)S(1)}, u32[]{:S(2)}) copy-start(bf16[32,16,1536]{2,1,0:T(8,128)(2,1)S(1)} %slice.30) | copy-start | bytes 4718596
  214.3 27.4 %collective-permute-start.6 = (bf16[192,1536]{1,0:T(8,128)(2,1)S(1)}, bf16[192,1536]{1,0:T(8,128)(2,1)S(1)}, u32[]{:S(2)}, u32[]{:S(2)}) collective-permute-start(bf16[192,1536]{1,0:T(8,128)(2,1)S(1)} %get-tuple-element.164), channel_id=1, source_target_pairs={{0,8},{8,16},{16,24},{24,0},{1,9},{9,17},{17,25},{25,1},{2,10},{10... | collective-permute-start | bytes 1769480 | tf_op jit(solution)/shard_map/ppermute | solution.py:693
  216.0 39.3 %collective-permute-start.7 = (bf16[192,1536]{1,0:T(8,128)(2,1)S(1)}, bf16[192,1536]{1,0:T(8,128)(2,1)S(1)}, u32[]{:S(2)}, u32[]{:S(2)}) collective-permute-start(bf16[192,1536]{1,0:T(8,128)(2,1)S(1)} %get-tuple-element.163), channel_id=1, source_target_pairs={{0,16},{8,24},{16,0},{24,8},{1,17},{9,25},{17,1},{25,9},{2,18},{10... | collective-permute-start | bytes 1769480 | tf_op jit(solution)/shard_map/ppermute | solution.py:693
  217.5 39.7 %collective-permute-start.8 = (bf16[192,1536]{1,0:T(8,128)(2,1)S(1)}, bf16[192,1536]{1,0:T(8,128)(2,1)S(1)}, u32[]{:S(2)}, u32[]{:S(2)}) collective-permute-start(bf16[192,1536]{1,0:T(8,128)(2,1)S(1)} %get-tuple-element.162), channel_id=1, source_target_pairs={{0,24},{8,0},{16,8},{24,16},{1,25},{9,1},{17,9},{25,17},{2,26},{10... | collective-permute-start | bytes 1769480 | tf_op jit(solution)/shard_map/ppermute | solution.py:693
  258.1 43.2 %all-to-all-start.2 = ((bf16[32,16,1536]{2,1,0:T(8,128)(2,1)}), bf16[32,16,1536]{2,1,0:T(8,128)(2,1)S(1)}, u32[]{:S(2)}, u32[]{:S(2)}) async-start(bf16[32,16,1536]{2,1,0:T(8,128)(2,1)} %bitcast.215), calls=%async_computation.2 | async-start | bytes 3145728 | tf_op jit(solution)/shard_map/all_to_all | solution.py:66
  301.3 64.7 %all-to-all-start.3 = ((bf16[32,24,1536]{2,1,0:T(8,128)(2,1)}), bf16[32,24,1536]{2,1,0:T(8,128)(2,1)}, u32[]{:S(2)}, u32[]{:S(2)}) async-start(bf16[32,24,1536]{2,1,0:T(8,128)(2,1)} %bitcast.220), calls=%async_computation.3 | async-start | bytes 4718592 | tf_op jit(solution)/shard_map/all_to_all | solution.py:66
  327.6 22.8 %collective-permute-start.10 = (bf16[384,768]{1,0:T(8,128)(2,1)S(1)}, bf16[384,768]{1,0:T(8,128)(2,1)}, u32[]{:S(2)}, u32[]{:S(2)}) collective-permute-start(bf16[384,768]{1,0:T(8,128)(2,1)S(1)} %get-tuple-element.159), channel_id=1, source_target_pairs={{0,16},{8,24},{16,0},{24,8},{1,17},{9,25},{17,1},{25,9},{2,18},{10... | collective-permute-start | bytes 1769480 | tf_op jit(solution)/shard_map/ppermute | solution.py:693
  329.3 21.1 %collective-permute-start.11 = (bf16[384,768]{1,0:T(8,128)(2,1)S(1)}, bf16[384,768]{1,0:T(8,128)(2,1)}, u32[]{:S(2)}, u32[]{:S(2)}) collective-permute-start(bf16[384,768]{1,0:T(8,128)(2,1)S(1)} %get-tuple-element.158), channel_id=1, source_target_pairs={{0,24},{8,0},{16,8},{24,16},{1,25},{9,1},{17,9},{25,17},{2,26},{10... | collective-permute-start | bytes 1769480 | tf_op jit(solution)/shard_map/ppermute | solution.py:693
  330.8 35.2 %collective-permute-start.9 = (bf16[384,768]{1,0:T(8,128)(2,1)S(1)}, bf16[384,768]{1,0:T(8,128)(2,1)}, u32[]{:S(2)}, u32[]{:S(2)}) collective-permute-start(bf16[384,768]{1,0:T(8,128)(2,1)S(1)} %get-tuple-element.160), channel_id=1, source_target_pairs={{0,8},{8,16},{16,24},{24,0},{1,9},{9,17},{17,25},{25,1},{2,10},{10... | collective-permute-start | bytes 1769480 | tf_op jit(solution)/shard_map/ppermute | solution.py:693
  366.0 53.0 %all-to-all-start.4 = ((bf16[32,16,1536]{2,1,0:T(8,128)(2,1)}), bf16[32,16,1536]{2,1,0:T(8,128)(2,1)}, u32[]{:S(2)}, u32[]{:S(2)}) async-start(bf16[32,16,1536]{2,1,0:T(8,128)(2,1)} %bitcast.223), calls=%async_computation.4 | async-start | bytes 3145728 | tf_op jit(solution)/shard_map/all_to_all | solution.py:66
  372.0 33.8 %collective-permute-start.12 = (bf16[384,768]{1,0:T(8,128)(2,1)S(1)}, bf16[384,768]{1,0:T(8,128)(2,1)S(1)}, u32[]{:S(2)}, u32[]{:S(2)}) collective-permute-start(bf16[384,768]{1,0:T(8,128)(2,1)S(1)} %get-tuple-element.157), channel_id=1, source_target_pairs={{0,8},{8,16},{16,24},{24,0},{1,9},{9,17},{17,25},{25,1},{2,10},{10... | collective-permute-start | bytes 1769480 | tf_op jit(solution)/shard_map/ppermute | solution.py:693
  373.7 43.0 %collective-permute-start.13 = (bf16[384,768]{1,0:T(8,128)(2,1)S(1)}, bf16[384,768]{1,0:T(8,128)(2,1)S(1)}, u32[]{:S(2)}, u32[]{:S(2)}) collective-permute-start(bf16[384,768]{1,0:T(8,128)(2,1)S(1)} %get-tuple-element.156), channel_id=1, source_target_pairs={{0,16},{8,24},{16,0},{24,8},{1,17},{9,25},{17,1},{25,9},{2,18},{10... | collective-permute-start | bytes 1769480 | tf_op jit(solution)/shard_map/ppermute | solution.py:693
  375.2 42.6 %collective-permute-start.14 = (bf16[384,768]{1,0:T(8,128)(2,1)S(1)}, bf16[384,768]{1,0:T(8,128)(2,1)S(1)}, u32[]{:S(2)}, u32[]{:S(2)}) collective-permute-start(bf16[384,768]{1,0:T(8,128)(2,1)S(1)} %get-tuple-element.155), channel_id=1, source_target_pairs={{0,24},{8,0},{16,8},{24,16},{1,25},{9,1},{17,9},{25,17},{2,26},{10... | collective-permute-start | bytes 1769480 | tf_op jit(solution)/shard_map/ppermute | solution.py:693
  418.9 161.7 %all-to-all-start.5 = ((bf16[32,40,1536]{2,1,0:T(8,128)(2,1)}), bf16[32,40,1536]{2,1,0:T(8,128)(2,1)}, u32[]{:S(2)}, u32[]{:S(2)}) async-start(bf16[32,40,1536]{2,1,0:T(8,128)(2,1)} %bitcast.216), calls=%async_computation.5 | async-start | bytes 7864320 | tf_op jit(solution)/shard_map/all_to_all | solution.py:66
  (60 other events, 777.0 us)

commit v19 on v18

--- a/solution.py
+++ b/solution.py
@@ -160,7 +160,7 @@
 
 def in_steps(count, stages, after=None):
     for step in range((count + 1) // 2 + len(stages) - 1):
-        if after is not None and step == (count + 1) // 2 + 1:
+        if after is not None and step == 1:
             after()
         for behind, stage in enumerate(stages):
             for i in (2 * (step - behind), 2 * (step - behind) + 1):
@@ -466,7 +466,7 @@
                 acc_ref[h] = acc_ref[h] * shrink + tn(values, weights.astype(BF16))
                 return carry
 
-            lax.fori_loop(0, group, one_head, 0, unroll=2)
+            lax.fori_loop(0, group, one_head, 0, unroll=3)
 
     key_block(me)
 
@@ -572,7 +572,7 @@
                 dq_ref[:, cols] += tn(score_grad, keys)
                 return carry
 
-            lax.fori_loop(0, group, one_head, 0, unroll=3)
+            lax.fori_loop(0, group, one_head, 0, unroll=6)
         part_ref[:, :kv_width] = part_ref[:, :kv_width] * scale
 
     def to_owner(j):

time: 597 us -> 600 us (level)
  no operation moved by 1% of the time
where the time goes in v19:
time: 600 us; the launch traced here: 591 us
  Pallas kernels  259 us (43%)
  waiting for transfers between devices  105 us (18%)
  matrix products  85.5 us (14%)
  starting transfers between devices  69.6 us (12%)
  local copies, waits for them, and re-layouts  42.2 us (7%)
  other arithmetic  25.7 us (4%)
    pallas_call x1, Pallas kernels, staged_scatter(): pl.pallas_call(functools.partial(scatter_kernel, line, chunks, n, len(ext...  102 us
    ppermute x15, waiting for transfers between devices, seq_permutes(): lax.ppermute(block_for(lax.rem(me + step, count)), 'seq', ring)  92.3 us
    dot_general x23, matrix products, dot(): lax.dot_general(left, right, (contract, ((), ())), preferred_element_type...  85.5 us
    pallas_call x1, Pallas kernels, staged_gather(): pl.pallas_call(functools.partial(gather_kernel, line, chunks, n, len(extr...  69.3 us
    pallas_call x1, Pallas kernels, attention(): pl.pallas_call(functools.partial(attention_kernel, count, heads, kv_heads...  40.5 us
    ppermute x15, starting transfers between devices, seq_permutes(): lax.ppermute(block_for(lax.rem(me + step, count)), 'seq', ring)  37 us
    all_to_all x6, starting transfers between devices, swap(): return lax.all_to_all(blocks, axes, split_axis=0, concat_axis=0, tiled=True)  32.6 us
    pallas_call x1, Pallas kernels, attention_back(): pl.pallas_call(functools.partial(attention_back_kernel, count, heads, kv_...  32.5 us
  transfers between devices with their start and end apart: 21, of which 10 were waited for; matrix products, arithmetic and copies ran while one was open for 24% of the time, Pallas kernels for 44%

profile of v19, /device:TPU:0, one launch (start us, length us, event | category | flops | bytes accessed | tf_op | source)
XLA Modules:
  0.0 590.5 jit_solution(1830363930028160726)
XLA Ops:
  15.1 69.3 %gather_attention_weights.1 = (bf16[2,2,4,2,48,2048]{5,4,3,2,1,0:T(8,128)(2,1)}, bf16[2,2,4,2,48,128]{5,4,3,2,1,0:T(8,128)(2,1)}, bf16[2,2,4,2,48,1536]{5,4,3,2,1,0:T(8,128)(2,1)}) custom-call(bf16[48,2048]{1,0:T(8,128)(2,1)} %pad_maximum_fusion.1.refs_0_, bf16[48,128]{1,0:T(8,128)(2,1)} %maximum_maximum_fusion.refs_1_, bf16[48,1536]{1,0:T(8,128)(2,1)} %refs_2_.1), custom_call_target="tpu_custom_call" | custom-call | bytes 11403264 | tf_op jit(solution)/shard_map/gather_attention_weights/pallas_call | solution.py:254
  90.4 5.1 all-to-all-start
  98.7 4.6 fusion.24.refs_1_
  103.4 40.5 %attention_forward.1 = (bf16[256,1536]{1,0:T(8,128)(2,1)S(1)}, f32[12,256]{1,0:T(8,128)S(1)}, bf16[256,1536]{1,0:T(8,128)(2,1)S(1)}, bf16[4,256,512]{2,1,0:T(8,128)(2,1)S(1)}) custom-call(s32[1]{0:T(128)} %copy.69.refs_0_, f32[256,2048]{1,0:T(8,128)S(1)} %fusion.24.refs_1_, f32[256,128]{1,0:T(8,128)S(1)} %get-tuple-element.186.refs_2_.refs_6_, ...), custom_call_target="tpu_custom_call" | custom-call | bytes 1048576 | tf_op jit(solution)/shard_map/attention_forward/pallas_call | solution.py:508
  145.1 17.9 %collective-permute-start.4 = (bf16[384,768]{1,0:T(8,128)(2,1)S(1)}, bf16[384,768]{1,0:T(8,128)(2,1)S(1)}, u32[]{:S(2)}, u32[]{:S(2)}) collective-permute-start(bf16[384,768]{1,0:T(8,128)(2,1)S(1)} %get-tuple-element.167), channel_id=1, source_target_pairs={{0,16},{8,24},{16,0},{24,8},{1,17},{9,25},{17,1},{25,9},{2,18},{10... | collective-permute-start | bytes 1769480 | tf_op jit(solution)/shard_map/ppermute | solution.py:693
  171.1 12.3 %collective-permute-done.3 = bf16[384,768]{1,0:T(8,128)(2,1)S(1)} collective-permute-done((bf16[384,768]{1,0:T(8,128)(2,1)S(1)}, bf16[384,768]{1,0:T(8,128)(2,1)S(1)}, u32[]{:S(2)}, u32[]{:S(2)}) %collective-permute-start.3) | collective-permute-done | bytes 589856 | tf_op jit(solution)/shard_map/ppermute | solution.py:693
  184.2 9.2 %collective-permute-done.4 = bf16[384,768]{1,0:T(8,128)(2,1)S(1)} collective-permute-done((bf16[384,768]{1,0:T(8,128)(2,1)S(1)}, bf16[384,768]{1,0:T(8,128)(2,1)S(1)}, u32[]{:S(2)}, u32[]{:S(2)}) %collective-permute-start.4) | collective-permute-done | bytes 589856 | tf_op jit(solution)/shard_map/ppermute | solution.py:693
  194.2 5.7 all-to-all-start.1
  224.3 16.8 %collective-permute-done.6 = bf16[192,1536]{1,0:T(8,128)(2,1)S(1)} collective-permute-done((bf16[192,1536]{1,0:T(8,128)(2,1)S(1)}, bf16[192,1536]{1,0:T(8,128)(2,1)S(1)}, u32[]{:S(2)}, u32[]{:S(2)}) %collective-permute-start.6) | collective-permute-done | bytes 589856 | tf_op jit(solution)/shard_map/ppermute | solution.py:693
  241.9 12.7 %collective-permute-done.7 = bf16[192,1536]{1,0:T(8,128)(2,1)S(1)} collective-permute-done((bf16[192,1536]{1,0:T(8,128)(2,1)S(1)}, bf16[192,1536]{1,0:T(8,128)(2,1)S(1)}, u32[]{:S(2)}, u32[]{:S(2)}) %collective-permute-start.7) | collective-permute-done | bytes 589856 | tf_op jit(solution)/shard_map/ppermute | solution.py:693
  257.4 6.1 %all-to-all-start.2 = ((bf16[32,16,1536]{2,1,0:T(8,128)(2,1)}), bf16[32,16,1536]{2,1,0:T(8,128)(2,1)S(1)}, u32[]{:S(2)}, u32[]{:S(2)}) async-start(bf16[32,16,1536]{2,1,0:T(8,128)(2,1)} %bitcast.215), calls=%async_computation.2 | async-start | bytes 3145728 | tf_op jit(solution)/shard_map/all_to_all | solution.py:66
  272.3 6.1 %multiply_convert_fusion.2 = (bf16[768,768]{1,0:T(8,128)(2,1)}, bf16[768,768]{1,0:T(8,128)(2,1)S(1)}, bf16[768,768]{1,0:T(8,128)(2,1)S(1)}) fusion(f32[768,768]{1,0:T(8,128)S(1)} %fusion.41, f32[768,768]{1,0:T(8,128)S(1)} %fusion.42, bf16[768,1536]{1,0:T(8,128)(2,1)} %bitcast.40.refs_0_, bf16[1536,768]{1,0:T(8,128)(2,1)} %bitcast.32), kind=kOutput, calls=%fused_computation.28 | convolution fusion | flops 1820786688 | bytes 12976128 | tf_op jit(solution)/shard_map/dot_general | solution.py:34
  283.0 5.1 add_convert_fusion
  288.0 12.9 %all-to-all-done.2 = bf16[32,16,1536]{2,1,0:T(8,128)(2,1)S(1)} async-done(((bf16[32,16,1536]{2,1,0:T(8,128)(2,1)}), bf16[32,16,1536]{2,1,0:T(8,128)(2,1)S(1)}, u32[]{:S(2)}, u32[]{:S(2)}) %all-to-all-start.2) | async-done | bytes 1572896 | tf_op jit(solution)/shard_map/all_to_all | solution.py:66
  315.0 9.8 %gate_up_grads.1 = (bf16[1536,768]{1,0:T(8,128)(2,1)}, bf16[1536,768]{1,0:T(8,128)(2,1)}) custom-call(bf16[768,1536]{1,0:T(8,128)(2,1)} %bitcast.40.refs_0_, bf16[512,1536]{1,0:T(8,128)(2,1)S(1)} %bitcast.209, bf16[768,768]{1,0:T(8,128)(2,1)S(1)} %copy-done.8, bf16[512,768]{1,0:T(8,128)(2,1)S(1)} %get-tuple-element.153.refs_3_, ...), custom_call_target="tpu_custom_call" | custom-call | bytes 1048576 | tf_op jit(solution)/shard_map/gate_up_grads/pallas_call | solution.py:675
  338.6 11.6 %collective-permute-done.10 = bf16[384,768]{1,0:T(8,128)(2,1)} collective-permute-done((bf16[384,768]{1,0:T(8,128)(2,1)S(1)}, bf16[384,768]{1,0:T(8,128)(2,1)}, u32[]{:S(2)}, u32[]{:S(2)}) %collective-permute-start.10) | collective-permute-done | bytes 589856 | tf_op jit(solution)/shard_map/ppermute | solution.py:693
  350.2 15.5 %collective-permute-done.9 = bf16[384,768]{1,0:T(8,128)(2,1)} collective-permute-done((bf16[384,768]{1,0:T(8,128)(2,1)S(1)}, bf16[384,768]{1,0:T(8,128)(2,1)}, u32[]{:S(2)}, u32[]{:S(2)}) %collective-permute-start.9) | collective-permute-done | bytes 589856 | tf_op jit(solution)/shard_map/ppermute | solution.py:693
  365.7 5.9 all-to-all-start.4
  382.4 6.4 %convolution_convert_fusion.2 = bf16[1280,1536]{1,0:T(8,128)(2,1)} fusion(bf16[1280,768]{1,0:T(8,128)(2,1)S(1)} %bitcast.222, bf16[768,1536]{1,0:T(8,128)(2,1)} %bitcast.39), kind=kOutput, calls=%fused_computation.4 | convolution fusion | flops 3021864960 | bytes 8257536 | tf_op jit(solution)/shard_map/dot_general | solution.py:34
  396.8 5.4 down_grads.1
  406.7 9.8 %collective-permute-done.13 = bf16[384,768]{1,0:T(8,128)(2,1)S(1)} collective-permute-done((bf16[384,768]{1,0:T(8,128)(2,1)S(1)}, bf16[384,768]{1,0:T(8,128)(2,1)S(1)}, u32[]{:S(2)}, u32[]{:S(2)}) %collective-permute-start.13) | collective-permute-done | bytes 589856 | tf_op jit(solution)/shard_map/ppermute | solution.py:693
  418.7 5.6 all-to-all-start.5
  434.9 32.5 %attention_backward.1 = bf16[256,2048]{1,0:T(8,128)(2,1)S(1)} custom-call(s32[1]{0:T(128)} %copy.69.refs_0_, bf16[256,1536]{1,0:T(8,128)(2,1)S(1)} %copy-done.16, bf16[1024,512]{1,0:T(8,128)(2,1)S(1)} %bitcast.212, bf16[256,1536]{1,0:T(8,128)(2,1)S(1)} %convolution_convert_fusion.5.refs_3_, f32[12,256]{1,0:T(8,128)S(1)} %get-tuple-element.129.refs_4_, ...), custom_call_target="tpu_custom_call" | custom-call | flops 4026531840 | bytes 1048576 | tf_op jit(solution)/shard_map/attention_backward/pallas_call | solution.py:640
  476.3 102.0 %scatter_attention_grads.1 = (f32[48,1536]{1,0:T(8,128)S(1)}, f32[48,128]{1,0:T(8,128)S(1)}, f32[48,2048]{1,0:T(8,128)S(1)}, bf16[4,192,1536]{2,1,0:T(8,128)(2,1)S(1)}) custom-call(bf16[2,2,4,2,48,1536]{5,4,3,2,1,0:T(8,128)(2,1)S(1)} %bitcast.203, bf16[2,2,4,2,48,128]{5,4,3,2,1,0:T(8,128)(2,1)S(1)} %select_convert_fusion.refs_1_, ...), custom_call_target="tpu_custom_call" | custom-call | bytes 11403264 | tf_op jit(solution)/shard_map/scatter_attention_grads/pallas_call | solution.py:376
  (251 shorter events, 159.0 us)
Async XLA Ops:
  3.7 80.7 %copy-start.55 = (f32[1,256,4]{1,2,0:T(4,128)S(1)}, f32[1,256,4]{1,2,0:T(4,128)}, u32[]{:S(2)}) copy-start(f32[1,256,4]{1,2,0:T(4,128)} %param.18) | copy-start | bytes 12292
  3.7 82.7 %copy-start.33 = (bf16[1,256,1536]{2,1,0:T(8,128)(2,1)S(1)}, bf16[1,256,1536]{2,1,0:T(8,128)(2,1)}, u32[]{:S(2)}) copy-start(bf16[1,256,1536]{2,1,0:T(8,128)(2,1)} %param.29) | copy-start | bytes 2359300
  3.7 85.9 %collective-permute-start = (bf16[384,768]{1,0:T(8,128)(2,1)}, bf16[384,768]{1,0:T(8,128)(2,1)S(1)}, u32[]{:S(2)}, u32[]{:S(2)}) collective-permute-start(bf16[384,768]{1,0:T(8,128)(2,1)} %get-tuple-element.171), channel_id=1, source_target_pairs={{0,8},{8,16},{16,24},{24,0},{1,9},{9,17},{17,25},{25,1},{2,10},{10... | collective-permute-start | bytes 1769480 | tf_op jit(solution)/shard_map/ppermute | solution.py:693
  6.6 83.0 %collective-permute-start.1 = (bf16[384,768]{1,0:T(8,128)(2,1)}, bf16[384,768]{1,0:T(8,128)(2,1)S(1)}, u32[]{:S(2)}, u32[]{:S(2)}) collective-permute-start(bf16[384,768]{1,0:T(8,128)(2,1)} %get-tuple-element.173), channel_id=1, source_target_pairs={{0,16},{8,24},{16,0},{24,8},{1,17},{9,25},{17,1},{25,9},{2,18},{10... | collective-permute-start | bytes 1769480 | tf_op jit(solution)/shard_map/ppermute | solution.py:693
  8.1 81.5 %collective-permute-start.2 = (bf16[384,768]{1,0:T(8,128)(2,1)}, bf16[384,768]{1,0:T(8,128)(2,1)}, u32[]{:S(2)}, u32[]{:S(2)}) collective-permute-start(bf16[384,768]{1,0:T(8,128)(2,1)} %get-tuple-element.170), channel_id=1, source_target_pairs={{0,24},{8,0},{16,8},{24,16},{1,25},{9,1},{17,9},{25,17},{2,26},{10... | collective-permute-start | bytes 1769480 | tf_op jit(solution)/shard_map/ppermute | solution.py:693
  90.4 103.8 %all-to-all-start = ((bf16[32,40,1536]{2,1,0:T(8,128)(2,1)}), bf16[32,40,1536]{2,1,0:T(8,128)(2,1)}, u32[]{:S(2)}, u32[]{:S(2)}) async-start(bf16[32,40,1536]{2,1,0:T(8,128)(2,1)} %bitcast.217), calls=%async_computation | async-start | bytes 7864320 | tf_op jit(solution)/shard_map/all_to_all | solution.py:66
  145.1 38.3 %collective-permute-start.3 = (bf16[384,768]{1,0:T(8,128)(2,1)S(1)}, bf16[384,768]{1,0:T(8,128)(2,1)S(1)}, u32[]{:S(2)}, u32[]{:S(2)}) collective-permute-start(bf16[384,768]{1,0:T(8,128)(2,1)S(1)} %get-tuple-element.168), channel_id=1, source_target_pairs={{0,8},{8,16},{16,24},{24,0},{1,9},{9,17},{17,25},{25,1},{2,10},{10... | collective-permute-start | bytes 1769480 | tf_op jit(solution)/shard_map/ppermute | solution.py:693
  145.1 48.3 %collective-permute-start.4 = (bf16[384,768]{1,0:T(8,128)(2,1)S(1)}, bf16[384,768]{1,0:T(8,128)(2,1)S(1)}, u32[]{:S(2)}, u32[]{:S(2)}) collective-permute-start(bf16[384,768]{1,0:T(8,128)(2,1)S(1)} %get-tuple-element.167), channel_id=1, source_target_pairs={{0,16},{8,24},{16,0},{24,8},{1,17},{9,25},{17,1},{25,9},{2,18},{10... | collective-permute-start | bytes 1769480 | tf_op jit(solution)/shard_map/ppermute | solution.py:693
  163.1 31.2 %collective-permute-start.5 = (bf16[384,768]{1,0:T(8,128)(2,1)S(1)}, bf16[384,768]{1,0:T(8,128)(2,1)}, u32[]{:S(2)}, u32[]{:S(2)}) collective-permute-start(bf16[384,768]{1,0:T(8,128)(2,1)S(1)} %get-tuple-element.166), channel_id=1, source_target_pairs={{0,24},{8,0},{16,8},{24,16},{1,25},{9,1},{17,9},{25,17},{2,26},{10... | collective-permute-start | bytes 1769480 | tf_op jit(solution)/shard_map/ppermute | solution.py:693
  194.2 63.2 %all-to-all-start.1 = ((bf16[32,24,1536]{2,1,0:T(8,128)(2,1)}), bf16[32,24,1536]{2,1,0:T(8,128)(2,1)}, u32[]{:S(2)}, u32[]{:S(2)}) async-start(bf16[32,24,1536]{2,1,0:T(8,128)(2,1)} %bitcast.16), calls=%async_computation.1 | async-start | bytes 4718592 | tf_op jit(solution)/shard_map/all_to_all | solution.py:66
  210.9 94.3 %copy-start = (bf16[32,16,1536]{2,1,0:T(8,128)(2,1)}, bf16[32,16,1536]{2,1,0:T(8,128)(2,1)S(1)}, u32[]{:S(2)}) copy-start(bf16[32,16,1536]{2,1,0:T(8,128)(2,1)S(1)} %slice.30) | copy-start | bytes 4718596
  213.6 27.4 %collective-permute-start.6 = (bf16[192,1536]{1,0:T(8,128)(2,1)S(1)}, bf16[192,1536]{1,0:T(8,128)(2,1)S(1)}, u32[]{:S(2)}, u32[]{:S(2)}) collective-permute-start(bf16[192,1536]{1,0:T(8,128)(2,1)S(1)} %get-tuple-element.164), channel_id=1, source_target_pairs={{0,8},{8,16},{16,24},{24,0},{1,9},{9,17},{17,25},{25,1},{2,10},{10... | collective-permute-start | bytes 1769480 | tf_op jit(solution)/shard_map/ppermute | solution.py:693
  215.3 39.3 %collective-permute-start.7 = (bf16[192,1536]{1,0:T(8,128)(2,1)S(1)}, bf16[192,1536]{1,0:T(8,128)(2,1)S(1)}, u32[]{:S(2)}, u32[]{:S(2)}) collective-permute-start(bf16[192,1536]{1,0:T(8,128)(2,1)S(1)} %get-tuple-element.163), channel_id=1, source_target_pairs={{0,16},{8,24},{16,0},{24,8},{1,17},{9,25},{17,1},{25,9},{2,18},{10... | collective-permute-start | bytes 1769480 | tf_op jit(solution)/shard_map/ppermute | solution.py:693
  216.8 39.7 %collective-permute-start.8 = (bf16[192,1536]{1,0:T(8,128)(2,1)S(1)}, bf16[192,1536]{1,0:T(8,128)(2,1)S(1)}, u32[]{:S(2)}, u32[]{:S(2)}) collective-permute-start(bf16[192,1536]{1,0:T(8,128)(2,1)S(1)} %get-tuple-element.162), channel_id=1, source_target_pairs={{0,24},{8,0},{16,8},{24,16},{1,25},{9,1},{17,9},{25,17},{2,26},{10... | collective-permute-start | bytes 1769480 | tf_op jit(solution)/shard_map/ppermute | solution.py:693
  257.4 43.6 %all-to-all-start.2 = ((bf16[32,16,1536]{2,1,0:T(8,128)(2,1)}), bf16[32,16,1536]{2,1,0:T(8,128)(2,1)S(1)}, u32[]{:S(2)}, u32[]{:S(2)}) async-start(bf16[32,16,1536]{2,1,0:T(8,128)(2,1)} %bitcast.215), calls=%async_computation.2 | async-start | bytes 3145728 | tf_op jit(solution)/shard_map/all_to_all | solution.py:66
  301.0 64.7 %all-to-all-start.3 = ((bf16[32,24,1536]{2,1,0:T(8,128)(2,1)}), bf16[32,24,1536]{2,1,0:T(8,128)(2,1)}, u32[]{:S(2)}, u32[]{:S(2)}) async-start(bf16[32,24,1536]{2,1,0:T(8,128)(2,1)} %bitcast.220), calls=%async_computation.3 | async-start | bytes 4718592 | tf_op jit(solution)/shard_map/all_to_all | solution.py:66
  327.4 22.8 %collective-permute-start.10 = (bf16[384,768]{1,0:T(8,128)(2,1)S(1)}, bf16[384,768]{1,0:T(8,128)(2,1)}, u32[]{:S(2)}, u32[]{:S(2)}) collective-permute-start(bf16[384,768]{1,0:T(8,128)(2,1)S(1)} %get-tuple-element.159), channel_id=1, source_target_pairs={{0,16},{8,24},{16,0},{24,8},{1,17},{9,25},{17,1},{25,9},{2,18},{10... | collective-permute-start | bytes 1769480 | tf_op jit(solution)/shard_map/ppermute | solution.py:693
  329.1 21.1 %collective-permute-start.11 = (bf16[384,768]{1,0:T(8,128)(2,1)S(1)}, bf16[384,768]{1,0:T(8,128)(2,1)}, u32[]{:S(2)}, u32[]{:S(2)}) collective-permute-start(bf16[384,768]{1,0:T(8,128)(2,1)S(1)} %get-tuple-element.158), channel_id=1, source_target_pairs={{0,24},{8,0},{16,8},{24,16},{1,25},{9,1},{17,9},{25,17},{2,26},{10... | collective-permute-start | bytes 1769480 | tf_op jit(solution)/shard_map/ppermute | solution.py:693
  330.5 35.2 %collective-permute-start.9 = (bf16[384,768]{1,0:T(8,128)(2,1)S(1)}, bf16[384,768]{1,0:T(8,128)(2,1)}, u32[]{:S(2)}, u32[]{:S(2)}) collective-permute-start(bf16[384,768]{1,0:T(8,128)(2,1)S(1)} %get-tuple-element.160), channel_id=1, source_target_pairs={{0,8},{8,16},{16,24},{24,0},{1,9},{9,17},{17,25},{25,1},{2,10},{10... | collective-permute-start | bytes 1769480 | tf_op jit(solution)/shard_map/ppermute | solution.py:693
  365.7 52.9 %all-to-all-start.4 = ((bf16[32,16,1536]{2,1,0:T(8,128)(2,1)}), bf16[32,16,1536]{2,1,0:T(8,128)(2,1)}, u32[]{:S(2)}, u32[]{:S(2)}) async-start(bf16[32,16,1536]{2,1,0:T(8,128)(2,1)} %bitcast.223), calls=%async_computation.4 | async-start | bytes 3145728 | tf_op jit(solution)/shard_map/all_to_all | solution.py:66
  371.7 33.8 %collective-permute-start.12 = (bf16[384,768]{1,0:T(8,128)(2,1)S(1)}, bf16[384,768]{1,0:T(8,128)(2,1)S(1)}, u32[]{:S(2)}, u32[]{:S(2)}) collective-permute-start(bf16[384,768]{1,0:T(8,128)(2,1)S(1)} %get-tuple-element.157), channel_id=1, source_target_pairs={{0,8},{8,16},{16,24},{24,0},{1,9},{9,17},{17,25},{25,1},{2,10},{10... | collective-permute-start | bytes 1769480 | tf_op jit(solution)/shard_map/ppermute | solution.py:693
  373.5 43.0 %collective-permute-start.13 = (bf16[384,768]{1,0:T(8,128)(2,1)S(1)}, bf16[384,768]{1,0:T(8,128)(2,1)S(1)}, u32[]{:S(2)}, u32[]{:S(2)}) collective-permute-start(bf16[384,768]{1,0:T(8,128)(2,1)S(1)} %get-tuple-element.156), channel_id=1, source_target_pairs={{0,16},{8,24},{16,0},{24,8},{1,17},{9,25},{17,1},{25,9},{2,18},{10... | collective-permute-start | bytes 1769480 | tf_op jit(solution)/shard_map/ppermute | solution.py:693
  375.0 42.6 %collective-permute-start.14 = (bf16[384,768]{1,0:T(8,128)(2,1)S(1)}, bf16[384,768]{1,0:T(8,128)(2,1)S(1)}, u32[]{:S(2)}, u32[]{:S(2)}) collective-permute-start(bf16[384,768]{1,0:T(8,128)(2,1)S(1)} %get-tuple-element.155), channel_id=1, source_target_pairs={{0,24},{8,0},{16,8},{24,16},{1,25},{9,1},{17,9},{25,17},{2,26},{10... | collective-permute-start | bytes 1769480 | tf_op jit(solution)/shard_map/ppermute | solution.py:693
  418.7 164.9 %all-to-all-start.5 = ((bf16[32,40,1536]{2,1,0:T(8,128)(2,1)}), bf16[32,40,1536]{2,1,0:T(8,128)(2,1)}, u32[]{:S(2)}, u32[]{:S(2)}) async-start(bf16[32,40,1536]{2,1,0:T(8,128)(2,1)} %bitcast.216), calls=%async_computation.5 | async-start | bytes 7864320 | tf_op jit(solution)/shard_map/all_to_all | solution.py:66
  (60 other events, 770.6 us)
